TPU v7x, 32 devices: a whole 2x2x4 slice. The times are simulated.
32 devices in a mesh: dp: 8 (over y, x, core), fsdp: 4 (over z).
Axes of the slice: x: 2, y: 2, z: 4, core: 2. Of those that a mesh axis runs over, the one named last changes fastest.
Arguments:
- latents: bfloat16 [16, 512, 1024], P('dp', 'fsdp'), may hold values from -6 to 6
- pixels: bfloat16 [16384, 261], P('dp'), may hold values from -6 to 6
- lengths: int32 [8, 2], P('dp'), may hold values from 1 to 1280, 1792 in all within a row
- pix_gain: bfloat16 [261], replicated, may hold values from 0.099609375 to 1.8984375
- pix_bias: bfloat16 [261], replicated, may hold values from -1.5 to 1.5
- pix_kv: bfloat16 [2, 261, 1024], P(None, None, ('dp', 'fsdp')), may hold values from -0.375 to 0.375
- enc_query: bfloat16 [1024, 1024], P(('dp', 'fsdp')), may hold values from -0.1875 to 0.1875
- enc_out: bfloat16 [1024, 1024], P(('dp', 'fsdp')), may hold values from -3 to 3
- enc_mlp: bfloat16 [2, 1024, 1024], P(None, ('dp', 'fsdp')), may hold values from -0.1875 to 0.1875
- enc_gains: bfloat16 [2, 1024], P(None, ('dp', 'fsdp')), may hold values from 0.099609375 to 1.8984375
- enc_biases: bfloat16 [4, 1024], P(None, ('dp', 'fsdp')), may hold values from -1.5 to 1.5
- lat_qkv: bfloat16 [3, 1024, 1024], P(None, ('dp', 'fsdp')), may hold values from -0.1875 to 0.1875
- lat_out: bfloat16 [1024, 1024], P(('dp', 'fsdp')), may hold values from -2 to 2
- lat_mlp: bfloat16 [2, 1024, 1024], P(None, ('dp', 'fsdp')), may hold values from -0.1875 to 0.1875
- lat_gains: bfloat16 [2, 1024], P(None, ('dp', 'fsdp')), may hold values from 0.099609375 to 1.8984375
- lat_biases: bfloat16 [4, 1024], P(None, ('dp', 'fsdp')), may hold values from -1.5 to 1.5
- cotangent: bfloat16 [16, 512, 1024], P('dp', 'fsdp'), may hold values from -6 to 6
Outputs:
- result: bfloat16 [16, 512, 1024], P('dp', 'fsdp')
- d_latents: float32 [16, 512, 1024], P('dp', 'fsdp')
- d_pixels: float32 [16384, 261], P(('dp', 'fsdp'))
- d_pix_gain: float32 [261], replicated
- d_pix_bias: float32 [261], replicated
- d_pix_kv: float32 [2, 261, 1024], P(None, None, ('dp', 'fsdp'))
- d_enc_query: float32 [1024, 1024], P(('dp', 'fsdp'))
- d_enc_out: float32 [1024, 1024], P(('dp', 'fsdp'))
- d_enc_mlp: float32 [2, 1024, 1024], P(None, ('dp', 'fsdp'))
- d_enc_gains: float32 [2, 1024], P(None, ('dp', 'fsdp'))
- d_enc_biases: float32 [4, 1024], P(None, ('dp', 'fsdp'))
- d_lat_qkv: float32 [3, 1024, 1024], P(None, ('dp', 'fsdp'))
- d_lat_out: float32 [1024, 1024], P(('dp', 'fsdp'))
- d_lat_mlp: float32 [2, 1024, 1024], P(None, ('dp', 'fsdp'))
- d_lat_gains: float32 [2, 1024], P(None, ('dp', 'fsdp'))
- d_lat_biases: float32 [4, 1024], P(None, ('dp', 'fsdp'))
Inputs may be any that keep to these rules, and one draw needn't show every extreme that they name: `lengths`: the pixel counts of one index of dp sum to 1792; on every index of dp each is at most 1280.
All inputs are finite; a program needn't handle non-finite values.
Results may differ from a plain program's by a relative error of at most 0.015.
Values may be sent and summed in bfloat16 or wider, within the bound.
No kernel may reach another device: no remote copies, remote signals or barrier semaphores. Data moves between devices by JAX's collectives and lax.ppermute only.
A program may use at most 192 MiB of HBM per device.

v0:
```python
from functools import partial

import jax
import jax.numpy as jnp
from jax import lax
from jax.sharding import PartitionSpec as P

HEADS = 8
HEAD = 128
MOST = 1280


EPSILON = 1e-05
MASKED = -1e30
ENC_DIMS = (2, 0, 0, 1, 1, 1)
LAT_DIMS = (1, 0, 1, 1, 1)


def layer_norm(values, gains, biases):
    average = jnp.mean(values, axis=-1, keepdims=True)
    centered = values - average
    variance = jnp.mean(centered * centered, axis=-1, keepdims=True)
    return centered * lax.rsqrt(variance + EPSILON) * gains + biases


def norm_back(values, gains, biases, grad_out):
    outputs, pullback = jax.vjp(layer_norm, values, gains, biases)
    return pullback(grad_out)


def gelu_back(inputs, grad_out):
    outputs, pullback = jax.vjp(partial(jax.nn.gelu, approximate=False), inputs)
    return pullback(grad_out)[0]


def matmul(left_in, right_in):
    return jnp.dot(left_in, right_in, preferred_element_type=jnp.float32)


def back_matmul(grad_low, matrix):
    return lax.dot_general(
        grad_low,
        matrix,
        (((grad_low.ndim - 1,), (1,)), ((), ())),
        preferred_element_type=jnp.float32,
    )


def weight_grad(inputs_low, grad_low):
    left_flat = inputs_low.reshape(-1, inputs_low.shape[-1])
    right_flat = grad_low.reshape(-1, grad_low.shape[-1])
    return lax.dot_general(
        left_flat, right_flat, (((0,), (0,)), ((), ())), preferred_element_type=jnp.float32
    )


def row_total(values):
    return jnp.sum(values.reshape(-1, values.shape[-1]), axis=0)


def softmax_lse(scores):
    largest = jnp.max(scores, axis=-1, keepdims=True)
    powers = jnp.exp(scores - largest)
    totals = jnp.sum(powers, axis=-1, keepdims=True)
    return (powers / totals, largest + jnp.log(totals))


def scaled_grad(probs, grad_probs, inner, scale):
    return (probs * (grad_probs - inner) * scale).astype(jnp.bfloat16)


def score_grad(probs, grad_probs, scale):
    inner = jnp.sum(probs * grad_probs, axis=-1, keepdims=True)
    return scaled_grad(probs, grad_probs, inner, scale)


def to_front(arrays, dims):
    return tuple((jnp.moveaxis(array_in, place, 0) for array_in, place in zip(arrays, dims)))


def from_front(arrays, dims):
    return tuple((jnp.moveaxis(array_in, 0, place) for array_in, place in zip(arrays, dims)))


def feed_forward(resid, gains, biases, mlp_w):
    normed_low = layer_norm(resid, gains[1], biases[1]).astype(jnp.bfloat16)
    pre_act = matmul(normed_low, mlp_w[0]) + biases[2]
    act_low = jax.nn.gelu(pre_act, approximate=False).astype(jnp.bfloat16)
    return (resid + matmul(act_low, mlp_w[1]) + biases[3], (normed_low, pre_act, act_low))


def feed_back(resid, gains, biases, mlp_w, kept, grad_out):
    normed_low, pre_act, act_low = kept
    grad_low = grad_out.astype(jnp.bfloat16)
    d_second = weight_grad(act_low, grad_low)
    d_bias_two = row_total(grad_out)
    d_act = back_matmul(grad_low, mlp_w[1])
    d_pre = gelu_back(pre_act, d_act)
    d_bias_one = row_total(d_pre)
    d_pre_low = d_pre.astype(jnp.bfloat16)
    d_first = weight_grad(normed_low, d_pre_low)
    d_normed = back_matmul(d_pre_low, mlp_w[0])
    d_resid, d_gain, d_shift = norm_back(resid, gains[1], biases[1], d_normed)
    return (
        grad_out + d_resid,
        jnp.stack([d_first, d_second]),
        d_gain,
        d_shift,
        d_bias_one,
        d_bias_two,
    )


def encoder_weights(pix_kv, enc_query, enc_out, enc_mlp, enc_gains, enc_biases):
    fronted = to_front((pix_kv, enc_query, enc_out, enc_mlp, enc_gains, enc_biases), ENC_DIMS)
    gathered = (
        lax.all_gather(fronted[0], ("dp", "fsdp"), axis=0, tiled=True),
        lax.all_gather(fronted[1], ("dp", "fsdp"), axis=0, tiled=True),
        lax.all_gather(fronted[2], ("dp", "fsdp"), axis=0, tiled=True),
        lax.all_gather(fronted[3], ("dp", "fsdp"), axis=0, tiled=True),
        lax.all_gather(fronted[4], ("dp", "fsdp"), axis=0, tiled=True),
        lax.all_gather(fronted[5], ("dp", "fsdp"), axis=0, tiled=True),
    )
    return from_front(gathered, ENC_DIMS)


def latent_weights(lat_qkv, lat_out, lat_mlp, lat_gains, lat_biases):
    fronted = to_front((lat_qkv, lat_out, lat_mlp, lat_gains, lat_biases), LAT_DIMS)
    gathered = (
        lax.all_gather(fronted[0], ("dp", "fsdp"), axis=0, tiled=True),
        lax.all_gather(fronted[1], ("dp", "fsdp"), axis=0, tiled=True),
        lax.all_gather(fronted[2], ("dp", "fsdp"), axis=0, tiled=True),
        lax.all_gather(fronted[3], ("dp", "fsdp"), axis=0, tiled=True),
        lax.all_gather(fronted[4], ("dp", "fsdp"), axis=0, tiled=True),
    )
    return from_front(gathered, LAT_DIMS)


def body(
    latents,
    pixels,
    lengths,
    pix_gain,
    pix_bias,
    pix_kv,
    enc_query,
    enc_out,
    enc_mlp,
    enc_gains,
    enc_biases,
    lat_qkv,
    lat_out,
    lat_mlp,
    lat_gains,
    lat_biases,
    cotangent,
):
    images, lat_rows, model_width = latents.shape
    pix_rows = pixels.shape[0]
    sizes = lengths[0]
    starts = jnp.cumsum(sizes) - sizes
    valid = jnp.arange(MOST, dtype=jnp.int32)[None, :] < sizes[:, None]
    enc_scale = model_width ** (-0.5)
    lat_scale = HEAD ** (-0.5)
    enc_full = encoder_weights(pix_kv, enc_query, enc_out, enc_mlp, enc_gains, enc_biases)
    kv_full, query_full, out_full, mlp_full, gains_low, biases_low = enc_full
    gains_enc = gains_low.astype(jnp.float32)
    biases_enc = biases_low.astype(jnp.float32)
    pix_gain_f = pix_gain.astype(jnp.float32)
    pix_bias_f = pix_bias.astype(jnp.float32)
    latent_in = latents.astype(jnp.float32)
    pixel_in = pixels.astype(jnp.float32)
    pixel_low = layer_norm(pixel_in, pix_gain_f, pix_bias_f).astype(jnp.bfloat16)
    key_rows = matmul(pixel_low, kv_full[0]).astype(jnp.bfloat16)
    value_rows = matmul(pixel_low, kv_full[1]).astype(jnp.bfloat16)
    filler = jnp.zeros((MOST, model_width), jnp.bfloat16)
    key_pad = jnp.concatenate([key_rows, filler], axis=0)
    value_pad = jnp.concatenate([value_rows, filler], axis=0)

    def window(source, first):
        return lax.dynamic_slice_in_dim(source, first, MOST, 0)

    key_win = jax.vmap(window, (None, 0))(key_pad, starts)
    value_win = jax.vmap(window, (None, 0))(value_pad, starts)
    enc_normed_low = layer_norm(latent_in, gains_enc[0], biases_enc[0]).astype(jnp.bfloat16)
    enc_q = matmul(enc_normed_low, query_full).astype(jnp.bfloat16)

    def enc_scores_of(queries):
        raw_scores = (
            jnp.einsum("iqd,ikd->iqk", queries, key_win, preferred_element_type=jnp.float32)
            * enc_scale
        )
        return jnp.where(valid[:, None, :], raw_scores, MASKED)

    enc_probs, enc_lse = softmax_lse(enc_scores_of(enc_q))
    enc_mixed = jnp.einsum(
        "iqk,ikd->iqd",
        enc_probs.astype(jnp.bfloat16),
        value_win,
        preferred_element_type=jnp.float32,
    ).astype(jnp.bfloat16)
    enc_resid = latent_in + matmul(enc_mixed, out_full)
    first_out, enc_kept = feed_forward(enc_resid, gains_enc, biases_enc, mlp_full)
    lat_full = latent_weights(lat_qkv, lat_out, lat_mlp, lat_gains, lat_biases)
    qkv_full, lat_out_full, lat_mlp_full, lat_gains_low, lat_biases_low = lat_full
    gains_lat = lat_gains_low.astype(jnp.float32)
    biases_lat = lat_biases_low.astype(jnp.float32)
    lat_normed_low = layer_norm(first_out, gains_lat[0], biases_lat[0]).astype(jnp.bfloat16)
    lat_q = matmul(lat_normed_low, qkv_full[0]).astype(jnp.bfloat16)
    own_keys = matmul(lat_normed_low, qkv_full[1]).astype(jnp.bfloat16)
    own_values = matmul(lat_normed_low, qkv_full[2]).astype(jnp.bfloat16)
    all_keys, all_values = (
        lax.all_gather(own_keys, "fsdp", axis=1, tiled=True),
        lax.all_gather(own_values, "fsdp", axis=1, tiled=True),
    )
    query_heads = lat_q.reshape(images, lat_rows, HEADS, HEAD)
    key_heads = all_keys.reshape(images, -1, HEADS, HEAD)
    value_heads = all_values.reshape(images, -1, HEADS, HEAD)
    lat_scores = (
        jnp.einsum("iqhd,ikhd->ihqk", query_heads, key_heads, preferred_element_type=jnp.float32)
        * lat_scale
    )
    lat_probs, lat_lse = softmax_lse(lat_scores)
    lat_mixed = (
        jnp.einsum(
            "ihqk,ikhd->iqhd",
            lat_probs.astype(jnp.bfloat16),
            value_heads,
            preferred_element_type=jnp.float32,
        )
        .astype(jnp.bfloat16)
        .reshape(images, lat_rows, model_width)
    )
    lat_resid = first_out + matmul(lat_mixed, lat_out_full)
    second_out, lat_kept = feed_forward(lat_resid, gains_lat, biases_lat, lat_mlp_full)
    result = second_out.astype(jnp.bfloat16)
    lat_back = latent_weights(lat_qkv, lat_out, lat_mlp, lat_gains, lat_biases)
    qkv_back, lat_out_back, lat_mlp_back = (lat_back[0], lat_back[1], lat_back[2])
    grad_out = cotangent.astype(jnp.float32)
    grad_mid, d_lat_mlp, d_gain_b, d_shift_b, d_bias_one, d_bias_two = feed_back(
        lat_resid, gains_lat, biases_lat, lat_mlp_back, lat_kept, grad_out
    )
    grad_mid_low = grad_mid.astype(jnp.bfloat16)
    d_lat_out = weight_grad(lat_mixed, grad_mid_low)
    d_mixed = (
        back_matmul(grad_mid_low, lat_out_back)
        .astype(jnp.bfloat16)
        .reshape(images, lat_rows, HEADS, HEAD)
    )
    probs_again = jnp.exp(
        jnp.einsum("iqhd,ikhd->ihqk", query_heads, key_heads, preferred_element_type=jnp.float32)
        * lat_scale
        - lat_lse
    )
    d_probs = jnp.einsum(
        "iqhd,ikhd->ihqk", d_mixed, value_heads, preferred_element_type=jnp.float32
    )
    d_scores = score_grad(probs_again, d_probs, lat_scale)
    d_query = (
        jnp.einsum("ihqk,ikhd->iqhd", d_scores, key_heads, preferred_element_type=jnp.float32)
        .astype(jnp.bfloat16)
        .reshape(images, lat_rows, model_width)
    )
    d_key_part = jnp.einsum(
        "ihqk,iqhd->ikhd", d_scores, query_heads, preferred_element_type=jnp.float32
    ).reshape(images, -1, model_width)
    d_value_part = jnp.einsum(
        "ihqk,iqhd->ikhd",
        probs_again.astype(jnp.bfloat16),
        d_mixed,
        preferred_element_type=jnp.float32,
    ).reshape(images, -1, model_width)
    d_key, d_value = (
        lax.psum_scatter(
            d_key_part.astype(jnp.bfloat16), "fsdp", scatter_dimension=1, tiled=True
        ).astype(jnp.float32),
        lax.psum_scatter(
            d_value_part.astype(jnp.bfloat16), "fsdp", scatter_dimension=1, tiled=True
        ).astype(jnp.float32),
    )
    d_key_low = d_key.astype(jnp.bfloat16)
    d_value_low = d_value.astype(jnp.bfloat16)
    d_qkv = jnp.stack(
        [
            weight_grad(lat_normed_low, d_query),
            weight_grad(lat_normed_low, d_key_low),
            weight_grad(lat_normed_low, d_value_low),
        ]
    )
    d_lat_normed = (
        back_matmul(d_query, qkv_back[0])
        + back_matmul(d_key_low, qkv_back[1])
        + back_matmul(d_value_low, qkv_back[2])
    )
    d_first_part, d_gain_a, d_shift_a = norm_back(
        first_out, gains_lat[0], biases_lat[0], d_lat_normed
    )
    d_first_out = grad_mid + d_first_part
    lat_front = to_front(
        (
            d_qkv,
            d_lat_out,
            d_lat_mlp,
            jnp.stack([d_gain_a, d_gain_b]),
            jnp.stack([d_shift_a, d_shift_b, d_bias_one, d_bias_two]),
        ),
        LAT_DIMS,
    )
    lat_summed = (
        lax.psum_scatter(lat_front[0], ("dp", "fsdp"), scatter_dimension=0, tiled=True),
        lax.psum_scatter(lat_front[1], ("dp", "fsdp"), scatter_dimension=0, tiled=True),
        lax.psum_scatter(lat_front[2], ("dp", "fsdp"), scatter_dimension=0, tiled=True),
        lax.psum_scatter(lat_front[3], ("dp", "fsdp"), scatter_dimension=0, tiled=True),
        lax.psum_scatter(lat_front[4], ("dp", "fsdp"), scatter_dimension=0, tiled=True),
    )
    lat_results = from_front(lat_summed, LAT_DIMS)
    enc_back = encoder_weights(pix_kv, enc_query, enc_out, enc_mlp, enc_gains, enc_biases)
    kv_back, query_back, out_back, mlp_back = (enc_back[0], enc_back[1], enc_back[2], enc_back[3])
    grad_enc, d_enc_mlp, d_gain_d, d_shift_d, d_bias_three, d_bias_four = feed_back(
        enc_resid, gains_enc, biases_enc, mlp_back, enc_kept, d_first_out
    )
    grad_enc_low = grad_enc.astype(jnp.bfloat16)
    d_enc_out = weight_grad(enc_mixed, grad_enc_low)
    d_enc_mixed = back_matmul(grad_enc_low, out_back).astype(jnp.bfloat16)
    enc_again = jnp.exp(enc_scores_of(enc_q) - enc_lse)
    d_enc_probs = jnp.einsum(
        "iqd,ikd->iqk", d_enc_mixed, value_win, preferred_element_type=jnp.float32
    )
    enc_inner = jnp.sum(enc_again * d_enc_probs, axis=-1, keepdims=True)
    d_enc_scores = scaled_grad(enc_again, d_enc_probs, enc_inner, enc_scale)
    d_enc_q = jnp.einsum(
        "iqk,ikd->iqd", d_enc_scores, key_win, preferred_element_type=jnp.float32
    ).astype(jnp.bfloat16)
    share = pix_rows // lax.axis_size("fsdp")
    first_row = lax.axis_index("fsdp") * share
    d_key_win = jnp.einsum("iqk,iqd->ikd", d_enc_scores, enc_q, preferred_element_type=jnp.float32)
    d_value_win = jnp.einsum(
        "iqk,iqd->ikd",
        enc_again.astype(jnp.bfloat16),
        d_enc_mixed,
        preferred_element_type=jnp.float32,
    )

    def place(index, totals):
        key_total, value_total = totals
        first = lax.dynamic_index_in_dim(starts, index, 0, keepdims=False)
        key_piece = lax.dynamic_slice_in_dim(key_total, first, MOST, 0) + lax.dynamic_index_in_dim(
            d_key_win, index, 0, keepdims=False
        )
        value_piece = lax.dynamic_slice_in_dim(
            value_total, first, MOST, 0
        ) + lax.dynamic_index_in_dim(d_value_win, index, 0, keepdims=False)
        return (
            lax.dynamic_update_slice_in_dim(key_total, key_piece, first, 0),
            lax.dynamic_update_slice_in_dim(value_total, value_piece, first, 0),
        )

    empty = jnp.zeros((pix_rows + MOST, model_width), jnp.float32)
    key_total, value_total = lax.fori_loop(0, images, place, (empty, empty))
    d_pix_key, d_pix_value = (
        lax.psum_scatter(
            key_total[:pix_rows].astype(jnp.bfloat16), "fsdp", scatter_dimension=0, tiled=True
        ).astype(jnp.float32),
        lax.psum_scatter(
            value_total[:pix_rows].astype(jnp.bfloat16), "fsdp", scatter_dimension=0, tiled=True
        ).astype(jnp.float32),
    )
    d_pix_key_low = d_pix_key.astype(jnp.bfloat16)
    d_pix_value_low = d_pix_value.astype(jnp.bfloat16)
    pixel_part = lax.dynamic_slice_in_dim(pixel_in, first_row, share, 0)
    pixel_low_part = lax.dynamic_slice_in_dim(pixel_low, first_row, share, 0)
    d_kv = jnp.stack(
        [weight_grad(pixel_low_part, d_pix_key_low), weight_grad(pixel_low_part, d_pix_value_low)]
    )
    d_pixel_normed = back_matmul(d_pix_key_low, kv_back[0]) + back_matmul(
        d_pix_value_low, kv_back[1]
    )
    d_pixels, d_pix_gain_part, d_pix_bias_part = norm_back(
        pixel_part, pix_gain_f, pix_bias_f, d_pixel_normed
    )
    d_pix_gain, d_pix_bias = lax.psum((d_pix_gain_part, d_pix_bias_part), ("dp", "fsdp"))
    d_query_w = weight_grad(enc_normed_low, d_enc_q)
    d_enc_normed = back_matmul(d_enc_q, query_back)
    d_latent_part, d_gain_c, d_shift_c = norm_back(
        latent_in, gains_enc[0], biases_enc[0], d_enc_normed
    )
    d_latents = grad_enc + d_latent_part
    enc_front = to_front(
        (
            d_kv,
            d_query_w,
            d_enc_out,
            d_enc_mlp,
            jnp.stack([d_gain_c, d_gain_d]),
            jnp.stack([d_shift_c, d_shift_d, d_bias_three, d_bias_four]),
        ),
        ENC_DIMS,
    )
    enc_summed = (
        lax.psum_scatter(enc_front[0], ("dp", "fsdp"), scatter_dimension=0, tiled=True),
        lax.psum_scatter(enc_front[1], ("dp", "fsdp"), scatter_dimension=0, tiled=True),
        lax.psum_scatter(enc_front[2], ("dp", "fsdp"), scatter_dimension=0, tiled=True),
        lax.psum_scatter(enc_front[3], ("dp", "fsdp"), scatter_dimension=0, tiled=True),
        lax.psum_scatter(enc_front[4], ("dp", "fsdp"), scatter_dimension=0, tiled=True),
        lax.psum_scatter(enc_front[5], ("dp", "fsdp"), scatter_dimension=0, tiled=True),
    )
    enc_results = from_front(enc_summed, ENC_DIMS)
    return (
        result,
        d_latents,
        d_pixels,
        d_pix_gain,
        d_pix_bias,
        enc_results[0],
        enc_results[1],
        enc_results[2],
        enc_results[3],
        enc_results[4],
        enc_results[5],
        lat_results[0],
        lat_results[1],
        lat_results[2],
        lat_results[3],
        lat_results[4],
    )


def solution(mesh):
    return jax.shard_map(
        body,
        mesh=mesh,
        in_specs=(
            P("dp", "fsdp", None),
            P("dp", None),
            P("dp", None),
            P(),
            P(),
            P(None, None, ("dp", "fsdp")),
            P(("dp", "fsdp"), None),
            P(("dp", "fsdp"), None),
            P(None, ("dp", "fsdp"), None),
            P(None, ("dp", "fsdp")),
            P(None, ("dp", "fsdp")),
            P(None, ("dp", "fsdp"), None),
            P(("dp", "fsdp"), None),
            P(None, ("dp", "fsdp"), None),
            P(None, ("dp", "fsdp")),
            P(None, ("dp", "fsdp")),
            P("dp", "fsdp", None),
        ),
        out_specs=(
            P("dp", "fsdp", None),
            P("dp", "fsdp", None),
            P(("dp", "fsdp"), None),
            P(),
            P(),
            P(None, None, ("dp", "fsdp")),
            P(("dp", "fsdp"), None),
            P(("dp", "fsdp"), None),
            P(None, ("dp", "fsdp"), None),
            P(None, ("dp", "fsdp")),
            P(None, ("dp", "fsdp")),
            P(None, ("dp", "fsdp"), None),
            P(("dp", "fsdp"), None),
            P(None, ("dp", "fsdp"), None),
            P(None, ("dp", "fsdp")),
            P(None, ("dp", "fsdp")),
        ),
        check_vma=False,
    )
```

profile of v0, /device:TPU:0, one launch (start us, length us, event | category | flops | bytes accessed | tf_op | source)
XLA Modules:
  0.0 2737.1 jit_solution(13907139958719940067)
XLA Ops:
  13.6 69.5 %all-gather = bf16[32,32,2]{1,2,0:T(2,128)(2,1)S(1)} all-gather(bf16[1,32,2]{1,2,0:T(2,128)(2,1)} %bitcast.445), channel_id=1, replica_groups=mesh['dp'=8,'fsdp'=4] {'dp','fsdp'}, dimensions={0}, use_global_device_ids=true | all-gather | bytes 4224 | tf_op jit(solution)/shard_map/all_gather | solution.py:121
  83.2 63.3 %all-gather.2 = bf16[32,32,2]{1,2,0:T(2,128)(2,1)S(1)} all-gather(bf16[1,32,2]{1,2,0:T(2,128)(2,1)} %bitcast.446), channel_id=1, replica_groups=mesh['dp'=8,'fsdp'=4] {'dp','fsdp'}, dimensions={0}, use_global_device_ids=true | all-gather | bytes 4224 | tf_op jit(solution)/shard_map/all_gather | solution.py:133
  146.5 65.9 %all-gather.1 = bf16[32,32,4]{1,2,0:T(4,128)(2,1)S(1)} all-gather(bf16[1,32,4]{1,2,0:T(4,128)(2,1)} %bitcast.441), channel_id=1, replica_groups=mesh['dp'=8,'fsdp'=4] {'dp','fsdp'}, dimensions={0}, use_global_device_ids=true | all-gather | bytes 8448 | tf_op jit(solution)/shard_map/all_gather | solution.py:122
  212.6 63.9 %all-gather.3 = bf16[32,32,4]{1,2,0:T(4,128)(2,1)S(1)} all-gather(bf16[1,32,4]{1,2,0:T(4,128)(2,1)} %bitcast.442), channel_id=1, replica_groups=mesh['dp'=8,'fsdp'=4] {'dp','fsdp'}, dimensions={0}, use_global_device_ids=true | all-gather | bytes 8448 | tf_op jit(solution)/shard_map/all_gather | solution.py:134
  300.3 8.4 while.19
  311.7 8.4 while.18
  322.7 4.7 fusion.197
  350.4 36.6 %all-gather.26.cloned.1.call-done = bf16[2,512,1024]{2,1,0:T(8,128)(2,1)} async-done(((bf16[2,128,1024]{2,1,0:T(8,128)(2,1)}), bf16[2,512,1024]{2,1,0:T(8,128)(2,1)}) %all-gather.26.cloned.1.call-update) | async-done | bytes 2097168 | tf_op jit(solution)/shard_map/all_gather | solution.py:213
  387.0 4.3 copy.175
  397.0 36.8 %all-gather.24.cloned.1.call-done = bf16[2,512,1024]{2,1,0:T(8,128)(2,1)} async-done(((bf16[2,128,1024]{2,1,0:T(8,128)(2,1)}), bf16[2,512,1024]{2,1,0:T(8,128)(2,1)}) %all-gather.24.cloned.1.call-update) | async-done | bytes 2097168 | tf_op jit(solution)/shard_map/all_gather | solution.py:214
  433.8 5.2 fusion.86
  439.0 53.0 %all-gather.28.cloned.1.call-done = bf16[1024,1024]{1,0:T(8,128)(2,1)} async-done(((bf16[32,1024]{1,0:T(8,128)(2,1)}), bf16[1024,1024]{1,0:T(8,128)(2,1)}) %all-gather.28.cloned.1.call-update) | async-done | bytes 2097168 | tf_op jit(solution)/shard_map/all_gather | solution.py:131
  494.9 61.0 %all-gather.30.cloned.1.call-done = bf16[1024,2,1024]{2,0,1:T(8,128)(2,1)} async-done(((bf16[32,2,1024]{2,0,1:T(8,128)(2,1)}), bf16[1024,2,1024]{2,0,1:T(8,128)(2,1)}) %all-gather.30.cloned.1.call-update) | async-done | bytes 4194320 | tf_op jit(solution)/shard_map/all_gather | solution.py:132
  570.1 4.7 fusion.46
  578.8 4.5 fusion.22
  583.3 19.3 fusion.49
  606.8 18.9 fusion.101
  632.8 34.1 %reduce-scatter.23.cloned.1.call-done = bf16[2,128,1024]{2,1,0:T(8,128)(2,1)} async-done(((bf16[2,512,1024]{2,1,0:T(8,128)(2,1)}), bf16[2,128,1024]{2,1,0:T(8,128)(2,1)}) %reduce-scatter.23.cloned.1.call-update) | async-done | bytes 524304 | tf_op jit(solution)/shard_map/reduce_scatter | solution.py:274
  681.9 5.8 fusion.133
  687.8 8.3 fusion.106
  696.1 6.7 broadcast_in_dim.48.clone
  702.8 6.6 broadcast_in_dim.48
  709.4 86.8 %while.17 = (s32[]{:T(128)}, f32[3328,1024]{1,0:T(8,128)}, f32[3328,1024]{1,0:T(8,128)}, s32[2]{0:T(128)S(1)}, f32[2,1280,1024]{2,1,0:T(8,128)}, /*index=5*/f32[...) while((s32[]{:T(128)}, f32[3328,1024]{1,0:T(8,128)}, f32[3328,1024]{1,0:T(8,128)}, s32[2]{0:T(128)S(1)}, ...), condition=%wide.region_28.29_spmd, body=%wide.region_27.28_spmd.sunk | while | flops 2621445 | bytes 52428964 | solution.py:359
  711.9 12.2 bitcast_add_fusion.3
  724.2 14.3 dynamic_update_slice.16
  738.4 14.3 dynamic_update_slice.17
  755.3 12.2 bitcast_add_fusion.3
  767.5 14.4 dynamic_update_slice.16
  781.9 14.4 dynamic_update_slice.17
  796.2 6.1 slice.209
  802.4 6.2 slice.210
  809.9 5.5 convolution_convert_fusion.2
  824.3 54.2 %reduce-scatter.29.cloned.1.call-done = bf16[512,1024]{1,0:T(8,128)(2,1)} async-done(((bf16[2048,1024]{1,0:T(8,128)(2,1)}), bf16[512,1024]{1,0:T(8,128)(2,1)}) %reduce-scatter.29.cloned.1.call-update) | async-done | bytes 1048592 | tf_op jit(solution)/shard_map/reduce_scatter | solution.py:364
  881.2 76.9 %reduce-scatter.27.cloned.1.call-done = bf16[512,1024]{1,0:T(8,128)(2,1)} async-done(((bf16[2048,1024]{1,0:T(8,128)(2,1)}), bf16[512,1024]{1,0:T(8,128)(2,1)}) %reduce-scatter.27.cloned.1.call-update) | async-done | bytes 1048592 | tf_op jit(solution)/shard_map/reduce_scatter | solution.py:361
  962.8 5.2 copy.141
  1001.7 4.9 maximum_bitcast_fusion
  1015.4 79.8 %reduce-scatter.47.cloned.1.call-done = f32[32,2]{1,0:T(8,128)} async-done(((f32[1024,2]{1,0:T(8,128)}), f32[32,2]{1,0:T(8,128)}) %reduce-scatter.47.cloned.1.call-update) | async-done | bytes 272
  1096.6 131.4 %reduce-scatter.43.cloned.1.call-done = f32[32,2]{1,0:T(8,128)} async-done(((f32[1024,2]{1,0:T(8,128)}), f32[32,2]{1,0:T(8,128)}) %reduce-scatter.43.cloned.1.call-update) | async-done | bytes 272
  1229.4 131.3 %reduce-scatter.49.cloned.1.call-done = f32[32,4]{1,0:T(8,128)} async-done(((f32[1024,4]{1,0:T(8,128)}), f32[32,4]{1,0:T(8,128)}) %reduce-scatter.49.cloned.1.call-update) | async-done | bytes 528
  1362.0 131.6 %reduce-scatter.45.cloned.1.call-done = f32[32,4]{1,0:T(8,128)} async-done(((f32[1024,4]{1,0:T(8,128)}), f32[32,4]{1,0:T(8,128)}) %reduce-scatter.45.cloned.1.call-update) | async-done | bytes 528
  1499.2 37.4 %all-reduce.4 = (f32[261]{0:T(512)}, f32[261]{0:T(512)}) all-reduce(f32[261]{0:T(512)S(1)} %get-tuple-element.240, f32[261]{0:T(512)S(1)} %get-tuple-element.262), channel_id=1, replica_groups=mesh['dp'=8,'fsdp'=4] {'dp','fsdp'}, use_global_device_ids=true, to_apply=%region_36.37 | all-reduce | flops 522 | bytes 4176 | tf_op jit(solution)/shard_map/psum | solution.py:381
  1537.5 95.8 %all-reduce.7.cloned.1.call-done = f32[1024,2,261]{2,1,0:T(2,128)} async-done(((f32[1024,2,261]{2,1,0:T(2,128)}), f32[1024,2,261]{2,1,0:T(2,128)}) %all-reduce.7.cloned.1.call-update) | async-done | bytes 2138128
  1635.0 148.4 %reduce-scatter.39.cloned.1.call-done = f32[32,1024]{1,0:T(8,128)} async-done(((f32[1024,1024]{1,0:T(8,128)}), f32[32,1024]{1,0:T(8,128)}) %reduce-scatter.39.cloned.1.call-update) | async-done | bytes 131088 | tf_op jit(solution)/shard_map/reduce_scatter | solution.py:311
  1783.3 149.1 %reduce-scatter.33.cloned.1.call-done = f32[32,1024]{1,0:T(8,128)} async-done(((f32[1024,1024]{1,0:T(8,128)}), f32[32,1024]{1,0:T(8,128)}) %reduce-scatter.33.cloned.1.call-update) | async-done | bytes 131088 | tf_op jit(solution)/shard_map/reduce_scatter | solution.py:402
  1932.4 149.9 %reduce-scatter.31.cloned.1.call-done = f32[32,1024]{1,0:T(8,128)} async-done(((f32[1024,1024]{1,0:T(8,128)}), f32[32,1024]{1,0:T(8,128)}) %reduce-scatter.31.cloned.1.call-update) | async-done | bytes 131088 | tf_op jit(solution)/shard_map/reduce_scatter | solution.py:401
  2082.4 188.0 %reduce-scatter.41.cloned.1.call-done = f32[32,2,1024]{2,0,1:T(8,128)} async-done(((f32[1024,2,1024]{2,0,1:T(8,128)}), f32[32,2,1024]{2,0,1:T(8,128)}) %reduce-scatter.41.cloned.1.call-update) | async-done | bytes 262160 | tf_op jit(solution)/shard_map/reduce_scatter | solution.py:312
  2270.4 186.5 %reduce-scatter.35.cloned.1.call-done = f32[32,2,1024]{2,0,1:T(8,128)} async-done(((f32[1024,2,1024]{2,0,1:T(8,128)}), f32[32,2,1024]{2,0,1:T(8,128)}) %reduce-scatter.35.cloned.1.call-update) | async-done | bytes 262160 | tf_op jit(solution)/shard_map/reduce_scatter | solution.py:403
  2456.8 273.2 %reduce-scatter.37.cloned.1.call-done = f32[32,3,1024]{2,0,1:T(8,128)} async-done(((f32[1024,3,1024]{2,0,1:T(8,128)}), f32[32,3,1024]{2,0,1:T(8,128)}) %reduce-scatter.37.cloned.1.call-update) | async-done | bytes 393232 | tf_op jit(solution)/shard_map/reduce_scatter | solution.py:310
  (342 shorter events, 200.9 us)
Async XLA Ops:
  7.2 275.7 %copy-start.63 = (s32[1,2]{1,0:T(1,128)S(1)}, s32[1,2]{1,0:T(1,128)}, u32[]{:S(2)}) copy-start(s32[1,2]{1,0:T(1,128)} %param.21) | copy-start | bytes 28
  7.2 275.7 %copy-start.3 = (bf16[2048,261]{0,1:T(8,128)(2,1)S(1)}, bf16[2048,261]{0,1:T(8,128)(2,1)}, u32[]{:S(2)}) copy-start(bf16[2048,261]{0,1:T(8,128)(2,1)} %param.20) | copy-start | bytes 3207172
  7.2 276.2 %all-gather.16.cloned.1.call-start = ((), (), s32[]{:S(2)}) async-start(), calls=%async_computation.15 | async-start | bytes 1622016 | tf_op jit(solution)/shard_map/all_gather | solution.py:117
  7.9 312.1 %all-gather.14.cloned.1.call-start = ((), (), s32[]{:S(2)}) async-start(), calls=%async_computation.14 | async-start | bytes 2162688 | tf_op jit(solution)/shard_map/all_gather | solution.py:118
  8.7 320.7 %all-gather.18.cloned.1.call-start = ((), (), s32[]{:S(2)}) async-start(), calls=%async_computation.16 | async-start | bytes 2162688 | tf_op jit(solution)/shard_map/all_gather | solution.py:119
  9.4 322.8 %all-gather.20.cloned.1.call-start = ((), (), s32[]{:S(2)}) async-start(), calls=%async_computation.17 | async-start | bytes 4325376 | tf_op jit(solution)/shard_map/all_gather | solution.py:120
  10.0 329.7 %all-gather.22.cloned.1.call-start = ((), (), s32[]{:S(2)}) async-start(), calls=%async_computation.18 | async-start | bytes 6488064 | tf_op jit(solution)/shard_map/all_gather | solution.py:130
  10.6 376.4 %all-gather.26.cloned.1.call-start = ((), (), s32[]{:S(2)}) async-start(), calls=%async_computation.20 | async-start | bytes 2621440 | tf_op jit(solution)/shard_map/all_gather | solution.py:213
  12.9 274.4 %copy-start.48 = (f32[261]{0:T(512)}, f32[261]{0:T(512)S(1)}, u32[]{:S(2)}) copy-start(f32[261]{0:T(512)S(1)} %convert_element_type.175) | copy-start | bytes 3136
  277.8 42.3 %copy-start.50 = (f32[2,128]{1,0:T(2,128)}, f32[2,128]{1,0:T(2,128)S(1)}, u32[]{:S(2)}) copy-start(f32[2,128]{1,0:T(2,128)S(1)} %broadcast_multiply_fusion.5) | copy-start | bytes 3076
  279.1 8.2 copy-start.58
  282.1 38.0 %copy-start.52 = (f32[2,128]{1,0:T(2,128)}, f32[2,128]{1,0:T(2,128)S(1)}, u32[]{:S(2)}) copy-start(f32[2,128]{1,0:T(2,128)S(1)} %fusion.167) | copy-start | bytes 3076
  282.1 38.0 %copy-start.44 = (f32[1,1024]{1,0:T(1,128)}, f32[1,1024]{1,0:T(1,128)S(1)}, u32[]{:S(2)}) copy-start(f32[1,1024]{1,0:T(1,128)S(1)} %get-tuple-element.317) | copy-start | bytes 12292
  282.2 37.9 %copy-start.46 = (f32[1,1024]{1,0:T(1,128)}, f32[1,1024]{1,0:T(1,128)S(1)}, u32[]{:S(2)}) copy-start(f32[1,1024]{1,0:T(1,128)S(1)} %get-tuple-element.313) | copy-start | bytes 12292
  282.2 50.0 %copy-start.54 = (f32[1,1024]{1,0:T(1,128)}, f32[1,1024]{1,0:T(1,128)S(1)}, u32[]{:S(2)}) copy-start(f32[1,1024]{1,0:T(1,128)S(1)} %get-tuple-element.312) | copy-start | bytes 12292
  282.8 273.0 %copy-start.56 = (f32[1,1024]{1,0:T(1,128)}, f32[1,1024]{1,0:T(1,128)S(1)}, u32[]{:S(2)}) copy-start(f32[1,1024]{1,0:T(1,128)S(1)} %get-tuple-element.308) | copy-start | bytes 12292
  283.4 7.6 copy-start.23
  311.7 8.4 copy-start.1
  320.1 8.3 slice-start
  339.6 8.0 copy-start.7
  343.0 90.9 %all-gather.24.cloned.1.call-start = ((), (), s32[]{:S(2)}) async-start(), calls=%async_computation.19 | async-start | bytes 2621440 | tf_op jit(solution)/shard_map/all_gather | solution.py:214
  346.1 145.9 %all-gather.28.cloned.1.call-start = ((), (), s32[]{:S(2)}) async-start(), calls=%async_computation.21 | async-start | bytes 2162688 | tf_op jit(solution)/shard_map/all_gather | solution.py:131
  346.9 208.9 %all-gather.30.cloned.1.call-start = ((), (), s32[]{:S(2)}) async-start(), calls=%async_computation.22 | async-start | bytes 4325376 | tf_op jit(solution)/shard_map/all_gather | solution.py:132
  347.6 281.6 %reduce-scatter.25.cloned.1.call-start = ((), (), s32[]{:S(2)}) async-start(), calls=%async_computation.24 | async-start | bytes 2621440 | tf_op jit(solution)/shard_map/reduce_scatter | solution.py:277
  350.4 43.4 %copy-start.31 = (bf16[2,128,1024]{1,2,0:T(8,128)(2,1)}, bf16[2,128,1024]{1,2,0:T(8,128)(2,1)S(1)}, u32[]{:S(2)}) copy-start(bf16[2,128,1024]{1,2,0:T(8,128)(2,1)S(1)} %copy.174) | copy-start | bytes 1572868
  578.8 88.2 %reduce-scatter.23.cloned.1.call-start = ((), (), s32[]{:S(2)}) async-start(), calls=%async_computation.23 | async-start | bytes 2621440 | tf_op jit(solution)/shard_map/reduce_scatter | solution.py:274
  606.6 271.9 %reduce-scatter.29.cloned.1.call-start = ((), (), s32[]{:S(2)}) async-start(), calls=%async_computation.26 | async-start | bytes 5242880 | tf_op jit(solution)/shard_map/reduce_scatter | solution.py:364
  802.4 155.8 %reduce-scatter.27.cloned.1.call-start = ((), (), s32[]{:S(2)}) async-start(), calls=%async_computation.25 | async-start | bytes 5242880 | tf_op jit(solution)/shard_map/reduce_scatter | solution.py:361
  808.7 6.7 copy-start.2
  808.7 6.7 copy-start.45
  808.7 6.7 copy-start.51
  808.7 286.5 %reduce-scatter.47.cloned.1.call-start = ((), (), s32[]{:S(2)}) async-start(), calls=%async_computation.35 | async-start | bytes 540672
  809.8 9.2 copy-start.59
  815.4 7.6 copy-start.39
  819.0 409.0 %reduce-scatter.43.cloned.1.call-start = ((), (), s32[]{:S(2)}) async-start(), calls=%async_computation.33 | async-start | bytes 540672
  821.9 538.7 %reduce-scatter.49.cloned.1.call-start = ((), (), s32[]{:S(2)}) async-start(), calls=%async_computation.36 | async-start | bytes 540672
  823.1 670.5 %reduce-scatter.45.cloned.1.call-start = ((), (), s32[]{:S(2)}) async-start(), calls=%async_computation.34 | async-start | bytes 540672
  824.2 809.1 %all-reduce.7.cloned.1.call-start = ((), (), s32[]{:S(2)}) async-start(), calls=%async_computation.37 | async-start | bytes 6291456
  968.0 815.3 %reduce-scatter.39.cloned.1.call-start = ((), (), s32[]{:S(2)}) async-start(), calls=%async_computation.31 | async-start | bytes 4325376 | tf_op jit(solution)/shard_map/reduce_scatter | solution.py:311
  973.6 958.9 %reduce-scatter.33.cloned.1.call-start = ((), (), s32[]{:S(2)}) async-start(), calls=%async_computation.28 | async-start | bytes 4325376 | tf_op jit(solution)/shard_map/reduce_scatter | solution.py:402
  978.5 1103.9 %reduce-scatter.31.cloned.1.call-start = ((), (), s32[]{:S(2)}) async-start(), calls=%async_computation.27 | async-start | bytes 4325376 | tf_op jit(solution)/shard_map/reduce_scatter | solution.py:401
  982.5 1287.9 %reduce-scatter.41.cloned.1.call-start = ((), (), s32[]{:S(2)}) async-start(), calls=%async_computation.32 | async-start | bytes 8650752 | tf_op jit(solution)/shard_map/reduce_scatter | solution.py:312
  989.4 1467.5 %reduce-scatter.35.cloned.1.call-start = ((), (), s32[]{:S(2)}) async-start(), calls=%async_computation.29 | async-start | bytes 8650752 | tf_op jit(solution)/shard_map/reduce_scatter | solution.py:403
  997.5 1732.6 %reduce-scatter.37.cloned.1.call-start = ((), (), s32[]{:S(2)}) async-start(), calls=%async_computation.30 | async-start | bytes 12976128 | tf_op jit(solution)/shard_map/reduce_scatter | solution.py:310
  1007.8 6.2 copy-start.61
  1013.9 481.1 %copy-start.19 = (bf16[512,1024]{1,0:T(8,128)(2,1)S(1)}, bf16[512,1024]{1,0:T(8,128)(2,1)}, u32[]{:S(2)}) copy-start(bf16[512,1024]{1,0:T(8,128)(2,1)} %reduce-scatter.27.cloned.1.call-done) | copy-start | bytes 3145732
  1013.9 482.7 %copy-start.49 = (f32[261]{0:T(512)S(1)}, f32[261]{0:T(512)}, u32[]{:S(2)}) copy-start(f32[261]{0:T(512)} %copy-done.48) | copy-start | bytes 3136
  1015.4 483.5 %copy-start.15 = (f32[2048,261]{0,1:T(8,128)S(1)}, f32[2048,261]{0,1:T(8,128)}, u32[]{:S(2)}) copy-start(f32[2048,261]{0,1:T(8,128)} %convert_element_type.174) | copy-start | bytes 6414340
  (47 other events, 147.3 us)
Sparse Core Ops, SparseCore 0:
  11.0 57.7 all-gather.15
  71.7 55.3 all-gather.13
  130.0 55.3 all-gather.17
  188.3 60.8 all-gather.19
  252.1 67.6 all-gather.21
  343.1 43.8 all-gather.25
  389.2 44.6 all-gather.23
  436.8 55.1 all-gather.27
  495.0 60.7 all-gather.29
  578.9 42.4 reduce-scatter.24
  623.7 43.1 reduce-scatter.22
  802.5 75.9 reduce-scatter.28
  880.8 77.2 reduce-scatter.26
  960.3 134.9 reduce-scatter.46
  1097.4 130.5 reduce-scatter.42
  1230.1 130.5 reduce-scatter.48
  1362.8 130.7 reduce-scatter.44
  1498.9 134.3 all-reduce.6
  1636.3 146.9 reduce-scatter.38
  1786.1 146.2 reduce-scatter.32
  1935.4 146.9 reduce-scatter.30
  2085.4 184.9 reduce-scatter.40
  2273.3 183.4 reduce-scatter.34
  2459.7 270.3 reduce-scatter.36
where the time goes:
time: 2750 us; the launch traced here: 2740 us
  waiting for transfers between devices  2020 us (73%)
  blocking collectives  300 us (11%)
  matrix products  164 us (6%)
  local copies, waits for them, and re-layouts  161 us (6%)
  other arithmetic  67.9 us (2%)
    unnamed x29, waiting for transfers between devices  575 us
    reduce_scatter x1, waiting for transfers between devices, body(): lax.psum_scatter(lat_front[0], ('dp', 'fsdp'), scatter_dimension=0, tiled...  273 us
    reduce_scatter x1, waiting for transfers between devices, body(): lax.psum_scatter(lat_front[2], ('dp', 'fsdp'), scatter_dimension=0, tiled...  188 us
    reduce_scatter x1, waiting for transfers between devices, body(): lax.psum_scatter(enc_front[3], ('dp', 'fsdp'), scatter_dimension=0, tiled...  186 us
    reduce_scatter x1, waiting for transfers between devices, body(): lax.psum_scatter(enc_front[1], ('dp', 'fsdp'), scatter_dimension=0, tiled...  150 us
    reduce_scatter x1, waiting for transfers between devices, body(): lax.psum_scatter(enc_front[2], ('dp', 'fsdp'), scatter_dimension=0, tiled...  149 us
    reduce_scatter x1, waiting for transfers between devices, body(): lax.psum_scatter(lat_front[1], ('dp', 'fsdp'), scatter_dimension=0, tiled...  148 us
    reduce_scatter x1, waiting for transfers between devices, body(): lax.psum_scatter(key_total[:pix_rows].astype(jnp.bfloat16), 'fsdp', scatt...  76.9 us
  transfers between devices with their start and end apart: 24, of which 18 were waited for; matrix products, arithmetic and copies ran while one was open for 8% of the time, Pallas kernels for 0%

commit v1 on v0

v1 whole, which is shorter than its diff:
```python
from functools import partial

import jax
import jax.numpy as jnp
from jax import lax
from jax.experimental import pallas as pl
from jax.experimental.pallas import tpu as pltpu
from jax.sharding import PartitionSpec as P

HEADS = 8
HEAD = 128
USED = 1792
EPSILON = 1e-05
MASKED = -1e30
AXES = ("dp", "fsdp")
LANES = 128
BF = jnp.bfloat16
F32 = jnp.float32


def dot(left, right, dims):
    return lax.dot_general(left, right, ((dims[0], dims[1]), ((), ())), preferred_element_type=F32)


def mm(left, right):
    return dot(left, right, ((left.ndim - 1,), (0,)))


def mm_t(left, right):
    return dot(left, right, ((left.ndim - 1,), (1,)))


def tm(left, right):
    return dot(left, right, ((0,), (0,)))


def norm_parts(values):
    average = jnp.mean(values, axis=-1, keepdims=True)
    centered = values - average
    variance = jnp.mean(centered * centered, axis=-1, keepdims=True)
    inverse = lax.rsqrt(variance + EPSILON)
    return centered * inverse, inverse


def norm_back(hat, inverse, gains, grad_out):
    grad_hat = grad_out * gains
    first = jnp.mean(grad_hat, axis=-1, keepdims=True)
    second = jnp.mean(grad_hat * hat, axis=-1, keepdims=True)
    return inverse * (grad_hat - first - hat * second)


def gelu(values):
    return 0.5 * values * (1.0 + lax.erf(values * (0.5**0.5)))


def gelu_slope(values):
    density = jnp.exp(-0.5 * values * values) * ((0.5 / jnp.pi) ** 0.5)
    return 0.5 * (1.0 + lax.erf(values * (0.5**0.5))) + values * density


def xor_permute(values, sizes, step):
    dp_size, fsdp_size = sizes
    total = dp_size * fsdp_size
    return lax.ppermute(values, AXES, [(i, i ^ step) for i in range(total)])


def halve(values, bit, left, me, sizes):
    above = sum(1 for other in left if other > bit)
    below = len(left) - 1 - above
    rows, width = values.shape[-2:]
    view = values.reshape(2**above, 2, 2**below, rows, width)
    mine = (me >> bit) & 1
    send = lax.dynamic_index_in_dim(view, 1 - mine, 1, keepdims=False)
    keep = lax.dynamic_index_in_dim(view, mine, 1, keepdims=False)
    got = xor_permute(send, sizes, 1 << bit)
    summed = keep.astype(F32) + got.astype(F32)
    return summed.reshape(-1, rows, width)


def reduce_scatter(values, sizes, me):
    dp_size, fsdp_size = sizes
    low_bits = fsdp_size.bit_length() - 1
    all_bits = list(range((dp_size * fsdp_size).bit_length() - 1))
    core, far = all_bits[low_bits], all_bits[low_bits + 1 :]
    left = list(all_bits)
    values = halve(values, core, left, me, sizes).astype(BF)
    left.remove(core)
    half = values.shape[1] // 32 * 16 or values.shape[1] // 2
    pieces = []
    for piece, order in ((values[:, :half], far), (values[:, half:], far[::-1])):
        rest = list(left)
        for bit in order:
            piece = halve(piece, bit, rest, me, sizes).astype(BF)
            rest.remove(bit)
        pieces.append(piece)
    values = jnp.concatenate(pieces, axis=1)
    rest = all_bits[:low_bits]
    for bit in rest[::-1]:
        summed = halve(values, bit, list(rest), me, sizes)
        rest = rest[:-1]
        values = summed.astype(BF)
    return summed[0]


def butterfly(values, sizes):
    for bit in range((sizes[0] * sizes[1]).bit_length() - 1):
        values = values + xor_permute(values, sizes, 1 << bit)
    return values


def attend(q, k):
    scores = mm_t(q, k) * (HEAD**-0.5)
    powers = jnp.exp(scores - jnp.max(scores, axis=-1, keepdims=True))
    return powers / jnp.sum(powers, axis=-1, keepdims=True)


def attention_kernel(q_ref, k_ref, v_ref, o_ref):
    keys = k_ref.shape[0] * k_ref.shape[2]
    for head in range(q_ref.shape[2] // HEAD):
        cols = pl.ds(head * HEAD, HEAD)
        probs = attend(q_ref[0, :, cols], k_ref[:, 0, :, cols].reshape(keys, HEAD))
        o_ref[0, :, cols] = mm(probs.astype(BF), v_ref[:, 0, :, cols].reshape(keys, HEAD)).astype(BF)


def attention_back_kernel(q_ref, k_ref, v_ref, g_ref, dq_ref, dk_ref, dv_ref):
    shards, _, rows, _ = k_ref.shape
    keys = shards * rows
    scale = HEAD**-0.5
    for head in range(q_ref.shape[2] // HEAD):
        cols = pl.ds(head * HEAD, HEAD)
        q, grad = q_ref[0, :, cols], g_ref[0, :, cols]
        k = k_ref[:, 0, :, cols].reshape(keys, HEAD)
        v = v_ref[:, 0, :, cols].reshape(keys, HEAD)
        probs = attend(q, k)
        grad_probs = mm_t(grad, v)
        inner = jnp.sum(probs * grad_probs, axis=-1, keepdims=True)
        grad_scores = (probs * (grad_probs - inner) * scale).astype(BF)
        dq_ref[0, :, cols] = mm(grad_scores, k).astype(BF)
        dk_ref[:, 0, :, cols] = tm(grad_scores, q).astype(BF).reshape(shards, rows, HEAD)
        dv_ref[:, 0, :, cols] = tm(probs.astype(BF), grad).astype(BF).reshape(shards, rows, HEAD)


def attention_specs(images, rows, width, shards, group):
    own = pl.BlockSpec((1, rows, group), lambda i, h: (i, 0, h))
    whole = pl.BlockSpec((shards, 1, rows, group), lambda i, h: (0, i, 0, h))
    return own, whole, (images, width // group)


def attention(q, k, v):
    images, rows, width = q.shape
    own, whole, grid = attention_specs(images, rows, width, k.shape[0], 4 * HEAD)
    flops = 4 * images * rows * rows * k.shape[0] * width
    return pl.pallas_call(
        attention_kernel,
        grid=grid,
        in_specs=[own, whole, whole],
        out_specs=own,
        out_shape=jax.ShapeDtypeStruct(q.shape, BF),
        cost_estimate=pl.CostEstimate(flops=flops, bytes_accessed=5 * 2**20, transcendentals=2**20),
        name="attention",
    )(q, k, v)


def attention_back(q, k, v, grad):
    images, rows, width = q.shape
    own, whole, grid = attention_specs(images, rows, width, k.shape[0], 4 * HEAD)
    flops = 10 * images * rows * rows * k.shape[0] * width
    return pl.pallas_call(
        attention_back_kernel,
        grid=grid,
        in_specs=[own, whole, whole, own],
        out_specs=[own, whole, whole],
        out_shape=[jax.ShapeDtypeStruct(a.shape, BF) for a in (q, k, v)],
        cost_estimate=pl.CostEstimate(flops=flops, bytes_accessed=10 * 2**20, transcendentals=2**20),
        name="attention_back",
    )(q, k, v, grad)


def feed_forward(resid, gain, shift, bias_one, bias_two, first, second):
    hat, inverse = norm_parts(resid)
    normed = (hat * gain + shift).astype(BF)
    pre = mm(normed, first) + bias_one
    act = gelu(pre).astype(BF)
    return resid + mm(act, second) + bias_two, (hat, inverse, normed, pre, act)


def feed_back(kept, gain, first, second, grad_out):
    hat, inverse, normed, pre, act = kept
    grad_low = grad_out.astype(BF)
    d_second = tm(act, grad_low).astype(BF)
    d_pre = mm_t(grad_low, second) * gelu_slope(pre)
    d_pre_low = d_pre.astype(BF)
    d_first = tm(normed, d_pre_low).astype(BF)
    d_normed = mm_t(d_pre_low, first)
    d_resid = norm_back(hat, inverse, gain, d_normed)
    sums = (
        jnp.sum(d_normed * hat, axis=0),
        jnp.sum(d_normed, axis=0),
        jnp.sum(d_pre, axis=0),
        jnp.sum(grad_out, axis=0),
    )
    return grad_out + d_resid, d_first, d_second, sums


def pad_lanes(values, width):
    return jnp.pad(values, [(0, 0)] * (values.ndim - 1) + [(0, width - values.shape[-1])])


def body(
    sizes,
    latents,
    pixels,
    lengths,
    pix_gain,
    pix_bias,
    pix_kv,
    enc_query,
    enc_out,
    enc_mlp,
    enc_gains,
    enc_biases,
    lat_qkv,
    lat_out,
    lat_mlp,
    lat_gains,
    lat_biases,
    cotangent,
):
    dp_size, fsdp_size = sizes
    devices = dp_size * fsdp_size
    my_fsdp = lax.axis_index("fsdp")
    me = lax.axis_index("dp") * fsdp_size + my_fsdp
    images, lat_rows, width = latents.shape
    rows = images * lat_rows
    pix_rows, features = pixels.shape
    padded = -(-features // LANES) * LANES
    own = width // devices

    kv_t = pad_lanes(jnp.transpose(pix_kv, (2, 0, 1)), width // 2)
    small = jnp.concatenate([enc_gains, enc_biases, lat_gains, lat_biases], axis=0)
    kv_t = kv_t.at[:, 0, padded : padded + small.shape[0]].set(small.T)
    enc_pack = jnp.concatenate([kv_t.reshape(own, width), enc_query, enc_out, enc_mlp[0], enc_mlp[1]], axis=0)
    lat_pack = jnp.concatenate([lat_qkv[0], lat_qkv[1], lat_qkv[2], lat_out, lat_mlp[0], lat_mlp[1]], axis=0)
    enc_all = lax.all_gather(enc_pack, AXES, axis=0, tiled=False)
    lat_all = lax.all_gather(lat_pack, AXES, axis=0, tiled=False)

    def part(whole, index):
        return whole[:, index * own : (index + 1) * own].reshape(width, width)

    kv_full, w_query, w_out, w_first, w_second = [part(enc_all, i) for i in range(5)]
    l_query, l_key, l_value, l_out, l_first, l_second = [part(lat_all, i) for i in range(6)]
    key_t = kv_full[:, :padded]
    value_t = kv_full[:, width // 2 : width // 2 + padded]
    small_all = kv_full[:, padded : padded + small.shape[0]].T.astype(F32)
    n_gain, n_bias = enc_gains.shape[0], enc_biases.shape[0]
    gains_enc, biases_enc = small_all[:n_gain], small_all[n_gain : n_gain + n_bias]
    gains_lat, biases_lat = small_all[n_gain + n_bias : 2 * n_gain + n_bias], small_all[2 * n_gain + n_bias :]

    gain_f = pix_gain.astype(F32)
    pix_hat, pix_inverse = norm_parts(pixels.astype(F32))
    pix_low = pad_lanes((pix_hat * gain_f + pix_bias.astype(F32)).astype(BF), padded)[:USED]

    latent_in = latents.astype(F32).reshape(rows, width)
    in_hat, in_inverse = norm_parts(latent_in)
    in_low = (in_hat * gains_enc[0] + biases_enc[0]).astype(BF)
    enc_q = mm(in_low, w_query).astype(BF)
    query_pix = mm(enc_q, key_t).astype(BF)
    counts = lengths[0]
    ends = jnp.cumsum(counts)
    firsts = ends - counts
    column = lax.broadcasted_iota(jnp.int32, (images, lat_rows, USED), 2)
    valid = ((column >= firsts[:, None, None]) & (column < ends[:, None, None])).reshape(rows, USED)
    enc_scale = width**-0.5
    scores = jnp.where(valid, mm_t(query_pix, pix_low) * enc_scale, MASKED)
    powers = jnp.exp(scores - jnp.max(scores, axis=-1, keepdims=True))
    probs = powers / jnp.sum(powers, axis=-1, keepdims=True)
    probs_low = probs.astype(BF)
    mixed_pix = mm(probs_low, pix_low).astype(BF)
    enc_mixed = mm_t(mixed_pix, value_t).astype(BF)
    enc_resid = latent_in + mm(enc_mixed, w_out)
    first_out, enc_kept = feed_forward(
        enc_resid, gains_enc[1], biases_enc[1], biases_enc[2], biases_enc[3], w_first, w_second
    )

    lat_hat, lat_inverse = norm_parts(first_out)
    lat_low = (lat_hat * gains_lat[0] + biases_lat[0]).astype(BF)
    shards = [lat_low] + [xor_permute(lat_low, sizes, k) for k in range(1, fsdp_size)]
    lat_every = jnp.concatenate(shards, axis=0)
    shape = (images, lat_rows, width)
    lat_q = mm(lat_low, l_query).astype(BF).reshape(shape)
    lat_k = mm(lat_every, l_key).astype(BF).reshape((fsdp_size,) + shape)
    lat_v = mm(lat_every, l_value).astype(BF).reshape((fsdp_size,) + shape)
    lat_mixed = attention(lat_q, lat_k, lat_v).reshape(rows, width)
    lat_resid = first_out + mm(lat_mixed, l_out)
    second_out, lat_kept = feed_forward(
        lat_resid, gains_lat[1], biases_lat[1], biases_lat[2], biases_lat[3], l_first, l_second
    )
    result = second_out.astype(BF).reshape(shape)

    grad_out = cotangent.astype(F32).reshape(rows, width)
    grad_mid, d_l_first, d_l_second, lat_sums = feed_back(lat_kept, gains_lat[1], l_first, l_second, grad_out)
    grad_mid_low = grad_mid.astype(BF)
    d_l_out = tm(lat_mixed, grad_mid_low).astype(BF)
    d_mixed = mm_t(grad_mid_low, l_out).astype(BF).reshape(shape)
    d_q, d_k, d_v = attention_back(lat_q, lat_k, lat_v, d_mixed)
    d_q, d_k, d_v = d_q.reshape(rows, width), d_k.reshape(-1, width), d_v.reshape(-1, width)
    d_l_query = tm(lat_low, d_q).astype(BF)
    d_l_key = tm(lat_every, d_k).astype(BF)
    d_l_value = tm(lat_every, d_v).astype(BF)
    d_every = mm_t(d_k, l_key) + mm_t(d_v, l_value)
    d_lat_normed = mm_t(d_q, l_query) + d_every[:rows]
    for k in range(1, fsdp_size):
        piece = d_every[k * rows : (k + 1) * rows].astype(BF)
        d_lat_normed = d_lat_normed + xor_permute(piece, sizes, k).astype(F32)
    d_first_out = grad_mid + norm_back(lat_hat, lat_inverse, gains_lat[0], d_lat_normed)
    lat_front = (jnp.sum(d_lat_normed * lat_hat, axis=0), jnp.sum(d_lat_normed, axis=0))

    def stack(pieces):
        return jnp.concatenate([p.reshape(devices, own, width) for p in pieces], axis=1)

    lat_grads = reduce_scatter(
        stack([d_l_query, d_l_key, d_l_value, d_l_out, d_l_first, d_l_second]), sizes, me
    )

    grad_enc, d_first, d_second, enc_sums = feed_back(enc_kept, gains_enc[1], w_first, w_second, d_first_out)
    grad_enc_low = grad_enc.astype(BF)
    d_w_out = tm(enc_mixed, grad_enc_low).astype(BF)
    d_enc_mixed = mm_t(grad_enc_low, w_out).astype(BF)
    d_value_t = tm(d_enc_mixed, mixed_pix)
    mixed_back = mm(d_enc_mixed, value_t).astype(BF)
    d_probs = mm_t(mixed_back, pix_low)
    inner = jnp.sum(probs * d_probs, axis=-1, keepdims=True)
    d_scores = (probs * (d_probs - inner) * enc_scale).astype(BF)
    d_query_pix = mm(d_scores, pix_low).astype(BF)
    d_enc_q = mm_t(d_query_pix, key_t).astype(BF)
    d_key_t = tm(enc_q, d_query_pix)
    d_pix_low = tm(d_scores, query_pix) + tm(probs_low, mixed_back)
    d_w_query = tm(in_low, d_enc_q).astype(BF)
    d_in_normed = mm_t(d_enc_q, w_query)
    d_latents = grad_enc + norm_back(in_hat, in_inverse, gains_enc[0], d_in_normed)
    enc_front = (jnp.sum(d_in_normed * in_hat, axis=0), jnp.sum(d_in_normed, axis=0))

    d_pix_all = d_pix_low[:, :features]
    d_pix_sums = jnp.stack([jnp.sum(d_pix_all * pix_hat[:USED], axis=0), jnp.sum(d_pix_all, axis=0)])
    d_pix_sums = butterfly(pad_lanes(d_pix_sums, padded), sizes)[:, :features]
    share = pix_rows // fsdp_size
    d_pix_pad = jnp.pad(d_pix_low, ((0, pix_rows - USED), (0, 0)))
    d_pix_own = lax.dynamic_slice_in_dim(d_pix_pad, my_fsdp * share, share, 0)
    for k in range(1, fsdp_size):
        piece = lax.dynamic_slice_in_dim(d_pix_pad, (my_fsdp ^ k) * share, share, 0).astype(BF)
        d_pix_own = d_pix_own + xor_permute(piece, sizes, k).astype(F32)
    hat_own = lax.dynamic_slice_in_dim(pix_hat, my_fsdp * share, share, 0)
    inverse_own = lax.dynamic_slice_in_dim(pix_inverse, my_fsdp * share, share, 0)
    d_pixels = norm_back(hat_own, inverse_own, gain_f, d_pix_own[:, :features])

    small_grads = jnp.stack(
        [enc_front[0], enc_sums[0], enc_front[1], enc_sums[1], enc_sums[2], enc_sums[3]]
        + [lat_front[0], lat_sums[0], lat_front[1], lat_sums[1], lat_sums[2], lat_sums[3]]
    )
    high = small_grads.astype(BF)
    low = (small_grads - high.astype(F32)).astype(BF)
    n_small = small_grads.shape[0]
    half_pad = width // 2 - padded
    kv_grads = jnp.concatenate(
        [
            d_key_t.astype(BF),
            pad_lanes(high.T, half_pad),
            d_value_t.astype(BF),
            pad_lanes(low.T, half_pad),
        ],
        axis=1,
    )
    enc_grads = reduce_scatter(stack([kv_grads, d_w_query, d_w_out, d_first, d_second]), sizes, me)

    def mine(whole, index):
        return whole[index * own : (index + 1) * own]

    kv_own = mine(enc_grads, 0)
    d_pix_kv = jnp.stack([kv_own[:, :features].T, kv_own[:, width // 2 : width // 2 + features].T])
    start = width // 2 + padded
    small_own = (kv_own[:, padded : padded + n_small] + kv_own[:, start : start + n_small]).T
    return (
        result,
        d_latents.reshape(shape),
        d_pixels,
        d_pix_sums[0],
        d_pix_sums[1],
        d_pix_kv,
        mine(enc_grads, 1),
        mine(enc_grads, 2),
        jnp.stack([mine(enc_grads, 3), mine(enc_grads, 4)]),
        small_own[:n_gain],
        small_own[n_gain : n_gain + n_bias],
        jnp.stack([mine(lat_grads, 0), mine(lat_grads, 1), mine(lat_grads, 2)]),
        mine(lat_grads, 3),
        jnp.stack([mine(lat_grads, 4), mine(lat_grads, 5)]),
        small_own[n_gain + n_bias : 2 * n_gain + n_bias],
        small_own[2 * n_gain + n_bias :],
    )


def solution(mesh):
    split, rows, columns = P("dp", "fsdp", None), P(AXES, None), P(None, AXES)
    middle = P(None, AXES, None)
    weights = (P(None, None, AXES), rows, rows, middle, columns, columns, middle, rows, middle, columns, columns)
    return jax.shard_map(
        partial(body, (mesh.shape["dp"], mesh.shape["fsdp"])),
        mesh=mesh,
        in_specs=(split, P("dp", None), P("dp", None), P(), P()) + weights + (split,),
        out_specs=(split, split, rows, P(), P()) + weights,
        check_vma=False,
    )
```

time: 2750 us -> 644 us (0.23)
  waiting for transfers between devices: 2020 us -> 368 us
  blocking collectives: 300 us -> 0 us
  matrix products: 164 us -> 71 us
  local copies, waits for them, and re-layouts: 161 us -> 82.9 us
  starting transfers between devices: 1.72 us -> 29.5 us
    reduce_scatter x10 -> x0, waiting for transfers between devices: 1260 us -> none  [the longest x1 273 us: body(): lax.psum_scatter(lat_front[0], ('dp', 'fsdp'), scatter_dimension=0, tiled...]
    unnamed x29 -> x2, waiting for transfers between devices: 575 us -> 0.03 us
    all_gather x4 -> x0, blocking collectives: 263 us -> none  [the longest x1 69.5 us: encoder_weights(): lax.all_gather(fronted[4], ('dp', 'fsdp'), axis=0, tiled=True)]
    ppermute x0 -> x28, waiting for transfers between devices: none -> 176 us  [xor_permute(): return lax.ppermute(values, AXES, [(i, i ^ step) for i in range(total)])]
    dot_general x48 -> x42, matrix products: 164 us -> 71 us  [dot(): lax.dot_general(left, right, ((dims[0], dims[1]), ((), ())), preferred_el...]
    dynamic_update_slice x4 -> x0, local copies, waits for them, and re-layouts: 57.3 us -> none  [the longest x2 28.7 us: place(): lax.dynamic_update_slice_in_dim(key_total, key_piece, first, 0)]
    psum x1 -> x0, blocking collectives: 37.4 us -> none  [body(): lax.psum((d_pix_gain_part, d_pix_bias_part), ('dp', 'fsdp'))]
    ppermute x0 -> x28, starting transfers between devices: none -> 29.4 us  [xor_permute(): return lax.ppermute(values, AXES, [(i, i ^ step) for i in range(total)])]
  transfers between devices with their start and end apart: 24 -> 30, of which waited for: 18 -> 15; matrix products, arithmetic and copies ran while one was open for 8% -> 16% of each run, Pallas kernels for 0% -> 0%
where the time goes in v1:
time: 644 us; the launch traced here: 634 us
  waiting for transfers between devices  368 us (57%)
  local copies, waits for them, and re-layouts  82.9 us (13%)
  matrix products  71 us (11%)
  other arithmetic  46.6 us (7%)
  starting transfers between devices  29.5 us (5%)
  Pallas kernels  20.2 us (3%)
  between operations  16 us (2%)
    ppermute x28, waiting for transfers between devices, xor_permute(): return lax.ppermute(values, AXES, [(i, i ^ step) for i in range(total)])  176 us
    all_gather x1, waiting for transfers between devices, body(): lat_all = lax.all_gather(lat_pack, AXES, axis=0, tiled=False)  109 us
    all_gather x1, waiting for transfers between devices, body(): enc_all = lax.all_gather(enc_pack, AXES, axis=0, tiled=False)  82.6 us
    dot_general x42, matrix products, dot(): lax.dot_general(left, right, ((dims[0], dims[1]), ((), ())), preferred_el...  71 us
    unnamed x235, local copies, waits for them, and re-layouts  40 us
    ppermute x28, starting transfers between devices, xor_permute(): return lax.ppermute(values, AXES, [(i, i ^ step) for i in range(total)])  29.4 us
    convert_element_type x2, other arithmetic, reduce_scatter(): values = halve(values, core, left, me, sizes).astype(BF)  15.2 us
    slice x2, local copies, waits for them, and re-layouts, part(): return whole[:, index * own:(index + 1) * own].reshape(width, width)  13 us
  transfers between devices with their start and end apart: 30, of which 15 were waited for; matrix products, arithmetic and copies ran while one was open for 16% of the time, Pallas kernels for 0%

profile of v1, /device:TPU:0, one launch (start us, length us, event | category | flops | bytes accessed | tf_op | source)
XLA Modules:
  0.0 634.0 jit_solution(9090330630769722266)
XLA Ops:
  10.5 2.7 fusion.73
  23.9 2.1 fusion.10
  26.0 82.6 %all-gather.5.cloned.1.call-done = bf16[5120,1024]{1,0:T(8,128)(2,1)} async-done(((bf16[160,1024]{1,0:T(8,128)(2,1)}), bf16[5120,1024]{1,0:T(8,128)(2,1)}) %all-gather.5.cloned.1.call-update) | async-done | bytes 10485776 | tf_op jit(solution)/shard_map/all_gather | solution.py:244
  108.7 4.6 fusion.87
  113.4 3.7 slice_reduce_fusion.4
  129.4 109.0 %all-gather.7.cloned.1.call-done = bf16[6144,1024]{1,0:T(8,128)(2,1)} async-done(((bf16[192,1024]{1,0:T(8,128)(2,1)}), bf16[6144,1024]{1,0:T(8,128)(2,1)}) %all-gather.7.cloned.1.call-update) | async-done | bytes 12582928 | tf_op jit(solution)/shard_map/all_gather | solution.py:245
  238.4 8.4 %fusion.86 = (bf16[32,32,1024]{2,1,0:T(8,128)(2,1)}, bf16[32,32,1024]{2,1,0:T(8,128)(2,1)}, bf16[32,32,1024]{2,1,0:T(8,128)(2,1)}, bf16[32,32,1024]{2,1,0:T(8,12...) fusion(bf16[32,192,1024]{2,1,0:T(8,128)(2,1)} %bitcast.272), kind=kLoop, calls=%fused_computation.298 | loop fusion | bytes 25165824 | tf_op jit(solution)/shard_map/slice | solution.py:248
  246.9 2.0 convolution_convert_fusion.18
  248.9 5.2 convolution_convert_fusion.11
  254.1 5.1 convolution_convert_fusion.10
  259.2 8.2 %attention.1 = bf16[2,128,1024]{2,1,0:T(8,128)(2,1)} custom-call(bf16[2,128,1024]{2,1,0:T(8,128)(2,1)} %bitcast.331, bf16[4,2,128,1024]{3,2,1,0:T(8,128)(2,1)} %bitcast.290, bf16[4,2,128,1024]{3,2,1,0:T(8,128)(2,1)} %bitcast.292), custom_call_target="tpu_custom_call" | custom-call | flops 536870912 | bytes 5242880 | tf_op jit(solution)/shard_map/attention/pallas_call | solution.py:153
  267.4 2.7 fusion.97
  278.4 2.1 convolution_convert_fusion.2
  280.5 2.3 convolution_convert_fusion.1
  282.8 12.1 %attention_back.1 = (bf16[2,128,1024]{2,1,0:T(8,128)(2,1)}, bf16[4,2,128,1024]{3,2,1,0:T(8,128)(2,1)}, bf16[4,2,128,1024]{3,2,1,0:T(8,128)(2,1)}) custom-call(bf16[2,128,1024]{2,1,0:T(8,128)(2,1)} %bitcast.332, bf16[4,2,128,1024]{3,2,1,0:T(8,128)(2,1)} %bitcast.291, bf16[4,2,128,1024]{3,2,1,0:T(8,128)(2,1)} %bitcast.293, bf16[2,128,1024]{2,1,0:T(8,128)(2,1)} %bitcast.333), custom_call_target="tpu_custom_call" | custom-call | flops 1342177280 | bytes 10485760 | tf_op jit(solution)/shard_map/attention_back/pallas_call | solution.py:168
  294.9 4.7 fusion.101
  299.6 2.4 fusion.98
  304.6 2.0 collective-permute-start.3
  309.7 3.7 convolution_convert_fusion.4
  315.1 3.8 convolution_convert_fusion.3
  328.0 22.3 %collective-permute-done.4 = bf16[256,1024]{1,0:T(8,128)(2,1)S(1)} collective-permute-done((bf16[256,1024]{1,0:T(8,128)(2,1)S(1)}, bf16[256,1024]{1,0:T(8,128)(2,1)S(1)}, u32[]{:S(2)}, u32[]{:S(2)}) %collective-permute-start.4) | collective-permute-done | bytes 524320 | tf_op jit(solution)/shard_map/ppermute | solution.py:64
  350.4 2.0 multiply_reduce_fusion.2
  366.6 2.1 convolution_convert_fusion.8
  368.7 2.2 convolution_convert_fusion.7
  370.9 2.1 convolution_convert_fusion.6
  373.1 2.1 multiply_reduce_fusion.4
  377.0 3.0 copy.53
  380.0 1.9 constant_dynamic-update-slice_fusion.8
  387.7 3.9 copy-done.6
  391.6 3.2 dynamic-slice_bitcast_fusion.1
  394.8 6.5 %dynamic-slice_bitcast_fusion = bf16[4,4,192,1024]{3,2,1,0:T(8,128)(2,1)} fusion(bf16[4,2,4,192,1024]{4,3,2,1,0:T(8,128)(2,1)} %constant_dynamic-update-slice_fusion.9, s32[]{:T(128)S(6)} %select_n.84), kind=kLoop, calls=%fused_computation.6 | loop fusion | bytes 12582916 | tf_op jit(solution)/shard_map/jit(dynamic_index_in_dim)/squeeze | solution.py:73
  405.0 3.5 collective-permute-done.9
  409.2 3.7 fusion.27
  415.7 2.2 collective-permute-done.12
  419.5 2.2 collective-permute-start.8
  426.0 7.6 %collective-permute-done.8 = bf16[512,384]{0,1:T(8,128)(2,1)S(1)} collective-permute-done((bf16[512,384]{0,1:T(8,128)(2,1)S(1)}, bf16[512,384]{0,1:T(8,128)(2,1)S(1)}, u32[]{:S(2)}, u32[]{:S(2)}) %collective-permute-start.8) | collective-permute-done | bytes 393248 | tf_op jit(solution)/shard_map/ppermute | solution.py:64
  433.5 22.4 %collective-permute-done.7 = bf16[512,384]{0,1:T(8,128)(2,1)S(1)} collective-permute-done((bf16[512,384]{0,1:T(8,128)(2,1)S(1)}, bf16[512,384]{0,1:T(8,128)(2,1)S(1)}, u32[]{:S(2)}, u32[]{:S(2)}) %collective-permute-start.7) | collective-permute-done | bytes 393248 | tf_op jit(solution)/shard_map/ppermute | solution.py:64
  456.0 2.0 fusion.83
  458.0 7.1 %fusion.1 = bf16[4,4,160,1024]{3,2,1,0:T(8,128)(2,1)S(1)} fusion(bf16[4,4,160,1024]{3,2,1,0:T(8,128)(2,1)} %collective-permute-done.14, bf16[4,2,4,160,1024]{4,3,2,1,0:T(8,128)(2,1)} %copy-done.6, s32[]{:T(128)S(6)} %select_n.83), kind=kLoop, calls=%fused_computation.3 | loop fusion | flops 10485760 | bytes 15728644 | tf_op jit(solution)/shard_map/convert_element_type | solution.py:86
  470.4 8.1 %fusion = bf16[4,4,192,1024]{3,2,1,0:T(8,128)(2,1)S(1)} fusion(bf16[4,4,192,1024]{3,2,1,0:T(8,128)(2,1)} %collective-permute-done.21, bf16[4,2,4,192,1024]{4,3,2,1,0:T(8,128)(2,1)} %constant_dynamic-update-slice_fusion.9, s32[]{:T(128)S(6)} %select_n.83), kind=kLoop, calls=%fused_computation.1 | loop fusion | flops 12582912 | bytes 18874372 | tf_op jit(solution)/shard_map/convert_element_type | solution.py:86
  481.7 17.5 %collective-permute-done.15 = bf16[2,4,80,1024]{3,2,1,0:T(8,128)(2,1)} collective-permute-done((bf16[2,4,80,1024]{3,2,1,0:T(8,128)(2,1)}, bf16[2,4,80,1024]{3,2,1,0:T(8,128)(2,1)}, u32[]{:S(2)}, u32[]{:S(2)}) %collective-permute-start.15) | collective-permute-done | bytes 1310752 | tf_op jit(solution)/shard_map/ppermute | solution.py:64
  505.2 41.8 %collective-permute-done.16 = bf16[1,4,80,1024]{3,2,1,0:T(8,128)(2,1)S(1)} collective-permute-done((bf16[1,4,80,1024]{3,2,1,0:T(8,128)(2,1)S(1)}, bf16[1,4,80,1024]{3,2,1,0:T(8,128)(2,1)S(1)}, u32[]{:S(2)}, u32[]{:S(2)}) %collective-permute-start.16) | collective-permute-done | bytes 655392 | tf_op jit(solution)/shard_map/ppermute | solution.py:64
  551.3 2.0 subtract_multiply_fusion.3
  553.3 22.5 %collective-permute-done.19 = bf16[1,2,160,1024]{3,2,1,0:T(8,128)(2,1)S(1)} collective-permute-done((bf16[1,2,160,1024]{3,2,1,0:T(8,128)(2,1)S(1)}, bf16[1,2,160,1024]{3,2,1,0:T(8,128)(2,1)S(1)}, u32[]{:S(2)}, u32[]{:S(2)}) %collective-permute-start.19) | collective-permute-done | bytes 655392 | tf_op jit(solution)/shard_map/ppermute | solution.py:64
  576.9 3.2 collective-permute-start.26
  580.2 11.4 %collective-permute-done.20 = bf16[1,1,160,1024]{3,2,1,0:T(8,128)(2,1)S(1)} collective-permute-done((bf16[1,1,160,1024]{3,2,1,0:T(8,128)(2,1)S(1)}, bf16[1,1,160,1024]{3,2,1,0:T(8,128)(2,1)S(1)}, u32[]{:S(2)}, u32[]{:S(2)}) %collective-permute-start.20) | collective-permute-done | bytes 327712 | tf_op jit(solution)/shard_map/ppermute | solution.py:64
  599.2 15.0 %collective-permute-done.26 = bf16[1,2,192,1024]{3,2,1,0:T(8,128)(2,1)S(1)} collective-permute-done((bf16[1,2,192,1024]{3,2,1,0:T(8,128)(2,1)S(1)}, bf16[1,2,192,1024]{3,2,1,0:T(8,128)(2,1)S(1)}, u32[]{:S(2)}, u32[]{:S(2)}) %collective-permute-start.26) | collective-permute-done | bytes 786464 | tf_op jit(solution)/shard_map/ppermute | solution.py:64
  616.1 8.5 %collective-permute-done.27 = bf16[1,1,192,1024]{3,2,1,0:T(8,128)(2,1)S(1)} collective-permute-done((bf16[1,1,192,1024]{3,2,1,0:T(8,128)(2,1)S(1)}, bf16[1,1,192,1024]{3,2,1,0:T(8,128)(2,1)S(1)}, u32[]{:S(2)}, u32[]{:S(2)}) %collective-permute-start.27) | collective-permute-done | bytes 393248 | tf_op jit(solution)/shard_map/ppermute | solution.py:64
  (410 shorter events, 116.3 us)
Async XLA Ops:
  7.2 11.9 %copy-start.62 = (bf16[3,32,1024]{2,1,0:T(8,128)(2,1)S(1)}, bf16[3,32,1024]{2,1,0:T(8,128)(2,1)}, u32[]{:S(2)}) copy-start(bf16[3,32,1024]{2,1,0:T(8,128)(2,1)} %param.30) | copy-start | bytes 589828
  7.2 11.9 %copy-start.64 = (bf16[32,1024]{1,0:T(8,128)(2,1)S(1)}, bf16[32,1024]{1,0:T(8,128)(2,1)}, u32[]{:S(2)}) copy-start(bf16[32,1024]{1,0:T(8,128)(2,1)} %param.31) | copy-start | bytes 196612
  7.2 11.9 %copy-start.63 = (bf16[2,32,1024]{2,1,0:T(8,128)(2,1)S(1)}, bf16[2,32,1024]{2,1,0:T(8,128)(2,1)}, u32[]{:S(2)}) copy-start(bf16[2,32,1024]{2,1,0:T(8,128)(2,1)} %param.32) | copy-start | bytes 393220
  7.2 12.7 %copy-start.99 = (bf16[261]{0:T(512)(128)(2,1)S(1)}, bf16[261]{0:T(512)(128)(2,1)}, u32[]{:S(2)}) copy-start(bf16[261]{0:T(512)(128)(2,1)} %param.23) | copy-start | bytes 1570
  7.2 12.8 %copy-start.100 = (bf16[261]{0:T(512)(128)(2,1)S(1)}, bf16[261]{0:T(512)(128)(2,1)}, u32[]{:S(2)}) copy-start(bf16[261]{0:T(512)(128)(2,1)} %param.22) | copy-start | bytes 1570
  7.2 12.8 %copy-start.103 = (s32[1,2]{1,0:T(1,128)S(1)}, s32[1,2]{1,0:T(1,128)}, u32[]{:S(2)}) copy-start(s32[1,2]{1,0:T(1,128)} %param.21) | copy-start | bytes 28
  7.2 13.0 %copy-start.7 = (bf16[2,128,1024]{2,1,0:T(8,128)(2,1)S(1)}, bf16[2,128,1024]{2,1,0:T(8,128)(2,1)}, u32[]{:S(2)}) copy-start(bf16[2,128,1024]{2,1,0:T(8,128)(2,1)} %param.19) | copy-start | bytes 1572868
  7.3 13.1 %copy-start.30 = (bf16[2,128,1024]{2,1,0:T(8,128)(2,1)S(1)}, bf16[2,128,1024]{2,1,0:T(8,128)(2,1)}, u32[]{:S(2)}) copy-start(bf16[2,128,1024]{2,1,0:T(8,128)(2,1)} %param.35) | copy-start | bytes 1572868
  7.3 101.4 %all-gather.5.cloned.1.call-start = ((), (), s32[]{:S(2)}) async-start(), calls=%async_computation | async-start | bytes 10813440 | tf_op jit(solution)/shard_map/all_gather | solution.py:244
  19.0 219.4 %all-gather.7.cloned.1.call-start = ((), (), s32[]{:S(2)}) async-start(), calls=%async_computation.1 | async-start | bytes 12976128 | tf_op jit(solution)/shard_map/all_gather | solution.py:245
  124.9 129.2 %copy-start.49 = (bf16[256,1024]{1,0:T(8,128)(2,1)}, bf16[256,1024]{1,0:T(8,128)(2,1)S(1)}, u32[]{:S(2)}) copy-start(bf16[256,1024]{1,0:T(8,128)(2,1)S(1)} %add_convert_fusion.5) | copy-start | bytes 1572868
  125.0 124.0 %collective-permute-start.2 = (bf16[256,1024]{1,0:T(8,128)(2,1)S(1)}, bf16[256,1024]{1,0:T(8,128)(2,1)}, u32[]{:S(2)}, u32[]{:S(2)}) collective-permute-start(bf16[256,1024]{1,0:T(8,128)(2,1)S(1)} %add_convert_fusion.5), channel_id=1, source_target_pairs={{0,3},{1,2},{2,1},{3,0},{4,7},{5,6},{6,5},{7,4},{8,11},{9,10},{10,... | collective-permute-start | bytes 1572872 | tf_op jit(solution)/shard_map/ppermute | solution.py:64
  126.8 122.1 %collective-permute-start.1 = (bf16[256,1024]{1,0:T(8,128)(2,1)S(1)}, bf16[256,1024]{1,0:T(8,128)(2,1)}, u32[]{:S(2)}, u32[]{:S(2)}) collective-permute-start(bf16[256,1024]{1,0:T(8,128)(2,1)S(1)} %add_convert_fusion.5), channel_id=1, source_target_pairs={{0,2},{1,3},{2,0},{3,1},{4,6},{5,7},{6,4},{7,5},{8,10},{9,11},{10,... | collective-permute-start | bytes 1572872 | tf_op jit(solution)/shard_map/ppermute | solution.py:64
  127.8 121.2 %collective-permute-start = (bf16[256,1024]{1,0:T(8,128)(2,1)S(1)}, bf16[256,1024]{1,0:T(8,128)(2,1)}, u32[]{:S(2)}, u32[]{:S(2)}) collective-permute-start(bf16[256,1024]{1,0:T(8,128)(2,1)S(1)} %add_convert_fusion.5), channel_id=1, source_target_pairs={{0,1},{1,0},{2,3},{3,2},{4,5},{5,4},{6,7},{7,6},{8,9},{9,8},{10,11... | collective-permute-start | bytes 1572872 | tf_op jit(solution)/shard_map/ppermute | solution.py:64
  270.1 10.4 %copy-start.3 = (f32[256,1024]{1,0:T(8,128)}, f32[256,1024]{1,0:T(8,128)S(1)}, u32[]{:S(2)}) copy-start(f32[256,1024]{1,0:T(8,128)S(1)} %get-tuple-element.176) | copy-start | bytes 3145732
  302.2 25.9 %collective-permute-start.5 = (bf16[256,1024]{1,0:T(8,128)(2,1)S(1)}, bf16[256,1024]{1,0:T(8,128)(2,1)S(1)}, u32[]{:S(2)}, u32[]{:S(2)}) collective-permute-start(bf16[256,1024]{1,0:T(8,128)(2,1)S(1)} %get-tuple-element.139), channel_id=1, source_target_pairs={{0,3},{1,2},{2,1},{3,0},{4,7},{5,6},{6,5},{7,4},{8,11},{9,10},{10,... | collective-permute-start | bytes 1572872 | tf_op jit(solution)/shard_map/ppermute | solution.py:64
  303.8 46.6 %collective-permute-start.4 = (bf16[256,1024]{1,0:T(8,128)(2,1)S(1)}, bf16[256,1024]{1,0:T(8,128)(2,1)S(1)}, u32[]{:S(2)}, u32[]{:S(2)}) collective-permute-start(bf16[256,1024]{1,0:T(8,128)(2,1)S(1)} %get-tuple-element.140), channel_id=1, source_target_pairs={{0,2},{1,3},{2,0},{3,1},{4,6},{5,7},{6,4},{7,5},{8,10},{9,11},{10,... | collective-permute-start | bytes 1572872 | tf_op jit(solution)/shard_map/ppermute | solution.py:64
  304.6 45.8 %collective-permute-start.3 = (bf16[256,1024]{1,0:T(8,128)(2,1)S(1)}, bf16[256,1024]{1,0:T(8,128)(2,1)S(1)}, u32[]{:S(2)}, u32[]{:S(2)}) collective-permute-start(bf16[256,1024]{1,0:T(8,128)(2,1)S(1)} %get-tuple-element.138), channel_id=1, source_target_pairs={{0,1},{1,0},{2,3},{3,2},{4,5},{5,4},{6,7},{7,6},{8,9},{9,8},{10,11... | collective-permute-start | bytes 1572872 | tf_op jit(solution)/shard_map/ppermute | solution.py:64
  326.4 23.9 %copy-start.43 = (bf16[32,32,1024]{2,1,0:T(8,128)(2,1)S(1)}, bf16[32,32,1024]{2,1,0:T(8,128)(2,1)}, u32[]{:S(2)}) copy-start(bf16[32,32,1024]{2,1,0:T(8,128)(2,1)} %copy-done.42) | copy-start | bytes 6291460
  326.4 23.9 %copy-start.78 = (f32[256]{0:T(256)S(1)}, f32[256]{0:T(256)}, u32[]{:S(2)}) copy-start(f32[256]{0:T(256)} %copy-done.77) | copy-start | bytes 3076
  326.5 23.9 %copy-start.82 = (f32[256]{0:T(256)S(1)}, f32[256]{0:T(256)}, u32[]{:S(2)}) copy-start(f32[256]{0:T(256)} %copy-done.81) | copy-start | bytes 3076
  394.8 63.3 %collective-permute-start.14 = (bf16[4,4,160,1024]{3,2,1,0:T(8,128)(2,1)}, bf16[4,4,160,1024]{3,2,1,0:T(8,128)(2,1)}, u32[]{:S(2)}, u32[]{:S(2)}) collective-permute-start(bf16[4,4,160,1024]{3,2,1,0:T(8,128)(2,1)} %dynamic-slice_bitcast_fusion.1), channel_id=1, source_target_pairs={{0,4},{1,5},{2,6},{3,7},{4,0},{5,1},{6,2},{7,3},{8,12},{9,13},{10,... | collective-permute-start | bytes 15728648 | tf_op jit(solution)/shard_map/ppermute | solution.py:64
  401.3 69.1 %collective-permute-start.21 = (bf16[4,4,192,1024]{3,2,1,0:T(8,128)(2,1)}, bf16[4,4,192,1024]{3,2,1,0:T(8,128)(2,1)}, u32[]{:S(2)}, u32[]{:S(2)}) collective-permute-start(bf16[4,4,192,1024]{3,2,1,0:T(8,128)(2,1)} %dynamic-slice_bitcast_fusion), channel_id=1, source_target_pairs={{0,4},{1,5},{2,6},{3,7},{4,0},{5,1},{6,2},{7,3},{8,12},{9,13},{10,... | collective-permute-start | bytes 18874376 | tf_op jit(solution)/shard_map/ppermute | solution.py:64
  404.8 3.7 collective-permute-start.9
  408.5 4.6 collective-permute-start.10
  412.9 11.1 %copy-start.5 = (f32[256,1024]{1,0:T(8,128)S(1)}, f32[256,1024]{1,0:T(8,128)}, u32[]{:S(2)}) copy-start(f32[256,1024]{1,0:T(8,128)} %copy-done.4) | copy-start | bytes 3145732
  412.9 11.1 %copy-start.55 = (f32[256,1024]{1,0:T(8,128)S(1)}, f32[256,1024]{1,0:T(8,128)}, u32[]{:S(2)}) copy-start(f32[256,1024]{1,0:T(8,128)} %get-tuple-element.183) | copy-start | bytes 3145732
  413.0 1.2 collective-permute-start.11
  414.3 3.6 collective-permute-start.12
  417.9 5.1 collective-permute-start.13
  419.5 36.5 %copy-start.69 = (f32[261]{0:T(512)S(1)}, f32[261]{0:T(512)}, u32[]{:S(2)}) copy-start(f32[261]{0:T(512)} %copy-done.68) | copy-start | bytes 3136
  419.5 14.0 %collective-permute-start.8 = (bf16[512,384]{0,1:T(8,128)(2,1)S(1)}, bf16[512,384]{0,1:T(8,128)(2,1)S(1)}, u32[]{:S(2)}, u32[]{:S(2)}) collective-permute-start(bf16[512,384]{0,1:T(8,128)(2,1)S(1)} %get-tuple-element.137), channel_id=1, source_target_pairs={{0,3},{1,2},{2,1},{3,0},{4,7},{5,6},{6,5},{7,4},{8,11},{9,10},{10,... | collective-permute-start | bytes 1179656 | tf_op jit(solution)/shard_map/ppermute | solution.py:64
  421.7 34.2 %collective-permute-start.7 = (bf16[512,384]{0,1:T(8,128)(2,1)S(1)}, bf16[512,384]{0,1:T(8,128)(2,1)S(1)}, u32[]{:S(2)}, u32[]{:S(2)}) collective-permute-start(bf16[512,384]{0,1:T(8,128)(2,1)S(1)} %get-tuple-element.136), channel_id=1, source_target_pairs={{0,2},{1,3},{2,0},{3,1},{4,6},{5,7},{6,4},{7,5},{8,10},{9,11},{10,... | collective-permute-start | bytes 1179656 | tf_op jit(solution)/shard_map/ppermute | solution.py:64
  423.0 33.0 %collective-permute-start.6 = (bf16[512,384]{0,1:T(8,128)(2,1)S(1)}, bf16[512,384]{0,1:T(8,128)(2,1)S(1)}, u32[]{:S(2)}, u32[]{:S(2)}) collective-permute-start(bf16[512,384]{0,1:T(8,128)(2,1)S(1)} %get-tuple-element.135), channel_id=1, source_target_pairs={{0,1},{1,0},{2,3},{3,2},{4,5},{5,4},{6,7},{7,6},{8,9},{9,8},{10,11... | collective-permute-start | bytes 1179656 | tf_op jit(solution)/shard_map/ppermute | solution.py:64
  467.2 32.0 %collective-permute-start.15 = (bf16[2,4,80,1024]{3,2,1,0:T(8,128)(2,1)}, bf16[2,4,80,1024]{3,2,1,0:T(8,128)(2,1)}, u32[]{:S(2)}, u32[]{:S(2)}) collective-permute-start(bf16[2,4,80,1024]{3,2,1,0:T(8,128)(2,1)} %dynamic-slice_bitcast_fusion.5), channel_id=1, source_target_pairs={{0,8},{1,9},{2,10},{3,11},{4,12},{5,13},{6,14},{7,15},{8,0},{9,1},... | collective-permute-start | bytes 3932168 | tf_op jit(solution)/shard_map/ppermute | solution.py:64
  469.0 32.8 %collective-permute-start.17 = (bf16[1,8,80,1024]{3,2,1,0:T(8,128)(2,1)}, bf16[1,8,80,1024]{3,2,1,0:T(8,128)(2,1)}, u32[]{:S(2)}, u32[]{:S(2)}) collective-permute-start(bf16[1,8,80,1024]{3,2,1,0:T(8,128)(2,1)} %dynamic-slice_bitcast_fusion.4), channel_id=1, source_target_pairs={{0,16},{1,17},{2,18},{3,19},{4,20},{5,21},{6,22},{7,23},{8,24},{9,... | collective-permute-start | bytes 3932168 | tf_op jit(solution)/shard_map/ppermute | solution.py:64
  479.3 19.9 %copy-start.13 = (bf16[16,80,1024]{2,1,0:T(8,128)(2,1)S(1)}, bf16[16,80,1024]{2,1,0:T(8,128)(2,1)}, u32[]{:S(2)}) copy-start(bf16[16,80,1024]{2,1,0:T(8,128)(2,1)} %copy-done.12) | copy-start | bytes 7864324
  479.3 68.3 %collective-permute-start.22 = (bf16[2,4,96,1024]{3,2,1,0:T(8,128)(2,1)S(1)}, bf16[2,4,96,1024]{3,2,1,0:T(8,128)(2,1)S(1)}, u32[]{:S(2)}, u32[]{:S(2)}) collective-permute-start(bf16[2,4,96,1024]{3,2,1,0:T(8,128)(2,1)S(1)} %dynamic-slice_bitcast_fusion.3), channel_id=1, source_target_pairs={{0,8},{1,9},{2,10},{3,11},{4,12},{5,13},{6,14},{7,15},{8,0},{9,1},... | collective-permute-start | bytes 4718600 | tf_op jit(solution)/shard_map/ppermute | solution.py:64
  480.1 21.6 %copy-start.11 = (bf16[16,80,1024]{2,1,0:T(8,128)(2,1)S(1)}, bf16[16,80,1024]{2,1,0:T(8,128)(2,1)}, u32[]{:S(2)}) copy-start(bf16[16,80,1024]{2,1,0:T(8,128)(2,1)} %copy-done.10) | copy-start | bytes 7864324
  480.1 69.6 %collective-permute-start.24 = (bf16[1,8,96,1024]{3,2,1,0:T(8,128)(2,1)S(1)}, bf16[1,8,96,1024]{3,2,1,0:T(8,128)(2,1)S(1)}, u32[]{:S(2)}, u32[]{:S(2)}) collective-permute-start(bf16[1,8,96,1024]{3,2,1,0:T(8,128)(2,1)S(1)} %dynamic-slice_bitcast_fusion.2), channel_id=1, source_target_pairs={{0,16},{1,17},{2,18},{3,19},{4,20},{5,21},{6,22},{7,23},{8,24},{9,... | collective-permute-start | bytes 4718600 | tf_op jit(solution)/shard_map/ppermute | solution.py:64
  501.1 45.9 %collective-permute-start.16 = (bf16[1,4,80,1024]{3,2,1,0:T(8,128)(2,1)S(1)}, bf16[1,4,80,1024]{3,2,1,0:T(8,128)(2,1)S(1)}, u32[]{:S(2)}, u32[]{:S(2)}) collective-permute-start(bf16[1,4,80,1024]{3,2,1,0:T(8,128)(2,1)S(1)} %constant_dynamic-slice_fusion.3), channel_id=1, source_target_pairs={{0,16},{1,17},{2,18},{3,19},{4,20},{5,21},{6,22},{7,23},{8,24},{9,... | collective-permute-start | bytes 1966088 | tf_op jit(solution)/shard_map/ppermute | solution.py:64
  503.7 43.6 %collective-permute-start.18 = (bf16[1,4,80,1024]{3,2,1,0:T(8,128)(2,1)S(1)}, bf16[1,4,80,1024]{3,2,1,0:T(8,128)(2,1)S(1)}, u32[]{:S(2)}, u32[]{:S(2)}) collective-permute-start(bf16[1,4,80,1024]{3,2,1,0:T(8,128)(2,1)S(1)} %dynamic-slice_bitcast_fusion.7), channel_id=1, source_target_pairs={{0,8},{1,9},{2,10},{3,11},{4,12},{5,13},{6,14},{7,15},{8,0},{9,1},... | collective-permute-start | bytes 1966088 | tf_op jit(solution)/shard_map/ppermute | solution.py:64
  547.6 28.2 %collective-permute-start.19 = (bf16[1,2,160,1024]{3,2,1,0:T(8,128)(2,1)S(1)}, bf16[1,2,160,1024]{3,2,1,0:T(8,128)(2,1)S(1)}, u32[]{:S(2)}, u32[]{:S(2)}) collective-permute-start(bf16[1,2,160,1024]{3,2,1,0:T(8,128)(2,1)S(1)} %fusion.49), channel_id=1, source_target_pairs={{0,2},{1,3},{2,0},{3,1},{4,6},{5,7},{6,4},{7,5},{8,10},{9,11},{10,... | collective-permute-start | bytes 1966088 | tf_op jit(solution)/shard_map/ppermute | solution.py:64
  548.5 27.7 %collective-permute-start.23 = (bf16[1,4,96,1024]{3,2,1,0:T(8,128)(2,1)S(1)}, bf16[1,4,96,1024]{3,2,1,0:T(8,128)(2,1)S(1)}, u32[]{:S(2)}, u32[]{:S(2)}) collective-permute-start(bf16[1,4,96,1024]{3,2,1,0:T(8,128)(2,1)S(1)} %constant_dynamic-slice_fusion.1), channel_id=1, source_target_pairs={{0,16},{1,17},{2,18},{3,19},{4,20},{5,21},{6,22},{7,23},{8,24},{9,... | collective-permute-start | bytes 2359304 | tf_op jit(solution)/shard_map/ppermute | solution.py:64
  550.5 26.0 %collective-permute-start.25 = (bf16[1,4,96,1024]{3,2,1,0:T(8,128)(2,1)S(1)}, bf16[1,4,96,1024]{3,2,1,0:T(8,128)(2,1)S(1)}, u32[]{:S(2)}, u32[]{:S(2)}) collective-permute-start(bf16[1,4,96,1024]{3,2,1,0:T(8,128)(2,1)S(1)} %dynamic-slice_bitcast_fusion.6), channel_id=1, source_target_pairs={{0,8},{1,9},{2,10},{3,11},{4,12},{5,13},{6,14},{7,15},{8,0},{9,1},... | collective-permute-start | bytes 2359304 | tf_op jit(solution)/shard_map/ppermute | solution.py:64
  576.1 15.4 %collective-permute-start.20 = (bf16[1,1,160,1024]{3,2,1,0:T(8,128)(2,1)S(1)}, bf16[1,1,160,1024]{3,2,1,0:T(8,128)(2,1)S(1)}, u32[]{:S(2)}, u32[]{:S(2)}) collective-permute-start(bf16[1,1,160,1024]{3,2,1,0:T(8,128)(2,1)S(1)} %constant_dynamic-slice_fusion.2), channel_id=1, source_target_pairs={{0,1},{1,0},{2,3},{3,2},{4,5},{5,4},{6,7},{7,6},{8,9},{9,8},{10,11... | collective-permute-start | bytes 983048 | tf_op jit(solution)/shard_map/ppermute | solution.py:64
  576.9 37.3 %collective-permute-start.26 = (bf16[1,2,192,1024]{3,2,1,0:T(8,128)(2,1)S(1)}, bf16[1,2,192,1024]{3,2,1,0:T(8,128)(2,1)S(1)}, u32[]{:S(2)}, u32[]{:S(2)}) collective-permute-start(bf16[1,2,192,1024]{3,2,1,0:T(8,128)(2,1)S(1)} %fusion.38), channel_id=1, source_target_pairs={{0,2},{1,3},{2,0},{3,1},{4,6},{5,7},{6,4},{7,5},{8,10},{9,11},{10,... | collective-permute-start | bytes 2359304 | tf_op jit(solution)/shard_map/ppermute | solution.py:64
  614.6 10.0 %collective-permute-start.27 = (bf16[1,1,192,1024]{3,2,1,0:T(8,128)(2,1)S(1)}, bf16[1,1,192,1024]{3,2,1,0:T(8,128)(2,1)S(1)}, u32[]{:S(2)}, u32[]{:S(2)}) collective-permute-start(bf16[1,1,192,1024]{3,2,1,0:T(8,128)(2,1)S(1)} %constant_dynamic-slice_fusion), channel_id=1, source_target_pairs={{0,1},{1,0},{2,3},{3,2},{4,5},{5,4},{6,7},{7,6},{8,9},{9,8},{10,11... | collective-permute-start | bytes 1179656 | tf_op jit(solution)/shard_map/ppermute | solution.py:64
  (88 other events, 256.4 us)
Sparse Core Ops, SparseCore 0:
  19.1 89.4 all-gather.4
  112.1 126.2 all-gather.6

commit v2 on v1

--- a/solution.py
+++ b/solution.py
@@ -3,6 +3,7 @@
 import jax
 import jax.numpy as jnp
 from jax import lax
+from jax.experimental.layout import Layout, with_layout_constraint
 from jax.experimental import pallas as pl
 from jax.experimental.pallas import tpu as pltpu
 from jax.sharding import PartitionSpec as P
@@ -64,42 +65,143 @@
     return lax.ppermute(values, AXES, [(i, i ^ step) for i in range(total)])
 
 
-def halve(values, bit, left, me, sizes):
-    above = sum(1 for other in left if other > bit)
-    below = len(left) - 1 - above
-    rows, width = values.shape[-2:]
-    view = values.reshape(2**above, 2, 2**below, rows, width)
+def tie(*values):
+    return lax.optimization_barrier(values)
+
+
+def bits_of(sizes):
+    low = sizes[1].bit_length() - 1
+    every = list(range((sizes[0] * sizes[1]).bit_length() - 1))
+    return every[:low], every[low], every[low + 1 :]
+
+
+def gather_fsdp(values, sizes):
+    return [values] + [xor_permute(values, sizes, k) for k in range(1, sizes[1])]
+
+
+def order_fsdp(parts, sizes, me):
+    low, _, _ = bits_of(sizes)
+    for bit in low:
+        mine = ((me >> bit) & 1) == 1
+        parts = [jnp.where(mine, parts[k ^ (1 << bit)], parts[k]) for k in range(len(parts))]
+    return jnp.stack(parts)
+
+
+def merge(own, got, bit, above, me):
+    mine = ((me >> bit) & 1) == 1
+    view = (2**above, -1) + own.shape[1:]
+    own, got = own.reshape(view), got.reshape(view)
+    both = jnp.stack([jnp.where(mine, got, own), jnp.where(mine, own, got)], axis=1)
+    return both.reshape((-1,) + own.shape[2:])
+
+
+def far_step(groups, place, sizes, me):
+    _, _, far = bits_of(sizes)
+    result = []
+    for values, order in zip(groups, (far, far[::-1])):
+        bit, held = order[place], order[:place]
+        got = xor_permute(values, sizes, 1 << bit)
+        result.append(merge(values, got, bit, sum(1 for other in held if other > bit), me))
+    return result
+
+
+def merge_kernel(plan, *refs):
+    (own_a, got_a, own_b, got_b), outs = refs[:4], refs[4:]
+    fsdp_size, core = own_a.shape[1], lax.axis_index("dp") & 1
+    for flip in (0, 1):
+
+        @pl.when(core == flip)
+        def _(flip=flip):
+            sources = ((own_a, own_b), (got_a, got_b))
+            for out, (start, own, segments) in zip(outs, plan):
+                for side in (0, 1):
+                    for shard in range(fsdp_size):
+                        row, column = (side * fsdp_size + shard) * own, 0
+                        for group, first, count in segments:
+                            source = sources[side ^ flip][group]
+                            out[row : row + own, column : column + count] = source[
+                                0, shard, start : start + own, first : first + count
+                            ]
+                            column += count
+
+
+def core_merge(groups, plan, sizes, me):
+    _, core, _ = bits_of(sizes)
+    got = [xor_permute(values, sizes, 1 << core) for values in groups]
+    far_size, fsdp_size, _, columns = groups[0].shape
+    if plan[0][1] % 16:
+        mine = ((me >> core) & 1) == 1
+        both = [
+            jnp.stack([jnp.where(mine, g, v), jnp.where(mine, v, g)], axis=1) for v, g in zip(groups, got)
+        ]
+        wholes = []
+        for start, own, segments in plan:
+            parts = [both[p][:, :, :, start : start + own, a : a + n] for p, a, n in segments]
+            whole = jnp.concatenate(parts, axis=-1)
+            wholes.append(whole.reshape(-1, whole.shape[-1]))
+        return wholes
+    spec = pl.BlockSpec((1,) + groups[0].shape[1:], lambda i: (i, 0, 0, 0))
+    shapes = [(2 * fsdp_size * own, sum(n for _, _, n in segments)) for _, own, segments in plan]
+    return pl.pallas_call(
+        partial(merge_kernel, plan),
+        grid=(far_size,),
+        in_specs=[spec] * 4,
+        out_specs=[pl.BlockSpec(shape, lambda i: (i, 0)) for shape in shapes],
+        out_shape=[jax.ShapeDtypeStruct((far_size * r, w), BF) for r, w in shapes],
+        cost_estimate=pl.CostEstimate(flops=0, bytes_accessed=24 * 2**20, transcendentals=0),
+        name="merge",
+    )(groups[0], got[0], groups[1], got[1])
+
+
+def halves_of(values):
+    half = values.shape[-1] // 2
+    return [values[..., :half], values[..., half:]]
+
+
+def core_sum(grads, sizes, me):
+    _, core, _ = bits_of(sizes)
+    mine = (me >> core) & 1
+    sends, keeps = [], []
+    for grad in grads:
+        view = grad.reshape(sizes[0] // 2, 2, -1, grad.shape[-1])
+        sends.append(lax.dynamic_index_in_dim(view, 1 - mine, 1, keepdims=False))
+        keeps.append(lax.dynamic_index_in_dim(view, mine, 1, keepdims=False))
+    got = xor_permute(jnp.stack(sends), sizes, 1 << core)
+    sums = [(keep.astype(F32) + got[i].astype(F32)).astype(BF) for i, keep in enumerate(keeps)]
+    return jnp.stack(sums, axis=1)
+
+
+def far_sum(values, bit, held, sizes, me):
+    above = sum(1 for other in held if other > bit)
+    view = values.reshape((2**above, 2, -1) + values.shape[1:])
     mine = (me >> bit) & 1
     send = lax.dynamic_index_in_dim(view, 1 - mine, 1, keepdims=False)
     keep = lax.dynamic_index_in_dim(view, mine, 1, keepdims=False)
     got = xor_permute(send, sizes, 1 << bit)
-    summed = keep.astype(F32) + got.astype(F32)
-    return summed.reshape(-1, rows, width)
-
-
-def reduce_scatter(values, sizes, me):
-    dp_size, fsdp_size = sizes
-    low_bits = fsdp_size.bit_length() - 1
-    all_bits = list(range((dp_size * fsdp_size).bit_length() - 1))
-    core, far = all_bits[low_bits], all_bits[low_bits + 1 :]
-    left = list(all_bits)
-    values = halve(values, core, left, me, sizes).astype(BF)
-    left.remove(core)
-    half = values.shape[1] // 32 * 16 or values.shape[1] // 2
-    pieces = []
-    for piece, order in ((values[:, :half], far), (values[:, half:], far[::-1])):
-        rest = list(left)
-        for bit in order:
-            piece = halve(piece, bit, rest, me, sizes).astype(BF)
-            rest.remove(bit)
-        pieces.append(piece)
-    values = jnp.concatenate(pieces, axis=1)
-    rest = all_bits[:low_bits]
-    for bit in rest[::-1]:
-        summed = halve(values, bit, list(rest), me, sizes)
-        rest = rest[:-1]
-        values = summed.astype(BF)
-    return summed[0]
+    summed = (keep.astype(F32) + got.astype(F32)).astype(BF)
+    return summed.reshape((-1,) + values.shape[1:])
+
+
+def fsdp_sum(values, sizes, my_fsdp):
+    view = values.reshape(values.shape[0], sizes[1], -1, values.shape[-1])
+    total = lax.dynamic_index_in_dim(view, my_fsdp, 1, keepdims=False).astype(F32)
+    for k in range(1, sizes[1]):
+        send = lax.dynamic_index_in_dim(view, my_fsdp ^ k, 1, keepdims=False)
+        total = total + xor_permute(send, sizes, k).astype(F32)
+    return total
+
+
+def far_pair(groups, place, sizes, me):
+    _, _, far = bits_of(sizes)
+    result = []
+    for group, order in zip(groups, (far, far[::-1])):
+        held = [bit for bit in far if bit not in order[:place]]
+        result.append(far_sum(group, order[place], held, sizes, me))
+    return result
+
+
+def finish_sum(groups, sizes, my_fsdp):
+    return fsdp_sum(jnp.concatenate([group[0] for group in groups], axis=-1), sizes, my_fsdp)
 
 
 def butterfly(values, sizes):
@@ -236,22 +338,32 @@
     padded = -(-features // LANES) * LANES
     own = width // devices
 
-    kv_t = pad_lanes(jnp.transpose(pix_kv, (2, 0, 1)), width // 2)
+    _, _, far = bits_of(sizes)
+    half = width // 2
+    whole_plan = [(0, 0, half), (1, 0, half)]
+    enc_parts = gather_fsdp(jnp.concatenate([enc_mlp[0], enc_mlp[1], enc_query, enc_out], axis=0), sizes)
+    kv_t = pad_lanes(jnp.transpose(pix_kv, (2, 0, 1)), half)
     small = jnp.concatenate([enc_gains, enc_biases, lat_gains, lat_biases], axis=0)
-    kv_t = kv_t.at[:, 0, padded : padded + small.shape[0]].set(small.T)
-    enc_pack = jnp.concatenate([kv_t.reshape(own, width), enc_query, enc_out, enc_mlp[0], enc_mlp[1]], axis=0)
-    lat_pack = jnp.concatenate([lat_qkv[0], lat_qkv[1], lat_qkv[2], lat_out, lat_mlp[0], lat_mlp[1]], axis=0)
-    enc_all = lax.all_gather(enc_pack, AXES, axis=0, tiled=False)
-    lat_all = lax.all_gather(lat_pack, AXES, axis=0, tiled=False)
-
-    def part(whole, index):
-        return whole[:, index * own : (index + 1) * own].reshape(width, width)
-
-    kv_full, w_query, w_out, w_first, w_second = [part(enc_all, i) for i in range(5)]
-    l_query, l_key, l_value, l_out, l_first, l_second = [part(lat_all, i) for i in range(6)]
-    key_t = kv_full[:, :padded]
-    value_t = kv_full[:, width // 2 : width // 2 + padded]
-    small_all = kv_full[:, padded : padded + small.shape[0]].T.astype(F32)
+    n_small = small.shape[0]
+    kv_t = jnp.concatenate([kv_t[:, 0, :padded], pad_lanes(small.T, half - padded), kv_t[:, 1]], axis=1)
+    kv_parts = gather_fsdp(kv_t, sizes)
+    parts = tie(*enc_parts, *kv_parts)
+    parts = [jnp.concatenate([e, k], axis=0) for e, k in zip(parts[:fsdp_size], parts[fsdp_size:])]
+    enc_groups = [v[None] for v in halves_of(order_fsdp(parts, sizes, me))]
+    other_parts = gather_fsdp(jnp.concatenate([lat_out, lat_mlp[0], lat_mlp[1]], axis=0), sizes)
+    for place in range(len(far)):
+        enc_groups = far_step(enc_groups, place, sizes, me)
+        if place == 0:
+            qkv, *enc_groups = tie(lat_qkv, *enc_groups)
+            qkv_parts = gather_fsdp(qkv.reshape(3 * own, width), sizes)
+    groups = tie(*enc_groups, *qkv_parts)
+    enc_groups, qkv_parts = groups[:2], list(groups[2:])
+    qkv_groups = [v[None] for v in halves_of(order_fsdp(qkv_parts, sizes, me))]
+    plan = [(i * own, own, whole_plan) for i in range(4)]
+    plan += [(4 * own, own, [(0, 0, padded)]), (4 * own, own, [(1, 0, padded)]), (4 * own, own, [(0, padded, half - padded)])]
+    w_first, w_second, w_query, w_out, key_t, value_t, small_t = core_merge(enc_groups, plan, sizes, me)
+    qkv_groups = far_step(qkv_groups, 0, sizes, me)
+    small_all = mm_t(jnp.eye(n_small, half - padded, dtype=BF), small_t)
     n_gain, n_bias = enc_gains.shape[0], enc_biases.shape[0]
     gains_enc, biases_enc = small_all[:n_gain], small_all[n_gain : n_gain + n_bias]
     gains_lat, biases_lat = small_all[n_gain + n_bias : 2 * n_gain + n_bias], small_all[2 * n_gain + n_bias :]
@@ -264,6 +376,9 @@
     in_hat, in_inverse = norm_parts(latent_in)
     in_low = (in_hat * gains_enc[0] + biases_enc[0]).astype(BF)
     enc_q = mm(in_low, w_query).astype(BF)
+    enc_q, *qkv_groups = tie(enc_q, *qkv_groups)
+    for place in range(1, len(far)):
+        qkv_groups = far_step(qkv_groups, place, sizes, me)
     query_pix = mm(enc_q, key_t).astype(BF)
     counts = lengths[0]
     ends = jnp.cumsum(counts)
@@ -284,12 +399,19 @@
 
     lat_hat, lat_inverse = norm_parts(first_out)
     lat_low = (lat_hat * gains_lat[0] + biases_lat[0]).astype(BF)
-    shards = [lat_low] + [xor_permute(lat_low, sizes, k) for k in range(1, fsdp_size)]
+    lat_low, *groups = tie(lat_low, *qkv_groups, *other_parts)
+    shards = gather_fsdp(lat_low, sizes)
+    plan = [(i * own, own, whole_plan) for i in range(3)]
+    l_query, l_key, l_value = core_merge(groups[:2], plan, sizes, me)
+    other_groups = [v[None] for v in halves_of(order_fsdp(list(groups[2:]), sizes, me))]
+    for place in range(len(far)):
+        other_groups = far_step(other_groups, place, sizes, me)
     lat_every = jnp.concatenate(shards, axis=0)
     shape = (images, lat_rows, width)
     lat_q = mm(lat_low, l_query).astype(BF).reshape(shape)
     lat_k = mm(lat_every, l_key).astype(BF).reshape((fsdp_size,) + shape)
     lat_v = mm(lat_every, l_value).astype(BF).reshape((fsdp_size,) + shape)
+    l_out, l_first, l_second = core_merge(other_groups, plan, sizes, me)
     lat_mixed = attention(lat_q, lat_k, lat_v).reshape(rows, width)
     lat_resid = first_out + mm(lat_mixed, l_out)
     second_out, lat_kept = feed_forward(
@@ -302,25 +424,29 @@
     grad_mid_low = grad_mid.astype(BF)
     d_l_out = tm(lat_mixed, grad_mid_low).astype(BF)
     d_mixed = mm_t(grad_mid_low, l_out).astype(BF).reshape(shape)
+    after_groups = halves_of(core_sum([d_l_first, d_l_second, d_l_out], sizes, me))
     d_q, d_k, d_v = attention_back(lat_q, lat_k, lat_v, d_mixed)
+    d_q, d_k, d_v, *after_groups = tie(d_q, d_k, d_v, *after_groups)
     d_q, d_k, d_v = d_q.reshape(rows, width), d_k.reshape(-1, width), d_v.reshape(-1, width)
-    d_l_query = tm(lat_low, d_q).astype(BF)
-    d_l_key = tm(lat_every, d_k).astype(BF)
-    d_l_value = tm(lat_every, d_v).astype(BF)
     d_every = mm_t(d_k, l_key) + mm_t(d_v, l_value)
     d_lat_normed = mm_t(d_q, l_query) + d_every[:rows]
     for k in range(1, fsdp_size):
         piece = d_every[k * rows : (k + 1) * rows].astype(BF)
         d_lat_normed = d_lat_normed + xor_permute(piece, sizes, k).astype(F32)
+    d_l_query = tm(lat_low, d_q).astype(BF)
+    d_l_key = tm(lat_every, d_k).astype(BF)
+    d_l_value = tm(lat_every, d_v).astype(BF)
+    for place in range(len(far)):
+        after_groups = far_pair(after_groups, place, sizes, me)
+    qkv_groups = halves_of(core_sum([d_l_query, d_l_key, d_l_value], sizes, me))
+    qkv_groups = far_pair(qkv_groups, 0, sizes, me)
+    d_lat_normed, *groups = tie(d_lat_normed, *after_groups, *qkv_groups)
+    after_groups, qkv_groups = groups[:2], groups[2:]
+    for place in range(1, len(far)):
+        qkv_groups = far_pair(qkv_groups, place, sizes, me)
+    after_grads = finish_sum(after_groups, sizes, my_fsdp)
     d_first_out = grad_mid + norm_back(lat_hat, lat_inverse, gains_lat[0], d_lat_normed)
     lat_front = (jnp.sum(d_lat_normed * lat_hat, axis=0), jnp.sum(d_lat_normed, axis=0))
-
-    def stack(pieces):
-        return jnp.concatenate([p.reshape(devices, own, width) for p in pieces], axis=1)
-
-    lat_grads = reduce_scatter(
-        stack([d_l_query, d_l_key, d_l_value, d_l_out, d_l_first, d_l_second]), sizes, me
-    )
 
     grad_enc, d_first, d_second, enc_sums = feed_back(enc_kept, gains_enc[1], w_first, w_second, d_first_out)
     grad_enc_low = grad_enc.astype(BF)
@@ -328,30 +454,37 @@
     d_enc_mixed = mm_t(grad_enc_low, w_out).astype(BF)
     d_value_t = tm(d_enc_mixed, mixed_pix)
     mixed_back = mm(d_enc_mixed, value_t).astype(BF)
+    mixed_back, after_grads, *qkv_groups = tie(mixed_back, after_grads, *qkv_groups)
+    qkv_grads = finish_sum(qkv_groups, sizes, my_fsdp)
+    mlp_groups = halves_of(core_sum([d_first, d_second, d_w_out], sizes, me))
+    mlp_groups = far_pair(mlp_groups, 0, sizes, me)
     d_probs = mm_t(mixed_back, pix_low)
     inner = jnp.sum(probs * d_probs, axis=-1, keepdims=True)
     d_scores = (probs * (d_probs - inner) * enc_scale).astype(BF)
     d_query_pix = mm(d_scores, pix_low).astype(BF)
+    d_query_pix, qkv_grads, *mlp_groups = tie(d_query_pix, qkv_grads, *mlp_groups)
+    for place in range(1, len(far)):
+        mlp_groups = far_pair(mlp_groups, place, sizes, me)
     d_enc_q = mm_t(d_query_pix, key_t).astype(BF)
     d_key_t = tm(enc_q, d_query_pix)
-    d_pix_low = tm(d_scores, query_pix) + tm(probs_low, mixed_back)
+    d_pix_t = tm(query_pix, d_scores) + tm(mixed_back, probs_low)
     d_w_query = tm(in_low, d_enc_q).astype(BF)
     d_in_normed = mm_t(d_enc_q, w_query)
     d_latents = grad_enc + norm_back(in_hat, in_inverse, gains_enc[0], d_in_normed)
     enc_front = (jnp.sum(d_in_normed * in_hat, axis=0), jnp.sum(d_in_normed, axis=0))
 
-    d_pix_all = d_pix_low[:, :features]
-    d_pix_sums = jnp.stack([jnp.sum(d_pix_all * pix_hat[:USED], axis=0), jnp.sum(d_pix_all, axis=0)])
+    d_pix_t = d_pix_t[:features]
+    d_pix_sums = jnp.stack([jnp.sum(d_pix_t * pix_hat[:USED].T, axis=1), jnp.sum(d_pix_t, axis=1)])
     d_pix_sums = butterfly(pad_lanes(d_pix_sums, padded), sizes)[:, :features]
     share = pix_rows // fsdp_size
-    d_pix_pad = jnp.pad(d_pix_low, ((0, pix_rows - USED), (0, 0)))
-    d_pix_own = lax.dynamic_slice_in_dim(d_pix_pad, my_fsdp * share, share, 0)
+    d_pix_pad = pad_lanes(d_pix_t, pix_rows)
+    d_pix_own = lax.dynamic_slice_in_dim(d_pix_pad, my_fsdp * share, share, 1)
     for k in range(1, fsdp_size):
-        piece = lax.dynamic_slice_in_dim(d_pix_pad, (my_fsdp ^ k) * share, share, 0).astype(BF)
+        piece = lax.dynamic_slice_in_dim(d_pix_pad, (my_fsdp ^ k) * share, share, 1).astype(BF)
         d_pix_own = d_pix_own + xor_permute(piece, sizes, k).astype(F32)
     hat_own = lax.dynamic_slice_in_dim(pix_hat, my_fsdp * share, share, 0)
     inverse_own = lax.dynamic_slice_in_dim(pix_inverse, my_fsdp * share, share, 0)
-    d_pixels = norm_back(hat_own, inverse_own, gain_f, d_pix_own[:, :features])
+    d_pixels = norm_back(hat_own, inverse_own, gain_f, d_pix_own.T)
 
     small_grads = jnp.stack(
         [enc_front[0], enc_sums[0], enc_front[1], enc_sums[1], enc_sums[2], enc_sums[3]]
@@ -359,23 +492,18 @@
     )
     high = small_grads.astype(BF)
     low = (small_grads - high.astype(F32)).astype(BF)
-    n_small = small_grads.shape[0]
-    half_pad = width // 2 - padded
+    half_pad = half - padded
+    spread = jnp.eye(n_small, half_pad, dtype=BF)
     kv_grads = jnp.concatenate(
-        [
-            d_key_t.astype(BF),
-            pad_lanes(high.T, half_pad),
-            d_value_t.astype(BF),
-            pad_lanes(low.T, half_pad),
-        ],
-        axis=1,
-    )
-    enc_grads = reduce_scatter(stack([kv_grads, d_w_query, d_w_out, d_first, d_second]), sizes, me)
-
-    def mine(whole, index):
-        return whole[index * own : (index + 1) * own]
-
-    kv_own = mine(enc_grads, 0)
+        [d_key_t.astype(BF), tm(high, spread).astype(BF), d_value_t.astype(BF), tm(low, spread).astype(BF)], axis=1
+    )
+    kv_grads = with_layout_constraint(kv_grads, Layout((0, 1)))
+    end_groups = halves_of(core_sum([kv_grads, d_w_query], sizes, me))
+    for place in range(len(far)):
+        end_groups = far_pair(end_groups, place, sizes, me)
+    mlp_grads = finish_sum(mlp_groups, sizes, my_fsdp)
+    end_grads = finish_sum(end_groups, sizes, my_fsdp)
+    kv_own = end_grads[0]
     d_pix_kv = jnp.stack([kv_own[:, :features].T, kv_own[:, width // 2 : width // 2 + features].T])
     start = width // 2 + padded
     small_own = (kv_own[:, padded : padded + n_small] + kv_own[:, start : start + n_small]).T
@@ -386,14 +514,14 @@
         d_pix_sums[0],
         d_pix_sums[1],
         d_pix_kv,
-        mine(enc_grads, 1),
-        mine(enc_grads, 2),
-        jnp.stack([mine(enc_grads, 3), mine(enc_grads, 4)]),
+        end_grads[1],
+        mlp_grads[2],
+        mlp_grads[:2],
         small_own[:n_gain],
         small_own[n_gain : n_gain + n_bias],
-        jnp.stack([mine(lat_grads, 0), mine(lat_grads, 1), mine(lat_grads, 2)]),
-        mine(lat_grads, 3),
-        jnp.stack([mine(lat_grads, 4), mine(lat_grads, 5)]),
+        qkv_grads,
+        after_grads[2],
+        after_grads[:2],
         small_own[n_gain + n_bias : 2 * n_gain + n_bias],
         small_own[2 * n_gain + n_bias :],
     )

time: 644 us -> 519 us (0.81)
  waiting for transfers between devices: 368 us -> 199 us
  starting transfers between devices: 29.5 us -> 104 us
  local copies, waits for them, and re-layouts: 82.9 us -> 46.1 us
  Pallas kernels: 20.2 us -> 40.7 us
  between operations: 16 us -> 3.18 us
  other arithmetic: 46.6 us -> 56.8 us
  matrix products: 71 us -> 63.4 us
    all_gather x2 -> x0, waiting for transfers between devices: 192 us -> none  [the longest x1 109 us: body(): lat_all = lax.all_gather(lat_pack, AXES, axis=0, tiled=False)]
    ppermute x28 -> x76, starting transfers between devices: 29.4 us -> 104 us  [xor_permute(): return lax.ppermute(values, AXES, [(i, i ^ step) for i in range(total)])]
    ppermute x28 -> x76, waiting for transfers between devices: 176 us -> 199 us  [xor_permute(): return lax.ppermute(values, AXES, [(i, i ^ step) for i in range(total)])]
    pallas_call x0 -> x3, Pallas kernels: none -> 20.5 us  [core_merge(): pl.pallas_call(partial(merge_kernel, plan), grid=(far_size,), in_specs=[s...]
    unnamed x235 -> x246, local copies, waits for them, and re-layouts: 40 us -> 28.3 us
    slice x4 -> x5, local copies, waits for them, and re-layouts: 14.3 us -> 4.14 us  [the longest x3 2.7 us: halves_of(): return [values[..., :half], values[..., half:]]]
    another operation x8 -> x30, other arithmetic: 6.45 us -> 16.1 us  [the longest x15 8.6 us: merge(): jnp.stack([jnp.where(mine, got, own), jnp.where(mine, own, got)], axis=1)]
    convert_element_type x13 -> x16, other arithmetic: 22 us -> 12.5 us  [the longest x8 11.4 us: core_sum(): (keep.astype(F32) + got[i].astype(F32)).astype(BF)]
  transfers between devices with their start and end apart: 30 -> 76, of which waited for: 15 -> 30; matrix products, arithmetic and copies ran while one was open for 16% -> 19% of each run, Pallas kernels for 0% -> 7%
where the time goes in v2:
time: 519 us; the launch traced here: 513 us
  waiting for transfers between devices  199 us (38%)
  starting transfers between devices  104 us (20%)
  matrix products  63.4 us (12%)
  other arithmetic  56.8 us (11%)
  local copies, waits for them, and re-layouts  46.1 us (9%)
  Pallas kernels  40.7 us (8%)
    ppermute x76, waiting for transfers between devices, xor_permute(): return lax.ppermute(values, AXES, [(i, i ^ step) for i in range(total)])  199 us
    ppermute x76, starting transfers between devices, xor_permute(): return lax.ppermute(values, AXES, [(i, i ^ step) for i in range(total)])  104 us
    dot_general x45, matrix products, dot(): lax.dot_general(left, right, ((dims[0], dims[1]), ((), ())), preferred_el...  63.4 us
    unnamed x246, local copies, waits for them, and re-layouts  28.3 us
    pallas_call x3, Pallas kernels, core_merge(): pl.pallas_call(partial(merge_kernel, plan), grid=(far_size,), in_specs=[s...  20.5 us
    pallas_call x1, Pallas kernels, attention_back(): pl.pallas_call(attention_back_kernel, grid=grid, in_specs=[own, whole, wh...  12.1 us
    convert_element_type x8, other arithmetic, core_sum(): (keep.astype(F32) + got[i].astype(F32)).astype(BF)  11.4 us
  transfers between devices with their start and end apart: 76, of which 30 were waited for; matrix products, arithmetic and copies ran while one was open for 19% of the time, Pallas kernels for 7%

profile of v2, /device:TPU:0, one launch (start us, length us, event | category | flops | bytes accessed | tf_op | source)
XLA Modules:
  0.0 513.0 jit_solution(7379262822286035419)
XLA Ops:
  2.4 3.1 collective-permute-start
  5.5 2.6 collective-permute-start.1
  11.4 3.5 collective-permute-start.4
  14.9 9.6 %collective-permute-done.3 = bf16[32,1024]{1,0:T(8,128)(2,1)S(1)} collective-permute-done((bf16[32,1024]{1,0:T(8,128)(2,1)S(1)}, bf16[32,1024]{1,0:T(8,128)(2,1)S(1)}, u32[]{:S(2)}, u32[]{:S(2)}) %collective-permute-start.3) | collective-permute-done | bytes 65568 | tf_op jit(solution)/shard_map/ppermute | solution.py:65
  24.5 2.6 collective-permute-start.5
  27.1 8.9 %collective-permute-done.4 = bf16[32,1024]{1,0:T(8,128)(2,1)S(1)} collective-permute-done((bf16[32,1024]{1,0:T(8,128)(2,1)S(1)}, bf16[32,1024]{1,0:T(8,128)(2,1)S(1)}, u32[]{:S(2)}, u32[]{:S(2)}) %collective-permute-start.4) | collective-permute-done | bytes 65568 | tf_op jit(solution)/shard_map/ppermute | solution.py:65
  39.9 11.3 %collective-permute-done.7 = bf16[1,4,160,512]{3,2,1,0:T(8,128)(2,1)S(1)} collective-permute-done((bf16[1,4,160,512]{3,2,1,0:T(8,128)(2,1)S(1)}, bf16[1,4,160,512]{3,2,1,0:T(8,128)(2,1)S(1)}, u32[]{:S(2)}, u32[]{:S(2)}) %collective-permute-start.7) | collective-permute-done | bytes 655392 | tf_op jit(solution)/shard_map/ppermute | solution.py:65
  61.7 3.0 collective-permute-start.11
  64.8 17.9 %collective-permute-done.8 = bf16[2,4,160,512]{3,2,1,0:T(8,128)(2,1)} collective-permute-done((bf16[2,4,160,512]{3,2,1,0:T(8,128)(2,1)}, bf16[2,4,160,512]{3,2,1,0:T(8,128)(2,1)}, u32[]{:S(2)}, u32[]{:S(2)}) %collective-permute-start.8) | collective-permute-done | bytes 1310752 | tf_op jit(solution)/shard_map/ppermute | solution.py:65
  96.8 6.9 %collective-permute-done.16 = bf16[1,4,96,512]{3,2,1,0:T(8,128)(2,1)S(1)} collective-permute-done((bf16[1,4,96,512]{3,2,1,0:T(8,128)(2,1)S(1)}, bf16[1,4,96,512]{3,2,1,0:T(8,128)(2,1)S(1)}, u32[]{:S(2)}, u32[]{:S(2)}) %collective-permute-start.16) | collective-permute-done | bytes 393248 | tf_op jit(solution)/shard_map/ppermute | solution.py:65
  103.7 3.6 collective-permute-start.20
  112.1 8.3 %merge.3 = (bf16[1024,1024]{1,0:T(8,128)(2,1)}, bf16[1024,1024]{1,0:T(8,128)(2,1)}, bf16[1024,1024]{1,0:T(8,128)(2,1)}, bf16[1024,1024]{1,0:T(8,128)(2,1)}, bf16...) custom-call(bf16[4,4,160,512]{3,2,1,0:T(8,128)(2,1)} %bitcast.593, ...), custom_call_target="tpu_custom_call" | custom-call | bytes 25165824 | tf_op jit(solution)/shard_map/merge/pallas_call | solution.py:145
  136.1 13.0 %collective-permute-done.17 = bf16[2,4,96,512]{3,2,1,0:T(8,128)(2,1)S(1)} collective-permute-done((bf16[2,4,96,512]{3,2,1,0:T(8,128)(2,1)S(1)}, bf16[2,4,96,512]{3,2,1,0:T(8,128)(2,1)S(1)}, u32[]{:S(2)}, u32[]{:S(2)}) %collective-permute-start.17) | collective-permute-done | bytes 786464 | tf_op jit(solution)/shard_map/ppermute | solution.py:65
  156.4 5.6 %collective-permute-done.30 = bf16[1,4,96,512]{3,2,1,0:T(8,128)(2,1)S(1)} collective-permute-done((bf16[1,4,96,512]{3,2,1,0:T(8,128)(2,1)S(1)}, bf16[1,4,96,512]{3,2,1,0:T(8,128)(2,1)S(1)}, u32[]{:S(2)}, u32[]{:S(2)}) %collective-permute-start.30) | collective-permute-done | bytes 393248 | tf_op jit(solution)/shard_map/ppermute | solution.py:65
  166.4 3.4 collective-permute-done.24
  170.9 17.4 %collective-permute-done.25 = bf16[256,1024]{1,0:T(8,128)(2,1)} collective-permute-done((bf16[256,1024]{1,0:T(8,128)(2,1)S(1)}, bf16[256,1024]{1,0:T(8,128)(2,1)}, u32[]{:S(2)}, u32[]{:S(2)}) %collective-permute-start.25) | collective-permute-done | bytes 524320 | tf_op jit(solution)/shard_map/ppermute | solution.py:65
  196.0 4.3 collective-permute-done.26
  201.7 6.3 %merge.4 = (bf16[1024,1024]{1,0:T(8,128)(2,1)}, bf16[1024,1024]{1,0:T(8,128)(2,1)}, bf16[1024,1024]{1,0:T(8,128)(2,1)}) custom-call(bf16[4,4,96,512]{3,2,1,0:T(8,128)(2,1)} %bitcast.64.refs_0_, bf16[4,4,96,512]{3,2,1,0:T(8,128)(2,1)} %collective-permute-done.22.refs_1_, bf16[4,4,96,512]{3,2,1,0:T(8,128)(2,1)} %bitcast.67.refs_2_, ...), custom_call_target="tpu_custom_call" | custom-call | bytes 25165824 | tf_op jit(solution)/shard_map/merge/pallas_call | solution.py:145
  208.1 3.2 convolution_convert_fusion.18
  211.4 5.4 %convolution_convert_fusion.11 = bf16[1024,1024]{1,0:T(8,128)(2,1)} fusion(bf16[1024,1024]{1,0:T(8,128)(2,1)S(1)} %copy-done.72, bf16[1024,1024]{1,0:T(8,128)(2,1)} %get-tuple-element.108), kind=kOutput, calls=%fused_computation.62 | convolution fusion | flops 2148532224 | bytes 6291456 | tf_op jit(solution)/shard_map/dot_general | solution.py:23
  216.7 3.7 convolution_convert_fusion.10
  220.4 8.2 %attention.1 = bf16[2,128,1024]{2,1,0:T(8,128)(2,1)} custom-call(bf16[2,128,1024]{2,1,0:T(8,128)(2,1)} %bitcast.654, bf16[4,2,128,1024]{3,2,1,0:T(8,128)(2,1)} %bitcast.610, bf16[4,2,128,1024]{3,2,1,0:T(8,128)(2,1)} %bitcast.612), custom_call_target="tpu_custom_call" | custom-call | flops 536870912 | bytes 5242880 | tf_op jit(solution)/shard_map/attention/pallas_call | solution.py:255
  228.6 5.8 %merge.5 = (bf16[1024,1024]{1,0:T(8,128)(2,1)}, bf16[1024,1024]{1,0:T(8,128)(2,1)}, bf16[1024,1024]{1,0:T(8,128)(2,1)}) custom-call(bf16[4,4,96,512]{3,2,1,0:T(8,128)(2,1)} %bitcast.86.refs_0_, bf16[4,4,96,512]{3,2,1,0:T(8,128)(2,1)} %collective-permute-done.29.refs_1_, bf16[4,4,96,512]{3,2,1,0:T(8,128)(2,1)} %bitcast.94.refs_2_, ...), custom_call_target="tpu_custom_call" | custom-call | bytes 25165824 | tf_op jit(solution)/shard_map/merge/pallas_call | solution.py:145
  249.7 3.1 convolution_convert_fusion.17
  252.8 12.1 %attention_back.1 = (bf16[2,128,1024]{2,1,0:T(8,128)(2,1)}, bf16[4,2,128,1024]{3,2,1,0:T(8,128)(2,1)}, bf16[4,2,128,1024]{3,2,1,0:T(8,128)(2,1)}) custom-call(bf16[2,128,1024]{2,1,0:T(8,128)(2,1)} %bitcast.655, bf16[4,2,128,1024]{3,2,1,0:T(8,128)(2,1)} %bitcast.611, bf16[4,2,128,1024]{3,2,1,0:T(8,128)(2,1)} %bitcast.613, bf16[2,128,1024]{2,1,0:T(8,128)(2,1)} %bitcast.656), custom_call_target="tpu_custom_call" | custom-call | flops 1342177280 | bytes 10485760 | tf_op jit(solution)/shard_map/attention_back/pallas_call | solution.py:270
  267.2 2.8 fusion.41
  293.7 4.0 fusion.177
  297.7 2.6 fusion.174
  300.4 2.6 collective-permute-start.36
  303.0 8.1 %collective-permute-start.35 = (bf16[256,1024]{1,0:T(8,128)(2,1)S(1)}, bf16[256,1024]{1,0:T(8,128)(2,1)S(1)}, u32[]{:S(2)}, u32[]{:S(2)}) collective-permute-start(bf16[256,1024]{1,0:T(8,128)(2,1)S(1)} %get-tuple-element.231), channel_id=1, source_target_pairs={{0,2},{1,3},{2,0},{3,1},{4,6},{5,7},{6,4},{7,5},{8,10},{9,11},{10,... | collective-permute-start | bytes 1572872 | tf_op jit(solution)/shard_map/ppermute | solution.py:65
  311.1 8.2 %collective-permute-start.34 = (bf16[256,1024]{1,0:T(8,128)(2,1)S(1)}, bf16[256,1024]{1,0:T(8,128)(2,1)S(1)}, u32[]{:S(2)}, u32[]{:S(2)}) collective-permute-start(bf16[256,1024]{1,0:T(8,128)(2,1)S(1)} %get-tuple-element.229), channel_id=1, source_target_pairs={{0,1},{1,0},{2,3},{3,2},{4,5},{5,4},{6,7},{7,6},{8,9},{9,8},{10,11... | collective-permute-start | bytes 1572872 | tf_op jit(solution)/shard_map/ppermute | solution.py:65
  328.8 20.5 %collective-permute-done.35 = bf16[256,1024]{1,0:T(8,128)(2,1)S(1)} collective-permute-done((bf16[256,1024]{1,0:T(8,128)(2,1)S(1)}, bf16[256,1024]{1,0:T(8,128)(2,1)S(1)}, u32[]{:S(2)}, u32[]{:S(2)}) %collective-permute-start.35) | collective-permute-done | bytes 524320 | tf_op jit(solution)/shard_map/ppermute | solution.py:65
  351.3 17.4 %collective-permute-done.43 = bf16[1,2,3,128,512]{4,3,2,1,0:T(8,128)(2,1)S(1)} collective-permute-done((bf16[1,2,3,128,512]{4,3,2,1,0:T(8,128)(2,1)S(1)}, bf16[1,2,3,128,512]{4,3,2,1,0:T(8,128)(2,1)S(1)}, u32[]{:S(2)}, u32[]{:S(2)}) %collective-permute-start.43) | collective-permute-done | bytes 786464 | tf_op jit(solution)/shard_map/ppermute | solution.py:65
  380.1 2.6 collective-permute-start.46
  386.8 3.2 collective-permute-done.46
  389.9 8.0 %collective-permute-done.45 = bf16[3,32,1024]{2,1,0:T(8,128)(2,1)S(1)} collective-permute-done((bf16[3,32,1024]{2,1,0:T(8,128)(2,1)S(1)}, bf16[3,32,1024]{2,1,0:T(8,128)(2,1)S(1)}, u32[]{:S(2)}, u32[]{:S(2)}) %collective-permute-start.45) | collective-permute-done | bytes 196640 | tf_op jit(solution)/shard_map/ppermute | solution.py:65
  407.9 3.1 collective-permute-done.59
  421.6 2.9 collective-permute-start.49
  426.1 3.8 collective-permute-done.51
  431.2 14.5 %collective-permute-done.50 = bf16[3,32,1024]{2,1,0:T(8,128)(2,1)S(1)} collective-permute-done((bf16[3,32,1024]{2,1,0:T(8,128)(2,1)S(1)}, bf16[3,32,1024]{2,1,0:T(8,128)(2,1)S(1)}, u32[]{:S(2)}, u32[]{:S(2)}) %collective-permute-start.50) | collective-permute-done | bytes 196640 | tf_op jit(solution)/shard_map/ppermute | solution.py:65
  445.8 5.0 collective-permute-start.55
  470.6 5.8 %collective-permute-done.71 = bf16[1,1,3,128,512]{4,3,2,1,0:T(8,128)(2,1)S(1)} collective-permute-done((bf16[1,1,3,128,512]{4,3,2,1,0:T(8,128)(2,1)S(1)}, bf16[1,1,3,128,512]{4,3,2,1,0:T(8,128)(2,1)S(1)}, u32[]{:S(2)}, u32[]{:S(2)}) %collective-permute-start.71) | collective-permute-done | bytes 393248 | tf_op jit(solution)/shard_map/ppermute | solution.py:65
  479.7 2.9 collective-permute-start.73
  482.6 5.4 %collective-permute-done.64 = bf16[2,1,2,128,512]{4,3,2,0,1:T(8,128)(2,1)S(1)} collective-permute-done((bf16[2,1,2,128,512]{4,3,2,0,1:T(8,128)(2,1)S(1)}, bf16[2,1,2,128,512]{4,3,2,0,1:T(8,128)(2,1)S(1)}, u32[]{:S(2)}, u32[]{:S(2)}) %collective-permute-start.64) | collective-permute-done | bytes 524320 | tf_op jit(solution)/shard_map/ppermute | solution.py:65
  490.2 4.9 collective-permute-done.74
  498.3 2.9 collective-permute-start.68
  501.9 2.7 collective-permute-done.70
  504.6 4.0 collective-permute-done.69
  (585 shorter events, 198.9 us)
Async XLA Ops:
  2.4 33.6 %collective-permute-start = (bf16[128,1024]{1,0:T(8,128)(2,1)S(1)}, bf16[128,1024]{1,0:T(8,128)(2,1)S(1)}, u32[]{:S(2)}, u32[]{:S(2)}) collective-permute-start(bf16[128,1024]{1,0:T(8,128)(2,1)S(1)} %pad_maximum_fusion.22), channel_id=1, source_target_pairs={{0,1},{1,0},{2,3},{3,2},{4,5},{5,4},{6,7},{7,6},{8,9},{9,8},{10,11... | collective-permute-start | bytes 786440 | tf_op jit(solution)/shard_map/ppermute | solution.py:65
  5.5 30.5 %collective-permute-start.1 = (bf16[128,1024]{1,0:T(8,128)(2,1)S(1)}, bf16[128,1024]{1,0:T(8,128)(2,1)S(1)}, u32[]{:S(2)}, u32[]{:S(2)}) collective-permute-start(bf16[128,1024]{1,0:T(8,128)(2,1)S(1)} %pad_maximum_fusion.22), channel_id=1, source_target_pairs={{0,2},{1,3},{2,0},{3,1},{4,6},{5,7},{6,4},{7,5},{8,10},{9,11},{10,... | collective-permute-start | bytes 786440 | tf_op jit(solution)/shard_map/ppermute | solution.py:65
  8.1 27.9 %collective-permute-start.2 = (bf16[128,1024]{1,0:T(8,128)(2,1)S(1)}, bf16[128,1024]{1,0:T(8,128)(2,1)S(1)}, u32[]{:S(2)}, u32[]{:S(2)}) collective-permute-start(bf16[128,1024]{1,0:T(8,128)(2,1)S(1)} %pad_maximum_fusion.22), channel_id=1, source_target_pairs={{0,3},{1,2},{2,1},{3,0},{4,7},{5,6},{6,5},{7,4},{8,11},{9,10},{10,... | collective-permute-start | bytes 786440 | tf_op jit(solution)/shard_map/ppermute | solution.py:65
  11.4 24.6 %collective-permute-start.4 = (bf16[32,1024]{1,0:T(8,128)(2,1)S(1)}, bf16[32,1024]{1,0:T(8,128)(2,1)S(1)}, u32[]{:S(2)}, u32[]{:S(2)}) collective-permute-start(bf16[32,1024]{1,0:T(8,128)(2,1)S(1)} %fusion.145), channel_id=1, source_target_pairs={{0,2},{1,3},{2,0},{3,1},{4,6},{5,7},{6,4},{7,5},{8,10},{9,11},{10,... | collective-permute-start | bytes 196616 | tf_op jit(solution)/shard_map/ppermute | solution.py:65
  36.8 14.4 %collective-permute-start.7 = (bf16[1,4,160,512]{3,2,1,0:T(8,128)(2,1)S(1)}, bf16[1,4,160,512]{3,2,1,0:T(8,128)(2,1)S(1)}, u32[]{:S(2)}, u32[]{:S(2)}) collective-permute-start(bf16[1,4,160,512]{3,2,1,0:T(8,128)(2,1)S(1)} %get-tuple-element.249), channel_id=1, source_target_pairs={{0,16},{1,17},{2,18},{3,19},{4,20},{5,21},{6,22},{7,23},{8,24},{9,... | collective-permute-start | bytes 1966088 | tf_op jit(solution)/shard_map/ppermute | solution.py:65
  38.4 14.2 %collective-permute-start.6 = (bf16[1,4,160,512]{3,2,1,0:T(8,128)(2,1)S(1)}, bf16[1,4,160,512]{3,2,1,0:T(8,128)(2,1)}, u32[]{:S(2)}, u32[]{:S(2)}) collective-permute-start(bf16[1,4,160,512]{3,2,1,0:T(8,128)(2,1)S(1)} %get-tuple-element.250), channel_id=1, source_target_pairs={{0,8},{1,9},{2,10},{3,11},{4,12},{5,13},{6,14},{7,15},{8,0},{9,1},... | collective-permute-start | bytes 1966088 | tf_op jit(solution)/shard_map/ppermute | solution.py:65
  55.2 27.5 %collective-permute-start.8 = (bf16[2,4,160,512]{3,2,1,0:T(8,128)(2,1)}, bf16[2,4,160,512]{3,2,1,0:T(8,128)(2,1)}, u32[]{:S(2)}, u32[]{:S(2)}) collective-permute-start(bf16[2,4,160,512]{3,2,1,0:T(8,128)(2,1)} %get-tuple-element.85), channel_id=1, source_target_pairs={{0,16},{1,17},{2,18},{3,19},{4,20},{5,21},{6,22},{7,23},{8,24},{9,... | collective-permute-start | bytes 3932168 | tf_op jit(solution)/shard_map/ppermute | solution.py:65
  55.8 96.4 %collective-permute-start.19 = (bf16[96,1024]{1,0:T(8,128)(2,1)S(1)}, bf16[96,1024]{1,0:T(8,128)(2,1)}, u32[]{:S(2)}, u32[]{:S(2)}) collective-permute-start(bf16[96,1024]{1,0:T(8,128)(2,1)S(1)} %pad_maximum_fusion.23), channel_id=1, source_target_pairs={{0,1},{1,0},{2,3},{3,2},{4,5},{5,4},{6,7},{7,6},{8,9},{9,8},{10,11... | collective-permute-start | bytes 589832 | tf_op jit(solution)/shard_map/ppermute | solution.py:65
  58.4 28.7 %collective-permute-start.9 = (bf16[2,4,160,512]{3,2,1,0:T(8,128)(2,1)S(1)}, bf16[2,4,160,512]{3,2,1,0:T(8,128)(2,1)S(1)}, u32[]{:S(2)}, u32[]{:S(2)}) collective-permute-start(bf16[2,4,160,512]{3,2,1,0:T(8,128)(2,1)S(1)} %get-tuple-element.86), channel_id=1, source_target_pairs={{0,8},{1,9},{2,10},{3,11},{4,12},{5,13},{6,14},{7,15},{8,0},{9,1},... | collective-permute-start | bytes 3932168 | tf_op jit(solution)/shard_map/ppermute | solution.py:65
  61.7 26.3 %collective-permute-start.10 = (bf16[96,1024]{1,0:T(8,128)(2,1)S(1)}, bf16[96,1024]{1,0:T(8,128)(2,1)S(1)}, u32[]{:S(2)}, u32[]{:S(2)}) collective-permute-start(bf16[96,1024]{1,0:T(8,128)(2,1)S(1)} %bitcast.678), channel_id=1, source_target_pairs={{0,1},{1,0},{2,3},{3,2},{4,5},{5,4},{6,7},{7,6},{8,9},{9,8},{10,11... | collective-permute-start | bytes 589832 | tf_op jit(solution)/shard_map/ppermute | solution.py:65
  61.7 26.3 %collective-permute-start.11 = (bf16[96,1024]{1,0:T(8,128)(2,1)S(1)}, bf16[96,1024]{1,0:T(8,128)(2,1)S(1)}, u32[]{:S(2)}, u32[]{:S(2)}) collective-permute-start(bf16[96,1024]{1,0:T(8,128)(2,1)S(1)} %bitcast.679), channel_id=1, source_target_pairs={{0,2},{1,3},{2,0},{3,1},{4,6},{5,7},{6,4},{7,5},{8,10},{9,11},{10,... | collective-permute-start | bytes 589832 | tf_op jit(solution)/shard_map/ppermute | solution.py:65
  90.3 20.4 %collective-permute-start.13 = (bf16[4,4,160,512]{3,2,1,0:T(8,128)(2,1)S(1)}, bf16[4,4,160,512]{3,2,1,0:T(8,128)(2,1)S(1)}, u32[]{:S(2)}, u32[]{:S(2)}) collective-permute-start(bf16[4,4,160,512]{3,2,1,0:T(8,128)(2,1)S(1)} %bitcast.592), channel_id=1, source_target_pairs={{0,4},{1,5},{2,6},{3,7},{4,0},{5,1},{6,2},{7,3},{8,12},{9,13},{10,... | collective-permute-start | bytes 7864328 | tf_op jit(solution)/shard_map/ppermute | solution.py:65
  90.3 21.9 %collective-permute-start.14 = (bf16[4,4,160,512]{3,2,1,0:T(8,128)(2,1)S(1)}, bf16[4,4,160,512]{3,2,1,0:T(8,128)(2,1)}, u32[]{:S(2)}, u32[]{:S(2)}) collective-permute-start(bf16[4,4,160,512]{3,2,1,0:T(8,128)(2,1)S(1)} %bitcast.590), channel_id=1, source_target_pairs={{0,4},{1,5},{2,6},{3,7},{4,0},{5,1},{6,2},{7,3},{8,12},{9,13},{10,... | collective-permute-start | bytes 7864328 | tf_op jit(solution)/shard_map/ppermute | solution.py:65
  103.7 48.5 %collective-permute-start.20 = (bf16[96,1024]{1,0:T(8,128)(2,1)S(1)}, bf16[96,1024]{1,0:T(8,128)(2,1)S(1)}, u32[]{:S(2)}, u32[]{:S(2)}) collective-permute-start(bf16[96,1024]{1,0:T(8,128)(2,1)S(1)} %pad_maximum_fusion.23), channel_id=1, source_target_pairs={{0,2},{1,3},{2,0},{3,1},{4,6},{5,7},{6,4},{7,5},{8,10},{9,11},{10,... | collective-permute-start | bytes 589832 | tf_op jit(solution)/shard_map/ppermute | solution.py:65
  107.3 44.8 %collective-permute-start.21 = (bf16[96,1024]{1,0:T(8,128)(2,1)S(1)}, bf16[96,1024]{1,0:T(8,128)(2,1)}, u32[]{:S(2)}, u32[]{:S(2)}) collective-permute-start(bf16[96,1024]{1,0:T(8,128)(2,1)S(1)} %pad_maximum_fusion.23), channel_id=1, source_target_pairs={{0,3},{1,2},{2,1},{3,0},{4,7},{5,6},{6,5},{7,4},{8,11},{9,10},{10,... | collective-permute-start | bytes 589832 | tf_op jit(solution)/shard_map/ppermute | solution.py:65
  130.9 18.1 %collective-permute-start.17 = (bf16[2,4,96,512]{3,2,1,0:T(8,128)(2,1)S(1)}, bf16[2,4,96,512]{3,2,1,0:T(8,128)(2,1)S(1)}, u32[]{:S(2)}, u32[]{:S(2)}) collective-permute-start(bf16[2,4,96,512]{3,2,1,0:T(8,128)(2,1)S(1)} %copy-done.46), channel_id=1, source_target_pairs={{0,16},{1,17},{2,18},{3,19},{4,20},{5,21},{6,22},{7,23},{8,24},{9,... | collective-permute-start | bytes 2359304 | tf_op jit(solution)/shard_map/ppermute | solution.py:65
  131.6 17.8 %collective-permute-start.18 = (bf16[2,4,96,512]{3,2,1,0:T(8,128)(2,1)S(1)}, bf16[2,4,96,512]{3,2,1,0:T(8,128)(2,1)S(1)}, u32[]{:S(2)}, u32[]{:S(2)}) collective-permute-start(bf16[2,4,96,512]{3,2,1,0:T(8,128)(2,1)S(1)} %copy-done.45), channel_id=1, source_target_pairs={{0,8},{1,9},{2,10},{3,11},{4,12},{5,13},{6,14},{7,15},{8,0},{9,1},... | collective-permute-start | bytes 2359304 | tf_op jit(solution)/shard_map/ppermute | solution.py:65
  164.2 27.0 %collective-permute-start.28 = (bf16[2,4,96,512]{3,2,1,0:T(8,128)(2,1)}, bf16[2,4,96,512]{3,2,1,0:T(8,128)(2,1)}, u32[]{:S(2)}, u32[]{:S(2)}) collective-permute-start(bf16[2,4,96,512]{3,2,1,0:T(8,128)(2,1)} %maximum_bitcast_fusion.4), channel_id=1, source_target_pairs={{0,16},{1,17},{2,18},{3,19},{4,20},{5,21},{6,22},{7,23},{8,24},{9,... | collective-permute-start | bytes 2359304 | tf_op jit(solution)/shard_map/ppermute | solution.py:65
  165.0 23.3 %collective-permute-start.25 = (bf16[256,1024]{1,0:T(8,128)(2,1)S(1)}, bf16[256,1024]{1,0:T(8,128)(2,1)}, u32[]{:S(2)}, u32[]{:S(2)}) collective-permute-start(bf16[256,1024]{1,0:T(8,128)(2,1)S(1)} %add_convert_fusion.2), channel_id=1, source_target_pairs={{0,2},{1,3},{2,0},{3,1},{4,6},{5,7},{6,4},{7,5},{8,10},{9,11},{10,... | collective-permute-start | bytes 1572872 | tf_op jit(solution)/shard_map/ppermute | solution.py:65
  165.0 36.7 %collective-permute-start.22 = (bf16[4,4,96,512]{3,2,1,0:T(8,128)(2,1)}, bf16[4,4,96,512]{3,2,1,0:T(8,128)(2,1)}, u32[]{:S(2)}, u32[]{:S(2)}) collective-permute-start(bf16[4,4,96,512]{3,2,1,0:T(8,128)(2,1)} %bitcast.64.refs_0_), channel_id=1, source_target_pairs={{0,4},{1,5},{2,6},{3,7},{4,0},{5,1},{6,2},{7,3},{8,12},{9,13},{10,... | collective-permute-start | bytes 4718600 | tf_op jit(solution)/shard_map/ppermute | solution.py:65
  165.0 36.7 %collective-permute-start.23 = (bf16[4,4,96,512]{3,2,1,0:T(8,128)(2,1)}, bf16[4,4,96,512]{3,2,1,0:T(8,128)(2,1)}, u32[]{:S(2)}, u32[]{:S(2)}) collective-permute-start(bf16[4,4,96,512]{3,2,1,0:T(8,128)(2,1)} %bitcast.67.refs_2_), channel_id=1, source_target_pairs={{0,4},{1,5},{2,6},{3,7},{4,0},{5,1},{6,2},{7,3},{8,12},{9,13},{10,... | collective-permute-start | bytes 4718600 | tf_op jit(solution)/shard_map/ppermute | solution.py:65
  169.8 24.2 %collective-permute-start.31 = (bf16[2,4,96,512]{3,2,1,0:T(8,128)(2,1)S(1)}, bf16[2,4,96,512]{3,2,1,0:T(8,128)(2,1)S(1)}, u32[]{:S(2)}, u32[]{:S(2)}) collective-permute-start(bf16[2,4,96,512]{3,2,1,0:T(8,128)(2,1)S(1)} %maximum_bitcast_fusion.5), channel_id=1, source_target_pairs={{0,8},{1,9},{2,10},{3,11},{4,12},{5,13},{6,14},{7,15},{8,0},{9,1},... | collective-permute-start | bytes 2359304 | tf_op jit(solution)/shard_map/ppermute | solution.py:65
  194.0 34.6 %collective-permute-start.29 = (bf16[4,4,96,512]{3,2,1,0:T(8,128)(2,1)}, bf16[4,4,96,512]{3,2,1,0:T(8,128)(2,1)}, u32[]{:S(2)}, u32[]{:S(2)}) collective-permute-start(bf16[4,4,96,512]{3,2,1,0:T(8,128)(2,1)} %bitcast.86.refs_0_), channel_id=1, source_target_pairs={{0,4},{1,5},{2,6},{3,7},{4,0},{5,1},{6,2},{7,3},{8,12},{9,13},{10,... | collective-permute-start | bytes 4718600 | tf_op jit(solution)/shard_map/ppermute | solution.py:65
  195.5 33.1 %collective-permute-start.32 = (bf16[4,4,96,512]{3,2,1,0:T(8,128)(2,1)}, bf16[4,4,96,512]{3,2,1,0:T(8,128)(2,1)}, u32[]{:S(2)}, u32[]{:S(2)}) collective-permute-start(bf16[4,4,96,512]{3,2,1,0:T(8,128)(2,1)} %bitcast.94.refs_2_), channel_id=1, source_target_pairs={{0,4},{1,5},{2,6},{3,7},{4,0},{5,1},{6,2},{7,3},{8,12},{9,13},{10,... | collective-permute-start | bytes 4718600 | tf_op jit(solution)/shard_map/ppermute | solution.py:65
  249.7 15.3 %collective-permute-start.33 = (bf16[3,4,128,1024]{3,2,1,0:T(8,128)(2,1)}, bf16[3,4,128,1024]{3,2,1,0:T(8,128)(2,1)}, u32[]{:S(2)}, u32[]{:S(2)}) collective-permute-start(bf16[3,4,128,1024]{3,2,1,0:T(8,128)(2,1)} %pad_maximum_fusion), channel_id=1, source_target_pairs={{0,4},{1,5},{2,6},{3,7},{4,0},{5,1},{6,2},{7,3},{8,12},{9,13},{10,... | collective-permute-start | bytes 9437192 | tf_op jit(solution)/shard_map/ppermute | solution.py:65
  287.2 34.0 %collective-permute-start.41 = (bf16[3,4,128,1024]{3,2,1,0:T(8,128)(2,1)}, bf16[3,4,128,1024]{3,2,1,0:T(8,128)(2,1)}, u32[]{:S(2)}, u32[]{:S(2)}) collective-permute-start(bf16[3,4,128,1024]{3,2,1,0:T(8,128)(2,1)} %pad_maximum_fusion.2), channel_id=1, source_target_pairs={{0,4},{1,5},{2,6},{3,7},{4,0},{5,1},{6,2},{7,3},{8,12},{9,13},{10,... | collective-permute-start | bytes 9437192 | tf_op jit(solution)/shard_map/ppermute | solution.py:65
  290.2 20.9 %collective-permute-start.37 = (bf16[2,1,3,128,512]{4,3,2,0,1:T(8,128)(2,1)S(1)}, bf16[2,1,3,128,512]{4,3,2,0,1:T(8,128)(2,1)S(1)}, u32[]{:S(2)}, u32[]{:S(2)}) collective-permute-start(bf16[2,1,3,128,512]{4,3,2,0,1:T(8,128)(2,1)S(1)} %dynamic-slice_bitcast_fusion.16), channel_id=1, source_target_pairs={{0,8},{1,9},{2,10},{3,11},{4,12},{5,13},{6,14},{7,15},{8,0},{9,1},... | collective-permute-start | bytes 2359304 | tf_op jit(solution)/shard_map/ppermute | solution.py:65
  291.9 27.7 %collective-permute-start.39 = (bf16[1,2,3,128,512]{4,3,2,1,0:T(8,128)(2,1)S(1)}, bf16[1,2,3,128,512]{4,3,2,1,0:T(8,128)(2,1)S(1)}, u32[]{:S(2)}, u32[]{:S(2)}) collective-permute-start(bf16[1,2,3,128,512]{4,3,2,1,0:T(8,128)(2,1)S(1)} %dynamic-slice_bitcast_fusion.15), channel_id=1, source_target_pairs={{0,16},{1,17},{2,18},{3,19},{4,20},{5,21},{6,22},{7,23},{8,24},{9,... | collective-permute-start | bytes 2359304 | tf_op jit(solution)/shard_map/ppermute | solution.py:65
  300.4 27.5 %collective-permute-start.36 = (bf16[256,1024]{1,0:T(8,128)(2,1)S(1)}, bf16[256,1024]{1,0:T(8,128)(2,1)S(1)}, u32[]{:S(2)}, u32[]{:S(2)}) collective-permute-start(bf16[256,1024]{1,0:T(8,128)(2,1)S(1)} %get-tuple-element.230), channel_id=1, source_target_pairs={{0,3},{1,2},{2,1},{3,0},{4,7},{5,6},{6,5},{7,4},{8,11},{9,10},{10,... | collective-permute-start | bytes 1572872 | tf_op jit(solution)/shard_map/ppermute | solution.py:65
  303.0 46.3 %collective-permute-start.35 = (bf16[256,1024]{1,0:T(8,128)(2,1)S(1)}, bf16[256,1024]{1,0:T(8,128)(2,1)S(1)}, u32[]{:S(2)}, u32[]{:S(2)}) collective-permute-start(bf16[256,1024]{1,0:T(8,128)(2,1)S(1)} %get-tuple-element.231), channel_id=1, source_target_pairs={{0,2},{1,3},{2,0},{3,1},{4,6},{5,7},{6,4},{7,5},{8,10},{9,11},{10,... | collective-permute-start | bytes 1572872 | tf_op jit(solution)/shard_map/ppermute | solution.py:65
  311.1 38.7 %collective-permute-start.34 = (bf16[256,1024]{1,0:T(8,128)(2,1)S(1)}, bf16[256,1024]{1,0:T(8,128)(2,1)S(1)}, u32[]{:S(2)}, u32[]{:S(2)}) collective-permute-start(bf16[256,1024]{1,0:T(8,128)(2,1)S(1)} %get-tuple-element.229), channel_id=1, source_target_pairs={{0,1},{1,0},{2,3},{3,2},{4,5},{5,4},{6,7},{7,6},{8,9},{9,8},{10,11... | collective-permute-start | bytes 1572872 | tf_op jit(solution)/shard_map/ppermute | solution.py:65
  319.6 31.2 %collective-permute-start.38 = (bf16[1,1,3,128,512]{4,3,2,0,1:T(8,128)(2,1)S(1)}, bf16[1,1,3,128,512]{4,3,2,0,1:T(8,128)(2,1)S(1)}, u32[]{:S(2)}, u32[]{:S(2)}) collective-permute-start(bf16[1,1,3,128,512]{4,3,2,0,1:T(8,128)(2,1)S(1)} %constant_dynamic-slice_fusion.3), channel_id=1, source_target_pairs={{0,16},{1,17},{2,18},{3,19},{4,20},{5,21},{6,22},{7,23},{8,24},{9,... | collective-permute-start | bytes 1179656 | tf_op jit(solution)/shard_map/ppermute | solution.py:65
  321.2 29.7 %collective-permute-start.40 = (bf16[1,1,3,128,512]{4,3,2,1,0:T(8,128)(2,1)S(1)}, bf16[1,1,3,128,512]{4,3,2,1,0:T(8,128)(2,1)S(1)}, u32[]{:S(2)}, u32[]{:S(2)}) collective-permute-start(bf16[1,1,3,128,512]{4,3,2,1,0:T(8,128)(2,1)S(1)} %constant_dynamic-slice_fusion.2), channel_id=1, source_target_pairs={{0,8},{1,9},{2,10},{3,11},{4,12},{5,13},{6,14},{7,15},{8,0},{9,1},... | collective-permute-start | bytes 1179656 | tf_op jit(solution)/shard_map/ppermute | solution.py:65
  327.9 23.1 %collective-permute-start.42 = (bf16[2,1,3,128,512]{4,3,2,0,1:T(8,128)(2,1)S(1)}, bf16[2,1,3,128,512]{4,3,2,0,1:T(8,128)(2,1)S(1)}, u32[]{:S(2)}, u32[]{:S(2)}) collective-permute-start(bf16[2,1,3,128,512]{4,3,2,0,1:T(8,128)(2,1)S(1)} %dynamic-slice_bitcast_fusion.14), channel_id=1, source_target_pairs={{0,8},{1,9},{2,10},{3,11},{4,12},{5,13},{6,14},{7,15},{8,0},{9,1},... | collective-permute-start | bytes 2359304 | tf_op jit(solution)/shard_map/ppermute | solution.py:65
  349.3 19.5 %collective-permute-start.43 = (bf16[1,2,3,128,512]{4,3,2,1,0:T(8,128)(2,1)S(1)}, bf16[1,2,3,128,512]{4,3,2,1,0:T(8,128)(2,1)S(1)}, u32[]{:S(2)}, u32[]{:S(2)}) collective-permute-start(bf16[1,2,3,128,512]{4,3,2,1,0:T(8,128)(2,1)S(1)} %dynamic-slice_bitcast_fusion.13), channel_id=1, source_target_pairs={{0,16},{1,17},{2,18},{3,19},{4,20},{5,21},{6,22},{7,23},{8,24},{9,... | collective-permute-start | bytes 2359304 | tf_op jit(solution)/shard_map/ppermute | solution.py:65
  382.7 15.2 %collective-permute-start.45 = (bf16[3,32,1024]{2,1,0:T(8,128)(2,1)S(1)}, bf16[3,32,1024]{2,1,0:T(8,128)(2,1)S(1)}, u32[]{:S(2)}, u32[]{:S(2)}) collective-permute-start(bf16[3,32,1024]{2,1,0:T(8,128)(2,1)S(1)} %get-tuple-element.272), channel_id=1, source_target_pairs={{0,2},{1,3},{2,0},{3,1},{4,6},{5,7},{6,4},{7,5},{8,10},{9,11},{10,... | collective-permute-start | bytes 589832 | tf_op jit(solution)/shard_map/ppermute | solution.py:65
  382.7 15.2 %collective-permute-start.44 = (bf16[3,32,1024]{2,1,0:T(8,128)(2,1)S(1)}, bf16[3,32,1024]{2,1,0:T(8,128)(2,1)S(1)}, u32[]{:S(2)}, u32[]{:S(2)}) collective-permute-start(bf16[3,32,1024]{2,1,0:T(8,128)(2,1)S(1)} %get-tuple-element.271), channel_id=1, source_target_pairs={{0,1},{1,0},{2,3},{3,2},{4,5},{5,4},{6,7},{7,6},{8,9},{9,8},{10,11... | collective-permute-start | bytes 589832 | tf_op jit(solution)/shard_map/ppermute | solution.py:65
  389.9 22.6 %collective-permute-start.52 = (bf16[3,4,128,1024]{3,2,1,0:T(8,128)(2,1)S(1)}, bf16[3,4,128,1024]{3,2,1,0:T(8,128)(2,1)S(1)}, u32[]{:S(2)}, u32[]{:S(2)}) collective-permute-start(bf16[3,4,128,1024]{3,2,1,0:T(8,128)(2,1)S(1)} %pad_maximum_fusion.4), channel_id=1, source_target_pairs={{0,4},{1,5},{2,6},{3,7},{4,0},{5,1},{6,2},{7,3},{8,12},{9,13},{10,... | collective-permute-start | bytes 9437192 | tf_op jit(solution)/shard_map/ppermute | solution.py:65
  414.8 36.8 %collective-permute-start.53 = (bf16[2,1,3,128,512]{4,3,2,0,1:T(8,128)(2,1)S(1)}, bf16[2,1,3,128,512]{4,3,2,0,1:T(8,128)(2,1)S(1)}, u32[]{:S(2)}, u32[]{:S(2)}) collective-permute-start(bf16[2,1,3,128,512]{4,3,2,0,1:T(8,128)(2,1)S(1)} %dynamic-slice_bitcast_fusion.12), channel_id=1, source_target_pairs={{0,8},{1,9},{2,10},{3,11},{4,12},{5,13},{6,14},{7,15},{8,0},{9,1},... | collective-permute-start | bytes 2359304 | tf_op jit(solution)/shard_map/ppermute | solution.py:65
  417.8 35.0 %collective-permute-start.54 = (bf16[1,2,3,128,512]{4,3,2,1,0:T(8,128)(2,1)S(1)}, bf16[1,2,3,128,512]{4,3,2,1,0:T(8,128)(2,1)S(1)}, u32[]{:S(2)}, u32[]{:S(2)}) collective-permute-start(bf16[1,2,3,128,512]{4,3,2,1,0:T(8,128)(2,1)S(1)} %dynamic-slice_bitcast_fusion.11), channel_id=1, source_target_pairs={{0,16},{1,17},{2,18},{3,19},{4,20},{5,21},{6,22},{7,23},{8,24},{9,... | collective-permute-start | bytes 2359304 | tf_op jit(solution)/shard_map/ppermute | solution.py:65
  421.5 24.3 %collective-permute-start.50 = (bf16[3,32,1024]{2,1,0:T(8,128)(2,1)S(1)}, bf16[3,32,1024]{2,1,0:T(8,128)(2,1)S(1)}, u32[]{:S(2)}, u32[]{:S(2)}) collective-permute-start(bf16[3,32,1024]{2,1,0:T(8,128)(2,1)S(1)} %get-tuple-element.269), channel_id=1, source_target_pairs={{0,2},{1,3},{2,0},{3,1},{4,6},{5,7},{6,4},{7,5},{8,10},{9,11},{10,... | collective-permute-start | bytes 589832 | tf_op jit(solution)/shard_map/ppermute | solution.py:65
  421.6 24.1 %collective-permute-start.49 = (bf16[3,32,1024]{2,1,0:T(8,128)(2,1)S(1)}, bf16[3,32,1024]{2,1,0:T(8,128)(2,1)S(1)}, u32[]{:S(2)}, u32[]{:S(2)}) collective-permute-start(bf16[3,32,1024]{2,1,0:T(8,128)(2,1)S(1)} %get-tuple-element.268), channel_id=1, source_target_pairs={{0,1},{1,0},{2,3},{3,2},{4,5},{5,4},{6,7},{7,6},{8,9},{9,8},{10,11... | collective-permute-start | bytes 589832 | tf_op jit(solution)/shard_map/ppermute | solution.py:65
  429.9 32.4 %collective-permute-start.57 = (bf16[261,512]{1,0:T(8,128)(2,1)}, bf16[261,512]{1,0:T(8,128)(2,1)}, u32[]{:S(2)}, u32[]{:S(2)}) collective-permute-start(bf16[261,512]{1,0:T(8,128)(2,1)} %get-tuple-element.237), channel_id=1, source_target_pairs={{0,3},{1,2},{2,1},{3,0},{4,7},{5,6},{6,5},{7,4},{8,11},{9,10},{10,... | collective-permute-start | bytes 801800 | tf_op jit(solution)/shard_map/ppermute | solution.py:65
  445.8 16.5 %collective-permute-start.56 = (bf16[261,512]{1,0:T(8,128)(2,1)}, bf16[261,512]{1,0:T(8,128)(2,1)}, u32[]{:S(2)}, u32[]{:S(2)}) collective-permute-start(bf16[261,512]{1,0:T(8,128)(2,1)} %get-tuple-element.238), channel_id=1, source_target_pairs={{0,2},{1,3},{2,0},{3,1},{4,6},{5,7},{6,4},{7,5},{8,10},{9,11},{10,... | collective-permute-start | bytes 801800 | tf_op jit(solution)/shard_map/ppermute | solution.py:65
  445.8 16.5 %collective-permute-start.55 = (bf16[261,512]{1,0:T(8,128)(2,1)S(1)}, bf16[261,512]{1,0:T(8,128)(2,1)}, u32[]{:S(2)}, u32[]{:S(2)}) collective-permute-start(bf16[261,512]{1,0:T(8,128)(2,1)S(1)} %get-tuple-element.236), channel_id=1, source_target_pairs={{0,1},{1,0},{2,3},{3,2},{4,5},{5,4},{6,7},{7,6},{8,9},{9,8},{10,11... | collective-permute-start | bytes 801800 | tf_op jit(solution)/shard_map/ppermute | solution.py:65
  468.7 19.3 %collective-permute-start.64 = (bf16[2,1,2,128,512]{4,3,2,0,1:T(8,128)(2,1)S(1)}, bf16[2,1,2,128,512]{4,3,2,0,1:T(8,128)(2,1)S(1)}, u32[]{:S(2)}, u32[]{:S(2)}) collective-permute-start(bf16[2,1,2,128,512]{4,3,2,0,1:T(8,128)(2,1)S(1)} %dynamic-slice_bitcast_fusion.18), channel_id=1, source_target_pairs={{0,8},{1,9},{2,10},{3,11},{4,12},{5,13},{6,14},{7,15},{8,0},{9,1},... | collective-permute-start | bytes 1572872 | tf_op jit(solution)/shard_map/ppermute | solution.py:65
  478.8 16.3 %collective-permute-start.74 = (bf16[3,32,1024]{2,1,0:T(8,128)(2,1)S(1)}, bf16[3,32,1024]{2,1,0:T(8,128)(2,1)S(1)}, u32[]{:S(2)}, u32[]{:S(2)}) collective-permute-start(bf16[3,32,1024]{2,1,0:T(8,128)(2,1)S(1)} %get-tuple-element.266), channel_id=1, source_target_pairs={{0,2},{1,3},{2,0},{3,1},{4,6},{5,7},{6,4},{7,5},{8,10},{9,11},{10,... | collective-permute-start | bytes 589832 | tf_op jit(solution)/shard_map/ppermute | solution.py:65
  479.7 15.4 %collective-permute-start.73 = (bf16[3,32,1024]{2,1,0:T(8,128)(2,1)S(1)}, bf16[3,32,1024]{2,1,0:T(8,128)(2,1)S(1)}, u32[]{:S(2)}, u32[]{:S(2)}) collective-permute-start(bf16[3,32,1024]{2,1,0:T(8,128)(2,1)S(1)} %get-tuple-element.265), channel_id=1, source_target_pairs={{0,1},{1,0},{2,3},{3,2},{4,5},{5,4},{6,7},{7,6},{8,9},{9,8},{10,11... | collective-permute-start | bytes 589832 | tf_op jit(solution)/shard_map/ppermute | solution.py:65
  (147 other events, 904.4 us)

commit v3 on v1

v3 whole, which is shorter than its diff:
```python
from functools import partial

import jax
import jax.numpy as jnp
from jax import lax
from jax.experimental.layout import Layout, with_layout_constraint
from jax.experimental import pallas as pl
from jax.experimental.pallas import tpu as pltpu
from jax.sharding import PartitionSpec as P

HEADS = 8
HEAD = 128
USED = 1792
EPSILON = 1e-05
MASKED = -1e30
AXES = ("dp", "fsdp")
LANES = 128
HEADS_AT_ONCE = 2
BF = jnp.bfloat16
F32 = jnp.float32


def dot(left, right, dims):
    return lax.dot_general(left, right, ((dims[0], dims[1]), ((), ())), preferred_element_type=F32)


def mm(left, right):
    return dot(left, right, ((left.ndim - 1,), (0,)))


def mm_t(left, right):
    return dot(left, right, ((left.ndim - 1,), (1,)))


def tm(left, right):
    return dot(left, right, ((0,), (0,)))


def norm_parts(values):
    average = jnp.mean(values, axis=-1, keepdims=True)
    centered = values - average
    variance = jnp.mean(centered * centered, axis=-1, keepdims=True)
    inverse = lax.rsqrt(variance + EPSILON)
    return centered * inverse, inverse


def norm_back(hat, inverse, gains, grad_out):
    grad_hat = grad_out * gains
    first = jnp.mean(grad_hat, axis=-1, keepdims=True)
    second = jnp.mean(grad_hat * hat, axis=-1, keepdims=True)
    return inverse * (grad_hat - first - hat * second)


def gelu(values):
    return 0.5 * values * (1.0 + lax.erf(values * (0.5**0.5)))


def gelu_slope(values):
    density = jnp.exp(-0.5 * values * values) * ((0.5 / jnp.pi) ** 0.5)
    return 0.5 * (1.0 + lax.erf(values * (0.5**0.5))) + values * density


def xor_permute(values, sizes, step):
    dp_size, fsdp_size = sizes
    total = dp_size * fsdp_size
    return lax.ppermute(values, AXES, [(i, i ^ step) for i in range(total)])


def seal(*values):
    return lax.optimization_barrier(values)


def bits_of(sizes):
    low = sizes[1].bit_length() - 1
    every = list(range((sizes[0] * sizes[1]).bit_length() - 1))
    return every[:low], every[low], every[low + 1 :]


def gather_fsdp(values, sizes):
    return [values] + [xor_permute(values, sizes, k) for k in range(1, sizes[1])]


def slot_shift(values, size, j):
    return lax.ppermute(values, "fsdp", [(i, (i + j) % size) for i in range(size)])


def order_fsdp(parts, sizes, me):
    low, _, _ = bits_of(sizes)
    for bit in low:
        mine = ((me >> bit) & 1) == 1
        parts = [jnp.where(mine, parts[k ^ (1 << bit)], parts[k]) for k in range(len(parts))]
    return jnp.stack(parts)


def merge(own, got, bit, above, me):
    mine = ((me >> bit) & 1) == 1
    view = (2**above, -1) + own.shape[1:]
    own, got = own.reshape(view), got.reshape(view)
    both = jnp.stack([jnp.where(mine, got, own), jnp.where(mine, own, got)], axis=1)
    return both.reshape((-1,) + own.shape[2:])


def far_step(groups, place, sizes, me):
    _, _, far = bits_of(sizes)
    result = []
    for values, order in zip(groups, (far, far[::-1])):
        bit, held = order[place], order[:place]
        got = xor_permute(values, sizes, 1 << bit)
        result.append(merge(values, got, bit, sum(1 for other in held if other > bit), me))
    return result


def core_swap(groups, sizes):
    _, core, _ = bits_of(sizes)
    return [xor_permute(values, sizes, 1 << core) for values in groups]


def sources_of(groups, got, count, sizes, me):
    own = groups[0].shape[2] // count
    if own % 16 == 0:
        return [groups[0], got[0], groups[1], got[1]]
    _, core, _ = bits_of(sizes)
    mine = ((me >> core) & 1) == 1
    both = [jnp.stack([jnp.where(mine, g, v), jnp.where(mine, v, g)], axis=1) for v, g in zip(groups, got)]
    whole = jnp.concatenate(both, axis=-1)
    parts = [whole[:, :, :, i * own : (i + 1) * own] for i in range(count)]
    return [part.reshape(-1, part.shape[-1]) for part in parts]


def halves_of(values):
    half = values.shape[-1] // 2
    return [values[..., :half], values[..., half:]]


def core_terms(grads, sizes, me):
    _, core, _ = bits_of(sizes)
    if len(grads) == 1:
        mine = (me >> core) & 1
        count, width = grads[0].shape[0], grads[0].shape[-1]
        view = jnp.swapaxes(grads[0].reshape(count, sizes[0] // 2, 2, -1, width), 0, 1)
        send = lax.dynamic_index_in_dim(view, 1 - mine, 2, keepdims=False)
        keep = lax.dynamic_index_in_dim(view, mine, 2, keepdims=False)
    else:
        send, keep = grads
    got = xor_permute(send, sizes, 1 << core)
    return [list(terms) for terms in zip(halves_of(keep), halves_of(got))]


def sum_of(terms):
    total = terms[0].astype(F32)
    for term in terms[1:]:
        total = total + term.astype(F32)
    return total


def far_terms(terms, bit, held, sizes, me):
    above = sum(1 for other in held if other > bit)
    mine = (me >> bit) & 1

    def half(term, side):
        view = term.reshape((2**above, 2, -1) + term.shape[1:])
        part = lax.dynamic_index_in_dim(view, side, 1, keepdims=False)
        return part.reshape((-1,) + term.shape[1:])

    send = sum_of([half(term, 1 - mine) for term in terms]).astype(BF)
    return [half(term, mine) for term in terms] + [xor_permute(send, sizes, 1 << bit)]


def far_pair(groups, place, sizes, me):
    _, _, far = bits_of(sizes)
    result = []
    for terms, order in zip(groups, (far, far[::-1])):
        held = [bit for bit in far if bit not in order[:place]]
        result.append(far_terms(terms, order[place], held, sizes, me))
    return result


def finish_sum(groups, sizes, my_fsdp):
    def part(term, shard):
        view = term[0].reshape(term.shape[1], sizes[1], -1, term.shape[-1])
        return lax.dynamic_index_in_dim(view, shard, 1, keepdims=False)

    def both(shard):
        return jnp.concatenate([sum_of([part(term, shard) for term in terms]) for terms in groups], axis=-1)

    got = [xor_permute(both(my_fsdp ^ k).astype(BF), sizes, k) for k in range(1, sizes[1])]
    return sum_of([both(my_fsdp)] + got)


def total_over(values, bits, sizes):
    for bit in bits:
        values = values + xor_permute(values, sizes, 1 << bit)
    return values


class Pack:
    def __init__(self, sizes, own, width):
        self.far, self.fsdp, self.own, self.width = sizes[0] // 2, sizes[1], own, width
        self.block = width // sizes[0]
        self.packed = own % 16 == 0
        self.split = self.block % LANES == 0

    def sources(self, count):
        return 4 if self.packed else count

    def scratch(self):
        shape = (self.far, 2, self.fsdp, self.own, self.width) if self.packed else (self.width, self.width)
        return pltpu.VMEM(shape, BF)

    def fetch(self, sources, index, scratch, sem):
        if not self.packed:
            pltpu.make_async_copy(sources[index], scratch, sem).start()
            return
        core = lax.axis_index("dp") & 1
        rows, half = pl.ds(index * self.own, self.own), self.width // 2
        for start, mine, other in ((0, sources[0], sources[1]), (half, sources[2], sources[3])):
            for source, side in ((mine, core), (other, 1 - core)):
                target = scratch.at[:, side, :, :, pl.ds(start, half)]
                pltpu.make_async_copy(source.at[:, :, rows, :], target, sem).start()

    def ready(self, scratch, sem):
        pltpu.make_async_copy(scratch, scratch, sem).wait()
        return scratch[...].reshape(self.width, self.width)

    def grads(self, count):
        if not self.split:
            return [jax.ShapeDtypeStruct((count, self.width, self.width), BF)]
        return [jax.ShapeDtypeStruct((self.far, count, self.block, self.width), BF)] * 2

    def columns(self, ref):
        if not self.split:
            return [ref[...]]
        core = lax.axis_index("dp") & 1
        result = []
        for side in (1 - core, core):
            starts = [pl.multiple_of((2 * i + side) * self.block, self.block) for i in range(self.far)]
            result.append(jnp.concatenate([ref[:, pl.ds(start, self.block)] for start in starts], axis=1))
        return result

    def put(self, refs, index, values):
        for ref, value in zip(refs, values):
            value = value.astype(BF)
            if self.split:
                ref[:, index] = value.reshape(self.far, self.block, self.width)
            else:
                ref[index] = value

    def put_product(self, refs, index, left_ref, right):
        self.put(refs, index, [tm(left, right) for left in self.columns(left_ref)])


def kernel_call(kernel, name, operands, sources, outs, scratch, vmem_mb, work_mb, scalars=()):
    specs = [pl.BlockSpec(memory_space=pltpu.SMEM)] * len(scalars)
    specs += [pl.BlockSpec(memory_space=pltpu.VMEM)] * len(operands)
    specs += [pl.BlockSpec(memory_space=pl.ANY)] * len(sources)
    return pl.pallas_call(
        kernel,
        in_specs=specs,
        out_specs=[pl.BlockSpec(memory_space=pltpu.VMEM)] * len(outs),
        out_shape=outs,
        scratch_shapes=scratch,
        compiler_params=pltpu.CompilerParams(vmem_limit_bytes=vmem_mb * 2**20),
        cost_estimate=pl.CostEstimate(flops=2**30, bytes_accessed=work_mb * 2**20, transcendentals=2**20),
        name=name,
    )(*scalars, *operands, *sources)


def column_sum(values):
    return jnp.sum(values, axis=0, keepdims=True)


def softmax(scores):
    powers = jnp.exp(scores - jnp.max(scores, axis=-1, keepdims=True))
    return powers * (1.0 / jnp.sum(powers, axis=-1, keepdims=True))


def small_rows(small_ref):
    return lambda i: small_ref[i : i + 1]


def encoder_kernel(pack, n_source, padded, lat_rows, *refs):
    counts, latents, pix = refs[:3]
    sources, rest = refs[3 : 3 + n_source], refs[3 + n_source :]
    small_o, q_o, query_pix_o, probs_o, mixed_pix_o, mixed_o, resid_o, pre_o, act_o, first_o, low_o = rest[:11]
    scratch, sems = rest[11:16], rest[16]
    half = pack.width // 2
    for slot, index in enumerate((4, 2, 3, 0, 1)):
        pack.fetch(sources, index, scratch[slot], sems.at[slot])
    latent_in = latents[...].astype(F32)
    hat, _ = norm_parts(latent_in)
    kv = pack.ready(scratch[0], sems.at[0])
    shape = (small_o.shape[0], half - padded)
    eye = lax.broadcasted_iota(jnp.int32, shape, 0) == lax.broadcasted_iota(jnp.int32, shape, 1)
    small_o[...] = mm_t(eye.astype(F32).astype(BF), kv[:, padded:half])
    small = small_rows(small_o)
    in_low = (hat * small(0) + small(2)).astype(BF)
    query = mm(in_low, pack.ready(scratch[1], sems.at[1])).astype(BF)
    q_o[...] = query
    query_pix = mm(query, kv[:, :padded]).astype(BF)
    query_pix_o[...] = query_pix
    shape = probs_o.shape
    row, column = lax.broadcasted_iota(jnp.int32, shape, 0), lax.broadcasted_iota(jnp.int32, shape, 1)
    first, end, total = jnp.zeros(shape, jnp.int32), jnp.zeros(shape, jnp.int32), 0
    for image in range(shape[0] // lat_rows):
        here = (row >= image * lat_rows) & (row < (image + 1) * lat_rows)
        first = jnp.where(here, total, first)
        total = total + counts[0, image]
        end = jnp.where(here, total, end)
    scores = mm_t(query_pix, pix[...]) * pack.width**-0.5
    probs = softmax(jnp.where((column >= first) & (column < end), scores, MASKED))
    probs_o[...] = probs
    mixed_pix = mm(probs.astype(BF), pix[...]).astype(BF)
    mixed_pix_o[...] = mixed_pix
    mixed = mm_t(mixed_pix, kv[:, half : half + padded]).astype(BF)
    mixed_o[...] = mixed
    resid = latent_in + mm(mixed, pack.ready(scratch[2], sems.at[2]))
    resid_o[...] = resid
    hat, _ = norm_parts(resid)
    normed = (hat * small(1) + small(3)).astype(BF)
    pre = mm(normed, pack.ready(scratch[3], sems.at[3])) + small(4)
    pre_o[...] = pre
    act = gelu(pre).astype(BF)
    act_o[...] = act
    out = resid + mm(act, pack.ready(scratch[4], sems.at[4])) + small(5)
    first_o[...] = out
    hat, _ = norm_parts(out)
    low_o[...] = (hat * small(6) + small(8)).astype(BF)


def fill_every(every, own, others, lat_rows, rows):
    every[0:rows] = own[...]
    count = len(others) // (rows // lat_rows)
    for i, shard in enumerate(others):
        start = (1 + i % count) * rows + i // count * lat_rows
        every[start : start + lat_rows] = shard[...]


def attention_kernel(pack, n_source, n_other, lat_rows, *refs):
    own, others, rest = refs[0], refs[1 : 1 + n_other], refs[1 + n_other :]
    sources, rest = rest[:n_source], rest[n_source:]
    q_o, k_o, v_o, mixed_o = rest[:4]
    scratch, every, sems = rest[4:7], rest[7], rest[8]
    for index in range(3):
        pack.fetch(sources, index, scratch[index], sems.at[index])
    rows = own.shape[0]
    fill_every(every, own, others, lat_rows, rows)
    q_o[...] = mm(own[...], pack.ready(scratch[0], sems.at[0])).astype(BF)
    k_o[...] = mm(every[...], pack.ready(scratch[1], sems.at[1])).astype(BF).reshape(k_o.shape)
    v_o[...] = mm(every[...], pack.ready(scratch[2], sems.at[2])).astype(BF).reshape(k_o.shape)

    def some_heads(step, carry):
        places, loaded = [], []
        for head in range(HEADS_AT_ONCE):
            cols = pl.ds(pl.multiple_of((step * HEADS_AT_ONCE + head) * HEAD, HEAD), HEAD)
            for start in range(0, rows, lat_rows):
                part = pl.ds(start, lat_rows)
                places.append((part, cols))
                loaded.append((q_o[part, cols], k_o[:, part, cols].reshape(-1, HEAD), v_o[:, part, cols].reshape(-1, HEAD)))
        scores = [mm_t(q, k) * HEAD**-0.5 for q, k, _ in loaded]
        probs = [softmax(score).astype(BF) for score in scores]
        mixed = [mm(prob, v).astype(BF) for prob, (_, _, v) in zip(probs, loaded)]
        for place, value in zip(places, mixed):
            mixed_o[place] = value
        return carry

    lax.fori_loop(0, HEADS // HEADS_AT_ONCE, some_heads, 0)


def attention_back_kernel(pack, n_source, n_other, lat_rows, *refs):
    q, k_ref, v_ref, grad, own = refs[:5]
    others, rest = refs[5 : 5 + n_other], refs[5 + n_other :]
    sources, rest = rest[:n_source], rest[n_source:]
    outs = 2 + len(pack.grads(3))
    slot_o, slots_o, *grad_o = rest[:outs]
    scratch, (every, dq, dk, dv, sems) = rest[outs : outs + 3], rest[outs + 3 :]
    for index in range(3):
        pack.fetch(sources, index, scratch[index], sems.at[index])
    rows = q.shape[0]
    scale = HEAD**-0.5
    fill_every(every, own, others, lat_rows, rows)

    def some_heads(step, carry):
        places, loaded = [], []
        for head in range(HEADS_AT_ONCE):
            cols = pl.ds(pl.multiple_of((step * HEADS_AT_ONCE + head) * HEAD, HEAD), HEAD)
            for start in range(0, rows, lat_rows):
                part = pl.ds(start, lat_rows)
                places.append((part, cols))
                k, v = k_ref[:, part, cols].reshape(-1, HEAD), v_ref[:, part, cols].reshape(-1, HEAD)
                loaded.append((q[part, cols], k, v, grad[part, cols]))
        scores = [mm_t(query, k) * scale for query, k, _, _ in loaded]
        grad_probs = [mm_t(out_grad, v) for _, _, v, out_grad in loaded]
        results = []
        for score, grad_prob, (query, k, v, out_grad) in zip(scores, grad_probs, loaded):
            prob = softmax(score)
            inner = jnp.sum(prob * grad_prob, axis=-1, keepdims=True)
            grad_score = (prob * (grad_prob - inner) * scale).astype(BF)
            results.append((mm(grad_score, k), tm(grad_score, query), tm(prob.astype(BF), out_grad)))
        for (part, cols), (one, two, three) in zip(places, results):
            dq[part, cols] = one.astype(BF)
            dk[:, part, cols] = two.astype(BF).reshape(pack.fsdp, lat_rows, HEAD)
            dv[:, part, cols] = three.astype(BF).reshape(pack.fsdp, lat_rows, HEAD)
        return carry

    lax.fori_loop(0, HEADS // HEADS_AT_ONCE, some_heads, 0)
    d_q, d_k, d_v = dq[...], dk[...].reshape(-1, pack.width), dv[...].reshape(-1, pack.width)
    w_query = pack.ready(scratch[0], sems.at[0])
    w_key, w_value = pack.ready(scratch[1], sems.at[1]), pack.ready(scratch[2], sems.at[2])
    slot_o[...] = mm_t(d_q, w_query) + mm_t(d_k[:rows], w_key) + mm_t(d_v[:rows], w_value)
    others = mm_t(d_k[rows:], w_key) + mm_t(d_v[rows:], w_value)
    slots_o[...] = others.astype(BF).reshape(slots_o.shape)
    pack.put(grad_o, 0, [tm(left, d_q) for left in pack.columns(every.at[pl.ds(0, rows)])])
    columns = pack.columns(every)
    pack.put(grad_o, 1, [tm(left, d_k) for left in columns])
    pack.put(grad_o, 2, [tm(left, d_v) for left in columns])


def latent_kernel(pack, n_source, *refs):
    mixed, first_out, cotangent, small_ref = refs[:4]
    sources, rest = refs[4 : 4 + n_source], refs[4 + n_source :]
    outs = 4 + len(pack.grads(3))
    result_o, grad_o, d_mixed_o, sums_o, *grads_o = rest[:outs]
    scratch, (act_s, normed_s, sems) = rest[outs : outs + 3], rest[outs + 3 :]
    for index in range(3):
        pack.fetch(sources, index, scratch[index], sems.at[index])
    small = small_rows(small_ref)
    w_out = pack.ready(scratch[0], sems.at[0])
    resid = first_out[...] + mm(mixed[...], w_out)
    hat, inverse = norm_parts(resid)
    normed_s[...] = (hat * small(7) + small(9)).astype(BF)
    w_first = pack.ready(scratch[1], sems.at[1])
    pre = mm(normed_s[...], w_first) + small(10)
    act_s[...] = gelu(pre).astype(BF)
    w_second = pack.ready(scratch[2], sems.at[2])
    result_o[...] = (resid + mm(act_s[...], w_second) + small(11)).astype(BF)
    grad_low = cotangent[...]
    grad_out = grad_low.astype(F32)
    pack.put_product(grads_o, 1, act_s, grad_low)
    d_pre = mm_t(grad_low, w_second) * gelu_slope(pre)
    d_pre_low = d_pre.astype(BF)
    pack.put_product(grads_o, 0, normed_s, d_pre_low)
    d_normed = mm_t(d_pre_low, w_first)
    grad_mid = grad_out + norm_back(hat, inverse, small(7), d_normed)
    grad_o[...] = grad_mid
    grad_low = grad_mid.astype(BF)
    d_mixed_o[...] = mm_t(grad_low, w_out).astype(BF)
    pack.put_product(grads_o, 2, mixed, grad_low)
    sums_o[0:1] = column_sum(d_normed * hat)
    sums_o[1:2] = column_sum(d_normed)
    sums_o[2:3] = column_sum(d_pre)
    sums_o[3:4] = column_sum(grad_out)


def encoder_back_kernel(pack, n_source, n_other, images, *refs):
    slot, grad_mid, first_out, resid, pre_ref, act, small_ref = refs[:7]
    others, rest = refs[7 : 7 + n_other], refs[7 + n_other :]
    sources, rest = rest[:n_source], rest[n_source:]
    outs = 2 + len(pack.grads(2))
    grad_o, sums_o, *grads_o = rest[:outs]
    scratch, (normed_s, sems) = rest[outs : outs + 2], rest[outs + 2 :]
    for index in range(2):
        pack.fetch(sources, index, scratch[index], sems.at[index])
    small = small_rows(small_ref)
    parts, count = [], n_other // images
    for image in range(images):
        parts.append(sum(ref[...].astype(F32) for ref in others[image * count : (image + 1) * count]))
    d_normed = slot[...] + jnp.concatenate(parts, axis=0)
    hat, inverse = norm_parts(first_out[...])
    sums_o[0:1] = column_sum(d_normed * hat)
    sums_o[1:2] = column_sum(d_normed)
    grad_out = grad_mid[...] + norm_back(hat, inverse, small(6), d_normed)
    grad_low = grad_out.astype(BF)
    w_second = pack.ready(scratch[1], sems.at[1])
    d_pre = mm_t(grad_low, w_second) * gelu_slope(pre_ref[...])
    d_pre_low = d_pre.astype(BF)
    d_normed = mm_t(d_pre_low, pack.ready(scratch[0], sems.at[0]))
    hat, inverse = norm_parts(resid[...])
    grad_o[...] = grad_out + norm_back(hat, inverse, small(1), d_normed)
    normed_s[...] = (hat * small(1) + small(3)).astype(BF)
    pack.put_product(grads_o, 0, normed_s, d_pre_low)
    pack.put_product(grads_o, 1, act, grad_low)
    sums_o[2:3] = column_sum(d_normed * hat)
    sums_o[3:4] = column_sum(d_normed)
    sums_o[4:5] = column_sum(d_pre)
    sums_o[5:6] = column_sum(grad_out)


def cross_back_kernel(pack, n_source, padded, share, *refs):
    grad_ref, latents, mixed, mixed_pix, probs_ref, pix, query_pix, enc_q, small_ref, lat_sums, enc_sums, pix_hat = refs[:12]
    sources, rest = refs[12 : 12 + n_source], refs[12 + n_source :]
    outs = 3 + len(pack.grads(3))
    d_latents_o, d_pix_o, pix_sums_o, *grads_o = rest[:outs]
    scratch, (d_mixed_s, in_low_s, high_s, low_s, sems) = rest[outs : outs + 3], rest[outs + 3 :]
    for slot, index in enumerate((3, 4, 2)):
        pack.fetch(sources, index, scratch[slot], sems.at[slot])
    small = small_rows(small_ref)
    half = pack.width // 2
    scale = pack.width**-0.5
    grad_enc = grad_ref[...]
    grad_low = grad_enc.astype(BF)
    d_mixed_s[...] = mm_t(grad_low, pack.ready(scratch[0], sems.at[0])).astype(BF)
    kv = pack.ready(scratch[1], sems.at[1])
    mixed_back = mm(d_mixed_s[...], kv[:, half : half + padded]).astype(BF)
    d_probs = mm_t(mixed_back, pix[...])
    probs = probs_ref[...]
    inner = jnp.sum(probs * d_probs, axis=-1, keepdims=True)
    d_scores = (probs * (d_probs - inner) * scale).astype(BF)
    d_pix = tm(query_pix[...], d_scores) + tm(mixed_back, probs.astype(BF))
    kept, used = pix_hat.shape
    d_pix = d_pix[:kept]
    gain_sum = jnp.sum(d_pix * pix_hat[...], axis=-1, keepdims=True)
    bias_sum = jnp.sum(d_pix, axis=-1, keepdims=True)
    lane = lax.broadcasted_iota(jnp.int32, pix_sums_o.shape, 1)
    pix_sums_o[...] = jnp.where(lane == 0, gain_sum, jnp.where(lane == 1, bias_sum, 0.0))
    shard = lax.axis_index("fsdp")
    for target in range(pack.fsdp):
        slot = lax.rem(shard + pack.fsdp - target, pack.fsdp)
        last = min(used, (target + 1) * share)
        piece = d_pix[:, target * share : last]
        if last < (target + 1) * share:
            piece = jnp.concatenate([piece, jnp.zeros((kept, (target + 1) * share - last), F32)], axis=1)
        d_pix_o[slot] = piece
    d_query_pix = mm(d_scores, pix[...]).astype(BF)
    d_enc_q = mm_t(d_query_pix, kv[:, :padded]).astype(BF)
    hat, inverse = norm_parts(latents[...].astype(F32))
    in_low_s[...] = (hat * small(0) + small(2)).astype(BF)
    d_normed = mm_t(d_enc_q, pack.ready(scratch[2], sems.at[2]))
    d_latents_o[...] = grad_enc + norm_back(hat, inverse, small(0), d_normed)
    order = [column_sum(d_normed * hat), enc_sums[2:3], column_sum(d_normed), enc_sums[3:4], enc_sums[4:5], enc_sums[5:6]]
    order += [enc_sums[0:1], lat_sums[0:1], enc_sums[1:2], lat_sums[1:2], lat_sums[2:3], lat_sums[3:4]]
    sums = jnp.concatenate(order + [jnp.zeros((16 - len(order), pack.width), F32)], axis=0)
    high = sums.astype(BF)
    high_s[...] = high
    low_s[...] = (sums - high.astype(F32)).astype(BF)
    shape = (16, half - padded)
    eye = lax.broadcasted_iota(jnp.int32, shape, 0) == lax.broadcasted_iota(jnp.int32, shape, 1)
    eye = eye.astype(F32).astype(BF)
    blocks = []
    for left, high_c, right, low_c in zip(*(pack.columns(r) for r in (enc_q, high_s, d_mixed_s, low_s))):
        columns = [tm(left, d_query_pix), tm(high_c, eye), tm(right, mixed_pix[...]), tm(low_c, eye)]
        blocks.append(jnp.concatenate(columns, axis=1))
    pack.put(grads_o, 0, blocks)
    pack.put_product(grads_o, 1, in_low_s, d_enc_q)
    pack.put_product(grads_o, 2, mixed, grad_low)


def pad_lanes(values, width):
    return jnp.pad(values, [(0, 0)] * (values.ndim - 1) + [(0, width - values.shape[-1])])


def body(
    sizes,
    latents,
    pixels,
    lengths,
    pix_gain,
    pix_bias,
    pix_kv,
    enc_query,
    enc_out,
    enc_mlp,
    enc_gains,
    enc_biases,
    lat_qkv,
    lat_out,
    lat_mlp,
    lat_gains,
    lat_biases,
    cotangent,
):
    dp_size, fsdp_size = sizes
    devices = dp_size * fsdp_size
    my_fsdp = lax.axis_index("fsdp")
    me = lax.axis_index("dp") * fsdp_size + my_fsdp
    images, lat_rows, width = latents.shape
    rows = images * lat_rows
    pix_rows, features = pixels.shape
    padded = -(-features // LANES) * LANES
    own = width // devices

    _, _, far = bits_of(sizes)
    steps = range(1, len(far))
    half = width // 2

    small = jnp.concatenate([enc_gains, enc_biases, lat_gains, lat_biases], axis=0)
    n_small = small.shape[0]
    place_pix, place_small = jnp.eye(features, padded, dtype=BF), jnp.eye(n_small, half - padded, dtype=BF)
    kv_t = jnp.concatenate(
        [tm(pix_kv[0], place_pix), tm(small, place_small), pad_lanes(tm(pix_kv[1], place_pix), half)], axis=1
    ).astype(BF)
    enc_parts = gather_fsdp(jnp.concatenate([enc_mlp[0], enc_mlp[1], enc_query, enc_out, kv_t], axis=0), sizes)
    gain_f = pix_gain.astype(F32)
    pix_hat, pix_inverse = norm_parts(pixels.astype(F32))
    pix_low = pad_lanes((pix_hat * gain_f + pix_bias.astype(F32)).astype(BF), padded)[:USED]
    pix_hat_t = jnp.pad(pix_hat[:USED].T, ((0, -features % 8), (0, 0)))
    enc_parts, pix_low, pix_hat, pix_hat_t, pix_inverse, lat_qkv = seal(
        enc_parts, pix_low, pix_hat, pix_hat_t, pix_inverse, lat_qkv
    )

    enc_groups = far_step([v[None] for v in halves_of(order_fsdp(enc_parts, sizes, me))], 0, sizes, me)
    qkv_parts = gather_fsdp(lat_qkv.reshape(3 * own, width), sizes)
    enc_groups, qkv_parts, lat_out, lat_mlp = seal(enc_groups, qkv_parts, lat_out, lat_mlp)

    for place in steps:
        enc_groups = far_step(enc_groups, place, sizes, me)
    other_parts = gather_fsdp(jnp.concatenate([lat_out, lat_mlp[0], lat_mlp[1]], axis=0), sizes)
    qkv_groups = [v[None] for v in halves_of(order_fsdp(qkv_parts, sizes, me))]
    enc_groups, qkv_groups, other_parts = seal(enc_groups, qkv_groups, other_parts)

    enc_got = core_swap(enc_groups, sizes)
    qkv_groups = far_step(qkv_groups, 0, sizes, me)
    other_groups = [v[None] for v in halves_of(order_fsdp(other_parts, sizes, me))]
    enc_groups, enc_got, qkv_groups, other_groups = seal(enc_groups, enc_got, qkv_groups, other_groups)

    pack = Pack(sizes, own, width)
    for place in steps:
        qkv_groups = far_step(qkv_groups, place, sizes, me)
    enc_sources = sources_of(enc_groups, enc_got, 5, sizes, me)
    n_gain, n_bias = enc_gains.shape[0], enc_biases.shape[0]
    wide, dma = jax.ShapeDtypeStruct, pltpu.SemaphoreType.DMA

    small_all, enc_q, query_pix, probs, mixed_pix, enc_mixed, enc_resid, enc_pre, enc_act, first_out, lat_low = kernel_call(
        partial(encoder_kernel, pack, len(enc_sources), padded, lat_rows),
        "encoder",
        [latents.reshape(rows, width), pix_low],
        enc_sources,
        [wide((16, width), F32), wide((rows, width), BF), wide((rows, padded), BF), wide((rows, USED), F32)]
        + [wide((rows, padded), BF), wide((rows, width), BF), wide((rows, width), F32), wide((rows, width), F32)]
        + [wide((rows, width), BF), wide((rows, width), F32), wide((rows, width), BF)],
        [pack.scratch()] * 5 + [dma((5,))],
        36,
        36,
        scalars=[lengths],
    )
    lat_low, qkv_groups, other_groups = seal(lat_low, qkv_groups, other_groups)

    shards = []
    for image in range(images):
        part = lat_low[image * lat_rows : (image + 1) * lat_rows]
        shards += [slot_shift(part, fsdp_size, j) for j in range(1, fsdp_size)]
        if image == 0:
            qkv_got = core_swap(qkv_groups, sizes)
            qkv_got, other_groups = seal(qkv_got, other_groups)
        if image < len(far):
            other_groups = far_step(other_groups, image, sizes, me)
        lat_low, shards, qkv_got, other_groups = seal(lat_low, shards, qkv_got, other_groups)

    for place in range(images, len(far)):
        other_groups = far_step(other_groups, place, sizes, me)
    other_got = core_swap(other_groups, sizes)
    qkv_sources = sources_of(qkv_groups, qkv_got, 3, sizes, me)
    every = wide((fsdp_size, rows, width), BF)
    every_flat = pltpu.VMEM((fsdp_size * rows, width), BF)
    lat_q, lat_k, lat_v, lat_mixed = kernel_call(
        partial(attention_kernel, pack, len(qkv_sources), len(shards), lat_rows),
        "attention",
        [lat_low] + list(shards),
        qkv_sources,
        [wide((rows, width), BF), every, every, wide((rows, width), BF)],
        [pack.scratch()] * 3 + [every_flat, dma((3,))],
        32,
        40,
    )
    other_sources = sources_of(other_groups, other_got, 3, sizes, me)
    result, grad_mid, d_mixed, lat_sums, *grads_m = kernel_call(
        partial(latent_kernel, pack, len(other_sources)),
        "latent",
        [lat_mixed, first_out, cotangent.reshape(rows, width), small_all],
        other_sources,
        [wide((rows, width), BF), wide((rows, width), F32), wide((rows, width), BF), wide((8, width), F32)] + pack.grads(3),
        [pack.scratch()] * 3 + [pltpu.VMEM((rows, width), BF)] * 2 + [dma((3,))],
        36,
        36,
    )

    grads_m = core_terms(grads_m, sizes, me)
    slot, slots, *grads_q = kernel_call(
        partial(attention_back_kernel, pack, len(qkv_sources), len(shards), lat_rows),
        "attention_back",
        [lat_q, lat_k, lat_v, d_mixed, lat_low] + list(shards),
        qkv_sources,
        [wide((rows, width), F32), wide((fsdp_size - 1, rows, width), BF)] + pack.grads(3),
        [pack.scratch()] * 3
        + [every_flat, pltpu.VMEM((rows, width), BF)]
        + [pltpu.VMEM(every.shape, BF)] * 2
        + [dma((3,))],
        46,
        72,
    )
    slot, slots, grads_q = seal(slot, slots, grads_q)

    received = []
    for image in range(images):
        part = slots[:, image * lat_rows : (image + 1) * lat_rows]
        received += [slot_shift(part[j - 1], fsdp_size, fsdp_size - j) for j in range(1, fsdp_size)]
        if image < len(far):
            grads_m = far_pair(grads_m, image, sizes, me)
        slots, received, grads_m = seal(slots, received, grads_m)
    for place in range(images, len(far)):
        grads_m = far_pair(grads_m, place, sizes, me)
    l_other_grads = finish_sum(grads_m, sizes, my_fsdp)
    grads_q = core_terms(grads_q, sizes, me)
    grad_enc, enc_sums, *grads_e = kernel_call(
        partial(encoder_back_kernel, pack, len(enc_sources), len(received), images),
        "encoder_back",
        [slot, grad_mid, first_out, enc_resid, enc_pre, enc_act, small_all] + list(received),
        enc_sources,
        [wide((rows, width), F32), wide((8, width), F32)] + pack.grads(2),
        [pack.scratch()] * 2 + [pltpu.VMEM((rows, width), BF), dma((2,))],
        34,
        36,
    )
    grad_enc, grads_e, grads_q = seal(grad_enc, grads_e, grads_q)

    grads_q = far_pair(grads_q, 0, sizes, me)
    share = pix_rows // fsdp_size
    kept = pix_hat_t.shape[0]
    d_latents, pieces, d_pix_sums, *grads_f = kernel_call(
        partial(cross_back_kernel, pack, len(enc_sources), padded, share),
        "cross_back",
        [grad_enc, latents.reshape(rows, width), enc_mixed, mixed_pix, probs, pix_low, query_pix, enc_q, small_all]
        + [lat_sums, enc_sums, pix_hat_t],
        enc_sources,
        [wide((rows, width), F32), wide((fsdp_size, kept, share), F32), wide((kept, LANES), F32)] + pack.grads(3),
        [pack.scratch()] * 3
        + [pltpu.VMEM((rows, width), BF)] * 2
        + [pltpu.VMEM((16, width), BF)] * 2
        + [dma((3,))],
        44,
        50,
    )
    pieces, grads_f, d_pix_sums, grads_q = seal(pieces, grads_f, d_pix_sums, grads_q)

    low_bits, core, _ = bits_of(sizes)
    grads_e = core_terms([jnp.concatenate(both, axis=-3) for both in zip(grads_e, grads_f)], sizes, me)
    for place in steps:
        grads_q = far_pair(grads_q, place, sizes, me)
    d_pix_sums = total_over(d_pix_sums[:features, :2].T, [core], sizes)
    pieces, grads_e, grads_q, d_pix_sums = seal(pieces, grads_e, grads_q, d_pix_sums)

    d_pix_own = pieces[0]
    for j in range(1, fsdp_size):
        d_pix_own = d_pix_own + slot_shift(pieces[j].astype(BF), fsdp_size, fsdp_size - j).astype(F32)
    grads_e = far_pair(grads_e, 0, sizes, me)
    d_pix_own, grads_e, grads_q, d_pix_sums = seal(d_pix_own, grads_e, grads_q, d_pix_sums)

    l_qkv_grads = finish_sum(grads_q, sizes, my_fsdp)
    for place in steps:
        grads_e = far_pair(grads_e, place, sizes, me)
    l_qkv_grads, grads_e, d_pix_sums = seal(l_qkv_grads, grads_e, d_pix_sums)
    d_pix_sums = total_over(d_pix_sums, far + low_bits, sizes)
    enc_grads = finish_sum(grads_e, sizes, my_fsdp)
    hat_own = lax.dynamic_slice_in_dim(pix_hat, my_fsdp * share, share, 0)
    inverse_own = lax.dynamic_slice_in_dim(pix_inverse, my_fsdp * share, share, 0)
    d_pixels = norm_back(hat_own, inverse_own, gain_f, d_pix_own[:features].T)
    kv_own = enc_grads[2]
    d_pix_kv = jnp.stack([kv_own[:, :features].T, kv_own[:, width // 2 : width // 2 + features].T])
    start = width // 2 + padded
    small_own = (kv_own[:, padded : padded + n_small] + kv_own[:, start : start + n_small]).T
    return (
        result.reshape(latents.shape),
        d_latents.reshape(latents.shape),
        d_pixels,
        d_pix_sums[0],
        d_pix_sums[1],
        d_pix_kv,
        enc_grads[3],
        enc_grads[4],
        enc_grads[:2],
        small_own[:n_gain],
        small_own[n_gain : n_gain + n_bias],
        l_qkv_grads,
        l_other_grads[2],
        l_other_grads[:2],
        small_own[n_gain + n_bias : 2 * n_gain + n_bias],
        small_own[2 * n_gain + n_bias :],
    )


def solution(mesh):
    split, rows, columns = P("dp", "fsdp", None), P(AXES, None), P(None, AXES)
    middle = P(None, AXES, None)
    weights = (P(None, None, AXES), rows, rows, middle, columns, columns, middle, rows, middle, columns, columns)
    return jax.shard_map(
        partial(body, (mesh.shape["dp"], mesh.shape["fsdp"])),
        mesh=mesh,
        in_specs=(split, P("dp", None), P("dp", None), P(), P()) + weights + (split,),
        out_specs=(split, split, rows, P(), P()) + weights,
        check_vma=False,
    )
```

time: 644 us -> 471 us (0.73)
  waiting for transfers between devices: 368 us -> 205 us
  matrix products: 71 us -> 2.78 us
  starting transfers between devices: 29.5 us -> 95.9 us
  Pallas kernels: 20.2 us -> 64.4 us
  local copies, waits for them, and re-layouts: 82.9 us -> 65.4 us
  other arithmetic: 46.6 us -> 29.5 us
  between operations: 16 us -> 2.55 us
    all_gather x2 -> x0, waiting for transfers between devices: 192 us -> none  [the longest x1 109 us: body(): lat_all = lax.all_gather(lat_pack, AXES, axis=0, tiled=False)]
    dot_general x42 -> x3, matrix products: 71 us -> 2.78 us  [dot(): lax.dot_general(left, right, ((dims[0], dims[1]), ((), ())), preferred_el...]
    ppermute x0 -> x15, waiting for transfers between devices: none -> 60.8 us  [slot_shift(): lax.ppermute(values, 'fsdp', [(i, (i + j) % size) for i in range(size)])]
    pallas_call x2 -> x6, Pallas kernels: 20.2 us -> 64.4 us  [kernel_call(): pl.pallas_call(kernel, in_specs=specs, out_specs=[pl.BlockSpec(memory_spa...]
    ppermute x28 -> x56, starting transfers between devices: 29.4 us -> 65.2 us  [xor_permute(): return lax.ppermute(values, AXES, [(i, i ^ step) for i in range(total)])]
    ppermute x28 -> x56, waiting for transfers between devices: 176 us -> 144 us  [xor_permute(): return lax.ppermute(values, AXES, [(i, i ^ step) for i in range(total)])]
    ppermute x0 -> x15, starting transfers between devices: none -> 30.6 us  [slot_shift(): lax.ppermute(values, 'fsdp', [(i, (i + j) % size) for i in range(size)])]
    convert_element_type x17 -> x12, other arithmetic: 24 us -> 2.99 us  [far_terms(): send = sum_of([half(term, 1 - mine) for term in terms]).astype(BF)]
  transfers between devices with their start and end apart: 30 -> 71, of which waited for: 15 -> 39; matrix products, arithmetic and copies ran while one was open for 16% -> 10% of each run, Pallas kernels for 0% -> 11%
where the time goes in v3:
time: 471 us; the launch traced here: 465 us
  waiting for transfers between devices  205 us (44%)
  starting transfers between devices  95.9 us (20%)
  local copies, waits for them, and re-layouts  65.4 us (14%)
  Pallas kernels  64.4 us (14%)
  other arithmetic  29.5 us (6%)
    ppermute x56, waiting for transfers between devices, xor_permute(): return lax.ppermute(values, AXES, [(i, i ^ step) for i in range(total)])  144 us
    ppermute x56, starting transfers between devices, xor_permute(): return lax.ppermute(values, AXES, [(i, i ^ step) for i in range(total)])  65.2 us
    pallas_call x6, Pallas kernels, kernel_call(): pl.pallas_call(kernel, in_specs=specs, out_specs=[pl.BlockSpec(memory_spa...  64.4 us
    ppermute x15, waiting for transfers between devices, slot_shift(): lax.ppermute(values, 'fsdp', [(i, (i + j) % size) for i in range(size)])  60.8 us
    unnamed x147, local copies, waits for them, and re-layouts  35.6 us
    ppermute x15, starting transfers between devices, slot_shift(): lax.ppermute(values, 'fsdp', [(i, (i + j) % size) for i in range(size)])  30.6 us
    slice x6, local copies, waits for them, and re-layouts, halves_of(): return [values[..., :half], values[..., half:]]  10.8 us
  transfers between devices with their start and end apart: 71, of which 39 were waited for; matrix products, arithmetic and copies ran while one was open for 10% of the time, Pallas kernels for 11%

profile of v3, /device:TPU:0, one launch (start us, length us, event | category | flops | bytes accessed | tf_op | source)
XLA Modules:
  0.0 465.4 jit_solution(13431728680003826425)
XLA Ops:
  6.8 5.1 %collective-permute-start.2 = (bf16[160,1024]{1,0:T(8,128)(2,1)S(1)}, bf16[160,1024]{1,0:T(8,128)(2,1)}, u32[]{:S(2)}, u32[]{:S(2)}) collective-permute-start(bf16[160,1024]{1,0:T(8,128)(2,1)S(1)} %fusion.47), channel_id=1, source_target_pairs={{0,3},{1,2},{2,1},{3,0},{4,7},{5,6},{6,5},{7,4},{8,11},{9,10},{10,... | collective-permute-start | bytes 983048 | tf_op jit(solution)/shard_map/ppermute | solution.py:66
  20.7 19.2 %collective-permute-done.1 = bf16[160,1024]{1,0:T(8,128)(2,1)} collective-permute-done((bf16[160,1024]{1,0:T(8,128)(2,1)S(1)}, bf16[160,1024]{1,0:T(8,128)(2,1)}, u32[]{:S(2)}, u32[]{:S(2)}) %collective-permute-start.1) | collective-permute-done | bytes 327712 | tf_op jit(solution)/shard_map/ppermute | solution.py:66
  44.7 2.5 collective-permute-start.7
  49.1 8.4 %collective-permute-done.4 = bf16[1,4,160,512]{3,2,1,0:T(8,128)(2,1)S(1)} collective-permute-done((bf16[1,4,160,512]{3,2,1,0:T(8,128)(2,1)S(1)}, bf16[1,4,160,512]{3,2,1,0:T(8,128)(2,1)S(1)}, u32[]{:S(2)}, u32[]{:S(2)}) %collective-permute-start.4) | collective-permute-done | bytes 655392 | tf_op jit(solution)/shard_map/ppermute | solution.py:66
  64.8 2.7 collective-permute-start.10
  67.8 23.5 %collective-permute-done.8 = bf16[2,4,160,512]{3,2,1,0:T(8,128)(2,1)S(1)} collective-permute-done((bf16[2,4,160,512]{3,2,1,0:T(8,128)(2,1)S(1)}, bf16[2,4,160,512]{3,2,1,0:T(8,128)(2,1)S(1)}, u32[]{:S(2)}, u32[]{:S(2)}) %collective-permute-start.8) | collective-permute-done | bytes 1310752 | tf_op jit(solution)/shard_map/ppermute | solution.py:66
  96.2 7.9 %collective-permute-done.15 = bf16[1,4,96,512]{3,2,1,0:T(8,128)(2,1)S(1)} collective-permute-done((bf16[1,4,96,512]{3,2,1,0:T(8,128)(2,1)S(1)}, bf16[1,4,96,512]{3,2,1,0:T(8,128)(2,1)S(1)}, u32[]{:S(2)}, u32[]{:S(2)}) %collective-permute-start.15) | collective-permute-done | bytes 393248 | tf_op jit(solution)/shard_map/ppermute | solution.py:66
  111.4 2.7 copy.44.refs_2_.refs_5_
  120.0 8.4 %encoder.1 = (f32[16,1024]{1,0:T(8,128)S(1)}, bf16[256,1024]{1,0:T(8,128)(2,1)S(1)}, bf16[256,384]{1,0:T(8,128)(2,1)S(1)}, f32[256,1792]{1,0:T(8,128)S(1)}, bf16...) custom-call(s32[1,2]{1,0:T(1,128)S(1)} %copy-done.46, ...), custom_call_target="tpu_custom_call" | custom-call | flops 1073741824 | bytes 37748736 | tf_op jit(solution)/shard_map/encoder/pallas_call | solution.py:256
  132.0 2.6 select_bitcast_fusion.9
  137.7 2.9 collective-permute-done.22.refs_8_.refs_12_
  144.7 2.3 collective-permute-start.21
  147.7 6.3 %collective-permute-done.24 = bf16[1,4,96,512]{3,2,1,0:T(8,128)(2,1)S(1)} collective-permute-done((bf16[1,4,96,512]{3,2,1,0:T(8,128)(2,1)S(1)}, bf16[1,4,96,512]{3,2,1,0:T(8,128)(2,1)S(1)}, u32[]{:S(2)}, u32[]{:S(2)}) %collective-permute-start.24) | collective-permute-done | bytes 393248 | tf_op jit(solution)/shard_map/ppermute | solution.py:66
  155.3 13.0 %collective-permute-done.20.refs_2_.refs_6_ = bf16[128,1024]{1,0:T(8,128)(2,1)S(1)} collective-permute-done((bf16[128,1024]{1,0:T(8,128)(2,1)S(1)}, bf16[128,1024]{1,0:T(8,128)(2,1)S(1)}, u32[]{:S(2)}, u32[]{:S(2)}) %collective-permute-start.20) | collective-permute-done | bytes 262176 | tf_op jit(solution)/shard_map/ppermute | solution.py:84
  170.6 11.4 %collective-permute-start.27 = (bf16[128,1024]{1,0:T(8,128)(2,1)S(1)}, bf16[128,1024]{1,0:T(8,128)(2,1)S(1)}, u32[]{:S(2)}, u32[]{:S(2)}) collective-permute-start(bf16[128,1024]{1,0:T(8,128)(2,1)S(1)} %slice.194), channel_id=1, source_target_pairs={{0,2},{1,3},{2,0},{3,1},{4,6},{5,7},{6,4},{7,5},{8,10},{9,11},{10,... | collective-permute-start | bytes 786440 | tf_op jit(solution)/shard_map/ppermute | solution.py:84
  184.0 2.5 collective-permute-done.29
  188.3 7.8 %collective-permute-done.27.refs_5_.refs_9_ = bf16[128,1024]{1,0:T(8,128)(2,1)S(1)} collective-permute-done((bf16[128,1024]{1,0:T(8,128)(2,1)S(1)}, bf16[128,1024]{1,0:T(8,128)(2,1)S(1)}, u32[]{:S(2)}, u32[]{:S(2)}) %collective-permute-start.27) | collective-permute-done | bytes 262176 | tf_op jit(solution)/shard_map/ppermute | solution.py:84
  196.6 10.2 %attention.1 = (bf16[256,1024]{1,0:T(8,128)(2,1)S(1)}, bf16[4,256,1024]{2,1,0:T(8,128)(2,1)S(1)}, bf16[4,256,1024]{2,1,0:T(8,128)(2,1)S(1)}, bf16[256,1024]{1,0:T(8,128)(2,1)S(1)}) custom-call(bf16[256,1024]{1,0:T(8,128)(2,1)S(1)} %get-tuple-element.240.refs_0_.refs_4_, bf16[128,1024]{1,0:T(8,128)(2,1)S(1)} %collective-permute-done.19.refs_1_.refs_5_, ...), custom_call_target="tpu_custom_call" | custom-call | flops 1073741824 | bytes 41943040 | tf_op jit(solution)/shard_map/attention/pallas_call | solution.py:256
  212.0 8.7 %latent.1 = (bf16[256,1024]{1,0:T(8,128)(2,1)}, f32[256,1024]{1,0:T(8,128)S(1)}, bf16[256,1024]{1,0:T(8,128)(2,1)S(1)}, f32[8,1024]{1,0:T(8,128)S(1)}, bf16[4,3,...) custom-call(bf16[256,1024]{1,0:T(8,128)(2,1)S(1)} %get-tuple-element.249.refs_0_, ...), custom_call_target="tpu_custom_call" | custom-call | flops 1073741824 | bytes 37748736 | tf_op jit(solution)/shard_map/latent/pallas_call | solution.py:256
  223.4 21.1 %attention_back.1 = (f32[256,1024]{1,0:T(8,128)S(1)}, bf16[3,256,1024]{2,1,0:T(8,128)(2,1)S(1)}, bf16[4,3,128,1024]{3,2,1,0:T(8,128)(2,1)}, bf16[4,3,128,1024]{3,2,1,0:T(8,128)(2,1)}) custom-call(bf16[256,1024]{1,0:T(8,128)(2,1)S(1)} %get-tuple-element.255.refs_0_, bf16[4,256,1024]{2,1,0:T(8,128)(2,1)} %copy-done.23, bf16[4,256,1024]{2,1,0:T(8,128)(2,1)} %copy-done.24, ...), custom_call_target="tpu_custom_call" | custom-call | flops 1073741824 | bytes 75497472 | tf_op jit(solution)/shard_map/attention_back/pallas_call | solution.py:256
  248.4 2.3 fusion.65
  256.7 3.8 collective-permute-start.33
  260.5 2.3 fusion.64
  262.8 6.9 %collective-permute-done.34.refs_8_ = bf16[128,1024]{1,0:T(8,128)(2,1)S(1)} collective-permute-done((bf16[128,1024]{1,0:T(8,128)(2,1)S(1)}, bf16[128,1024]{1,0:T(8,128)(2,1)S(1)}, u32[]{:S(2)}, u32[]{:S(2)}) %collective-permute-start.34) | collective-permute-done | bytes 262176 | tf_op jit(solution)/shard_map/ppermute | solution.py:84
  271.2 2.5 collective-permute-done.37
  279.2 3.7 collective-permute-start.41
  287.7 2.7 collective-permute-done.41.refs_12_
  290.4 8.8 %collective-permute-done.40.refs_11_ = bf16[128,1024]{1,0:T(8,128)(2,1)S(1)} collective-permute-done((bf16[128,1024]{1,0:T(8,128)(2,1)S(1)}, bf16[128,1024]{1,0:T(8,128)(2,1)S(1)}, u32[]{:S(2)}, u32[]{:S(2)}) %collective-permute-start.40) | collective-permute-done | bytes 262176 | tf_op jit(solution)/shard_map/ppermute | solution.py:84
  300.2 5.3 %encoder_back.1 = (f32[256,1024]{1,0:T(8,128)S(1)}, f32[8,1024]{1,0:T(8,128)S(1)}, bf16[4,2,128,1024]{3,2,1,0:T(8,128)(2,1)S(1)}, bf16[4,2,128,1024]{3,2,1,0:T(8,128)(2,1)S(1)}) custom-call(f32[256,1024]{1,0:T(8,128)S(1)} %copy-done.38, f32[256,1024]{1,0:T(8,128)S(1)} %copy-done.36, f32[256,1024]{1,0:T(8,128)S(1)} %copy-done.14, f32[256,1024]{1,0:T(8,128)S(1)} %copy-done.32, ...), custom_call_target="tpu_custom_call" | custom-call | flops 1073741824 | bytes 37748736 | tf_op jit(solution)/shard_map/encoder_back/pallas_call | solution.py:256
  311.3 10.7 %cross_back.1 = (f32[256,1024]{1,0:T(8,128)}, f32[4,264,512]{2,1,0:T(8,128)}, f32[264,128]{1,0:T(8,128)S(1)}, bf16[4,3,128,1024]{3,2,1,0:T(8,128)(2,1)}, bf16[4,3,128,1024]{3,2,1,0:T(8,128)(2,1)}) custom-call(f32[256,1024]{1,0:T(8,128)S(1)} %get-tuple-element.288.refs_0_, bf16[256,1024]{1,0:T(8,128)(2,1)S(1)} %bitcast.521, bf16[256,1024]{1,0:T(8,128)(2,1)S(1)} %copy-done.41, ...), custom_call_target="tpu_custom_call" | custom-call | flops 1073741824 | bytes 52428800 | tf_op jit(solution)/shard_map/cross_back/pallas_call | solution.py:256
  322.3 5.6 %collective-permute-done.46 = bf16[2,3,128,512]{3,2,1,0:T(8,128)(2,1)S(1)} collective-permute-done((bf16[2,3,128,512]{3,2,1,0:T(8,128)(2,1)S(1)}, bf16[2,3,128,512]{3,2,1,0:T(8,128)(2,1)S(1)}, u32[]{:S(2)}, u32[]{:S(2)}) %collective-permute-start.46) | collective-permute-done | bytes 786464 | tf_op jit(solution)/shard_map/ppermute | solution.py:66
  329.0 3.0 pad_maximum_fusion
  335.0 4.4 collective-permute-start.70
  339.6 3.4 collective-permute-start.69
  345.0 12.5 %collective-permute-done.69 = bf16[3,32,1024]{2,1,0:T(8,128)(2,1)S(1)} collective-permute-done((bf16[3,32,1024]{2,1,0:T(8,128)(2,1)S(1)}, bf16[3,32,1024]{2,1,0:T(8,128)(2,1)S(1)}, u32[]{:S(2)}, u32[]{:S(2)}) %collective-permute-start.69) | collective-permute-done | bytes 196640 | tf_op jit(solution)/shard_map/ppermute | solution.py:66
  364.0 2.9 fusion.62
  366.9 3.3 collective-permute-done.49
  375.6 3.6 collective-permute-start.51
  380.4 5.8 %collective-permute-done.51 = bf16[264,512]{1,0:T(8,128)(2,1)S(1)} collective-permute-done((bf16[264,512]{1,0:T(8,128)(2,1)S(1)}, bf16[264,512]{1,0:T(8,128)(2,1)S(1)}, u32[]{:S(2)}, u32[]{:S(2)}) %collective-permute-start.51) | collective-permute-done | bytes 270368 | tf_op jit(solution)/shard_map/ppermute | solution.py:84
  386.2 6.4 %collective-permute-done.53 = bf16[264,512]{1,0:T(8,128)(2,1)S(1)} collective-permute-done((bf16[264,512]{1,0:T(8,128)(2,1)S(1)}, bf16[264,512]{1,0:T(8,128)(2,1)S(1)}, u32[]{:S(2)}, u32[]{:S(2)}) %collective-permute-start.53) | collective-permute-done | bytes 270368 | tf_op jit(solution)/shard_map/ppermute | solution.py:84
  392.5 7.9 %collective-permute-done.52 = bf16[264,512]{1,0:T(8,128)(2,1)S(1)} collective-permute-done((bf16[264,512]{1,0:T(8,128)(2,1)S(1)}, bf16[264,512]{1,0:T(8,128)(2,1)S(1)}, u32[]{:S(2)}, u32[]{:S(2)}) %collective-permute-start.52) | collective-permute-done | bytes 270368 | tf_op jit(solution)/shard_map/ppermute | solution.py:84
  404.5 3.6 collective-permute-start.58
  411.4 2.8 collective-permute-done.58
  414.2 8.1 %collective-permute-done.57 = bf16[3,32,1024]{2,1,0:T(8,128)(2,1)S(1)} collective-permute-done((bf16[3,32,1024]{2,1,0:T(8,128)(2,1)S(1)}, bf16[3,32,1024]{2,1,0:T(8,128)(2,1)S(1)}, u32[]{:S(2)}, u32[]{:S(2)}) %collective-permute-start.57) | collective-permute-done | bytes 196640 | tf_op jit(solution)/shard_map/ppermute | solution.py:66
  430.3 2.6 collective-permute-start.66
  436.9 8.7 %collective-permute-done.63 = f32[2,261]{0,1:T(8,128)S(1)} collective-permute-done((f32[2,261]{0,1:T(8,128)S(1)}, f32[2,261]{0,1:T(8,128)S(1)}, u32[]{:S(2)}, u32[]{:S(2)}) %collective-permute-start.63) | collective-permute-done | bytes 2120 | tf_op jit(solution)/shard_map/ppermute | solution.py:66
  445.6 3.3 collective-permute-start.64
  449.8 9.3 %collective-permute-done.64 = f32[2,261]{0,1:T(8,128)S(1)} collective-permute-done((f32[2,261]{0,1:T(8,128)S(1)}, f32[2,261]{0,1:T(8,128)S(1)}, u32[]{:S(2)}, u32[]{:S(2)}) %collective-permute-start.64) | collective-permute-done | bytes 2120 | tf_op jit(solution)/shard_map/ppermute | solution.py:66
  (398 shorter events, 147.5 us)
Async XLA Ops:
  6.8 13.9 %collective-permute-start.2 = (bf16[160,1024]{1,0:T(8,128)(2,1)S(1)}, bf16[160,1024]{1,0:T(8,128)(2,1)}, u32[]{:S(2)}, u32[]{:S(2)}) collective-permute-start(bf16[160,1024]{1,0:T(8,128)(2,1)S(1)} %fusion.47), channel_id=1, source_target_pairs={{0,3},{1,2},{2,1},{3,0},{4,7},{5,6},{6,5},{7,4},{8,11},{9,10},{10,... | collective-permute-start | bytes 983048 | tf_op jit(solution)/shard_map/ppermute | solution.py:66
  12.0 28.0 %collective-permute-start.1 = (bf16[160,1024]{1,0:T(8,128)(2,1)S(1)}, bf16[160,1024]{1,0:T(8,128)(2,1)}, u32[]{:S(2)}, u32[]{:S(2)}) collective-permute-start(bf16[160,1024]{1,0:T(8,128)(2,1)S(1)} %fusion.47), channel_id=1, source_target_pairs={{0,2},{1,3},{2,0},{3,1},{4,6},{5,7},{6,4},{7,5},{8,10},{9,11},{10,... | collective-permute-start | bytes 983048 | tf_op jit(solution)/shard_map/ppermute | solution.py:66
  12.0 28.0 %collective-permute-start = (bf16[160,1024]{1,0:T(8,128)(2,1)S(1)}, bf16[160,1024]{1,0:T(8,128)(2,1)}, u32[]{:S(2)}, u32[]{:S(2)}) collective-permute-start(bf16[160,1024]{1,0:T(8,128)(2,1)S(1)} %fusion.47), channel_id=1, source_target_pairs={{0,1},{1,0},{2,3},{3,2},{4,5},{5,4},{6,7},{7,6},{8,9},{9,8},{10,11... | collective-permute-start | bytes 983048 | tf_op jit(solution)/shard_map/ppermute | solution.py:66
  41.6 15.9 %collective-permute-start.4 = (bf16[1,4,160,512]{3,2,1,0:T(8,128)(2,1)S(1)}, bf16[1,4,160,512]{3,2,1,0:T(8,128)(2,1)S(1)}, u32[]{:S(2)}, u32[]{:S(2)}) collective-permute-start(bf16[1,4,160,512]{3,2,1,0:T(8,128)(2,1)S(1)} %get-tuple-element.459), channel_id=1, source_target_pairs={{0,16},{1,17},{2,18},{3,19},{4,20},{5,21},{6,22},{7,23},{8,24},{9,... | collective-permute-start | bytes 1966088 | tf_op jit(solution)/shard_map/ppermute | solution.py:66
  43.2 15.6 %collective-permute-start.3 = (bf16[1,4,160,512]{3,2,1,0:T(8,128)(2,1)S(1)}, bf16[1,4,160,512]{3,2,1,0:T(8,128)(2,1)}, u32[]{:S(2)}, u32[]{:S(2)}) collective-permute-start(bf16[1,4,160,512]{3,2,1,0:T(8,128)(2,1)S(1)} %get-tuple-element.460), channel_id=1, source_target_pairs={{0,8},{1,9},{2,10},{3,11},{4,12},{5,13},{6,14},{7,15},{8,0},{9,1},... | collective-permute-start | bytes 1966088 | tf_op jit(solution)/shard_map/ppermute | solution.py:66
  44.7 15.6 %collective-permute-start.7 = (bf16[96,1024]{1,0:T(8,128)(2,1)S(1)}, bf16[96,1024]{1,0:T(8,128)(2,1)S(1)}, u32[]{:S(2)}, u32[]{:S(2)}) collective-permute-start(bf16[96,1024]{1,0:T(8,128)(2,1)S(1)} %bitcast.583), channel_id=1, source_target_pairs={{0,3},{1,2},{2,1},{3,0},{4,7},{5,6},{6,5},{7,4},{8,11},{9,10},{10,... | collective-permute-start | bytes 589832 | tf_op jit(solution)/shard_map/ppermute | solution.py:66
  47.1 14.8 %collective-permute-start.6 = (bf16[96,1024]{1,0:T(8,128)(2,1)S(1)}, bf16[96,1024]{1,0:T(8,128)(2,1)S(1)}, u32[]{:S(2)}, u32[]{:S(2)}) collective-permute-start(bf16[96,1024]{1,0:T(8,128)(2,1)S(1)} %bitcast.584), channel_id=1, source_target_pairs={{0,2},{1,3},{2,0},{3,1},{4,6},{5,7},{6,4},{7,5},{8,10},{9,11},{10,... | collective-permute-start | bytes 589832 | tf_op jit(solution)/shard_map/ppermute | solution.py:66
  47.1 14.8 %collective-permute-start.5 = (bf16[96,1024]{1,0:T(8,128)(2,1)S(1)}, bf16[96,1024]{1,0:T(8,128)(2,1)S(1)}, u32[]{:S(2)}, u32[]{:S(2)}) collective-permute-start(bf16[96,1024]{1,0:T(8,128)(2,1)S(1)} %bitcast.585), channel_id=1, source_target_pairs={{0,1},{1,0},{2,3},{3,2},{4,5},{5,4},{6,7},{7,6},{8,9},{9,8},{10,11... | collective-permute-start | bytes 589832 | tf_op jit(solution)/shard_map/ppermute | solution.py:66
  62.0 29.3 %collective-permute-start.8 = (bf16[2,4,160,512]{3,2,1,0:T(8,128)(2,1)S(1)}, bf16[2,4,160,512]{3,2,1,0:T(8,128)(2,1)S(1)}, u32[]{:S(2)}, u32[]{:S(2)}) collective-permute-start(bf16[2,4,160,512]{3,2,1,0:T(8,128)(2,1)S(1)} %get-tuple-element.198), channel_id=1, source_target_pairs={{0,16},{1,17},{2,18},{3,19},{4,20},{5,21},{6,22},{7,23},{8,24},{9,... | collective-permute-start | bytes 3932168 | tf_op jit(solution)/shard_map/ppermute | solution.py:66
  62.5 29.0 %collective-permute-start.9 = (bf16[2,4,160,512]{3,2,1,0:T(8,128)(2,1)S(1)}, bf16[2,4,160,512]{3,2,1,0:T(8,128)(2,1)S(1)}, u32[]{:S(2)}, u32[]{:S(2)}) collective-permute-start(bf16[2,4,160,512]{3,2,1,0:T(8,128)(2,1)S(1)} %get-tuple-element.199), channel_id=1, source_target_pairs={{0,8},{1,9},{2,10},{3,11},{4,12},{5,13},{6,14},{7,15},{8,0},{9,1},... | collective-permute-start | bytes 3932168 | tf_op jit(solution)/shard_map/ppermute | solution.py:66
  63.1 29.3 %collective-permute-start.12 = (bf16[96,1024]{1,0:T(8,128)(2,1)S(1)}, bf16[96,1024]{1,0:T(8,128)(2,1)S(1)}, u32[]{:S(2)}, u32[]{:S(2)}) collective-permute-start(bf16[96,1024]{1,0:T(8,128)(2,1)S(1)} %pad_maximum_fusion.13), channel_id=1, source_target_pairs={{0,3},{1,2},{2,1},{3,0},{4,7},{5,6},{6,5},{7,4},{8,11},{9,10},{10,... | collective-permute-start | bytes 589832 | tf_op jit(solution)/shard_map/ppermute | solution.py:66
  64.8 27.6 %collective-permute-start.11 = (bf16[96,1024]{1,0:T(8,128)(2,1)S(1)}, bf16[96,1024]{1,0:T(8,128)(2,1)S(1)}, u32[]{:S(2)}, u32[]{:S(2)}) collective-permute-start(bf16[96,1024]{1,0:T(8,128)(2,1)S(1)} %pad_maximum_fusion.13), channel_id=1, source_target_pairs={{0,2},{1,3},{2,0},{3,1},{4,6},{5,7},{6,4},{7,5},{8,10},{9,11},{10,... | collective-permute-start | bytes 589832 | tf_op jit(solution)/shard_map/ppermute | solution.py:66
  64.8 27.6 %collective-permute-start.10 = (bf16[96,1024]{1,0:T(8,128)(2,1)S(1)}, bf16[96,1024]{1,0:T(8,128)(2,1)S(1)}, u32[]{:S(2)}, u32[]{:S(2)}) collective-permute-start(bf16[96,1024]{1,0:T(8,128)(2,1)S(1)} %pad_maximum_fusion.13), channel_id=1, source_target_pairs={{0,1},{1,0},{2,3},{3,2},{4,5},{5,4},{6,7},{7,6},{8,9},{9,8},{10,11... | collective-permute-start | bytes 589832 | tf_op jit(solution)/shard_map/ppermute | solution.py:66
  92.4 13.8 %collective-permute-start.13 = (bf16[4,4,160,512]{3,2,1,0:T(8,128)(2,1)S(1)}, bf16[4,4,160,512]{3,2,1,0:T(8,128)(2,1)S(1)}, u32[]{:S(2)}, u32[]{:S(2)}) collective-permute-start(bf16[4,4,160,512]{3,2,1,0:T(8,128)(2,1)S(1)} %bitcast.506), channel_id=1, source_target_pairs={{0,4},{1,5},{2,6},{3,7},{4,0},{5,1},{6,2},{7,3},{8,12},{9,13},{10,... | collective-permute-start | bytes 7864328 | tf_op jit(solution)/shard_map/ppermute | solution.py:66
  92.5 15.2 %collective-permute-start.14 = (bf16[4,4,160,512]{3,2,1,0:T(8,128)(2,1)S(1)}, bf16[4,4,160,512]{3,2,1,0:T(8,128)(2,1)S(1)}, u32[]{:S(2)}, u32[]{:S(2)}) collective-permute-start(bf16[4,4,160,512]{3,2,1,0:T(8,128)(2,1)S(1)} %bitcast.502), channel_id=1, source_target_pairs={{0,4},{1,5},{2,6},{3,7},{4,0},{5,1},{6,2},{7,3},{8,12},{9,13},{10,... | collective-permute-start | bytes 7864328 | tf_op jit(solution)/shard_map/ppermute | solution.py:66
  109.2 22.8 %collective-permute-start.18 = (bf16[2,4,96,512]{3,2,1,0:T(8,128)(2,1)}, bf16[2,4,96,512]{3,2,1,0:T(8,128)(2,1)}, u32[]{:S(2)}, u32[]{:S(2)}) collective-permute-start(bf16[2,4,96,512]{3,2,1,0:T(8,128)(2,1)} %maximum_bitcast_fusion.3), channel_id=1, source_target_pairs={{0,8},{1,9},{2,10},{3,11},{4,12},{5,13},{6,14},{7,15},{8,0},{9,1},... | collective-permute-start | bytes 2359304 | tf_op jit(solution)/shard_map/ppermute | solution.py:66
  110.0 24.9 %collective-permute-start.17 = (bf16[2,4,96,512]{3,2,1,0:T(8,128)(2,1)}, bf16[2,4,96,512]{3,2,1,0:T(8,128)(2,1)}, u32[]{:S(2)}, u32[]{:S(2)}) collective-permute-start(bf16[2,4,96,512]{3,2,1,0:T(8,128)(2,1)} %maximum_bitcast_fusion.2), channel_id=1, source_target_pairs={{0,16},{1,17},{2,18},{3,19},{4,20},{5,21},{6,22},{7,23},{8,24},{9,... | collective-permute-start | bytes 2359304 | tf_op jit(solution)/shard_map/ppermute | solution.py:66
  147.1 21.3 %collective-permute-start.20 = (bf16[128,1024]{1,0:T(8,128)(2,1)S(1)}, bf16[128,1024]{1,0:T(8,128)(2,1)S(1)}, u32[]{:S(2)}, u32[]{:S(2)}) collective-permute-start(bf16[128,1024]{1,0:T(8,128)(2,1)S(1)} %slice.193), channel_id=1, source_target_pairs={{0,2},{1,3},{2,0},{3,1},{4,6},{5,7},{6,4},{7,5},{8,10},{9,11},{10,... | collective-permute-start | bytes 786440 | tf_op jit(solution)/shard_map/ppermute | solution.py:84
  147.1 21.3 %collective-permute-start.19 = (bf16[128,1024]{1,0:T(8,128)(2,1)S(1)}, bf16[128,1024]{1,0:T(8,128)(2,1)S(1)}, u32[]{:S(2)}, u32[]{:S(2)}) collective-permute-start(bf16[128,1024]{1,0:T(8,128)(2,1)S(1)} %slice.193), channel_id=1, source_target_pairs={{0,1},{1,2},{2,3},{3,0},{4,5},{5,6},{6,7},{7,4},{8,9},{9,10},{10,1... | collective-permute-start | bytes 786440 | tf_op jit(solution)/shard_map/ppermute | solution.py:84
  168.3 18.1 %collective-permute-start.29 = (bf16[2,4,96,512]{3,2,1,0:T(8,128)(2,1)S(1)}, bf16[2,4,96,512]{3,2,1,0:T(8,128)(2,1)S(1)}, u32[]{:S(2)}, u32[]{:S(2)}) collective-permute-start(bf16[2,4,96,512]{3,2,1,0:T(8,128)(2,1)S(1)} %maximum_bitcast_fusion.4), channel_id=1, source_target_pairs={{0,16},{1,17},{2,18},{3,19},{4,20},{5,21},{6,22},{7,23},{8,24},{9,... | collective-permute-start | bytes 2359304 | tf_op jit(solution)/shard_map/ppermute | solution.py:66
  169.9 17.8 %collective-permute-start.30 = (bf16[2,4,96,512]{3,2,1,0:T(8,128)(2,1)S(1)}, bf16[2,4,96,512]{3,2,1,0:T(8,128)(2,1)S(1)}, u32[]{:S(2)}, u32[]{:S(2)}) collective-permute-start(bf16[2,4,96,512]{3,2,1,0:T(8,128)(2,1)S(1)} %maximum_bitcast_fusion.5), channel_id=1, source_target_pairs={{0,8},{1,9},{2,10},{3,11},{4,12},{5,13},{6,14},{7,15},{8,0},{9,1},... | collective-permute-start | bytes 2359304 | tf_op jit(solution)/shard_map/ppermute | solution.py:66
  170.6 17.7 %collective-permute-start.28 = (bf16[128,1024]{1,0:T(8,128)(2,1)S(1)}, bf16[128,1024]{1,0:T(8,128)(2,1)S(1)}, u32[]{:S(2)}, u32[]{:S(2)}) collective-permute-start(bf16[128,1024]{1,0:T(8,128)(2,1)S(1)} %slice.194), channel_id=1, source_target_pairs={{0,3},{1,0},{2,1},{3,2},{4,7},{5,4},{6,5},{7,6},{8,11},{9,8},{10,9... | collective-permute-start | bytes 786440 | tf_op jit(solution)/shard_map/ppermute | solution.py:84
  170.6 25.4 %collective-permute-start.27 = (bf16[128,1024]{1,0:T(8,128)(2,1)S(1)}, bf16[128,1024]{1,0:T(8,128)(2,1)S(1)}, u32[]{:S(2)}, u32[]{:S(2)}) collective-permute-start(bf16[128,1024]{1,0:T(8,128)(2,1)S(1)} %slice.194), channel_id=1, source_target_pairs={{0,2},{1,3},{2,0},{3,1},{4,6},{5,7},{6,4},{7,5},{8,10},{9,11},{10,... | collective-permute-start | bytes 786440 | tf_op jit(solution)/shard_map/ppermute | solution.py:84
  182.0 14.0 %collective-permute-start.26 = (bf16[128,1024]{1,0:T(8,128)(2,1)S(1)}, bf16[128,1024]{1,0:T(8,128)(2,1)S(1)}, u32[]{:S(2)}, u32[]{:S(2)}) collective-permute-start(bf16[128,1024]{1,0:T(8,128)(2,1)S(1)} %slice.194), channel_id=1, source_target_pairs={{0,1},{1,2},{2,3},{3,0},{4,5},{5,6},{6,7},{7,4},{8,9},{9,10},{10,1... | collective-permute-start | bytes 786440 | tf_op jit(solution)/shard_map/ppermute | solution.py:84
  223.4 28.3 %collective-permute-start.36 = (bf16[4,3,128,1024]{3,2,1,0:T(8,128)(2,1)}, bf16[4,3,128,1024]{3,2,1,0:T(8,128)(2,1)}, u32[]{:S(2)}, u32[]{:S(2)}) collective-permute-start(bf16[4,3,128,1024]{3,2,1,0:T(8,128)(2,1)} %get-tuple-element.266), channel_id=1, source_target_pairs={{0,4},{1,5},{2,6},{3,7},{4,0},{5,1},{6,2},{7,3},{8,12},{9,13},{10,... | collective-permute-start | bytes 9437192 | tf_op jit(solution)/shard_map/ppermute | solution.py:66
  248.3 14.5 %collective-permute-start.35 = (bf16[128,1024]{1,0:T(8,128)(2,1)S(1)}, bf16[128,1024]{1,0:T(8,128)(2,1)S(1)}, u32[]{:S(2)}, u32[]{:S(2)}) collective-permute-start(bf16[128,1024]{1,0:T(8,128)(2,1)S(1)} %get-tuple-element.446), channel_id=1, source_target_pairs={{0,1},{1,2},{2,3},{3,0},{4,5},{5,6},{6,7},{7,4},{8,9},{9,10},{10,1... | collective-permute-start | bytes 786440 | tf_op jit(solution)/shard_map/ppermute | solution.py:84
  248.4 21.4 %collective-permute-start.34 = (bf16[128,1024]{1,0:T(8,128)(2,1)S(1)}, bf16[128,1024]{1,0:T(8,128)(2,1)S(1)}, u32[]{:S(2)}, u32[]{:S(2)}) collective-permute-start(bf16[128,1024]{1,0:T(8,128)(2,1)S(1)} %get-tuple-element.447), channel_id=1, source_target_pairs={{0,2},{1,3},{2,0},{3,1},{4,6},{5,7},{6,4},{7,5},{8,10},{9,11},{10,... | collective-permute-start | bytes 786440 | tf_op jit(solution)/shard_map/ppermute | solution.py:84
  254.1 19.6 %collective-permute-start.37 = (bf16[2,3,128,512]{3,2,1,0:T(8,128)(2,1)S(1)}, bf16[2,3,128,512]{3,2,1,0:T(8,128)(2,1)S(1)}, u32[]{:S(2)}, u32[]{:S(2)}) collective-permute-start(bf16[2,3,128,512]{3,2,1,0:T(8,128)(2,1)S(1)} %fusion.7), channel_id=1, source_target_pairs={{0,8},{1,9},{2,10},{3,11},{4,12},{5,13},{6,14},{7,15},{8,0},{9,1},... | collective-permute-start | bytes 2359304 | tf_op jit(solution)/shard_map/ppermute | solution.py:66
  255.8 19.3 %collective-permute-start.38 = (bf16[2,3,128,512]{3,2,1,0:T(8,128)(2,1)S(1)}, bf16[2,3,128,512]{3,2,1,0:T(8,128)(2,1)S(1)}, u32[]{:S(2)}, u32[]{:S(2)}) collective-permute-start(bf16[2,3,128,512]{3,2,1,0:T(8,128)(2,1)S(1)} %fusion.8), channel_id=1, source_target_pairs={{0,16},{1,17},{2,18},{3,19},{4,20},{5,21},{6,22},{7,23},{8,24},{9,... | collective-permute-start | bytes 2359304 | tf_op jit(solution)/shard_map/ppermute | solution.py:66
  256.7 14.5 %collective-permute-start.33 = (bf16[128,1024]{1,0:T(8,128)(2,1)S(1)}, bf16[128,1024]{1,0:T(8,128)(2,1)S(1)}, u32[]{:S(2)}, u32[]{:S(2)}) collective-permute-start(bf16[128,1024]{1,0:T(8,128)(2,1)S(1)} %get-tuple-element.448), channel_id=1, source_target_pairs={{0,3},{1,0},{2,1},{3,2},{4,7},{5,4},{6,5},{7,6},{8,11},{9,8},{10,9... | collective-permute-start | bytes 786440 | tf_op jit(solution)/shard_map/ppermute | solution.py:84
  277.0 22.2 %collective-permute-start.43 = (bf16[1,3,128,512]{3,2,1,0:T(8,128)(2,1)S(1)}, bf16[1,3,128,512]{3,2,1,0:T(8,128)(2,1)S(1)}, u32[]{:S(2)}, u32[]{:S(2)}) collective-permute-start(bf16[1,3,128,512]{3,2,1,0:T(8,128)(2,1)S(1)} %add_convert_fusion.11), channel_id=1, source_target_pairs={{0,8},{1,9},{2,10},{3,11},{4,12},{5,13},{6,14},{7,15},{8,0},{9,1},... | collective-permute-start | bytes 1179656 | tf_op jit(solution)/shard_map/ppermute | solution.py:66
  277.8 21.5 %collective-permute-start.42 = (bf16[1,3,128,512]{3,2,1,0:T(8,128)(2,1)S(1)}, bf16[1,3,128,512]{3,2,1,0:T(8,128)(2,1)S(1)}, u32[]{:S(2)}, u32[]{:S(2)}) collective-permute-start(bf16[1,3,128,512]{3,2,1,0:T(8,128)(2,1)S(1)} %add_convert_fusion.12), channel_id=1, source_target_pairs={{0,16},{1,17},{2,18},{3,19},{4,20},{5,21},{6,22},{7,23},{8,24},{9,... | collective-permute-start | bytes 1179656 | tf_op jit(solution)/shard_map/ppermute | solution.py:66
  283.0 16.3 %collective-permute-start.40 = (bf16[128,1024]{1,0:T(8,128)(2,1)S(1)}, bf16[128,1024]{1,0:T(8,128)(2,1)S(1)}, u32[]{:S(2)}, u32[]{:S(2)}) collective-permute-start(bf16[128,1024]{1,0:T(8,128)(2,1)S(1)} %get-tuple-element.444), channel_id=1, source_target_pairs={{0,2},{1,3},{2,0},{3,1},{4,6},{5,7},{6,4},{7,5},{8,10},{9,11},{10,... | collective-permute-start | bytes 786440 | tf_op jit(solution)/shard_map/ppermute | solution.py:84
  283.2 16.0 %collective-permute-start.39 = (bf16[128,1024]{1,0:T(8,128)(2,1)S(1)}, bf16[128,1024]{1,0:T(8,128)(2,1)S(1)}, u32[]{:S(2)}, u32[]{:S(2)}) collective-permute-start(bf16[128,1024]{1,0:T(8,128)(2,1)S(1)} %get-tuple-element.445), channel_id=1, source_target_pairs={{0,3},{1,0},{2,1},{3,2},{4,7},{5,4},{6,5},{7,6},{8,11},{9,8},{10,9... | collective-permute-start | bytes 786440 | tf_op jit(solution)/shard_map/ppermute | solution.py:84
  308.4 19.4 %collective-permute-start.46 = (bf16[2,3,128,512]{3,2,1,0:T(8,128)(2,1)S(1)}, bf16[2,3,128,512]{3,2,1,0:T(8,128)(2,1)S(1)}, u32[]{:S(2)}, u32[]{:S(2)}) collective-permute-start(bf16[2,3,128,512]{3,2,1,0:T(8,128)(2,1)S(1)} %fusion.10), channel_id=1, source_target_pairs={{0,16},{1,17},{2,18},{3,19},{4,20},{5,21},{6,22},{7,23},{8,24},{9,... | collective-permute-start | bytes 2359304 | tf_op jit(solution)/shard_map/ppermute | solution.py:66
  309.8 19.2 %collective-permute-start.45 = (bf16[2,3,128,512]{3,2,1,0:T(8,128)(2,1)S(1)}, bf16[2,3,128,512]{3,2,1,0:T(8,128)(2,1)S(1)}, u32[]{:S(2)}, u32[]{:S(2)}) collective-permute-start(bf16[2,3,128,512]{3,2,1,0:T(8,128)(2,1)S(1)} %fusion.9), channel_id=1, source_target_pairs={{0,8},{1,9},{2,10},{3,11},{4,12},{5,13},{6,14},{7,15},{8,0},{9,1},... | collective-permute-start | bytes 2359304 | tf_op jit(solution)/shard_map/ppermute | solution.py:66
  332.0 32.1 %collective-permute-start.47 = (bf16[4,5,128,1024]{3,2,1,0:T(8,128)(2,1)}, bf16[4,5,128,1024]{3,2,1,0:T(8,128)(2,1)}, u32[]{:S(2)}, u32[]{:S(2)}) collective-permute-start(bf16[4,5,128,1024]{3,2,1,0:T(8,128)(2,1)} %pad_maximum_fusion), channel_id=1, source_target_pairs={{0,4},{1,5},{2,6},{3,7},{4,0},{5,1},{6,2},{7,3},{8,12},{9,13},{10,... | collective-permute-start | bytes 15728648 | tf_op jit(solution)/shard_map/ppermute | solution.py:66
  339.6 18.0 %collective-permute-start.69 = (bf16[3,32,1024]{2,1,0:T(8,128)(2,1)S(1)}, bf16[3,32,1024]{2,1,0:T(8,128)(2,1)S(1)}, u32[]{:S(2)}, u32[]{:S(2)}) collective-permute-start(bf16[3,32,1024]{2,1,0:T(8,128)(2,1)S(1)} %pad_maximum_fusion.18), channel_id=1, source_target_pairs={{0,2},{1,3},{2,0},{3,1},{4,6},{5,7},{6,4},{7,5},{8,10},{9,11},{10,... | collective-permute-start | bytes 589832 | tf_op jit(solution)/shard_map/ppermute | solution.py:66
  343.0 14.6 %collective-permute-start.68 = (bf16[3,32,1024]{2,1,0:T(8,128)(2,1)S(1)}, bf16[3,32,1024]{2,1,0:T(8,128)(2,1)S(1)}, u32[]{:S(2)}, u32[]{:S(2)}) collective-permute-start(bf16[3,32,1024]{2,1,0:T(8,128)(2,1)S(1)} %pad_maximum_fusion.17), channel_id=1, source_target_pairs={{0,1},{1,0},{2,3},{3,2},{4,5},{5,4},{6,7},{7,6},{8,9},{9,8},{10,11... | collective-permute-start | bytes 589832 | tf_op jit(solution)/shard_map/ppermute | solution.py:66
  372.0 30.1 %collective-permute-start.55 = (bf16[2,5,128,512]{3,2,1,0:T(8,128)(2,1)S(1)}, bf16[2,5,128,512]{3,2,1,0:T(8,128)(2,1)S(1)}, u32[]{:S(2)}, u32[]{:S(2)}) collective-permute-start(bf16[2,5,128,512]{3,2,1,0:T(8,128)(2,1)S(1)} %fusion.4), channel_id=1, source_target_pairs={{0,16},{1,17},{2,18},{3,19},{4,20},{5,21},{6,22},{7,23},{8,24},{9,... | collective-permute-start | bytes 3932168 | tf_op jit(solution)/shard_map/ppermute | solution.py:66
  373.0 29.8 %collective-permute-start.54 = (bf16[2,5,128,512]{3,2,1,0:T(8,128)(2,1)S(1)}, bf16[2,5,128,512]{3,2,1,0:T(8,128)(2,1)S(1)}, u32[]{:S(2)}, u32[]{:S(2)}) collective-permute-start(bf16[2,5,128,512]{3,2,1,0:T(8,128)(2,1)S(1)} %fusion.3), channel_id=1, source_target_pairs={{0,8},{1,9},{2,10},{3,11},{4,12},{5,13},{6,14},{7,15},{8,0},{9,1},... | collective-permute-start | bytes 3932168 | tf_op jit(solution)/shard_map/ppermute | solution.py:66
  379.2 21.2 %collective-permute-start.52 = (bf16[264,512]{1,0:T(8,128)(2,1)S(1)}, bf16[264,512]{1,0:T(8,128)(2,1)S(1)}, u32[]{:S(2)}, u32[]{:S(2)}) collective-permute-start(bf16[264,512]{1,0:T(8,128)(2,1)S(1)} %get-tuple-element.469), channel_id=1, source_target_pairs={{0,2},{1,3},{2,0},{3,1},{4,6},{5,7},{6,4},{7,5},{8,10},{9,11},{10,... | collective-permute-start | bytes 811016 | tf_op jit(solution)/shard_map/ppermute | solution.py:84
  408.1 14.2 %collective-permute-start.57 = (bf16[3,32,1024]{2,1,0:T(8,128)(2,1)S(1)}, bf16[3,32,1024]{2,1,0:T(8,128)(2,1)S(1)}, u32[]{:S(2)}, u32[]{:S(2)}) collective-permute-start(bf16[3,32,1024]{2,1,0:T(8,128)(2,1)S(1)} %pad_maximum_fusion.15), channel_id=1, source_target_pairs={{0,2},{1,3},{2,0},{3,1},{4,6},{5,7},{6,4},{7,5},{8,10},{9,11},{10,... | collective-permute-start | bytes 589832 | tf_op jit(solution)/shard_map/ppermute | solution.py:66
  408.2 15.0 %collective-permute-start.60 = (bf16[1,5,128,512]{3,2,1,0:T(8,128)(2,1)S(1)}, bf16[1,5,128,512]{3,2,1,0:T(8,128)(2,1)S(1)}, u32[]{:S(2)}, u32[]{:S(2)}) collective-permute-start(bf16[1,5,128,512]{3,2,1,0:T(8,128)(2,1)S(1)} %add_convert_fusion.7), channel_id=1, source_target_pairs={{0,8},{1,9},{2,10},{3,11},{4,12},{5,13},{6,14},{7,15},{8,0},{9,1},... | collective-permute-start | bytes 1966088 | tf_op jit(solution)/shard_map/ppermute | solution.py:66
  409.9 14.2 %collective-permute-start.59 = (bf16[1,5,128,512]{3,2,1,0:T(8,128)(2,1)S(1)}, bf16[1,5,128,512]{3,2,1,0:T(8,128)(2,1)S(1)}, u32[]{:S(2)}, u32[]{:S(2)}) collective-permute-start(bf16[1,5,128,512]{3,2,1,0:T(8,128)(2,1)S(1)} %add_convert_fusion.8), channel_id=1, source_target_pairs={{0,16},{1,17},{2,18},{3,19},{4,20},{5,21},{6,22},{7,23},{8,24},{9,... | collective-permute-start | bytes 1966088 | tf_op jit(solution)/shard_map/ppermute | solution.py:66
  425.8 34.2 %collective-permute-start.67 = (bf16[5,32,1024]{2,1,0:T(8,128)(2,1)S(1)}, bf16[5,32,1024]{2,1,0:T(8,128)(2,1)S(1)}, u32[]{:S(2)}, u32[]{:S(2)}) collective-permute-start(bf16[5,32,1024]{2,1,0:T(8,128)(2,1)S(1)} %pad_maximum_fusion.12), channel_id=1, source_target_pairs={{0,3},{1,2},{2,1},{3,0},{4,7},{5,6},{6,5},{7,4},{8,11},{9,10},{10,... | collective-permute-start | bytes 983048 | tf_op jit(solution)/shard_map/ppermute | solution.py:66
  430.3 29.7 %collective-permute-start.66 = (bf16[5,32,1024]{2,1,0:T(8,128)(2,1)S(1)}, bf16[5,32,1024]{2,1,0:T(8,128)(2,1)S(1)}, u32[]{:S(2)}, u32[]{:S(2)}) collective-permute-start(bf16[5,32,1024]{2,1,0:T(8,128)(2,1)S(1)} %pad_maximum_fusion.11), channel_id=1, source_target_pairs={{0,2},{1,3},{2,0},{3,1},{4,6},{5,7},{6,4},{7,5},{8,10},{9,11},{10,... | collective-permute-start | bytes 983048 | tf_op jit(solution)/shard_map/ppermute | solution.py:66
  435.3 24.7 %collective-permute-start.65 = (bf16[5,32,1024]{2,1,0:T(8,128)(2,1)S(1)}, bf16[5,32,1024]{2,1,0:T(8,128)(2,1)S(1)}, u32[]{:S(2)}, u32[]{:S(2)}) collective-permute-start(bf16[5,32,1024]{2,1,0:T(8,128)(2,1)S(1)} %pad_maximum_fusion.10), channel_id=1, source_target_pairs={{0,1},{1,0},{2,3},{3,2},{4,5},{5,4},{6,7},{7,6},{8,9},{9,8},{10,11... | collective-permute-start | bytes 983048 | tf_op jit(solution)/shard_map/ppermute | solution.py:66
  (92 other events, 1138.4 us)

commit v4 on v3

--- a/solution.py
+++ b/solution.py
@@ -84,6 +84,48 @@
     return lax.ppermute(values, "fsdp", [(i, (i + j) % size) for i in range(size)])
 
 
+def hop(values, pairs):
+    return lax.ppermute(values, "fsdp", pairs)
+
+
+UP, DOWN = [(0, 1), (1, 2), (2, 3)], [(3, 2), (2, 1), (1, 0)]
+
+
+def exchange_one(values):
+    return [hop(values, UP), hop(values, DOWN)]
+
+
+def exchange_two(first, shard):
+    up, down = first
+    far = jnp.where(shard == 1, up, down)
+    return first + [hop(up, UP[1:]), hop(down, DOWN[1:]), hop(far, [(1, 3), (2, 0)])]
+
+
+def fill_every(every, own, parts, n_shard):
+    rows = own.shape[0]
+    every[0:rows] = own[...]
+    if len(parts) == n_shard - 1:
+        slots = [part[...] for part in parts]
+    else:
+        shard = lax.axis_index("fsdp")
+        up, down, up_two, down_two, far = [part[...] for part in parts]
+        slots = [jnp.where(shard == 0, far, up), jnp.where(shard <= 1, down_two, up_two), jnp.where(shard == 3, far, down)]
+    for j, slot in enumerate(slots):
+        every[(j + 1) * rows : (j + 2) * rows] = slot
+
+
+def collect_one(slots, shard):
+    far = jnp.where(shard == 0, slots[0], slots[2])
+    return [hop(slots[1], UP[:2]), hop(slots[1], DOWN[:2]), hop(far, [(0, 2), (3, 1)])]
+
+
+def collect_two(slots, first, shard):
+    up, down, far = [part.astype(F32) for part in first]
+    up = slots[2].astype(F32) + up + jnp.where(shard == 2, far, 0.0)
+    down = slots[0].astype(F32) + down + jnp.where(shard == 1, far, 0.0)
+    return [hop(up.astype(BF), UP), hop(down.astype(BF), DOWN)]
+
+
 def order_fsdp(parts, sizes, me):
     low, _, _ = bits_of(sizes)
     for bit in low:
@@ -110,20 +152,19 @@
     return result
 
 
-def core_swap(groups, sizes):
+def core_swap(whole, sizes):
     _, core, _ = bits_of(sizes)
-    return [xor_permute(values, sizes, 1 << core) for values in groups]
-
-
-def sources_of(groups, got, count, sizes, me):
-    own = groups[0].shape[2] // count
+    return xor_permute(whole, sizes, 1 << core)
+
+
+def sources_of(whole, got, count, sizes, me):
+    own = whole.shape[2] // count
     if own % 16 == 0:
-        return [groups[0], got[0], groups[1], got[1]]
+        return [whole, got]
     _, core, _ = bits_of(sizes)
     mine = ((me >> core) & 1) == 1
-    both = [jnp.stack([jnp.where(mine, g, v), jnp.where(mine, v, g)], axis=1) for v, g in zip(groups, got)]
-    whole = jnp.concatenate(both, axis=-1)
-    parts = [whole[:, :, :, i * own : (i + 1) * own] for i in range(count)]
+    both = jnp.stack([jnp.where(mine, got, whole), jnp.where(mine, whole, got)], axis=1)
+    parts = [both[:, :, :, i * own : (i + 1) * own] for i in range(count)]
     return [part.reshape(-1, part.shape[-1]) for part in parts]
 
 
@@ -200,9 +241,6 @@
         self.packed = own % 16 == 0
         self.split = self.block % LANES == 0
 
-    def sources(self, count):
-        return 4 if self.packed else count
-
     def scratch(self):
         shape = (self.far, 2, self.fsdp, self.own, self.width) if self.packed else (self.width, self.width)
         return pltpu.VMEM(shape, BF)
@@ -212,14 +250,21 @@
             pltpu.make_async_copy(sources[index], scratch, sem).start()
             return
         core = lax.axis_index("dp") & 1
-        rows, half = pl.ds(index * self.own, self.own), self.width // 2
-        for start, mine, other in ((0, sources[0], sources[1]), (half, sources[2], sources[3])):
-            for source, side in ((mine, core), (other, 1 - core)):
-                target = scratch.at[:, side, :, :, pl.ds(start, half)]
-                pltpu.make_async_copy(source.at[:, :, rows, :], target, sem).start()
+        rows = pl.ds(index * self.own, self.own)
+        for source, side in ((sources[0], core), (sources[1], 1 - core)):
+            pltpu.make_async_copy(source.at[:, :, rows, :], scratch.at[:, side], sem).start()
 
     def ready(self, scratch, sem):
         pltpu.make_async_copy(scratch, scratch, sem).wait()
+        return scratch[...].reshape(self.width, self.width)
+
+    def build(self, sources, index, scratch):
+        if not self.packed:
+            return sources[index][...]
+        core = lax.axis_index("dp") & 1
+        rows = pl.ds(index * self.own, self.own)
+        for source, side in ((sources[0], core), (sources[1], 1 - core)):
+            scratch[:, side] = source[:, :, rows, :]
         return scratch[...].reshape(self.width, self.width)
 
     def grads(self, count):
@@ -237,28 +282,48 @@
             result.append(jnp.concatenate([ref[:, pl.ds(start, self.block)] for start in starts], axis=1))
         return result
 
-    def put(self, refs, index, values):
-        for ref, value in zip(refs, values):
+    def put(self, flush, refs, twins, index, values):
+        for ref, twin, value in zip(refs, twins, values):
             value = value.astype(BF)
             if self.split:
-                ref[:, index] = value.reshape(self.far, self.block, self.width)
+                twin[:, index] = value.reshape(self.far, self.block, self.width)
+                flush(twin.at[:, index], ref.at[:, index])
             else:
-                ref[index] = value
-
-    def put_product(self, refs, index, left_ref, right):
-        self.put(refs, index, [tm(left, right) for left in self.columns(left_ref)])
-
-
-def kernel_call(kernel, name, operands, sources, outs, scratch, vmem_mb, work_mb, scalars=()):
+                twin[index] = value
+                flush(twin.at[index], ref.at[index])
+
+    def put_product(self, flush, refs, twins, index, left_ref, right):
+        self.put(flush, refs, twins, index, [tm(left, right) for left in self.columns(left_ref)])
+
+
+class Flush:
+    def __init__(self, sems):
+        self.sems, self.copies = sems, []
+
+    def __call__(self, source, target):
+        copy = pltpu.make_async_copy(source, target, self.sems.at[len(self.copies)])
+        copy.start()
+        self.copies.append(copy)
+
+    def finish(self):
+        for copy in self.copies:
+            copy.wait()
+
+
+COPIES = 16
+
+
+def kernel_call(kernel, name, operands, sources, near, far, scratch, vmem_mb, work_mb, scalars=(), held=True):
     specs = [pl.BlockSpec(memory_space=pltpu.SMEM)] * len(scalars)
     specs += [pl.BlockSpec(memory_space=pltpu.VMEM)] * len(operands)
-    specs += [pl.BlockSpec(memory_space=pl.ANY)] * len(sources)
+    specs += [pl.BlockSpec(memory_space=pltpu.VMEM if held else pl.ANY)] * len(sources)
+    out_specs = [pl.BlockSpec(memory_space=pltpu.VMEM)] * len(near) + [pl.BlockSpec(memory_space=pltpu.HBM)] * len(far)
     return pl.pallas_call(
         kernel,
         in_specs=specs,
-        out_specs=[pl.BlockSpec(memory_space=pltpu.VMEM)] * len(outs),
-        out_shape=outs,
-        scratch_shapes=scratch,
+        out_specs=out_specs,
+        out_shape=list(near) + list(far),
+        scratch_shapes=[pltpu.VMEM(f.shape, f.dtype) for f in far] + scratch + [pltpu.SemaphoreType.DMA((COPIES,))],
         compiler_params=pltpu.CompilerParams(vmem_limit_bytes=vmem_mb * 2**20),
         cost_estimate=pl.CostEstimate(flops=2**30, bytes_accessed=work_mb * 2**20, transcendentals=2**20),
         name=name,
@@ -281,23 +346,24 @@
 def encoder_kernel(pack, n_source, padded, lat_rows, *refs):
     counts, latents, pix = refs[:3]
     sources, rest = refs[3 : 3 + n_source], refs[3 + n_source :]
-    small_o, q_o, query_pix_o, probs_o, mixed_pix_o, mixed_o, resid_o, pre_o, act_o, first_o, low_o = rest[:11]
-    scratch, sems = rest[11:16], rest[16]
+    (small_o, low_o), outs, twins = rest[:2], rest[2:11], rest[11:20]
+    q_o, query_pix_o, probs_o, mixed_pix_o, mixed_o, resid_o, pre_o, act_o, first_o = twins
+    scratch, flush = rest[20:25], Flush(rest[25])
     half = pack.width // 2
-    for slot, index in enumerate((4, 2, 3, 0, 1)):
-        pack.fetch(sources, index, scratch[slot], sems.at[slot])
     latent_in = latents[...].astype(F32)
     hat, _ = norm_parts(latent_in)
-    kv = pack.ready(scratch[0], sems.at[0])
+    kv = pack.build(sources, 4, scratch[0])
     shape = (small_o.shape[0], half - padded)
     eye = lax.broadcasted_iota(jnp.int32, shape, 0) == lax.broadcasted_iota(jnp.int32, shape, 1)
     small_o[...] = mm_t(eye.astype(F32).astype(BF), kv[:, padded:half])
     small = small_rows(small_o)
     in_low = (hat * small(0) + small(2)).astype(BF)
-    query = mm(in_low, pack.ready(scratch[1], sems.at[1])).astype(BF)
+    query = mm(in_low, pack.build(sources, 2, scratch[1])).astype(BF)
     q_o[...] = query
+    flush(twins[0], outs[0])
     query_pix = mm(query, kv[:, :padded]).astype(BF)
     query_pix_o[...] = query_pix
+    flush(twins[1], outs[1])
     shape = probs_o.shape
     row, column = lax.broadcasted_iota(jnp.int32, shape, 0), lax.broadcasted_iota(jnp.int32, shape, 1)
     first, end, total = jnp.zeros(shape, jnp.int32), jnp.zeros(shape, jnp.int32), 0
@@ -309,44 +375,45 @@
     scores = mm_t(query_pix, pix[...]) * pack.width**-0.5
     probs = softmax(jnp.where((column >= first) & (column < end), scores, MASKED))
     probs_o[...] = probs
+    flush(twins[2], outs[2])
     mixed_pix = mm(probs.astype(BF), pix[...]).astype(BF)
     mixed_pix_o[...] = mixed_pix
+    flush(twins[3], outs[3])
     mixed = mm_t(mixed_pix, kv[:, half : half + padded]).astype(BF)
     mixed_o[...] = mixed
-    resid = latent_in + mm(mixed, pack.ready(scratch[2], sems.at[2]))
+    flush(twins[4], outs[4])
+    resid = latent_in + mm(mixed, pack.build(sources, 3, scratch[2]))
     resid_o[...] = resid
+    flush(twins[5], outs[5])
     hat, _ = norm_parts(resid)
     normed = (hat * small(1) + small(3)).astype(BF)
-    pre = mm(normed, pack.ready(scratch[3], sems.at[3])) + small(4)
+    pre = mm(normed, pack.build(sources, 0, scratch[3])) + small(4)
     pre_o[...] = pre
+    flush(twins[6], outs[6])
     act = gelu(pre).astype(BF)
     act_o[...] = act
-    out = resid + mm(act, pack.ready(scratch[4], sems.at[4])) + small(5)
+    flush(twins[7], outs[7])
+    out = resid + mm(act, pack.build(sources, 1, scratch[4])) + small(5)
     first_o[...] = out
+    flush(twins[8], outs[8])
     hat, _ = norm_parts(out)
     low_o[...] = (hat * small(6) + small(8)).astype(BF)
-
-
-def fill_every(every, own, others, lat_rows, rows):
-    every[0:rows] = own[...]
-    count = len(others) // (rows // lat_rows)
-    for i, shard in enumerate(others):
-        start = (1 + i % count) * rows + i // count * lat_rows
-        every[start : start + lat_rows] = shard[...]
+    flush.finish()
 
 
 def attention_kernel(pack, n_source, n_other, lat_rows, *refs):
     own, others, rest = refs[0], refs[1 : 1 + n_other], refs[1 + n_other :]
     sources, rest = rest[:n_source], rest[n_source:]
-    q_o, k_o, v_o, mixed_o = rest[:4]
-    scratch, every, sems = rest[4:7], rest[7], rest[8]
-    for index in range(3):
-        pack.fetch(sources, index, scratch[index], sems.at[index])
+    mixed_o, outs, twins = rest[0], rest[1:5], rest[5:9]
+    every, q_o, k_o, v_o = twins
+    scratch, flush = rest[9:12], Flush(rest[12])
     rows = own.shape[0]
-    fill_every(every, own, others, lat_rows, rows)
-    q_o[...] = mm(own[...], pack.ready(scratch[0], sems.at[0])).astype(BF)
-    k_o[...] = mm(every[...], pack.ready(scratch[1], sems.at[1])).astype(BF).reshape(k_o.shape)
-    v_o[...] = mm(every[...], pack.ready(scratch[2], sems.at[2])).astype(BF).reshape(k_o.shape)
+    fill_every(every, own, others, pack.fsdp)
+    q_o[...] = mm(own[...], pack.build(sources, 0, scratch[0])).astype(BF)
+    k_o[...] = mm(every[...], pack.build(sources, 1, scratch[1])).astype(BF).reshape(k_o.shape)
+    v_o[...] = mm(every[...], pack.build(sources, 2, scratch[2])).astype(BF).reshape(k_o.shape)
+    for twin, out in zip(twins, outs):
+        flush(twin, out)
 
     def some_heads(step, carry):
         places, loaded = [], []
@@ -364,20 +431,22 @@
         return carry
 
     lax.fori_loop(0, HEADS // HEADS_AT_ONCE, some_heads, 0)
-
-
-def attention_back_kernel(pack, n_source, n_other, lat_rows, *refs):
-    q, k_ref, v_ref, grad, own = refs[:5]
-    others, rest = refs[5 : 5 + n_other], refs[5 + n_other :]
+    flush.finish()
+
+
+def attention_back_kernel(pack, n_source, lat_rows, *refs):
+    q, k_ref, v_ref, grad, every = refs[:5]
+    rest = refs[5:]
     sources, rest = rest[:n_source], rest[n_source:]
-    outs = 2 + len(pack.grads(3))
-    slot_o, slots_o, *grad_o = rest[:outs]
-    scratch, (every, dq, dk, dv, sems) = rest[outs : outs + 3], rest[outs + 3 :]
+    count = len(pack.grads(3))
+    slots_o, slot_h, grads_h = rest[0], rest[1], rest[2 : 2 + count]
+    slot_o, grads_o, rest = rest[2 + count], rest[3 + count : 3 + 2 * count], rest[3 + 2 * count :]
+    scratch, (dq, dk, dv, sems, out_sems) = rest[:3], rest[3:]
+    flush = Flush(out_sems)
     for index in range(3):
         pack.fetch(sources, index, scratch[index], sems.at[index])
     rows = q.shape[0]
     scale = HEAD**-0.5
-    fill_every(every, own, others, lat_rows, rows)
 
     def some_heads(step, carry):
         places, loaded = [], []
@@ -409,62 +478,66 @@
     slot_o[...] = mm_t(d_q, w_query) + mm_t(d_k[:rows], w_key) + mm_t(d_v[:rows], w_value)
     others = mm_t(d_k[rows:], w_key) + mm_t(d_v[rows:], w_value)
     slots_o[...] = others.astype(BF).reshape(slots_o.shape)
-    pack.put(grad_o, 0, [tm(left, d_q) for left in pack.columns(every.at[pl.ds(0, rows)])])
+    flush(slot_o, slot_h)
+    pack.put(flush, grads_h, grads_o, 0, [tm(left, d_q) for left in pack.columns(every.at[pl.ds(0, rows)])])
     columns = pack.columns(every)
-    pack.put(grad_o, 1, [tm(left, d_k) for left in columns])
-    pack.put(grad_o, 2, [tm(left, d_v) for left in columns])
+    pack.put(flush, grads_h, grads_o, 1, [tm(left, d_k) for left in columns])
+    pack.put(flush, grads_h, grads_o, 2, [tm(left, d_v) for left in columns])
+    flush.finish()
 
 
 def latent_kernel(pack, n_source, *refs):
     mixed, first_out, cotangent, small_ref = refs[:4]
     sources, rest = refs[4 : 4 + n_source], refs[4 + n_source :]
-    outs = 4 + len(pack.grads(3))
-    result_o, grad_o, d_mixed_o, sums_o, *grads_o = rest[:outs]
-    scratch, (act_s, normed_s, sems) = rest[outs : outs + 3], rest[outs + 3 :]
-    for index in range(3):
-        pack.fetch(sources, index, scratch[index], sems.at[index])
+    (d_mixed_o, sums_o), rest = rest[:2], rest[2:]
+    count = 2 + len(pack.grads(3))
+    (result_h, grad_h, *grads_h), (result_o, grad_o, *grads_o) = rest[:count], rest[count : 2 * count]
+    scratch, (act_s, normed_s, out_sems) = rest[2 * count : 2 * count + 3], rest[2 * count + 3 :]
+    flush = Flush(out_sems)
     small = small_rows(small_ref)
-    w_out = pack.ready(scratch[0], sems.at[0])
+    w_out = pack.build(sources, 0, scratch[0])
     resid = first_out[...] + mm(mixed[...], w_out)
     hat, inverse = norm_parts(resid)
     normed_s[...] = (hat * small(7) + small(9)).astype(BF)
-    w_first = pack.ready(scratch[1], sems.at[1])
+    w_first = pack.build(sources, 1, scratch[1])
     pre = mm(normed_s[...], w_first) + small(10)
     act_s[...] = gelu(pre).astype(BF)
-    w_second = pack.ready(scratch[2], sems.at[2])
+    w_second = pack.build(sources, 2, scratch[2])
     result_o[...] = (resid + mm(act_s[...], w_second) + small(11)).astype(BF)
+    flush(result_o, result_h)
     grad_low = cotangent[...]
     grad_out = grad_low.astype(F32)
-    pack.put_product(grads_o, 1, act_s, grad_low)
+    pack.put_product(flush, grads_h, grads_o, 1, act_s, grad_low)
     d_pre = mm_t(grad_low, w_second) * gelu_slope(pre)
     d_pre_low = d_pre.astype(BF)
-    pack.put_product(grads_o, 0, normed_s, d_pre_low)
+    pack.put_product(flush, grads_h, grads_o, 0, normed_s, d_pre_low)
     d_normed = mm_t(d_pre_low, w_first)
     grad_mid = grad_out + norm_back(hat, inverse, small(7), d_normed)
     grad_o[...] = grad_mid
+    flush(grad_o, grad_h)
     grad_low = grad_mid.astype(BF)
     d_mixed_o[...] = mm_t(grad_low, w_out).astype(BF)
-    pack.put_product(grads_o, 2, mixed, grad_low)
+    pack.put_product(flush, grads_h, grads_o, 2, mixed, grad_low)
     sums_o[0:1] = column_sum(d_normed * hat)
     sums_o[1:2] = column_sum(d_normed)
     sums_o[2:3] = column_sum(d_pre)
     sums_o[3:4] = column_sum(grad_out)
-
-
-def encoder_back_kernel(pack, n_source, n_other, images, *refs):
+    flush.finish()
+
+
+def encoder_back_kernel(pack, n_source, n_other, *refs):
     slot, grad_mid, first_out, resid, pre_ref, act, small_ref = refs[:7]
     others, rest = refs[7 : 7 + n_other], refs[7 + n_other :]
     sources, rest = rest[:n_source], rest[n_source:]
-    outs = 2 + len(pack.grads(2))
-    grad_o, sums_o, *grads_o = rest[:outs]
-    scratch, (normed_s, sems) = rest[outs : outs + 2], rest[outs + 2 :]
+    (grad_o, sums_o), rest = rest[:2], rest[2:]
+    count = len(pack.grads(2))
+    grads_h, grads_o, rest = rest[:count], rest[count : 2 * count], rest[2 * count :]
+    scratch, (normed_s, sems, out_sems) = rest[:2], rest[2:]
+    flush = Flush(out_sems)
     for index in range(2):
         pack.fetch(sources, index, scratch[index], sems.at[index])
     small = small_rows(small_ref)
-    parts, count = [], n_other // images
-    for image in range(images):
-        parts.append(sum(ref[...].astype(F32) for ref in others[image * count : (image + 1) * count]))
-    d_normed = slot[...] + jnp.concatenate(parts, axis=0)
+    d_normed = slot[...] + sum(ref[...].astype(F32) for ref in others)
     hat, inverse = norm_parts(first_out[...])
     sums_o[0:1] = column_sum(d_normed * hat)
     sums_o[1:2] = column_sum(d_normed)
@@ -477,20 +550,24 @@
     hat, inverse = norm_parts(resid[...])
     grad_o[...] = grad_out + norm_back(hat, inverse, small(1), d_normed)
     normed_s[...] = (hat * small(1) + small(3)).astype(BF)
-    pack.put_product(grads_o, 0, normed_s, d_pre_low)
-    pack.put_product(grads_o, 1, act, grad_low)
+    pack.put_product(flush, grads_h, grads_o, 0, normed_s, d_pre_low)
+    pack.put_product(flush, grads_h, grads_o, 1, act, grad_low)
     sums_o[2:3] = column_sum(d_normed * hat)
     sums_o[3:4] = column_sum(d_normed)
     sums_o[4:5] = column_sum(d_pre)
     sums_o[5:6] = column_sum(grad_out)
+    flush.finish()
 
 
 def cross_back_kernel(pack, n_source, padded, share, *refs):
     grad_ref, latents, mixed, mixed_pix, probs_ref, pix, query_pix, enc_q, small_ref, lat_sums, enc_sums, pix_hat = refs[:12]
     sources, rest = refs[12 : 12 + n_source], refs[12 + n_source :]
-    outs = 3 + len(pack.grads(3))
-    d_latents_o, d_pix_o, pix_sums_o, *grads_o = rest[:outs]
-    scratch, (d_mixed_s, in_low_s, high_s, low_s, sems) = rest[outs : outs + 3], rest[outs + 3 :]
+    (d_pix_o, pix_sums_o), rest = rest[:2], rest[2:]
+    count = 1 + len(pack.grads(3))
+    (d_latents_h, *grads_h), (d_latents_o, *grads_o) = rest[:count], rest[count : 2 * count]
+    scratch, rest = rest[2 * count : 2 * count + 3], rest[2 * count + 3 :]
+    d_mixed_s, in_low_s, high_s, low_s, sems, out_sems = rest
+    flush = Flush(out_sems)
     for slot, index in enumerate((3, 4, 2)):
         pack.fetch(sources, index, scratch[slot], sems.at[slot])
     small = small_rows(small_ref)
@@ -526,6 +603,7 @@
     in_low_s[...] = (hat * small(0) + small(2)).astype(BF)
     d_normed = mm_t(d_enc_q, pack.ready(scratch[2], sems.at[2]))
     d_latents_o[...] = grad_enc + norm_back(hat, inverse, small(0), d_normed)
+    flush(d_latents_o, d_latents_h)
     order = [column_sum(d_normed * hat), enc_sums[2:3], column_sum(d_normed), enc_sums[3:4], enc_sums[4:5], enc_sums[5:6]]
     order += [enc_sums[0:1], lat_sums[0:1], enc_sums[1:2], lat_sums[1:2], lat_sums[2:3], lat_sums[3:4]]
     sums = jnp.concatenate(order + [jnp.zeros((16 - len(order), pack.width), F32)], axis=0)
@@ -539,9 +617,29 @@
     for left, high_c, right, low_c in zip(*(pack.columns(r) for r in (enc_q, high_s, d_mixed_s, low_s))):
         columns = [tm(left, d_query_pix), tm(high_c, eye), tm(right, mixed_pix[...]), tm(low_c, eye)]
         blocks.append(jnp.concatenate(columns, axis=1))
-    pack.put(grads_o, 0, blocks)
-    pack.put_product(grads_o, 1, in_low_s, d_enc_q)
-    pack.put_product(grads_o, 2, mixed, grad_low)
+    pack.put(flush, grads_h, grads_o, 0, blocks)
+    pack.put_product(flush, grads_h, grads_o, 1, in_low_s, d_enc_q)
+    pack.put_product(flush, grads_h, grads_o, 2, mixed, grad_low)
+    flush.finish()
+
+
+def pack_kernel(own, padded, *refs):
+    gains_biases, pix_kv, query, out, mlp, packed = refs[:4], *refs[4:]
+    half = packed.shape[1] // 2
+
+    def turned(values, columns):
+        rows = values.shape[0]
+        eye = lax.broadcasted_iota(jnp.int32, (rows, columns), 0) == lax.broadcasted_iota(jnp.int32, (rows, columns), 1)
+        return tm(values, eye.astype(F32).astype(BF)).astype(BF)
+
+    packed[0:own], packed[own : 2 * own] = mlp[0], mlp[1]
+    packed[2 * own : 3 * own], packed[3 * own : 4 * own] = query[...], out[...]
+    small = jnp.concatenate([ref[...].astype(F32) for ref in gains_biases], axis=0).astype(BF)
+    last = packed.at[pl.ds(4 * own, own)]
+    last[:, 0:padded] = turned(pix_kv[0], padded)
+    last[:, padded:half] = turned(small, half - padded)
+    last[:, half : half + padded] = turned(pix_kv[1], padded)
+    last[:, half + padded :] = jnp.zeros((own, half - padded), BF)
 
 
 def pad_lanes(values, width):
@@ -582,13 +680,11 @@
     steps = range(1, len(far))
     half = width // 2
 
-    small = jnp.concatenate([enc_gains, enc_biases, lat_gains, lat_biases], axis=0)
-    n_small = small.shape[0]
-    place_pix, place_small = jnp.eye(features, padded, dtype=BF), jnp.eye(n_small, half - padded, dtype=BF)
-    kv_t = jnp.concatenate(
-        [tm(pix_kv[0], place_pix), tm(small, place_small), pad_lanes(tm(pix_kv[1], place_pix), half)], axis=1
-    ).astype(BF)
-    enc_parts = gather_fsdp(jnp.concatenate([enc_mlp[0], enc_mlp[1], enc_query, enc_out, kv_t], axis=0), sizes)
+    wide, dma = jax.ShapeDtypeStruct, pltpu.SemaphoreType.DMA
+    enc_pack = pl.pallas_call(
+        partial(pack_kernel, own, padded), out_shape=wide((5 * own, width), BF), name="pack"
+    )(enc_gains, enc_biases, lat_gains, lat_biases, pix_kv, enc_query, enc_out, enc_mlp)
+    enc_parts = gather_fsdp(enc_pack, sizes)
     gain_f = pix_gain.astype(F32)
     pix_hat, pix_inverse = norm_parts(pixels.astype(F32))
     pix_low = pad_lanes((pix_hat * gain_f + pix_bias.astype(F32)).astype(BF), padded)[:USED]
@@ -607,137 +703,152 @@
     qkv_groups = [v[None] for v in halves_of(order_fsdp(qkv_parts, sizes, me))]
     enc_groups, qkv_groups, other_parts = seal(enc_groups, qkv_groups, other_parts)
 
-    enc_got = core_swap(enc_groups, sizes)
+    enc_whole = jnp.concatenate(enc_groups, axis=-1)
+    enc_got = core_swap(enc_whole, sizes)
     qkv_groups = far_step(qkv_groups, 0, sizes, me)
     other_groups = [v[None] for v in halves_of(order_fsdp(other_parts, sizes, me))]
-    enc_groups, enc_got, qkv_groups, other_groups = seal(enc_groups, enc_got, qkv_groups, other_groups)
+    enc_whole, enc_got, qkv_groups, other_groups = seal(enc_whole, enc_got, qkv_groups, other_groups)
 
     pack = Pack(sizes, own, width)
     for place in steps:
         qkv_groups = far_step(qkv_groups, place, sizes, me)
-    enc_sources = sources_of(enc_groups, enc_got, 5, sizes, me)
+    enc_sources = sources_of(enc_whole, enc_got, 5, sizes, me)
     n_gain, n_bias = enc_gains.shape[0], enc_biases.shape[0]
-    wide, dma = jax.ShapeDtypeStruct, pltpu.SemaphoreType.DMA
-
-    small_all, enc_q, query_pix, probs, mixed_pix, enc_mixed, enc_resid, enc_pre, enc_act, first_out, lat_low = kernel_call(
+
+    small_all, lat_low, enc_q, query_pix, probs, mixed_pix, enc_mixed, enc_resid, enc_pre, enc_act, first_out = kernel_call(
         partial(encoder_kernel, pack, len(enc_sources), padded, lat_rows),
         "encoder",
         [latents.reshape(rows, width), pix_low],
         enc_sources,
-        [wide((16, width), F32), wide((rows, width), BF), wide((rows, padded), BF), wide((rows, USED), F32)]
-        + [wide((rows, padded), BF), wide((rows, width), BF), wide((rows, width), F32), wide((rows, width), F32)]
-        + [wide((rows, width), BF), wide((rows, width), F32), wide((rows, width), BF)],
-        [pack.scratch()] * 5 + [dma((5,))],
-        36,
+        [wide((16, width), F32), wide((rows, width), BF)],
+        [wide((rows, width), BF), wide((rows, padded), BF), wide((rows, USED), F32), wide((rows, padded), BF)]
+        + [wide((rows, width), BF), wide((rows, width), F32), wide((rows, width), F32), wide((rows, width), BF)]
+        + [wide((rows, width), F32)],
+        [pack.scratch()] * 5,
+        48,
         36,
         scalars=[lengths],
     )
-    lat_low, qkv_groups, other_groups = seal(lat_low, qkv_groups, other_groups)
-
-    shards = []
-    for image in range(images):
-        part = lat_low[image * lat_rows : (image + 1) * lat_rows]
-        shards += [slot_shift(part, fsdp_size, j) for j in range(1, fsdp_size)]
-        if image == 0:
-            qkv_got = core_swap(qkv_groups, sizes)
-            qkv_got, other_groups = seal(qkv_got, other_groups)
-        if image < len(far):
-            other_groups = far_step(other_groups, image, sizes, me)
-        lat_low, shards, qkv_got, other_groups = seal(lat_low, shards, qkv_got, other_groups)
-
-    for place in range(images, len(far)):
+    qkv_whole = jnp.concatenate(qkv_groups, axis=-1)
+    lat_low, qkv_whole, other_groups = seal(lat_low, qkv_whole, other_groups)
+
+    in_two = fsdp_size == 4
+    if in_two:
+        shards = exchange_one(lat_low)
+    else:
+        shards = [slot_shift(lat_low, fsdp_size, j) for j in range(1, fsdp_size)]
+    qkv_got = core_swap(qkv_whole, sizes)
+    other_groups = far_step(other_groups, 0, sizes, me)
+    lat_low, shards, qkv_got, other_groups = seal(lat_low, shards, qkv_got, other_groups)
+    if in_two:
+        shards = exchange_two(list(shards), my_fsdp)
+    for place in steps:
         other_groups = far_step(other_groups, place, sizes, me)
-    other_got = core_swap(other_groups, sizes)
-    qkv_sources = sources_of(qkv_groups, qkv_got, 3, sizes, me)
+    other_whole = jnp.concatenate(other_groups, axis=-1)
+    shards, other_whole = seal(list(shards), other_whole)
+    other_got = core_swap(other_whole, sizes)
+    qkv_sources = sources_of(qkv_whole, qkv_got, 3, sizes, me)
     every = wide((fsdp_size, rows, width), BF)
-    every_flat = pltpu.VMEM((fsdp_size * rows, width), BF)
-    lat_q, lat_k, lat_v, lat_mixed = kernel_call(
+    lat_mixed, lat_every, lat_q, lat_k, lat_v = kernel_call(
         partial(attention_kernel, pack, len(qkv_sources), len(shards), lat_rows),
         "attention",
-        [lat_low] + list(shards),
+        [lat_low] + shards,
         qkv_sources,
-        [wide((rows, width), BF), every, every, wide((rows, width), BF)],
-        [pack.scratch()] * 3 + [every_flat, dma((3,))],
-        32,
+        [wide((rows, width), BF)],
+        [wide((fsdp_size * rows, width), BF), wide((rows, width), BF), every, every],
+        [pack.scratch()] * 3,
+        40,
         40,
     )
-    other_sources = sources_of(other_groups, other_got, 3, sizes, me)
-    result, grad_mid, d_mixed, lat_sums, *grads_m = kernel_call(
+    other_sources = sources_of(other_whole, other_got, 3, sizes, me)
+    d_mixed, lat_sums, result, grad_mid, *grads_m = kernel_call(
         partial(latent_kernel, pack, len(other_sources)),
         "latent",
         [lat_mixed, first_out, cotangent.reshape(rows, width), small_all],
         other_sources,
-        [wide((rows, width), BF), wide((rows, width), F32), wide((rows, width), BF), wide((8, width), F32)] + pack.grads(3),
-        [pack.scratch()] * 3 + [pltpu.VMEM((rows, width), BF)] * 2 + [dma((3,))],
-        36,
+        [wide((rows, width), BF), wide((8, width), F32)],
+        [wide((rows, width), BF), wide((rows, width), F32)] + pack.grads(3),
+        [pack.scratch()] * 3 + [pltpu.VMEM((rows, width), BF)] * 2,
+        44,
         36,
     )
 
     grads_m = core_terms(grads_m, sizes, me)
-    slot, slots, *grads_q = kernel_call(
-        partial(attention_back_kernel, pack, len(qkv_sources), len(shards), lat_rows),
+    slots, slot, *grads_q = kernel_call(
+        partial(attention_back_kernel, pack, len(qkv_sources), lat_rows),
         "attention_back",
-        [lat_q, lat_k, lat_v, d_mixed, lat_low] + list(shards),
+        [lat_q, lat_k, lat_v, d_mixed, lat_every],
         qkv_sources,
-        [wide((rows, width), F32), wide((fsdp_size - 1, rows, width), BF)] + pack.grads(3),
+        [wide((fsdp_size - 1, rows, width), BF)],
+        [wide((rows, width), F32)] + pack.grads(3),
         [pack.scratch()] * 3
-        + [every_flat, pltpu.VMEM((rows, width), BF)]
+        + [pltpu.VMEM((rows, width), BF)]
         + [pltpu.VMEM(every.shape, BF)] * 2
         + [dma((3,))],
-        46,
+        48,
         72,
+        held=False,
     )
-    slot, slots, grads_q = seal(slot, slots, grads_q)
-
-    received = []
-    for image in range(images):
-        part = slots[:, image * lat_rows : (image + 1) * lat_rows]
-        received += [slot_shift(part[j - 1], fsdp_size, fsdp_size - j) for j in range(1, fsdp_size)]
-        if image < len(far):
-            grads_m = far_pair(grads_m, image, sizes, me)
-        slots, received, grads_m = seal(slots, received, grads_m)
-    for place in range(images, len(far)):
+    slots, grads_q = seal(slots, grads_q)
+
+    slots = [slots[j] for j in range(fsdp_size - 1)]
+    if in_two:
+        received = collect_one(slots, my_fsdp)
+    else:
+        received = [slot_shift(slots[j - 1], fsdp_size, fsdp_size - j) for j in range(1, fsdp_size)]
+    grads_m = far_pair(grads_m, 0, sizes, me)
+    slots, received, grads_m = seal(slots, received, grads_m)
+    if in_two:
+        received = collect_two(slots, received, my_fsdp)
+    for place in steps:
         grads_m = far_pair(grads_m, place, sizes, me)
+    grads_q = core_terms(grads_q, sizes, me)
+    received, grads_m, grads_q = seal(received, grads_m, grads_q)
+    received = list(received)
+    grad_enc, enc_sums, *grads_e = kernel_call(
+        partial(encoder_back_kernel, pack, len(enc_sources), len(received)),
+        "encoder_back",
+        [slot, grad_mid, first_out, enc_resid, enc_pre, enc_act, small_all] + received,
+        enc_sources,
+        [wide((rows, width), F32), wide((8, width), F32)],
+        pack.grads(2),
+        [pack.scratch()] * 2 + [pltpu.VMEM((rows, width), BF), dma((2,))],
+        40,
+        36,
+        held=False,
+    )
     l_other_grads = finish_sum(grads_m, sizes, my_fsdp)
-    grads_q = core_terms(grads_q, sizes, me)
-    grad_enc, enc_sums, *grads_e = kernel_call(
-        partial(encoder_back_kernel, pack, len(enc_sources), len(received), images),
-        "encoder_back",
-        [slot, grad_mid, first_out, enc_resid, enc_pre, enc_act, small_all] + list(received),
-        enc_sources,
-        [wide((rows, width), F32), wide((8, width), F32)] + pack.grads(2),
-        [pack.scratch()] * 2 + [pltpu.VMEM((rows, width), BF), dma((2,))],
-        34,
-        36,
-    )
-    grad_enc, grads_e, grads_q = seal(grad_enc, grads_e, grads_q)
-
     grads_q = far_pair(grads_q, 0, sizes, me)
     share = pix_rows // fsdp_size
     kept = pix_hat_t.shape[0]
-    d_latents, pieces, d_pix_sums, *grads_f = kernel_call(
+    pieces, d_pix_sums, d_latents, *grads_f = kernel_call(
         partial(cross_back_kernel, pack, len(enc_sources), padded, share),
         "cross_back",
         [grad_enc, latents.reshape(rows, width), enc_mixed, mixed_pix, probs, pix_low, query_pix, enc_q, small_all]
         + [lat_sums, enc_sums, pix_hat_t],
         enc_sources,
-        [wide((rows, width), F32), wide((fsdp_size, kept, share), F32), wide((kept, LANES), F32)] + pack.grads(3),
+        [wide((fsdp_size, kept, share), F32), wide((kept, LANES), F32)],
+        [wide((rows, width), F32)] + pack.grads(3),
         [pack.scratch()] * 3
         + [pltpu.VMEM((rows, width), BF)] * 2
         + [pltpu.VMEM((16, width), BF)] * 2
         + [dma((3,))],
-        44,
+        48,
         50,
+        held=False,
     )
-    pieces, grads_f, d_pix_sums, grads_q = seal(pieces, grads_f, d_pix_sums, grads_q)
+    pieces, grads_e, grads_f, d_pix_sums, grads_q, l_other_grads = seal(
+        pieces, grads_e, grads_f, d_pix_sums, grads_q, l_other_grads
+    )
 
     low_bits, core, _ = bits_of(sizes)
-    grads_e = core_terms([jnp.concatenate(both, axis=-3) for both in zip(grads_e, grads_f)], sizes, me)
+    grads_e, grads_f = core_terms(grads_e, sizes, me), core_terms(grads_f, sizes, me)
     for place in steps:
         grads_q = far_pair(grads_q, place, sizes, me)
-    d_pix_sums = total_over(d_pix_sums[:features, :2].T, [core], sizes)
-    pieces, grads_e, grads_q, d_pix_sums = seal(pieces, grads_e, grads_q, d_pix_sums)
-
+    d_pix_sums = total_over(d_pix_sums[:features, :2].T, low_bits, sizes)
+    pieces, grads_e, grads_f, grads_q, d_pix_sums = seal(pieces, grads_e, grads_f, grads_q, d_pix_sums)
+
+    grads_e = [[jnp.concatenate(both, axis=1) for both in zip(e, f)] for e, f in zip(grads_e, grads_f)]
     d_pix_own = pieces[0]
     for j in range(1, fsdp_size):
         d_pix_own = d_pix_own + slot_shift(pieces[j].astype(BF), fsdp_size, fsdp_size - j).astype(F32)
@@ -748,7 +859,7 @@
     for place in steps:
         grads_e = far_pair(grads_e, place, sizes, me)
     l_qkv_grads, grads_e, d_pix_sums = seal(l_qkv_grads, grads_e, d_pix_sums)
-    d_pix_sums = total_over(d_pix_sums, far + low_bits, sizes)
+    d_pix_sums = total_over(d_pix_sums, [core] + far, sizes)
     enc_grads = finish_sum(grads_e, sizes, my_fsdp)
     hat_own = lax.dynamic_slice_in_dim(pix_hat, my_fsdp * share, share, 0)
     inverse_own = lax.dynamic_slice_in_dim(pix_inverse, my_fsdp * share, share, 0)
@@ -756,6 +867,7 @@
     kv_own = enc_grads[2]
     d_pix_kv = jnp.stack([kv_own[:, :features].T, kv_own[:, width // 2 : width // 2 + features].T])
     start = width // 2 + padded
+    n_small = 2 * (n_gain + n_bias)
     small_own = (kv_own[:, padded : padded + n_small] + kv_own[:, start : start + n_small]).T
     return (
         result.reshape(latents.shape),

time: 471 us -> 430 us (0.913)
  waiting for transfers between devices: 205 us -> 174 us
  local copies, waits for them, and re-layouts: 65.4 us -> 50 us
  Pallas kernels: 64.4 us -> 79.8 us
  starting transfers between devices: 95.9 us -> 86.9 us
    ppermute x15 -> x3, waiting for transfers between devices: 60.8 us -> 19.3 us  [slot_shift(): lax.ppermute(values, 'fsdp', [(i, (i + j) % size) for i in range(size)])]
    ppermute x15 -> x3, starting transfers between devices: 30.6 us -> 3.35 us  [slot_shift(): lax.ppermute(values, 'fsdp', [(i, (i + j) % size) for i in range(size)])]
    ppermute x0 -> x10, starting transfers between devices: none -> 20.6 us  [hop(): return lax.ppermute(values, 'fsdp', pairs)]
    ppermute x0 -> x10, waiting for transfers between devices: none -> 19.4 us  [hop(): return lax.ppermute(values, 'fsdp', pairs)]
    pallas_call x6 -> x7, Pallas kernels: 64.4 us -> 79.8 us  [the longest x6 77.8 us: kernel_call(): pl.pallas_call(kernel, in_specs=specs, out_specs=out_specs, out_shape=lis...]
    unnamed x147 -> x124, local copies, waits for them, and re-layouts: 35.6 us -> 24.7 us
    ppermute x56 -> x54, waiting for transfers between devices: 144 us -> 136 us  [xor_permute(): return lax.ppermute(values, AXES, [(i, i ^ step) for i in range(total)])]
    slice x6 -> x8, local copies, waits for them, and re-layouts: 10.8 us -> 7.97 us  [halves_of(): return [values[..., :half], values[..., half:]]]
  transfers between devices with their start and end apart: 71 -> 67, of which waited for: 39 -> 28; matrix products, arithmetic and copies ran while one was open for 10% -> 11% of each run, Pallas kernels for 11% -> 16%
where the time goes in v4:
time: 430 us; the launch traced here: 424 us
  waiting for transfers between devices  174 us (40%)
  starting transfers between devices  86.9 us (20%)
  Pallas kernels  79.8 us (19%)
  local copies, waits for them, and re-layouts  50 us (12%)
  other arithmetic  30.6 us (7%)
    ppermute x54, waiting for transfers between devices, xor_permute(): return lax.ppermute(values, AXES, [(i, i ^ step) for i in range(total)])  136 us
    pallas_call x6, Pallas kernels, kernel_call(): pl.pallas_call(kernel, in_specs=specs, out_specs=out_specs, out_shape=lis...  77.8 us
    ppermute x54, starting transfers between devices, xor_permute(): return lax.ppermute(values, AXES, [(i, i ^ step) for i in range(total)])  63 us
    unnamed x124, local copies, waits for them, and re-layouts  24.7 us
    ppermute x10, starting transfers between devices, hop(): return lax.ppermute(values, 'fsdp', pairs)  20.6 us
    ppermute x10, waiting for transfers between devices, hop(): return lax.ppermute(values, 'fsdp', pairs)  19.4 us
    ppermute x3, waiting for transfers between devices, slot_shift(): lax.ppermute(values, 'fsdp', [(i, (i + j) % size) for i in range(size)])  19.3 us
    another operation x13, other arithmetic, merge(): jnp.stack([jnp.where(mine, got, own), jnp.where(mine, own, got)], axis=1)  9.08 us
  transfers between devices with their start and end apart: 67, of which 28 were waited for; matrix products, arithmetic and copies ran while one was open for 11% of the time, Pallas kernels for 16%

profile of v4, /device:TPU:0, one launch (start us, length us, event | category | flops | bytes accessed | tf_op | source)
XLA Modules:
  0.0 424.4 jit_solution(2596350026486152043)
XLA Ops:
  2.3 2.1 pack.1
  4.4 5.0 %collective-permute-start.2 = (bf16[160,1024]{1,0:T(8,128)(2,1)}, bf16[160,1024]{1,0:T(8,128)(2,1)S(1)}, u32[]{:S(2)}, u32[]{:S(2)}) collective-permute-start(bf16[160,1024]{1,0:T(8,128)(2,1)} %pack.1), channel_id=1, source_target_pairs={{0,3},{1,2},{2,1},{3,0},{4,7},{5,6},{6,5},{7,4},{8,11},{9,10},{10,... | collective-permute-start | bytes 983048 | tf_op jit(solution)/shard_map/ppermute | solution.py:66
  18.3 19.2 %collective-permute-done.1 = bf16[160,1024]{1,0:T(8,128)(2,1)S(1)} collective-permute-done((bf16[160,1024]{1,0:T(8,128)(2,1)}, bf16[160,1024]{1,0:T(8,128)(2,1)S(1)}, u32[]{:S(2)}, u32[]{:S(2)}) %collective-permute-start.1) | collective-permute-done | bytes 327712 | tf_op jit(solution)/shard_map/ppermute | solution.py:66
  41.9 2.5 collective-permute-start.7
  44.4 1.9 collective-permute-start.5
  46.3 8.7 %collective-permute-done.4 = bf16[1,4,160,512]{3,2,1,0:T(8,128)(2,1)} collective-permute-done((bf16[1,4,160,512]{3,2,1,0:T(8,128)(2,1)}, bf16[1,4,160,512]{3,2,1,0:T(8,128)(2,1)}, u32[]{:S(2)}, u32[]{:S(2)}) %collective-permute-start.4) | collective-permute-done | bytes 655392 | tf_op jit(solution)/shard_map/ppermute | solution.py:66
  62.3 2.8 collective-permute-start.10
  65.3 23.2 %collective-permute-done.8 = bf16[2,4,160,512]{3,2,1,0:T(8,128)(2,1)S(1)} collective-permute-done((bf16[2,4,160,512]{3,2,1,0:T(8,128)(2,1)S(1)}, bf16[2,4,160,512]{3,2,1,0:T(8,128)(2,1)S(1)}, u32[]{:S(2)}, u32[]{:S(2)}) %collective-permute-start.8) | collective-permute-done | bytes 1310752 | tf_op jit(solution)/shard_map/ppermute | solution.py:66
  93.7 8.3 %collective-permute-done.14 = bf16[1,4,96,512]{3,2,1,0:T(8,128)(2,1)S(1)} collective-permute-done((bf16[1,4,96,512]{3,2,1,0:T(8,128)(2,1)S(1)}, bf16[1,4,96,512]{3,2,1,0:T(8,128)(2,1)S(1)}, u32[]{:S(2)}, u32[]{:S(2)}) %collective-permute-start.14) | collective-permute-done | bytes 393248 | tf_op jit(solution)/shard_map/ppermute | solution.py:66
  102.4 2.3 copy-done.34
  107.7 1.7 copy.46.refs_2_.refs_5_
  109.5 14.2 %encoder.1 = (f32[16,1024]{1,0:T(8,128)S(1)}, bf16[256,1024]{1,0:T(8,128)(2,1)S(1)}, bf16[256,1024]{1,0:T(8,128)(2,1)S(1)}, bf16[256,384]{1,0:T(8,128)(2,1)S(1)}...) custom-call(s32[1,2]{1,0:T(1,128)S(1)} %copy-done.31, ...), custom_call_target="tpu_custom_call" | custom-call | flops 1073741824 | bytes 37748736 | tf_op jit(solution)/shard_map/encoder/pallas_call | solution.py:321
  125.2 1.9 select_bitcast_fusion.9
  131.8 4.6 %collective-permute-start.18 = (bf16[256,1024]{1,0:T(8,128)(2,1)S(1)}, bf16[256,1024]{1,0:T(8,128)(2,1)S(1)}, u32[]{:S(2)}, u32[]{:S(2)}) collective-permute-start(bf16[256,1024]{1,0:T(8,128)(2,1)S(1)} %get-tuple-element.216.refs_0_), channel_id=1, source_target_pairs={{0,1},{1,2},{2,3},{4,5},{5,6},{6,7},{8,9},{9,10},{10,11},{12,13},{... | collective-permute-start | bytes 1572872 | tf_op jit(solution)/shard_map/ppermute | solution.py:88
  137.3 3.7 collective-permute-done.21
  142.0 4.6 %collective-permute-done.22 = bf16[1,4,96,512]{3,2,1,0:T(8,128)(2,1)S(1)} collective-permute-done((bf16[1,4,96,512]{3,2,1,0:T(8,128)(2,1)S(1)}, bf16[1,4,96,512]{3,2,1,0:T(8,128)(2,1)S(1)}, u32[]{:S(2)}, u32[]{:S(2)}) %collective-permute-start.22) | collective-permute-done | bytes 393248 | tf_op jit(solution)/shard_map/ppermute | solution.py:66
  155.8 10.7 %collective-permute-done.27 = bf16[2,4,96,512]{3,2,1,0:T(8,128)(2,1)} collective-permute-done((bf16[2,4,96,512]{3,2,1,0:T(8,128)(2,1)}, bf16[2,4,96,512]{3,2,1,0:T(8,128)(2,1)}, u32[]{:S(2)}, u32[]{:S(2)}) %collective-permute-start.27) | collective-permute-done | bytes 786464 | tf_op jit(solution)/shard_map/ppermute | solution.py:66
  170.4 9.0 %collective-permute-done.25.refs_5_ = bf16[256,1024]{1,0:T(8,128)(2,1)S(1)} collective-permute-done((bf16[256,1024]{1,0:T(8,128)(2,1)S(1)}, bf16[256,1024]{1,0:T(8,128)(2,1)S(1)}, u32[]{:S(2)}, u32[]{:S(2)}) %collective-permute-start.25) | collective-permute-done | bytes 524320 | tf_op jit(solution)/shard_map/ppermute | solution.py:88
  179.5 11.2 %attention.1 = (bf16[256,1024]{1,0:T(8,128)(2,1)S(1)}, bf16[1024,1024]{1,0:T(8,128)(2,1)S(1)}, bf16[256,1024]{1,0:T(8,128)(2,1)S(1)}, bf16[4,256,1024]{2,1,0:T(8,128)(2,1)S(1)}, bf16[4,256,1024]{2,1,0:T(8,128)(2,1)S(1)}) custom-call(bf16[256,1024]{1,0:T(8,128)(2,1)S(1)} %copy-done.28, bf16[256,1024]{1,0:T(8,128)(2,1)S(1)} %copy-done.11, ...), custom_call_target="tpu_custom_call" | custom-call | flops 1073741824 | bytes 41943040 | tf_op jit(solution)/shard_map/attention/pallas_call | solution.py:321
  195.0 11.3 %latent.1 = (bf16[256,1024]{1,0:T(8,128)(2,1)S(1)}, f32[8,1024]{1,0:T(8,128)S(1)}, bf16[256,1024]{1,0:T(8,128)(2,1)}, f32[256,1024]{1,0:T(8,128)S(1)}, bf16[4,3,...) custom-call(bf16[256,1024]{1,0:T(8,128)(2,1)S(1)} %get-tuple-element.227.refs_0_, ...), custom_call_target="tpu_custom_call" | custom-call | flops 1073741824 | bytes 37748736 | tf_op jit(solution)/shard_map/latent/pallas_call | solution.py:321
  208.6 20.5 %attention_back.1 = (bf16[3,256,1024]{2,1,0:T(8,128)(2,1)S(1)}, f32[256,1024]{1,0:T(8,128)S(1)}, bf16[4,3,128,1024]{3,2,1,0:T(8,128)(2,1)}, bf16[4,3,128,1024]{3,2,1,0:T(8,128)(2,1)}) custom-call(bf16[256,1024]{1,0:T(8,128)(2,1)S(1)} %get-tuple-element.232.refs_0_, bf16[4,256,1024]{2,1,0:T(8,128)(2,1)S(1)} %get-tuple-element.233.refs_1_, ...), custom_call_target="tpu_custom_call" | custom-call | flops 1073741824 | bytes 75497472 | tf_op jit(solution)/shard_map/attention_back/pallas_call | solution.py:321
  234.8 2.1 fusion.53
  240.2 2.8 collective-permute-start.31
  243.2 2.2 fusion.51
  245.4 10.3 %collective-permute-done.31 = bf16[256,1024]{1,0:T(8,128)(2,1)S(1)} collective-permute-done((bf16[256,1024]{1,0:T(8,128)(2,1)S(1)}, bf16[256,1024]{1,0:T(8,128)(2,1)S(1)}, u32[]{:S(2)}, u32[]{:S(2)}) %collective-permute-start.31) | collective-permute-done | bytes 524320 | tf_op jit(solution)/shard_map/ppermute | solution.py:88
  260.4 4.8 %collective-permute-start.35 = (bf16[256,1024]{1,0:T(8,128)(2,1)S(1)}, bf16[256,1024]{1,0:T(8,128)(2,1)S(1)}, u32[]{:S(2)}, u32[]{:S(2)}) collective-permute-start(bf16[256,1024]{1,0:T(8,128)(2,1)S(1)} %get-tuple-element.477), channel_id=1, source_target_pairs={{0,1},{1,2},{2,3},{4,5},{5,6},{6,7},{8,9},{9,10},{10,11},{12,13},{... | collective-permute-start | bytes 1572872 | tf_op jit(solution)/shard_map/ppermute | solution.py:88
  267.6 7.6 %collective-permute-done.38 = bf16[1,3,128,512]{3,2,1,0:T(8,128)(2,1)S(1)} collective-permute-done((bf16[1,3,128,512]{3,2,1,0:T(8,128)(2,1)S(1)}, bf16[1,3,128,512]{3,2,1,0:T(8,128)(2,1)S(1)}, u32[]{:S(2)}, u32[]{:S(2)}) %collective-permute-start.38) | collective-permute-done | bytes 393248 | tf_op jit(solution)/shard_map/ppermute | solution.py:66
  276.4 2.9 collective-permute-start.44
  285.3 6.9 %encoder_back.1 = (f32[256,1024]{1,0:T(8,128)S(1)}, f32[8,1024]{1,0:T(8,128)S(1)}, bf16[4,2,128,1024]{3,2,1,0:T(8,128)(2,1)S(1)}, bf16[4,2,128,1024]{3,2,1,0:T(8,128)(2,1)S(1)}) custom-call(f32[256,1024]{1,0:T(8,128)S(1)} %copy-done.19, f32[256,1024]{1,0:T(8,128)S(1)} %get-tuple-element.238.refs_1_, f32[256,1024]{1,0:T(8,128)S(1)} %copy-done.3, ...), custom_call_target="tpu_custom_call" | custom-call | flops 1073741824 | bytes 37748736 | tf_op jit(solution)/shard_map/encoder_back/pallas_call | solution.py:321
  295.3 13.8 %cross_back.1 = (f32[4,264,512]{2,1,0:T(8,128)}, f32[264,128]{1,0:T(8,128)S(1)}, f32[256,1024]{1,0:T(8,128)}, bf16[4,3,128,1024]{3,2,1,0:T(8,128)(2,1)}, bf16[4,3,128,1024]{3,2,1,0:T(8,128)(2,1)}) custom-call(f32[256,1024]{1,0:T(8,128)S(1)} %get-tuple-element.263.refs_0_, bf16[256,1024]{1,0:T(8,128)(2,1)S(1)} %bitcast.487, bf16[256,1024]{1,0:T(8,128)(2,1)S(1)} %copy-done.24, ...), custom_call_target="tpu_custom_call" | custom-call | flops 1073741824 | bytes 52428800 | tf_op jit(solution)/shard_map/cross_back/pallas_call | solution.py:321
  321.6 2.6 collective-permute-start.50
  324.4 5.9 %collective-permute-done.50 = f32[2,261]{0,1:T(8,128)S(1)} collective-permute-done((f32[2,261]{0,1:T(8,128)S(1)}, f32[2,261]{0,1:T(8,128)S(1)}, u32[]{:S(2)}, u32[]{:S(2)}) %collective-permute-start.50) | collective-permute-done | bytes 2120 | tf_op jit(solution)/shard_map/ppermute | solution.py:66
  330.6 2.2 fusion.49
  338.6 2.4 collective-permute-start.51
  342.4 10.4 %collective-permute-done.51 = bf16[264,512]{1,0:T(8,128)(2,1)S(1)} collective-permute-done((bf16[264,512]{1,0:T(8,128)(2,1)S(1)}, bf16[264,512]{1,0:T(8,128)(2,1)S(1)}, u32[]{:S(2)}, u32[]{:S(2)}) %collective-permute-start.51) | collective-permute-done | bytes 270368 | tf_op jit(solution)/shard_map/ppermute | solution.py:84
  354.0 7.6 %collective-permute-done.52 = bf16[264,512]{1,0:T(8,128)(2,1)S(1)} collective-permute-done((bf16[264,512]{1,0:T(8,128)(2,1)S(1)}, bf16[264,512]{1,0:T(8,128)(2,1)S(1)}, u32[]{:S(2)}, u32[]{:S(2)}) %collective-permute-start.52) | collective-permute-done | bytes 270368 | tf_op jit(solution)/shard_map/ppermute | solution.py:84
  361.7 2.1 collective-permute-done.54
  363.8 1.8 collective-permute-done.55
  367.2 2.0 collective-permute-start.58
  371.9 2.6 collective-permute-start.56
  374.7 2.2 collective-permute-done.58
  376.9 7.3 %collective-permute-done.57 = bf16[3,32,1024]{2,1,0:T(8,128)(2,1)S(1)} collective-permute-done((bf16[3,32,1024]{2,1,0:T(8,128)(2,1)S(1)}, bf16[3,32,1024]{2,1,0:T(8,128)(2,1)S(1)}, u32[]{:S(2)}, u32[]{:S(2)}) %collective-permute-start.57) | collective-permute-done | bytes 196640 | tf_op jit(solution)/shard_map/ppermute | solution.py:66
  386.1 2.0 collective-permute-start.66
  388.1 1.7 collective-permute-start.65
  391.6 3.8 collective-permute-done.62
  395.4 1.8 collective-permute-start.63
  398.1 2.3 collective-permute-done.63
  401.3 17.6 %collective-permute-done.65 = bf16[5,32,1024]{2,1,0:T(8,128)(2,1)S(1)} collective-permute-done((bf16[5,32,1024]{2,1,0:T(8,128)(2,1)S(1)}, bf16[5,32,1024]{2,1,0:T(8,128)(2,1)S(1)}, u32[]{:S(2)}, u32[]{:S(2)}) %collective-permute-start.65) | collective-permute-done | bytes 327712 | tf_op jit(solution)/shard_map/ppermute | solution.py:66
  (371 shorter events, 120.7 us)
Async XLA Ops:
  9.5 28.1 %collective-permute-start.1 = (bf16[160,1024]{1,0:T(8,128)(2,1)}, bf16[160,1024]{1,0:T(8,128)(2,1)S(1)}, u32[]{:S(2)}, u32[]{:S(2)}) collective-permute-start(bf16[160,1024]{1,0:T(8,128)(2,1)} %pack.1), channel_id=1, source_target_pairs={{0,2},{1,3},{2,0},{3,1},{4,6},{5,7},{6,4},{7,5},{8,10},{9,11},{10,... | collective-permute-start | bytes 983048 | tf_op jit(solution)/shard_map/ppermute | solution.py:66
  9.5 28.1 %collective-permute-start = (bf16[160,1024]{1,0:T(8,128)(2,1)}, bf16[160,1024]{1,0:T(8,128)(2,1)S(1)}, u32[]{:S(2)}, u32[]{:S(2)}) collective-permute-start(bf16[160,1024]{1,0:T(8,128)(2,1)} %pack.1), channel_id=1, source_target_pairs={{0,1},{1,0},{2,3},{3,2},{4,5},{5,4},{6,7},{7,6},{8,9},{9,8},{10,11... | collective-permute-start | bytes 983048 | tf_op jit(solution)/shard_map/ppermute | solution.py:66
  38.9 16.1 %collective-permute-start.4 = (bf16[1,4,160,512]{3,2,1,0:T(8,128)(2,1)}, bf16[1,4,160,512]{3,2,1,0:T(8,128)(2,1)}, u32[]{:S(2)}, u32[]{:S(2)}) collective-permute-start(bf16[1,4,160,512]{3,2,1,0:T(8,128)(2,1)} %get-tuple-element.442), channel_id=1, source_target_pairs={{0,16},{1,17},{2,18},{3,19},{4,20},{5,21},{6,22},{7,23},{8,24},{9,... | collective-permute-start | bytes 1966088 | tf_op jit(solution)/shard_map/ppermute | solution.py:66
  40.4 15.6 %collective-permute-start.3 = (bf16[1,4,160,512]{3,2,1,0:T(8,128)(2,1)S(1)}, bf16[1,4,160,512]{3,2,1,0:T(8,128)(2,1)}, u32[]{:S(2)}, u32[]{:S(2)}) collective-permute-start(bf16[1,4,160,512]{3,2,1,0:T(8,128)(2,1)S(1)} %get-tuple-element.443), channel_id=1, source_target_pairs={{0,8},{1,9},{2,10},{3,11},{4,12},{5,13},{6,14},{7,15},{8,0},{9,1},... | collective-permute-start | bytes 1966088 | tf_op jit(solution)/shard_map/ppermute | solution.py:66
  41.9 15.8 %collective-permute-start.7 = (bf16[96,1024]{1,0:T(8,128)(2,1)S(1)}, bf16[96,1024]{1,0:T(8,128)(2,1)S(1)}, u32[]{:S(2)}, u32[]{:S(2)}) collective-permute-start(bf16[96,1024]{1,0:T(8,128)(2,1)S(1)} %bitcast.555), channel_id=1, source_target_pairs={{0,3},{1,2},{2,1},{3,0},{4,7},{5,6},{6,5},{7,4},{8,11},{9,10},{10,... | collective-permute-start | bytes 589832 | tf_op jit(solution)/shard_map/ppermute | solution.py:66
  44.4 15.1 %collective-permute-start.6 = (bf16[96,1024]{1,0:T(8,128)(2,1)S(1)}, bf16[96,1024]{1,0:T(8,128)(2,1)S(1)}, u32[]{:S(2)}, u32[]{:S(2)}) collective-permute-start(bf16[96,1024]{1,0:T(8,128)(2,1)S(1)} %bitcast.556), channel_id=1, source_target_pairs={{0,2},{1,3},{2,0},{3,1},{4,6},{5,7},{6,4},{7,5},{8,10},{9,11},{10,... | collective-permute-start | bytes 589832 | tf_op jit(solution)/shard_map/ppermute | solution.py:66
  44.4 15.1 %collective-permute-start.5 = (bf16[96,1024]{1,0:T(8,128)(2,1)S(1)}, bf16[96,1024]{1,0:T(8,128)(2,1)S(1)}, u32[]{:S(2)}, u32[]{:S(2)}) collective-permute-start(bf16[96,1024]{1,0:T(8,128)(2,1)S(1)} %bitcast.557), channel_id=1, source_target_pairs={{0,1},{1,0},{2,3},{3,2},{4,5},{5,4},{6,7},{7,6},{8,9},{9,8},{10,11... | collective-permute-start | bytes 589832 | tf_op jit(solution)/shard_map/ppermute | solution.py:66
  59.5 29.0 %collective-permute-start.8 = (bf16[2,4,160,512]{3,2,1,0:T(8,128)(2,1)S(1)}, bf16[2,4,160,512]{3,2,1,0:T(8,128)(2,1)S(1)}, u32[]{:S(2)}, u32[]{:S(2)}) collective-permute-start(bf16[2,4,160,512]{3,2,1,0:T(8,128)(2,1)S(1)} %get-tuple-element.189), channel_id=1, source_target_pairs={{0,16},{1,17},{2,18},{3,19},{4,20},{5,21},{6,22},{7,23},{8,24},{9,... | collective-permute-start | bytes 3932168 | tf_op jit(solution)/shard_map/ppermute | solution.py:66
  60.0 28.7 %collective-permute-start.9 = (bf16[2,4,160,512]{3,2,1,0:T(8,128)(2,1)S(1)}, bf16[2,4,160,512]{3,2,1,0:T(8,128)(2,1)S(1)}, u32[]{:S(2)}, u32[]{:S(2)}) collective-permute-start(bf16[2,4,160,512]{3,2,1,0:T(8,128)(2,1)S(1)} %get-tuple-element.190), channel_id=1, source_target_pairs={{0,8},{1,9},{2,10},{3,11},{4,12},{5,13},{6,14},{7,15},{8,0},{9,1},... | collective-permute-start | bytes 3932168 | tf_op jit(solution)/shard_map/ppermute | solution.py:66
  60.6 29.1 %collective-permute-start.12 = (bf16[96,1024]{1,0:T(8,128)(2,1)S(1)}, bf16[96,1024]{1,0:T(8,128)(2,1)S(1)}, u32[]{:S(2)}, u32[]{:S(2)}) collective-permute-start(bf16[96,1024]{1,0:T(8,128)(2,1)S(1)} %pad_maximum_fusion.18), channel_id=1, source_target_pairs={{0,3},{1,2},{2,1},{3,0},{4,7},{5,6},{6,5},{7,4},{8,11},{9,10},{10,... | collective-permute-start | bytes 589832 | tf_op jit(solution)/shard_map/ppermute | solution.py:66
  62.3 27.4 %collective-permute-start.11 = (bf16[96,1024]{1,0:T(8,128)(2,1)S(1)}, bf16[96,1024]{1,0:T(8,128)(2,1)S(1)}, u32[]{:S(2)}, u32[]{:S(2)}) collective-permute-start(bf16[96,1024]{1,0:T(8,128)(2,1)S(1)} %pad_maximum_fusion.18), channel_id=1, source_target_pairs={{0,2},{1,3},{2,0},{3,1},{4,6},{5,7},{6,4},{7,5},{8,10},{9,11},{10,... | collective-permute-start | bytes 589832 | tf_op jit(solution)/shard_map/ppermute | solution.py:66
  62.3 27.4 %collective-permute-start.10 = (bf16[96,1024]{1,0:T(8,128)(2,1)S(1)}, bf16[96,1024]{1,0:T(8,128)(2,1)S(1)}, u32[]{:S(2)}, u32[]{:S(2)}) collective-permute-start(bf16[96,1024]{1,0:T(8,128)(2,1)S(1)} %pad_maximum_fusion.18), channel_id=1, source_target_pairs={{0,1},{1,0},{2,3},{3,2},{4,5},{5,4},{6,7},{7,6},{8,9},{9,8},{10,11... | collective-permute-start | bytes 589832 | tf_op jit(solution)/shard_map/ppermute | solution.py:66
  104.7 20.5 %collective-permute-start.17 = (bf16[2,4,96,512]{3,2,1,0:T(8,128)(2,1)S(1)}, bf16[2,4,96,512]{3,2,1,0:T(8,128)(2,1)}, u32[]{:S(2)}, u32[]{:S(2)}) collective-permute-start(bf16[2,4,96,512]{3,2,1,0:T(8,128)(2,1)S(1)} %maximum_bitcast_fusion.3), channel_id=1, source_target_pairs={{0,8},{1,9},{2,10},{3,11},{4,12},{5,13},{6,14},{7,15},{8,0},{9,1},... | collective-permute-start | bytes 2359304 | tf_op jit(solution)/shard_map/ppermute | solution.py:66
  106.2 21.2 %collective-permute-start.16 = (bf16[2,4,96,512]{3,2,1,0:T(8,128)(2,1)S(1)}, bf16[2,4,96,512]{3,2,1,0:T(8,128)(2,1)}, u32[]{:S(2)}, u32[]{:S(2)}) collective-permute-start(bf16[2,4,96,512]{3,2,1,0:T(8,128)(2,1)S(1)} %maximum_bitcast_fusion.2), channel_id=1, source_target_pairs={{0,16},{1,17},{2,18},{3,19},{4,20},{5,21},{6,22},{7,23},{8,24},{9,... | collective-permute-start | bytes 2359304 | tf_op jit(solution)/shard_map/ppermute | solution.py:66
  129.4 18.3 %collective-permute-start.20 = (bf16[4,4,96,1024]{3,2,1,0:T(8,128)(2,1)S(1)}, bf16[4,4,96,1024]{3,2,1,0:T(8,128)(2,1)S(1)}, u32[]{:S(2)}, u32[]{:S(2)}) collective-permute-start(bf16[4,4,96,1024]{3,2,1,0:T(8,128)(2,1)S(1)} %pad_maximum_fusion.refs_6_.refs_5_), channel_id=1, source_target_pairs={{0,4},{1,5},{2,6},{3,7},{4,0},{5,1},{6,2},{7,3},{8,12},{9,13},{10,... | collective-permute-start | bytes 9437192 | tf_op jit(solution)/shard_map/ppermute | solution.py:66
  130.5 17.2 %collective-permute-start.19 = (bf16[256,1024]{1,0:T(8,128)(2,1)S(1)}, bf16[256,1024]{1,0:T(8,128)(2,1)S(1)}, u32[]{:S(2)}, u32[]{:S(2)}) collective-permute-start(bf16[256,1024]{1,0:T(8,128)(2,1)S(1)} %get-tuple-element.216.refs_0_), channel_id=1, source_target_pairs={{3,2},{2,1},{1,0},{7,6},{6,5},{5,4},{11,10},{10,9},{9,8},{15,14},{... | collective-permute-start | bytes 1572872 | tf_op jit(solution)/shard_map/ppermute | solution.py:88
  131.8 15.9 %collective-permute-start.18 = (bf16[256,1024]{1,0:T(8,128)(2,1)S(1)}, bf16[256,1024]{1,0:T(8,128)(2,1)S(1)}, u32[]{:S(2)}, u32[]{:S(2)}) collective-permute-start(bf16[256,1024]{1,0:T(8,128)(2,1)S(1)} %get-tuple-element.216.refs_0_), channel_id=1, source_target_pairs={{0,1},{1,2},{2,3},{4,5},{5,6},{6,7},{8,9},{9,10},{10,11},{12,13},{... | collective-permute-start | bytes 1572872 | tf_op jit(solution)/shard_map/ppermute | solution.py:88
  148.5 18.0 %collective-permute-start.27 = (bf16[2,4,96,512]{3,2,1,0:T(8,128)(2,1)}, bf16[2,4,96,512]{3,2,1,0:T(8,128)(2,1)}, u32[]{:S(2)}, u32[]{:S(2)}) collective-permute-start(bf16[2,4,96,512]{3,2,1,0:T(8,128)(2,1)} %maximum_bitcast_fusion.5), channel_id=1, source_target_pairs={{0,8},{1,9},{2,10},{3,11},{4,12},{5,13},{6,14},{7,15},{8,0},{9,1},... | collective-permute-start | bytes 2359304 | tf_op jit(solution)/shard_map/ppermute | solution.py:66
  150.2 18.1 %collective-permute-start.26 = (bf16[2,4,96,512]{3,2,1,0:T(8,128)(2,1)}, bf16[2,4,96,512]{3,2,1,0:T(8,128)(2,1)}, u32[]{:S(2)}, u32[]{:S(2)}) collective-permute-start(bf16[2,4,96,512]{3,2,1,0:T(8,128)(2,1)} %maximum_bitcast_fusion.4), channel_id=1, source_target_pairs={{0,16},{1,17},{2,18},{3,19},{4,20},{5,21},{6,22},{7,23},{8,24},{9,... | collective-permute-start | bytes 2359304 | tf_op jit(solution)/shard_map/ppermute | solution.py:66
  151.0 28.4 %collective-permute-start.23 = (bf16[256,1024]{1,0:T(8,128)(2,1)}, bf16[256,1024]{1,0:T(8,128)(2,1)S(1)}, u32[]{:S(2)}, u32[]{:S(2)}) collective-permute-start(bf16[256,1024]{1,0:T(8,128)(2,1)} %copy-done.10), channel_id=1, source_target_pairs={{1,2},{2,3},{5,6},{6,7},{9,10},{10,11},{13,14},{14,15},{17,18},{18... | collective-permute-start | bytes 1572872 | tf_op jit(solution)/shard_map/ppermute | solution.py:88
  151.7 27.8 %collective-permute-start.24 = (bf16[256,1024]{1,0:T(8,128)(2,1)}, bf16[256,1024]{1,0:T(8,128)(2,1)S(1)}, u32[]{:S(2)}, u32[]{:S(2)}) collective-permute-start(bf16[256,1024]{1,0:T(8,128)(2,1)} %copy-done.8), channel_id=1, source_target_pairs={{2,1},{1,0},{6,5},{5,4},{10,9},{9,8},{14,13},{13,12},{18,17},{17,1... | collective-permute-start | bytes 1572872 | tf_op jit(solution)/shard_map/ppermute | solution.py:88
  154.1 25.3 %collective-permute-start.25 = (bf16[256,1024]{1,0:T(8,128)(2,1)S(1)}, bf16[256,1024]{1,0:T(8,128)(2,1)S(1)}, u32[]{:S(2)}, u32[]{:S(2)}) collective-permute-start(bf16[256,1024]{1,0:T(8,128)(2,1)S(1)} %broadcast_select_fusion.1), channel_id=1, source_target_pairs={{1,3},{2,0},{5,7},{6,4},{9,11},{10,8},{13,15},{14,12},{17,19},{18,... | collective-permute-start | bytes 1572872 | tf_op jit(solution)/shard_map/ppermute | solution.py:88
  208.0 26.7 %collective-permute-start.32 = (bf16[4,3,128,1024]{3,2,1,0:T(8,128)(2,1)}, bf16[4,3,128,1024]{3,2,1,0:T(8,128)(2,1)}, u32[]{:S(2)}, u32[]{:S(2)}) collective-permute-start(bf16[4,3,128,1024]{3,2,1,0:T(8,128)(2,1)} %get-tuple-element.247), channel_id=1, source_target_pairs={{0,4},{1,5},{2,6},{3,7},{4,0},{5,1},{6,2},{7,3},{8,12},{9,13},{10,... | collective-permute-start | bytes 9437192 | tf_op jit(solution)/shard_map/ppermute | solution.py:66
  230.2 15.2 %collective-permute-start.30 = (bf16[256,1024]{1,0:T(8,128)(2,1)S(1)}, bf16[256,1024]{1,0:T(8,128)(2,1)S(1)}, u32[]{:S(2)}, u32[]{:S(2)}) collective-permute-start(bf16[256,1024]{1,0:T(8,128)(2,1)S(1)} %get-tuple-element.430), channel_id=1, source_target_pairs={{3,2},{2,1},{7,6},{6,5},{11,10},{10,9},{15,14},{14,13},{19,18},{18... | collective-permute-start | bytes 1572872 | tf_op jit(solution)/shard_map/ppermute | solution.py:88
  231.0 14.4 %collective-permute-start.29 = (bf16[256,1024]{1,0:T(8,128)(2,1)S(1)}, bf16[256,1024]{1,0:T(8,128)(2,1)S(1)}, u32[]{:S(2)}, u32[]{:S(2)}) collective-permute-start(bf16[256,1024]{1,0:T(8,128)(2,1)S(1)} %get-tuple-element.430), channel_id=1, source_target_pairs={{0,1},{1,2},{4,5},{5,6},{8,9},{9,10},{12,13},{13,14},{16,17},{17,1... | collective-permute-start | bytes 1572872 | tf_op jit(solution)/shard_map/ppermute | solution.py:88
  237.1 20.0 %collective-permute-start.33 = (bf16[2,3,128,512]{3,2,1,0:T(8,128)(2,1)S(1)}, bf16[2,3,128,512]{3,2,1,0:T(8,128)(2,1)S(1)}, u32[]{:S(2)}, u32[]{:S(2)}) collective-permute-start(bf16[2,3,128,512]{3,2,1,0:T(8,128)(2,1)S(1)} %fusion.9), channel_id=1, source_target_pairs={{0,8},{1,9},{2,10},{3,11},{4,12},{5,13},{6,14},{7,15},{8,0},{9,1},... | collective-permute-start | bytes 2359304 | tf_op jit(solution)/shard_map/ppermute | solution.py:66
  238.5 19.7 %collective-permute-start.34 = (bf16[2,3,128,512]{3,2,1,0:T(8,128)(2,1)S(1)}, bf16[2,3,128,512]{3,2,1,0:T(8,128)(2,1)S(1)}, u32[]{:S(2)}, u32[]{:S(2)}) collective-permute-start(bf16[2,3,128,512]{3,2,1,0:T(8,128)(2,1)S(1)} %fusion.10), channel_id=1, source_target_pairs={{0,16},{1,17},{2,18},{3,19},{4,20},{5,21},{6,22},{7,23},{8,24},{9,... | collective-permute-start | bytes 2359304 | tf_op jit(solution)/shard_map/ppermute | solution.py:66
  240.2 15.5 %collective-permute-start.31 = (bf16[256,1024]{1,0:T(8,128)(2,1)S(1)}, bf16[256,1024]{1,0:T(8,128)(2,1)S(1)}, u32[]{:S(2)}, u32[]{:S(2)}) collective-permute-start(bf16[256,1024]{1,0:T(8,128)(2,1)S(1)} %broadcast_select_fusion), channel_id=1, source_target_pairs={{0,2},{3,1},{4,6},{7,5},{8,10},{11,9},{12,14},{15,13},{16,18},{19,... | collective-permute-start | bytes 1572872 | tf_op jit(solution)/shard_map/ppermute | solution.py:88
  259.1 16.8 %collective-permute-start.36 = (bf16[256,1024]{1,0:T(8,128)(2,1)S(1)}, bf16[256,1024]{1,0:T(8,128)(2,1)S(1)}, u32[]{:S(2)}, u32[]{:S(2)}) collective-permute-start(bf16[256,1024]{1,0:T(8,128)(2,1)S(1)} %get-tuple-element.476), channel_id=1, source_target_pairs={{3,2},{2,1},{1,0},{7,6},{6,5},{5,4},{11,10},{10,9},{9,8},{15,14},{... | collective-permute-start | bytes 1572872 | tf_op jit(solution)/shard_map/ppermute | solution.py:88
  260.4 15.5 %collective-permute-start.35 = (bf16[256,1024]{1,0:T(8,128)(2,1)S(1)}, bf16[256,1024]{1,0:T(8,128)(2,1)S(1)}, u32[]{:S(2)}, u32[]{:S(2)}) collective-permute-start(bf16[256,1024]{1,0:T(8,128)(2,1)S(1)} %get-tuple-element.477), channel_id=1, source_target_pairs={{0,1},{1,2},{2,3},{4,5},{5,6},{6,7},{8,9},{9,10},{10,11},{12,13},{... | collective-permute-start | bytes 1572872 | tf_op jit(solution)/shard_map/ppermute | solution.py:88
  276.4 33.6 %collective-permute-start.44 = (bf16[3,32,1024]{2,1,0:T(8,128)(2,1)S(1)}, bf16[3,32,1024]{2,1,0:T(8,128)(2,1)S(1)}, u32[]{:S(2)}, u32[]{:S(2)}) collective-permute-start(bf16[3,32,1024]{2,1,0:T(8,128)(2,1)S(1)} %pad_maximum_fusion.21), channel_id=1, source_target_pairs={{0,3},{1,2},{2,1},{3,0},{4,7},{5,6},{6,5},{7,4},{8,11},{9,10},{10,... | collective-permute-start | bytes 589832 | tf_op jit(solution)/shard_map/ppermute | solution.py:66
  279.3 30.8 %collective-permute-start.43 = (bf16[3,32,1024]{2,1,0:T(8,128)(2,1)S(1)}, bf16[3,32,1024]{2,1,0:T(8,128)(2,1)S(1)}, u32[]{:S(2)}, u32[]{:S(2)}) collective-permute-start(bf16[3,32,1024]{2,1,0:T(8,128)(2,1)S(1)} %pad_maximum_fusion.20), channel_id=1, source_target_pairs={{0,2},{1,3},{2,0},{3,1},{4,6},{5,7},{6,4},{7,5},{8,10},{9,11},{10,... | collective-permute-start | bytes 589832 | tf_op jit(solution)/shard_map/ppermute | solution.py:66
  280.0 30.0 %collective-permute-start.42 = (bf16[3,32,1024]{2,1,0:T(8,128)(2,1)S(1)}, bf16[3,32,1024]{2,1,0:T(8,128)(2,1)S(1)}, u32[]{:S(2)}, u32[]{:S(2)}) collective-permute-start(bf16[3,32,1024]{2,1,0:T(8,128)(2,1)S(1)} %pad_maximum_fusion.19), channel_id=1, source_target_pairs={{0,1},{1,0},{2,3},{3,2},{4,5},{5,4},{6,7},{7,6},{8,9},{9,8},{10,11... | collective-permute-start | bytes 589832 | tf_op jit(solution)/shard_map/ppermute | solution.py:66
  282.6 28.4 %collective-permute-start.41 = (bf16[2,3,128,512]{3,2,1,0:T(8,128)(2,1)S(1)}, bf16[2,3,128,512]{3,2,1,0:T(8,128)(2,1)S(1)}, u32[]{:S(2)}, u32[]{:S(2)}) collective-permute-start(bf16[2,3,128,512]{3,2,1,0:T(8,128)(2,1)S(1)} %fusion.12), channel_id=1, source_target_pairs={{0,16},{1,17},{2,18},{3,19},{4,20},{5,21},{6,22},{7,23},{8,24},{9,... | collective-permute-start | bytes 2359304 | tf_op jit(solution)/shard_map/ppermute | solution.py:66
  283.8 27.2 %collective-permute-start.40 = (bf16[2,3,128,512]{3,2,1,0:T(8,128)(2,1)S(1)}, bf16[2,3,128,512]{3,2,1,0:T(8,128)(2,1)S(1)}, u32[]{:S(2)}, u32[]{:S(2)}) collective-permute-start(bf16[2,3,128,512]{3,2,1,0:T(8,128)(2,1)S(1)} %fusion.11), channel_id=1, source_target_pairs={{0,8},{1,9},{2,10},{3,11},{4,12},{5,13},{6,14},{7,15},{8,0},{9,1},... | collective-permute-start | bytes 2359304 | tf_op jit(solution)/shard_map/ppermute | solution.py:66
  312.7 17.9 %collective-permute-start.46 = (bf16[4,3,128,1024]{3,2,1,0:T(8,128)(2,1)}, bf16[4,3,128,1024]{3,2,1,0:T(8,128)(2,1)}, u32[]{:S(2)}, u32[]{:S(2)}) collective-permute-start(bf16[4,3,128,1024]{3,2,1,0:T(8,128)(2,1)} %get-tuple-element.296), channel_id=1, source_target_pairs={{0,4},{1,5},{2,6},{3,7},{4,0},{5,1},{6,2},{7,3},{8,12},{9,13},{10,... | collective-permute-start | bytes 9437192 | tf_op jit(solution)/shard_map/ppermute | solution.py:66
  312.7 17.6 %collective-permute-start.45 = (bf16[4,2,128,1024]{3,2,1,0:T(8,128)(2,1)}, bf16[4,2,128,1024]{3,2,1,0:T(8,128)(2,1)S(1)}, u32[]{:S(2)}, u32[]{:S(2)}) collective-permute-start(bf16[4,2,128,1024]{3,2,1,0:T(8,128)(2,1)} %copy-done.32), channel_id=1, source_target_pairs={{0,4},{1,5},{2,6},{3,7},{4,0},{5,1},{6,2},{7,3},{8,12},{9,13},{10,... | collective-permute-start | bytes 6291464 | tf_op jit(solution)/shard_map/ppermute | solution.py:66
  316.9 15.9 %collective-permute-start.48 = (bf16[1,3,128,512]{3,2,1,0:T(8,128)(2,1)S(1)}, bf16[1,3,128,512]{3,2,1,0:T(8,128)(2,1)S(1)}, u32[]{:S(2)}, u32[]{:S(2)}) collective-permute-start(bf16[1,3,128,512]{3,2,1,0:T(8,128)(2,1)S(1)} %add_convert_fusion.9), channel_id=1, source_target_pairs={{0,8},{1,9},{2,10},{3,11},{4,12},{5,13},{6,14},{7,15},{8,0},{9,1},... | collective-permute-start | bytes 1179656 | tf_op jit(solution)/shard_map/ppermute | solution.py:66
  318.6 14.2 %collective-permute-start.47 = (bf16[1,3,128,512]{3,2,1,0:T(8,128)(2,1)S(1)}, bf16[1,3,128,512]{3,2,1,0:T(8,128)(2,1)S(1)}, u32[]{:S(2)}, u32[]{:S(2)}) collective-permute-start(bf16[1,3,128,512]{3,2,1,0:T(8,128)(2,1)S(1)} %add_convert_fusion.10), channel_id=1, source_target_pairs={{0,16},{1,17},{2,18},{3,19},{4,20},{5,21},{6,22},{7,23},{8,24},{9,... | collective-permute-start | bytes 1179656 | tf_op jit(solution)/shard_map/ppermute | solution.py:66
  333.7 30.1 %collective-permute-start.54 = (bf16[2,5,128,512]{3,2,1,0:T(8,128)(2,1)S(1)}, bf16[2,5,128,512]{3,2,1,0:T(8,128)(2,1)S(1)}, u32[]{:S(2)}, u32[]{:S(2)}) collective-permute-start(bf16[2,5,128,512]{3,2,1,0:T(8,128)(2,1)S(1)} %fusion.3), channel_id=1, source_target_pairs={{0,8},{1,9},{2,10},{3,11},{4,12},{5,13},{6,14},{7,15},{8,0},{9,1},... | collective-permute-start | bytes 3932168 | tf_op jit(solution)/shard_map/ppermute | solution.py:66
  335.7 29.9 %collective-permute-start.55 = (bf16[2,5,128,512]{3,2,1,0:T(8,128)(2,1)S(1)}, bf16[2,5,128,512]{3,2,1,0:T(8,128)(2,1)S(1)}, u32[]{:S(2)}, u32[]{:S(2)}) collective-permute-start(bf16[2,5,128,512]{3,2,1,0:T(8,128)(2,1)S(1)} %fusion.4), channel_id=1, source_target_pairs={{0,16},{1,17},{2,18},{3,19},{4,20},{5,21},{6,22},{7,23},{8,24},{9,... | collective-permute-start | bytes 3932168 | tf_op jit(solution)/shard_map/ppermute | solution.py:66
  341.3 20.3 %collective-permute-start.52 = (bf16[264,512]{1,0:T(8,128)(2,1)S(1)}, bf16[264,512]{1,0:T(8,128)(2,1)S(1)}, u32[]{:S(2)}, u32[]{:S(2)}) collective-permute-start(bf16[264,512]{1,0:T(8,128)(2,1)S(1)} %get-tuple-element.452), channel_id=1, source_target_pairs={{0,2},{1,3},{2,0},{3,1},{4,6},{5,7},{6,4},{7,5},{8,10},{9,11},{10,... | collective-permute-start | bytes 811016 | tf_op jit(solution)/shard_map/ppermute | solution.py:84
  369.3 14.9 %collective-permute-start.57 = (bf16[3,32,1024]{2,1,0:T(8,128)(2,1)S(1)}, bf16[3,32,1024]{2,1,0:T(8,128)(2,1)S(1)}, u32[]{:S(2)}, u32[]{:S(2)}) collective-permute-start(bf16[3,32,1024]{2,1,0:T(8,128)(2,1)S(1)} %pad_maximum_fusion.23), channel_id=1, source_target_pairs={{0,2},{1,3},{2,0},{3,1},{4,6},{5,7},{6,4},{7,5},{8,10},{9,11},{10,... | collective-permute-start | bytes 589832 | tf_op jit(solution)/shard_map/ppermute | solution.py:66
  369.3 15.7 %collective-permute-start.60 = (bf16[1,5,128,512]{3,2,1,0:T(8,128)(2,1)S(1)}, bf16[1,5,128,512]{3,2,1,0:T(8,128)(2,1)S(1)}, u32[]{:S(2)}, u32[]{:S(2)}) collective-permute-start(bf16[1,5,128,512]{3,2,1,0:T(8,128)(2,1)S(1)} %add_convert_fusion.7), channel_id=1, source_target_pairs={{0,8},{1,9},{2,10},{3,11},{4,12},{5,13},{6,14},{7,15},{8,0},{9,1},... | collective-permute-start | bytes 1966088 | tf_op jit(solution)/shard_map/ppermute | solution.py:66
  370.3 14.7 %collective-permute-start.59 = (bf16[1,5,128,512]{3,2,1,0:T(8,128)(2,1)S(1)}, bf16[1,5,128,512]{3,2,1,0:T(8,128)(2,1)S(1)}, u32[]{:S(2)}, u32[]{:S(2)}) collective-permute-start(bf16[1,5,128,512]{3,2,1,0:T(8,128)(2,1)S(1)} %add_convert_fusion.8), channel_id=1, source_target_pairs={{0,16},{1,17},{2,18},{3,19},{4,20},{5,21},{6,22},{7,23},{8,24},{9,... | collective-permute-start | bytes 1966088 | tf_op jit(solution)/shard_map/ppermute | solution.py:66
  386.1 15.2 %collective-permute-start.66 = (bf16[5,32,1024]{2,1,0:T(8,128)(2,1)S(1)}, bf16[5,32,1024]{2,1,0:T(8,128)(2,1)S(1)}, u32[]{:S(2)}, u32[]{:S(2)}) collective-permute-start(bf16[5,32,1024]{2,1,0:T(8,128)(2,1)S(1)} %pad_maximum_fusion.17), channel_id=1, source_target_pairs={{0,3},{1,2},{2,1},{3,0},{4,7},{5,6},{6,5},{7,4},{8,11},{9,10},{10,... | collective-permute-start | bytes 983048 | tf_op jit(solution)/shard_map/ppermute | solution.py:66
  388.1 30.8 %collective-permute-start.65 = (bf16[5,32,1024]{2,1,0:T(8,128)(2,1)S(1)}, bf16[5,32,1024]{2,1,0:T(8,128)(2,1)S(1)}, u32[]{:S(2)}, u32[]{:S(2)}) collective-permute-start(bf16[5,32,1024]{2,1,0:T(8,128)(2,1)S(1)} %pad_maximum_fusion.16), channel_id=1, source_target_pairs={{0,2},{1,3},{2,0},{3,1},{4,6},{5,7},{6,4},{7,5},{8,10},{9,11},{10,... | collective-permute-start | bytes 983048 | tf_op jit(solution)/shard_map/ppermute | solution.py:66
  390.6 28.3 %collective-permute-start.64 = (bf16[5,32,1024]{2,1,0:T(8,128)(2,1)S(1)}, bf16[5,32,1024]{2,1,0:T(8,128)(2,1)S(1)}, u32[]{:S(2)}, u32[]{:S(2)}) collective-permute-start(bf16[5,32,1024]{2,1,0:T(8,128)(2,1)S(1)} %pad_maximum_fusion.15), channel_id=1, source_target_pairs={{0,1},{1,0},{2,3},{3,2},{4,5},{5,4},{6,7},{7,6},{8,9},{9,8},{10,11... | collective-permute-start | bytes 983048 | tf_op jit(solution)/shard_map/ppermute | solution.py:66
  (78 other events, 525.8 us)

commit v5 on v4

--- a/solution.py
+++ b/solution.py
@@ -101,6 +101,24 @@
     return first + [hop(up, UP[1:]), hop(down, DOWN[1:]), hop(far, [(1, 3), (2, 0)])]
 
 
+def gather_slots(values, size):
+    return [values] + [slot_shift(values, size, j) for j in range(1, size)]
+
+
+def slots_of(parts, shard):
+    up, down, up_two, down_two, far = parts
+    return [jnp.where(shard == 0, far, up), jnp.where(shard <= 1, down_two, up_two), jnp.where(shard == 3, far, down)]
+
+
+def order_slots(slots, shard):
+    size = len(slots)
+    parts = [slots[-t % size] for t in range(size)]
+    for bit in range(size.bit_length() - 1):
+        mine = ((shard >> bit) & 1) == 1
+        parts = [jnp.where(mine, parts[(t - (1 << bit)) % size], parts[t]) for t in range(size)]
+    return jnp.stack(parts)
+
+
 def fill_every(every, own, parts, n_shard):
     rows = own.shape[0]
     every[0:rows] = own[...]
@@ -108,8 +126,7 @@
         slots = [part[...] for part in parts]
     else:
         shard = lax.axis_index("fsdp")
-        up, down, up_two, down_two, far = [part[...] for part in parts]
-        slots = [jnp.where(shard == 0, far, up), jnp.where(shard <= 1, down_two, up_two), jnp.where(shard == 3, far, down)]
+        slots = slots_of([part[...] for part in parts], shard)
     for j, slot in enumerate(slots):
         every[(j + 1) * rows : (j + 2) * rows] = slot
 
@@ -216,16 +233,20 @@
     return result
 
 
-def finish_sum(groups, sizes, my_fsdp):
-    def part(term, shard):
+def fsdp_part(groups, shard, sizes):
+    def part(term):
         view = term[0].reshape(term.shape[1], sizes[1], -1, term.shape[-1])
         return lax.dynamic_index_in_dim(view, shard, 1, keepdims=False)
 
-    def both(shard):
-        return jnp.concatenate([sum_of([part(term, shard) for term in terms]) for terms in groups], axis=-1)
-
-    got = [xor_permute(both(my_fsdp ^ k).astype(BF), sizes, k) for k in range(1, sizes[1])]
-    return sum_of([both(my_fsdp)] + got)
+    return jnp.concatenate([sum_of([part(term) for term in terms]) for terms in groups], axis=-1)
+
+
+def fsdp_swap(groups, sizes, my_fsdp):
+    return [xor_permute(fsdp_part(groups, my_fsdp ^ k, sizes).astype(BF), sizes, k) for k in range(1, sizes[1])]
+
+
+def fsdp_sum(own, got):
+    return sum_of([own] + list(got))
 
 
 def total_over(values, bits, sizes):
@@ -282,48 +303,28 @@
             result.append(jnp.concatenate([ref[:, pl.ds(start, self.block)] for start in starts], axis=1))
         return result
 
-    def put(self, flush, refs, twins, index, values):
-        for ref, twin, value in zip(refs, twins, values):
+    def put(self, refs, index, values):
+        for ref, value in zip(refs, values):
             value = value.astype(BF)
             if self.split:
-                twin[:, index] = value.reshape(self.far, self.block, self.width)
-                flush(twin.at[:, index], ref.at[:, index])
+                ref[:, index] = value.reshape(self.far, self.block, self.width)
             else:
-                twin[index] = value
-                flush(twin.at[index], ref.at[index])
-
-    def put_product(self, flush, refs, twins, index, left_ref, right):
-        self.put(flush, refs, twins, index, [tm(left, right) for left in self.columns(left_ref)])
-
-
-class Flush:
-    def __init__(self, sems):
-        self.sems, self.copies = sems, []
-
-    def __call__(self, source, target):
-        copy = pltpu.make_async_copy(source, target, self.sems.at[len(self.copies)])
-        copy.start()
-        self.copies.append(copy)
-
-    def finish(self):
-        for copy in self.copies:
-            copy.wait()
-
-
-COPIES = 16
-
-
-def kernel_call(kernel, name, operands, sources, near, far, scratch, vmem_mb, work_mb, scalars=(), held=True):
+                ref[index] = value
+
+    def put_product(self, refs, index, left_ref, right):
+        self.put(refs, index, [tm(left, right) for left in self.columns(left_ref)])
+
+
+def kernel_call(kernel, name, operands, sources, outs, scratch, vmem_mb, work_mb, scalars=(), held=True):
     specs = [pl.BlockSpec(memory_space=pltpu.SMEM)] * len(scalars)
     specs += [pl.BlockSpec(memory_space=pltpu.VMEM)] * len(operands)
     specs += [pl.BlockSpec(memory_space=pltpu.VMEM if held else pl.ANY)] * len(sources)
-    out_specs = [pl.BlockSpec(memory_space=pltpu.VMEM)] * len(near) + [pl.BlockSpec(memory_space=pltpu.HBM)] * len(far)
     return pl.pallas_call(
         kernel,
         in_specs=specs,
-        out_specs=out_specs,
-        out_shape=list(near) + list(far),
-        scratch_shapes=[pltpu.VMEM(f.shape, f.dtype) for f in far] + scratch + [pltpu.SemaphoreType.DMA((COPIES,))],
+        out_specs=[pl.BlockSpec(memory_space=pltpu.VMEM)] * len(outs),
+        out_shape=list(outs),
+        scratch_shapes=scratch,
         compiler_params=pltpu.CompilerParams(vmem_limit_bytes=vmem_mb * 2**20),
         cost_estimate=pl.CostEstimate(flops=2**30, bytes_accessed=work_mb * 2**20, transcendentals=2**20),
         name=name,
@@ -346,9 +347,8 @@
 def encoder_kernel(pack, n_source, padded, lat_rows, *refs):
     counts, latents, pix = refs[:3]
     sources, rest = refs[3 : 3 + n_source], refs[3 + n_source :]
-    (small_o, low_o), outs, twins = rest[:2], rest[2:11], rest[11:20]
-    q_o, query_pix_o, probs_o, mixed_pix_o, mixed_o, resid_o, pre_o, act_o, first_o = twins
-    scratch, flush = rest[20:25], Flush(rest[25])
+    small_o, low_o, q_o, query_pix_o, probs_o, mixed_pix_o, mixed_o, resid_o, pre_o, act_o, first_o = rest[:11]
+    scratch = rest[11:16]
     half = pack.width // 2
     latent_in = latents[...].astype(F32)
     hat, _ = norm_parts(latent_in)
@@ -360,10 +360,8 @@
     in_low = (hat * small(0) + small(2)).astype(BF)
     query = mm(in_low, pack.build(sources, 2, scratch[1])).astype(BF)
     q_o[...] = query
-    flush(twins[0], outs[0])
     query_pix = mm(query, kv[:, :padded]).astype(BF)
     query_pix_o[...] = query_pix
-    flush(twins[1], outs[1])
     shape = probs_o.shape
     row, column = lax.broadcasted_iota(jnp.int32, shape, 0), lax.broadcasted_iota(jnp.int32, shape, 1)
     first, end, total = jnp.zeros(shape, jnp.int32), jnp.zeros(shape, jnp.int32), 0
@@ -375,45 +373,34 @@
     scores = mm_t(query_pix, pix[...]) * pack.width**-0.5
     probs = softmax(jnp.where((column >= first) & (column < end), scores, MASKED))
     probs_o[...] = probs
-    flush(twins[2], outs[2])
     mixed_pix = mm(probs.astype(BF), pix[...]).astype(BF)
     mixed_pix_o[...] = mixed_pix
-    flush(twins[3], outs[3])
     mixed = mm_t(mixed_pix, kv[:, half : half + padded]).astype(BF)
     mixed_o[...] = mixed
-    flush(twins[4], outs[4])
     resid = latent_in + mm(mixed, pack.build(sources, 3, scratch[2]))
     resid_o[...] = resid
-    flush(twins[5], outs[5])
     hat, _ = norm_parts(resid)
     normed = (hat * small(1) + small(3)).astype(BF)
     pre = mm(normed, pack.build(sources, 0, scratch[3])) + small(4)
     pre_o[...] = pre
-    flush(twins[6], outs[6])
     act = gelu(pre).astype(BF)
     act_o[...] = act
-    flush(twins[7], outs[7])
     out = resid + mm(act, pack.build(sources, 1, scratch[4])) + small(5)
     first_o[...] = out
-    flush(twins[8], outs[8])
     hat, _ = norm_parts(out)
     low_o[...] = (hat * small(6) + small(8)).astype(BF)
-    flush.finish()
 
 
 def attention_kernel(pack, n_source, n_other, lat_rows, *refs):
     own, others, rest = refs[0], refs[1 : 1 + n_other], refs[1 + n_other :]
     sources, rest = rest[:n_source], rest[n_source:]
-    mixed_o, outs, twins = rest[0], rest[1:5], rest[5:9]
-    every, q_o, k_o, v_o = twins
-    scratch, flush = rest[9:12], Flush(rest[12])
+    mixed_o, every, q_o, k_o, v_o = rest[:5]
+    scratch = rest[5:8]
     rows = own.shape[0]
     fill_every(every, own, others, pack.fsdp)
     q_o[...] = mm(own[...], pack.build(sources, 0, scratch[0])).astype(BF)
     k_o[...] = mm(every[...], pack.build(sources, 1, scratch[1])).astype(BF).reshape(k_o.shape)
     v_o[...] = mm(every[...], pack.build(sources, 2, scratch[2])).astype(BF).reshape(k_o.shape)
-    for twin, out in zip(twins, outs):
-        flush(twin, out)
 
     def some_heads(step, carry):
         places, loaded = [], []
@@ -431,18 +418,15 @@
         return carry
 
     lax.fori_loop(0, HEADS // HEADS_AT_ONCE, some_heads, 0)
-    flush.finish()
 
 
 def attention_back_kernel(pack, n_source, lat_rows, *refs):
     q, k_ref, v_ref, grad, every = refs[:5]
     rest = refs[5:]
     sources, rest = rest[:n_source], rest[n_source:]
-    count = len(pack.grads(3))
-    slots_o, slot_h, grads_h = rest[0], rest[1], rest[2 : 2 + count]
-    slot_o, grads_o, rest = rest[2 + count], rest[3 + count : 3 + 2 * count], rest[3 + 2 * count :]
-    scratch, (dq, dk, dv, sems, out_sems) = rest[:3], rest[3:]
-    flush = Flush(out_sems)
+    outs = 2 + len(pack.grads(3))
+    slots_o, slot_o, *grads_o = rest[:outs]
+    scratch, (dq, dk, dv, sems) = rest[outs : outs + 3], rest[outs + 3 :]
     for index in range(3):
         pack.fetch(sources, index, scratch[index], sems.at[index])
     rows = q.shape[0]
@@ -478,22 +462,18 @@
     slot_o[...] = mm_t(d_q, w_query) + mm_t(d_k[:rows], w_key) + mm_t(d_v[:rows], w_value)
     others = mm_t(d_k[rows:], w_key) + mm_t(d_v[rows:], w_value)
     slots_o[...] = others.astype(BF).reshape(slots_o.shape)
-    flush(slot_o, slot_h)
-    pack.put(flush, grads_h, grads_o, 0, [tm(left, d_q) for left in pack.columns(every.at[pl.ds(0, rows)])])
+    pack.put(grads_o, 0, [tm(left, d_q) for left in pack.columns(every.at[pl.ds(0, rows)])])
     columns = pack.columns(every)
-    pack.put(flush, grads_h, grads_o, 1, [tm(left, d_k) for left in columns])
-    pack.put(flush, grads_h, grads_o, 2, [tm(left, d_v) for left in columns])
-    flush.finish()
+    pack.put(grads_o, 1, [tm(left, d_k) for left in columns])
+    pack.put(grads_o, 2, [tm(left, d_v) for left in columns])
 
 
 def latent_kernel(pack, n_source, *refs):
     mixed, first_out, cotangent, small_ref = refs[:4]
     sources, rest = refs[4 : 4 + n_source], refs[4 + n_source :]
-    (d_mixed_o, sums_o), rest = rest[:2], rest[2:]
-    count = 2 + len(pack.grads(3))
-    (result_h, grad_h, *grads_h), (result_o, grad_o, *grads_o) = rest[:count], rest[count : 2 * count]
-    scratch, (act_s, normed_s, out_sems) = rest[2 * count : 2 * count + 3], rest[2 * count + 3 :]
-    flush = Flush(out_sems)
+    outs = 4 + len(pack.grads(3))
+    d_mixed_o, sums_o, result_o, grad_o, *grads_o = rest[:outs]
+    scratch, (act_s, normed_s) = rest[outs : outs + 3], rest[outs + 3 :]
     small = small_rows(small_ref)
     w_out = pack.build(sources, 0, scratch[0])
     resid = first_out[...] + mm(mixed[...], w_out)
@@ -504,36 +484,31 @@
     act_s[...] = gelu(pre).astype(BF)
     w_second = pack.build(sources, 2, scratch[2])
     result_o[...] = (resid + mm(act_s[...], w_second) + small(11)).astype(BF)
-    flush(result_o, result_h)
     grad_low = cotangent[...]
     grad_out = grad_low.astype(F32)
-    pack.put_product(flush, grads_h, grads_o, 1, act_s, grad_low)
+    pack.put_product(grads_o, 1, act_s, grad_low)
     d_pre = mm_t(grad_low, w_second) * gelu_slope(pre)
     d_pre_low = d_pre.astype(BF)
-    pack.put_product(flush, grads_h, grads_o, 0, normed_s, d_pre_low)
+    pack.put_product(grads_o, 0, normed_s, d_pre_low)
     d_normed = mm_t(d_pre_low, w_first)
     grad_mid = grad_out + norm_back(hat, inverse, small(7), d_normed)
     grad_o[...] = grad_mid
-    flush(grad_o, grad_h)
     grad_low = grad_mid.astype(BF)
     d_mixed_o[...] = mm_t(grad_low, w_out).astype(BF)
-    pack.put_product(flush, grads_h, grads_o, 2, mixed, grad_low)
+    pack.put_product(grads_o, 2, mixed, grad_low)
     sums_o[0:1] = column_sum(d_normed * hat)
     sums_o[1:2] = column_sum(d_normed)
     sums_o[2:3] = column_sum(d_pre)
     sums_o[3:4] = column_sum(grad_out)
-    flush.finish()
 
 
 def encoder_back_kernel(pack, n_source, n_other, *refs):
     slot, grad_mid, first_out, resid, pre_ref, act, small_ref = refs[:7]
     others, rest = refs[7 : 7 + n_other], refs[7 + n_other :]
     sources, rest = rest[:n_source], rest[n_source:]
-    (grad_o, sums_o), rest = rest[:2], rest[2:]
-    count = len(pack.grads(2))
-    grads_h, grads_o, rest = rest[:count], rest[count : 2 * count], rest[2 * count :]
-    scratch, (normed_s, sems, out_sems) = rest[:2], rest[2:]
-    flush = Flush(out_sems)
+    outs = 2 + len(pack.grads(2))
+    grad_o, sums_o, *grads_o = rest[:outs]
+    scratch, (normed_s, sems) = rest[outs : outs + 2], rest[outs + 2 :]
     for index in range(2):
         pack.fetch(sources, index, scratch[index], sems.at[index])
     small = small_rows(small_ref)
@@ -550,24 +525,20 @@
     hat, inverse = norm_parts(resid[...])
     grad_o[...] = grad_out + norm_back(hat, inverse, small(1), d_normed)
     normed_s[...] = (hat * small(1) + small(3)).astype(BF)
-    pack.put_product(flush, grads_h, grads_o, 0, normed_s, d_pre_low)
-    pack.put_product(flush, grads_h, grads_o, 1, act, grad_low)
+    pack.put_product(grads_o, 0, normed_s, d_pre_low)
+    pack.put_product(grads_o, 1, act, grad_low)
     sums_o[2:3] = column_sum(d_normed * hat)
     sums_o[3:4] = column_sum(d_normed)
     sums_o[4:5] = column_sum(d_pre)
     sums_o[5:6] = column_sum(grad_out)
-    flush.finish()
 
 
 def cross_back_kernel(pack, n_source, padded, share, *refs):
     grad_ref, latents, mixed, mixed_pix, probs_ref, pix, query_pix, enc_q, small_ref, lat_sums, enc_sums, pix_hat = refs[:12]
     sources, rest = refs[12 : 12 + n_source], refs[12 + n_source :]
-    (d_pix_o, pix_sums_o), rest = rest[:2], rest[2:]
-    count = 1 + len(pack.grads(3))
-    (d_latents_h, *grads_h), (d_latents_o, *grads_o) = rest[:count], rest[count : 2 * count]
-    scratch, rest = rest[2 * count : 2 * count + 3], rest[2 * count + 3 :]
-    d_mixed_s, in_low_s, high_s, low_s, sems, out_sems = rest
-    flush = Flush(out_sems)
+    outs = 3 + len(pack.grads(3))
+    d_pix_o, pix_sums_o, d_latents_o, *grads_o = rest[:outs]
+    scratch, (d_mixed_s, in_low_s, high_s, low_s, sems) = rest[outs : outs + 3], rest[outs + 3 :]
     for slot, index in enumerate((3, 4, 2)):
         pack.fetch(sources, index, scratch[slot], sems.at[slot])
     small = small_rows(small_ref)
@@ -603,7 +574,6 @@
     in_low_s[...] = (hat * small(0) + small(2)).astype(BF)
     d_normed = mm_t(d_enc_q, pack.ready(scratch[2], sems.at[2]))
     d_latents_o[...] = grad_enc + norm_back(hat, inverse, small(0), d_normed)
-    flush(d_latents_o, d_latents_h)
     order = [column_sum(d_normed * hat), enc_sums[2:3], column_sum(d_normed), enc_sums[3:4], enc_sums[4:5], enc_sums[5:6]]
     order += [enc_sums[0:1], lat_sums[0:1], enc_sums[1:2], lat_sums[1:2], lat_sums[2:3], lat_sums[3:4]]
     sums = jnp.concatenate(order + [jnp.zeros((16 - len(order), pack.width), F32)], axis=0)
@@ -617,10 +587,9 @@
     for left, high_c, right, low_c in zip(*(pack.columns(r) for r in (enc_q, high_s, d_mixed_s, low_s))):
         columns = [tm(left, d_query_pix), tm(high_c, eye), tm(right, mixed_pix[...]), tm(low_c, eye)]
         blocks.append(jnp.concatenate(columns, axis=1))
-    pack.put(flush, grads_h, grads_o, 0, blocks)
-    pack.put_product(flush, grads_h, grads_o, 1, in_low_s, d_enc_q)
-    pack.put_product(flush, grads_h, grads_o, 2, mixed, grad_low)
-    flush.finish()
+    pack.put(grads_o, 0, blocks)
+    pack.put_product(grads_o, 1, in_low_s, d_enc_q)
+    pack.put_product(grads_o, 2, mixed, grad_low)
 
 
 def pack_kernel(own, padded, *refs):
@@ -684,29 +653,35 @@
     enc_pack = pl.pallas_call(
         partial(pack_kernel, own, padded), out_shape=wide((5 * own, width), BF), name="pack"
     )(enc_gains, enc_biases, lat_gains, lat_biases, pix_kv, enc_query, enc_out, enc_mlp)
-    enc_parts = gather_fsdp(enc_pack, sizes)
+    in_two = fsdp_size == 4
+    enc_parts = exchange_one(enc_pack) if in_two else gather_slots(enc_pack, fsdp_size)
     gain_f = pix_gain.astype(F32)
     pix_hat, pix_inverse = norm_parts(pixels.astype(F32))
     pix_low = pad_lanes((pix_hat * gain_f + pix_bias.astype(F32)).astype(BF), padded)[:USED]
     pix_hat_t = jnp.pad(pix_hat[:USED].T, ((0, -features % 8), (0, 0)))
+    if in_two:
+        enc_parts, enc_pack = seal(enc_parts, enc_pack)
+        enc_parts = [enc_pack] + slots_of(exchange_two(list(enc_parts), my_fsdp), my_fsdp)
     enc_parts, pix_low, pix_hat, pix_hat_t, pix_inverse, lat_qkv = seal(
         enc_parts, pix_low, pix_hat, pix_hat_t, pix_inverse, lat_qkv
     )
 
-    enc_groups = far_step([v[None] for v in halves_of(order_fsdp(enc_parts, sizes, me))], 0, sizes, me)
-    qkv_parts = gather_fsdp(lat_qkv.reshape(3 * own, width), sizes)
-    enc_groups, qkv_parts, lat_out, lat_mlp = seal(enc_groups, qkv_parts, lat_out, lat_mlp)
+    enc_groups = far_step([v[None] for v in halves_of(order_slots(list(enc_parts), my_fsdp))], 0, sizes, me)
+    lat_pack = jnp.concatenate([lat_qkv.reshape(3 * own, width), lat_out, lat_mlp[0], lat_mlp[1]], axis=0)
+    lat_one = slot_shift(lat_pack, fsdp_size, 1)
+    enc_groups, lat_pack, lat_one = seal(enc_groups, lat_pack, lat_one)
 
     for place in steps:
         enc_groups = far_step(enc_groups, place, sizes, me)
-    other_parts = gather_fsdp(jnp.concatenate([lat_out, lat_mlp[0], lat_mlp[1]], axis=0), sizes)
-    qkv_groups = [v[None] for v in halves_of(order_fsdp(qkv_parts, sizes, me))]
-    enc_groups, qkv_groups, other_parts = seal(enc_groups, qkv_groups, other_parts)
+    lat_parts = [lat_pack, lat_one] + [slot_shift(lat_pack, fsdp_size, j) for j in range(2, fsdp_size)]
+    enc_groups, lat_parts = seal(enc_groups, lat_parts)
+    lat_whole = order_slots(list(lat_parts), my_fsdp)[None]
+    qkv_groups = halves_of(lat_whole[:, :, : 3 * own])
 
     enc_whole = jnp.concatenate(enc_groups, axis=-1)
     enc_got = core_swap(enc_whole, sizes)
     qkv_groups = far_step(qkv_groups, 0, sizes, me)
-    other_groups = [v[None] for v in halves_of(order_fsdp(other_parts, sizes, me))]
+    other_groups = halves_of(lat_whole[:, :, 3 * own :])
     enc_whole, enc_got, qkv_groups, other_groups = seal(enc_whole, enc_got, qkv_groups, other_groups)
 
     pack = Pack(sizes, own, width)
@@ -720,8 +695,8 @@
         "encoder",
         [latents.reshape(rows, width), pix_low],
         enc_sources,
-        [wide((16, width), F32), wide((rows, width), BF)],
-        [wide((rows, width), BF), wide((rows, padded), BF), wide((rows, USED), F32), wide((rows, padded), BF)]
+        [wide((16, width), F32), wide((rows, width), BF)]
+        + [wide((rows, width), BF), wide((rows, padded), BF), wide((rows, USED), F32), wide((rows, padded), BF)]
         + [wide((rows, width), BF), wide((rows, width), F32), wide((rows, width), F32), wide((rows, width), BF)]
         + [wide((rows, width), F32)],
         [pack.scratch()] * 5,
@@ -732,7 +707,6 @@
     qkv_whole = jnp.concatenate(qkv_groups, axis=-1)
     lat_low, qkv_whole, other_groups = seal(lat_low, qkv_whole, other_groups)
 
-    in_two = fsdp_size == 4
     if in_two:
         shards = exchange_one(lat_low)
     else:
@@ -754,8 +728,8 @@
         "attention",
         [lat_low] + shards,
         qkv_sources,
-        [wide((rows, width), BF)],
-        [wide((fsdp_size * rows, width), BF), wide((rows, width), BF), every, every],
+        [wide((rows, width), BF)]
+        + [wide((fsdp_size * rows, width), BF), wide((rows, width), BF), every, every],
         [pack.scratch()] * 3,
         40,
         40,
@@ -766,8 +740,8 @@
         "latent",
         [lat_mixed, first_out, cotangent.reshape(rows, width), small_all],
         other_sources,
-        [wide((rows, width), BF), wide((8, width), F32)],
-        [wide((rows, width), BF), wide((rows, width), F32)] + pack.grads(3),
+        [wide((rows, width), BF), wide((8, width), F32)]
+        + [wide((rows, width), BF), wide((rows, width), F32)] + pack.grads(3),
         [pack.scratch()] * 3 + [pltpu.VMEM((rows, width), BF)] * 2,
         44,
         36,
@@ -779,8 +753,8 @@
         "attention_back",
         [lat_q, lat_k, lat_v, d_mixed, lat_every],
         qkv_sources,
-        [wide((fsdp_size - 1, rows, width), BF)],
-        [wide((rows, width), F32)] + pack.grads(3),
+        [wide((fsdp_size - 1, rows, width), BF)]
+        + [wide((rows, width), F32)] + pack.grads(3),
         [pack.scratch()] * 3
         + [pltpu.VMEM((rows, width), BF)]
         + [pltpu.VMEM(every.shape, BF)] * 2
@@ -810,14 +784,14 @@
         "encoder_back",
         [slot, grad_mid, first_out, enc_resid, enc_pre, enc_act, small_all] + received,
         enc_sources,
-        [wide((rows, width), F32), wide((8, width), F32)],
-        pack.grads(2),
+        [wide((rows, width), F32), wide((8, width), F32)] + pack.grads(2),
         [pack.scratch()] * 2 + [pltpu.VMEM((rows, width), BF), dma((2,))],
         40,
         36,
         held=False,
     )
-    l_other_grads = finish_sum(grads_m, sizes, my_fsdp)
+    grad_enc, grads_m, grads_q = seal(grad_enc, grads_m, grads_q)
+    l_other_own, l_other_got = fsdp_part(grads_m, my_fsdp, sizes), fsdp_swap(grads_m, sizes, my_fsdp)
     grads_q = far_pair(grads_q, 0, sizes, me)
     share = pix_rows // fsdp_size
     kept = pix_hat_t.shape[0]
@@ -827,8 +801,8 @@
         [grad_enc, latents.reshape(rows, width), enc_mixed, mixed_pix, probs, pix_low, query_pix, enc_q, small_all]
         + [lat_sums, enc_sums, pix_hat_t],
         enc_sources,
-        [wide((fsdp_size, kept, share), F32), wide((kept, LANES), F32)],
-        [wide((rows, width), F32)] + pack.grads(3),
+        [wide((fsdp_size, kept, share), F32), wide((kept, LANES), F32)]
+        + [wide((rows, width), F32)] + pack.grads(3),
         [pack.scratch()] * 3
         + [pltpu.VMEM((rows, width), BF)] * 2
         + [pltpu.VMEM((16, width), BF)] * 2
@@ -837,15 +811,15 @@
         50,
         held=False,
     )
-    pieces, grads_e, grads_f, d_pix_sums, grads_q, l_other_grads = seal(
-        pieces, grads_e, grads_f, d_pix_sums, grads_q, l_other_grads
+    pieces, grads_e, grads_f, d_pix_sums, grads_q, l_other_got = seal(
+        pieces, grads_e, grads_f, d_pix_sums, grads_q, l_other_got
     )
 
     low_bits, core, _ = bits_of(sizes)
     grads_e, grads_f = core_terms(grads_e, sizes, me), core_terms(grads_f, sizes, me)
     for place in steps:
         grads_q = far_pair(grads_q, place, sizes, me)
-    d_pix_sums = total_over(d_pix_sums[:features, :2].T, low_bits, sizes)
+    d_pix_sums = total_over(d_pix_sums[:features, :2].T, low_bits[::-1][:1], sizes)
     pieces, grads_e, grads_f, grads_q, d_pix_sums = seal(pieces, grads_e, grads_f, grads_q, d_pix_sums)
 
     grads_e = [[jnp.concatenate(both, axis=1) for both in zip(e, f)] for e, f in zip(grads_e, grads_f)]
@@ -855,12 +829,15 @@
     grads_e = far_pair(grads_e, 0, sizes, me)
     d_pix_own, grads_e, grads_q, d_pix_sums = seal(d_pix_own, grads_e, grads_q, d_pix_sums)
 
-    l_qkv_grads = finish_sum(grads_q, sizes, my_fsdp)
+    l_qkv_own, l_qkv_got = fsdp_part(grads_q, my_fsdp, sizes), fsdp_swap(grads_q, sizes, my_fsdp)
     for place in steps:
         grads_e = far_pair(grads_e, place, sizes, me)
-    l_qkv_grads, grads_e, d_pix_sums = seal(l_qkv_grads, grads_e, d_pix_sums)
-    d_pix_sums = total_over(d_pix_sums, [core] + far, sizes)
-    enc_grads = finish_sum(grads_e, sizes, my_fsdp)
+    l_qkv_got, l_other_got, grads_e, d_pix_sums = seal(l_qkv_got, l_other_got, grads_e, d_pix_sums)
+    d_pix_sums = total_over(d_pix_sums, [core] + far + low_bits[::-1][1:], sizes)
+    enc_got = fsdp_swap(grads_e, sizes, my_fsdp)
+    l_other_grads = fsdp_sum(l_other_own, l_other_got)
+    l_qkv_grads = fsdp_sum(l_qkv_own, l_qkv_got)
+    enc_grads = fsdp_sum(fsdp_part(grads_e, my_fsdp, sizes), enc_got)
     hat_own = lax.dynamic_slice_in_dim(pix_hat, my_fsdp * share, share, 0)
     inverse_own = lax.dynamic_slice_in_dim(pix_inverse, my_fsdp * share, share, 0)
     d_pixels = norm_back(hat_own, inverse_own, gain_f, d_pix_own[:features].T)

time: 430 us -> 418 us (0.972)
  local copies, waits for them, and re-layouts: 50 us -> 44.5 us
    ppermute x10 -> x15, waiting for transfers between devices: 19.4 us -> 40.2 us  [hop(): return lax.ppermute(values, 'fsdp', pairs)]
    ppermute x54 -> x45, waiting for transfers between devices: 136 us -> 115 us  [xor_permute(): return lax.ppermute(values, AXES, [(i, i ^ step) for i in range(total)])]
    ppermute x54 -> x45, starting transfers between devices: 63 us -> 43.1 us  [xor_permute(): return lax.ppermute(values, AXES, [(i, i ^ step) for i in range(total)])]
    ppermute x10 -> x15, starting transfers between devices: 20.6 us -> 31.5 us  [hop(): return lax.ppermute(values, 'fsdp', pairs)]
    ppermute x3 -> x6, starting transfers between devices: 3.35 us -> 11.3 us  [slot_shift(): lax.ppermute(values, 'fsdp', [(i, (i + j) % size) for i in range(size)])]
    unnamed x124 -> x128, local copies, waits for them, and re-layouts: 24.7 us -> 20.6 us
    ppermute x3 -> x6, waiting for transfers between devices: 19.3 us -> 20.5 us  [slot_shift(): lax.ppermute(values, 'fsdp', [(i, (i + j) % size) for i in range(size)])]
  transfers between devices with their start and end apart: 67 -> 66, of which waited for: 28 -> 36; matrix products, arithmetic and copies ran while one was open for 11% -> 10% of each run, Pallas kernels for 16% -> 14%
where the time goes in v5:
time: 418 us; the launch traced here: 414 us
  waiting for transfers between devices  176 us (42%)
  starting transfers between devices  85.9 us (21%)
  Pallas kernels  76.2 us (18%)
  local copies, waits for them, and re-layouts  44.5 us (11%)
  other arithmetic  28.2 us (7%)
    ppermute x45, waiting for transfers between devices, xor_permute(): return lax.ppermute(values, AXES, [(i, i ^ step) for i in range(total)])  115 us
    pallas_call x6, Pallas kernels, kernel_call(): pl.pallas_call(kernel, in_specs=specs, out_specs=[pl.BlockSpec(memory_spa...  74.2 us
    ppermute x45, starting transfers between devices, xor_permute(): return lax.ppermute(values, AXES, [(i, i ^ step) for i in range(total)])  43.1 us
    ppermute x15, waiting for transfers between devices, hop(): return lax.ppermute(values, 'fsdp', pairs)  40.2 us
    ppermute x15, starting transfers between devices, hop(): return lax.ppermute(values, 'fsdp', pairs)  31.5 us
    unnamed x128, local copies, waits for them, and re-layouts  20.6 us
    ppermute x6, waiting for transfers between devices, slot_shift(): lax.ppermute(values, 'fsdp', [(i, (i + j) % size) for i in range(size)])  20.5 us
    ppermute x6, starting transfers between devices, slot_shift(): lax.ppermute(values, 'fsdp', [(i, (i + j) % size) for i in range(size)])  11.3 us
  transfers between devices with their start and end apart: 66, of which 36 were waited for; matrix products, arithmetic and copies ran while one was open for 10% of the time, Pallas kernels for 14%

profile of v5, /device:TPU:0, one launch (start us, length us, event | category | flops | bytes accessed | tf_op | source)
XLA Modules:
  0.0 413.7 jit_solution(2049961777824348958)
XLA Ops:
  0.7 1.7 copy.43.refs_4_
  2.3 2.1 pack.1
  5.7 5.6 %collective-permute-start = (bf16[160,1024]{1,0:T(8,128)(2,1)}, bf16[160,1024]{1,0:T(8,128)(2,1)S(1)}, u32[]{:S(2)}, u32[]{:S(2)}) collective-permute-start(bf16[160,1024]{1,0:T(8,128)(2,1)} %pack.1), channel_id=1, source_target_pairs={{0,1},{1,2},{2,3},{4,5},{5,6},{6,7},{8,9},{9,10},{10,11},{12,13},{... | collective-permute-start | bytes 983048 | tf_op jit(solution)/shard_map/ppermute | solution.py:88
  14.9 2.4 collective-permute-done.1
  24.6 5.5 %collective-permute-done.2 = bf16[160,1024]{1,0:T(8,128)(2,1)} collective-permute-done((bf16[160,1024]{1,0:T(8,128)(2,1)S(1)}, bf16[160,1024]{1,0:T(8,128)(2,1)}, u32[]{:S(2)}, u32[]{:S(2)}) %collective-permute-start.2) | collective-permute-done | bytes 327712 | tf_op jit(solution)/shard_map/ppermute | solution.py:88
  31.2 5.8 %collective-permute-done.3 = bf16[160,1024]{1,0:T(8,128)(2,1)S(1)} collective-permute-done((bf16[160,1024]{1,0:T(8,128)(2,1)S(1)}, bf16[160,1024]{1,0:T(8,128)(2,1)S(1)}, u32[]{:S(2)}, u32[]{:S(2)}) %collective-permute-start.3) | collective-permute-done | bytes 327712 | tf_op jit(solution)/shard_map/ppermute | solution.py:88
  43.0 9.9 %collective-permute-done.6 = bf16[1,4,160,512]{3,2,1,0:T(8,128)(2,1)S(1)} collective-permute-done((bf16[1,4,160,512]{3,2,1,0:T(8,128)(2,1)S(1)}, bf16[1,4,160,512]{3,2,1,0:T(8,128)(2,1)S(1)}, u32[]{:S(2)}, u32[]{:S(2)}) %collective-permute-start.6) | collective-permute-done | bytes 655392 | tf_op jit(solution)/shard_map/ppermute | solution.py:66
  57.7 5.8 %collective-permute-start.11 = (bf16[192,1024]{1,0:T(8,128)(2,1)S(1)}, bf16[192,1024]{1,0:T(8,128)(2,1)S(1)}, u32[]{:S(2)}, u32[]{:S(2)}) collective-permute-start(bf16[192,1024]{1,0:T(8,128)(2,1)S(1)} %pad_maximum_fusion.13), channel_id=1, source_target_pairs={{0,3},{1,0},{2,1},{3,2},{4,7},{5,4},{6,5},{7,6},{8,11},{9,8},{10,9... | collective-permute-start | bytes 1179656 | tf_op jit(solution)/shard_map/ppermute | solution.py:84
  63.5 20.5 %collective-permute-done.9 = bf16[2,4,160,512]{3,2,1,0:T(8,128)(2,1)S(1)} collective-permute-done((bf16[2,4,160,512]{3,2,1,0:T(8,128)(2,1)S(1)}, bf16[2,4,160,512]{3,2,1,0:T(8,128)(2,1)S(1)}, u32[]{:S(2)}, u32[]{:S(2)}) %collective-permute-start.9) | collective-permute-done | bytes 1310752 | tf_op jit(solution)/shard_map/ppermute | solution.py:66
  88.3 10.0 %collective-permute-done.14 = bf16[1,4,96,512]{3,2,1,0:T(8,128)(2,1)S(1)} collective-permute-done((bf16[1,4,96,512]{3,2,1,0:T(8,128)(2,1)S(1)}, bf16[1,4,96,512]{3,2,1,0:T(8,128)(2,1)S(1)}, u32[]{:S(2)}, u32[]{:S(2)}) %collective-permute-start.14) | collective-permute-done | bytes 393248 | tf_op jit(solution)/shard_map/ppermute | solution.py:66
  100.9 2.3 copy-done.29
  106.8 12.2 %encoder.1 = (f32[16,1024]{1,0:T(8,128)S(1)}, bf16[256,1024]{1,0:T(8,128)(2,1)S(1)}, bf16[256,1024]{1,0:T(8,128)(2,1)S(1)}, bf16[256,384]{1,0:T(8,128)(2,1)S(1)}...) custom-call(s32[1,2]{1,0:T(1,128)S(1)} %copy-done.27, ...), custom_call_target="tpu_custom_call" | custom-call | flops 1073741824 | bytes 37748736 | tf_op jit(solution)/shard_map/encoder/pallas_call | solution.py:322
  120.5 1.8 collective-permute-done.15
  128.5 5.4 %collective-permute-start.17 = (bf16[256,1024]{1,0:T(8,128)(2,1)S(1)}, bf16[256,1024]{1,0:T(8,128)(2,1)S(1)}, u32[]{:S(2)}, u32[]{:S(2)}) collective-permute-start(bf16[256,1024]{1,0:T(8,128)(2,1)S(1)} %get-tuple-element.230.refs_0_), channel_id=1, source_target_pairs={{0,1},{1,2},{2,3},{4,5},{5,6},{6,7},{8,9},{9,10},{10,11},{12,13},{... | collective-permute-start | bytes 1572872 | tf_op jit(solution)/shard_map/ppermute | solution.py:88
  134.6 3.0 collective-permute-done.20
  137.7 6.7 %collective-permute-done.21 = bf16[1,4,96,512]{3,2,1,0:T(8,128)(2,1)S(1)} collective-permute-done((bf16[1,4,96,512]{3,2,1,0:T(8,128)(2,1)S(1)}, bf16[1,4,96,512]{3,2,1,0:T(8,128)(2,1)S(1)}, u32[]{:S(2)}, u32[]{:S(2)}) %collective-permute-start.21) | collective-permute-done | bytes 393248 | tf_op jit(solution)/shard_map/ppermute | solution.py:66
  149.0 1.7 collective-permute-start.24
  150.7 12.4 %collective-permute-done.26 = bf16[2,4,96,512]{3,2,1,0:T(8,128)(2,1)S(1)} collective-permute-done((bf16[2,4,96,512]{3,2,1,0:T(8,128)(2,1)S(1)}, bf16[2,4,96,512]{3,2,1,0:T(8,128)(2,1)S(1)}, u32[]{:S(2)}, u32[]{:S(2)}) %collective-permute-start.26) | collective-permute-done | bytes 786464 | tf_op jit(solution)/shard_map/ppermute | solution.py:66
  165.1 13.4 %collective-permute-done.24.refs_5_ = bf16[256,1024]{1,0:T(8,128)(2,1)S(1)} collective-permute-done((bf16[256,1024]{1,0:T(8,128)(2,1)S(1)}, bf16[256,1024]{1,0:T(8,128)(2,1)S(1)}, u32[]{:S(2)}, u32[]{:S(2)}) %collective-permute-start.24) | collective-permute-done | bytes 524320 | tf_op jit(solution)/shard_map/ppermute | solution.py:88
  178.5 10.6 %attention.1 = (bf16[256,1024]{1,0:T(8,128)(2,1)S(1)}, bf16[1024,1024]{1,0:T(8,128)(2,1)S(1)}, bf16[256,1024]{1,0:T(8,128)(2,1)S(1)}, bf16[4,256,1024]{2,1,0:T(8,128)(2,1)S(1)}, bf16[4,256,1024]{2,1,0:T(8,128)(2,1)S(1)}) custom-call(bf16[256,1024]{1,0:T(8,128)(2,1)S(1)} %get-tuple-element.230.refs_0_, bf16[256,1024]{1,0:T(8,128)(2,1)S(1)} %collective-permute-done.17.refs_1_, ...), custom_call_target="tpu_custom_call" | custom-call | flops 1073741824 | bytes 41943040 | tf_op jit(solution)/shard_map/attention/pallas_call | solution.py:322
  191.8 10.9 %latent.1 = (bf16[256,1024]{1,0:T(8,128)(2,1)S(1)}, f32[8,1024]{1,0:T(8,128)S(1)}, bf16[256,1024]{1,0:T(8,128)(2,1)}, f32[256,1024]{1,0:T(8,128)S(1)}, bf16[4,3,...) custom-call(bf16[256,1024]{1,0:T(8,128)(2,1)S(1)} %get-tuple-element.241.refs_0_, ...), custom_call_target="tpu_custom_call" | custom-call | flops 1073741824 | bytes 37748736 | tf_op jit(solution)/shard_map/latent/pallas_call | solution.py:322
  202.7 1.7 copy-done.3
  205.9 20.7 %attention_back.1 = (bf16[3,256,1024]{2,1,0:T(8,128)(2,1)S(1)}, f32[256,1024]{1,0:T(8,128)S(1)}, bf16[4,3,128,1024]{3,2,1,0:T(8,128)(2,1)}, bf16[4,3,128,1024]{3,2,1,0:T(8,128)(2,1)}) custom-call(bf16[256,1024]{1,0:T(8,128)(2,1)S(1)} %get-tuple-element.246.refs_0_, bf16[4,256,1024]{2,1,0:T(8,128)(2,1)S(1)} %get-tuple-element.247.refs_1_, ...), custom_call_target="tpu_custom_call" | custom-call | flops 1073741824 | bytes 75497472 | tf_op jit(solution)/shard_map/attention_back/pallas_call | solution.py:322
  230.1 1.7 copy-done.4
  232.1 2.2 fusion.53
  236.6 2.8 collective-permute-start.30
  239.6 2.1 fusion.51
  242.1 11.1 %collective-permute-done.30 = bf16[256,1024]{1,0:T(8,128)(2,1)S(1)} collective-permute-done((bf16[256,1024]{1,0:T(8,128)(2,1)S(1)}, bf16[256,1024]{1,0:T(8,128)(2,1)S(1)}, u32[]{:S(2)}, u32[]{:S(2)}) %collective-permute-start.30) | collective-permute-done | bytes 524320 | tf_op jit(solution)/shard_map/ppermute | solution.py:88
  257.7 4.8 %collective-permute-start.34 = (bf16[256,1024]{1,0:T(8,128)(2,1)S(1)}, bf16[256,1024]{1,0:T(8,128)(2,1)S(1)}, u32[]{:S(2)}, u32[]{:S(2)}) collective-permute-start(bf16[256,1024]{1,0:T(8,128)(2,1)S(1)} %get-tuple-element.511), channel_id=1, source_target_pairs={{0,1},{1,2},{2,3},{4,5},{5,6},{6,7},{8,9},{9,10},{10,11},{12,13},{... | collective-permute-start | bytes 1572872 | tf_op jit(solution)/shard_map/ppermute | solution.py:88
  264.6 8.0 %collective-permute-done.37 = bf16[1,3,128,512]{3,2,1,0:T(8,128)(2,1)S(1)} collective-permute-done((bf16[1,3,128,512]{3,2,1,0:T(8,128)(2,1)S(1)}, bf16[1,3,128,512]{3,2,1,0:T(8,128)(2,1)S(1)}, u32[]{:S(2)}, u32[]{:S(2)}) %collective-permute-start.37) | collective-permute-done | bytes 393248 | tf_op jit(solution)/shard_map/ppermute | solution.py:66
  274.2 6.9 %encoder_back.1 = (f32[256,1024]{1,0:T(8,128)S(1)}, f32[8,1024]{1,0:T(8,128)S(1)}, bf16[4,2,128,1024]{3,2,1,0:T(8,128)(2,1)}, bf16[4,2,128,1024]{3,2,1,0:T(8,128)(2,1)S(1)}) custom-call(f32[256,1024]{1,0:T(8,128)S(1)} %copy-done.17, f32[256,1024]{1,0:T(8,128)S(1)} %copy-done.15, f32[256,1024]{1,0:T(8,128)S(1)} %copy-done.2, f32[256,1024]{1,0:T(8,128)S(1)} %copy-done.11, ...), custom_call_target="tpu_custom_call" | custom-call | flops 1073741824 | bytes 37748736 | tf_op jit(solution)/shard_map/encoder_back/pallas_call | solution.py:322
  287.4 1.8 collective-permute-start.43
  292.1 13.0 %cross_back.1 = (f32[4,264,512]{2,1,0:T(8,128)}, f32[264,128]{1,0:T(8,128)S(1)}, f32[256,1024]{1,0:T(8,128)}, bf16[4,3,128,1024]{3,2,1,0:T(8,128)(2,1)}, bf16[4,3,128,1024]{3,2,1,0:T(8,128)(2,1)}) custom-call(f32[256,1024]{1,0:T(8,128)S(1)} %get-tuple-element.290.refs_0_, bf16[256,1024]{1,0:T(8,128)(2,1)S(1)} %bitcast.475, bf16[256,1024]{1,0:T(8,128)(2,1)S(1)} %copy-done.22, ...), custom_call_target="tpu_custom_call" | custom-call | flops 1073741824 | bytes 52428800 | tf_op jit(solution)/shard_map/cross_back/pallas_call | solution.py:322
  317.9 1.7 fusion.55
  321.1 1.9 collective-permute-done.46
  328.7 1.8 collective-permute-start.49
  330.8 1.8 collective-permute-start.50
  333.0 7.1 %collective-permute-done.49 = bf16[264,512]{1,0:T(8,128)(2,1)S(1)} collective-permute-done((bf16[264,512]{1,0:T(8,128)(2,1)S(1)}, bf16[264,512]{1,0:T(8,128)(2,1)S(1)}, u32[]{:S(2)}, u32[]{:S(2)}) %collective-permute-start.49) | collective-permute-done | bytes 270368 | tf_op jit(solution)/shard_map/ppermute | solution.py:84
  340.1 5.0 %collective-permute-done.51 = bf16[264,512]{1,0:T(8,128)(2,1)S(1)} collective-permute-done((bf16[264,512]{1,0:T(8,128)(2,1)S(1)}, bf16[264,512]{1,0:T(8,128)(2,1)S(1)}, u32[]{:S(2)}, u32[]{:S(2)}) %collective-permute-start.51) | collective-permute-done | bytes 270368 | tf_op jit(solution)/shard_map/ppermute | solution.py:84
  345.1 8.4 %collective-permute-done.50 = bf16[264,512]{1,0:T(8,128)(2,1)S(1)} collective-permute-done((bf16[264,512]{1,0:T(8,128)(2,1)S(1)}, bf16[264,512]{1,0:T(8,128)(2,1)S(1)}, u32[]{:S(2)}, u32[]{:S(2)}) %collective-permute-start.50) | collective-permute-done | bytes 270368 | tf_op jit(solution)/shard_map/ppermute | solution.py:84
  361.5 2.0 collective-permute-start.56
  364.7 9.1 %collective-permute-done.55 = bf16[3,32,1024]{2,1,0:T(8,128)(2,1)S(1)} collective-permute-done((bf16[3,32,1024]{2,1,0:T(8,128)(2,1)S(1)}, bf16[3,32,1024]{2,1,0:T(8,128)(2,1)S(1)}, u32[]{:S(2)}, u32[]{:S(2)}) %collective-permute-start.55) | collective-permute-done | bytes 196640 | tf_op jit(solution)/shard_map/ppermute | solution.py:66
  377.0 2.2 collective-permute-start.64
  379.2 1.8 collective-permute-start.63
  382.2 4.0 collective-permute-done.60
  387.8 3.5 collective-permute-done.61
  393.1 8.4 %collective-permute-done.62 = f32[2,261]{0,1:T(8,128)S(1)} collective-permute-done((f32[2,261]{0,1:T(8,128)S(1)}, f32[2,261]{0,1:T(8,128)S(1)}, u32[]{:S(2)}, u32[]{:S(2)}) %collective-permute-start.62) | collective-permute-done | bytes 2120 | tf_op jit(solution)/shard_map/ppermute | solution.py:66
  402.5 5.8 %collective-permute-done.64 = bf16[5,32,1024]{2,1,0:T(8,128)(2,1)S(1)} collective-permute-done((bf16[5,32,1024]{2,1,0:T(8,128)(2,1)S(1)}, bf16[5,32,1024]{2,1,0:T(8,128)(2,1)S(1)}, u32[]{:S(2)}, u32[]{:S(2)}) %collective-permute-start.64) | collective-permute-done | bytes 327712 | tf_op jit(solution)/shard_map/ppermute | solution.py:66
  (371 shorter events, 120.0 us)
Async XLA Ops:
  4.4 12.8 %collective-permute-start.1 = (bf16[160,1024]{1,0:T(8,128)(2,1)}, bf16[160,1024]{1,0:T(8,128)(2,1)S(1)}, u32[]{:S(2)}, u32[]{:S(2)}) collective-permute-start(bf16[160,1024]{1,0:T(8,128)(2,1)} %pack.1), channel_id=1, source_target_pairs={{3,2},{2,1},{1,0},{7,6},{6,5},{5,4},{11,10},{10,9},{9,8},{15,14},{... | collective-permute-start | bytes 983048 | tf_op jit(solution)/shard_map/ppermute | solution.py:88
  5.7 12.8 %collective-permute-start = (bf16[160,1024]{1,0:T(8,128)(2,1)}, bf16[160,1024]{1,0:T(8,128)(2,1)S(1)}, u32[]{:S(2)}, u32[]{:S(2)}) collective-permute-start(bf16[160,1024]{1,0:T(8,128)(2,1)} %pack.1), channel_id=1, source_target_pairs={{0,1},{1,2},{2,3},{4,5},{5,6},{6,7},{8,9},{9,10},{10,11},{12,13},{... | collective-permute-start | bytes 983048 | tf_op jit(solution)/shard_map/ppermute | solution.py:88
  18.6 11.6 %collective-permute-start.2 = (bf16[160,1024]{1,0:T(8,128)(2,1)S(1)}, bf16[160,1024]{1,0:T(8,128)(2,1)}, u32[]{:S(2)}, u32[]{:S(2)}) collective-permute-start(bf16[160,1024]{1,0:T(8,128)(2,1)S(1)} %broadcast_select_fusion.12), channel_id=1, source_target_pairs={{1,3},{2,0},{5,7},{6,4},{9,11},{10,8},{13,15},{14,12},{17,19},{18,... | collective-permute-start | bytes 983048 | tf_op jit(solution)/shard_map/ppermute | solution.py:88
  20.7 16.3 %collective-permute-start.3 = (bf16[160,1024]{1,0:T(8,128)(2,1)S(1)}, bf16[160,1024]{1,0:T(8,128)(2,1)S(1)}, u32[]{:S(2)}, u32[]{:S(2)}) collective-permute-start(bf16[160,1024]{1,0:T(8,128)(2,1)S(1)} %collective-permute-done.1), channel_id=1, source_target_pairs={{2,1},{1,0},{6,5},{5,4},{10,9},{9,8},{14,13},{13,12},{18,17},{17,1... | collective-permute-start | bytes 983048 | tf_op jit(solution)/shard_map/ppermute | solution.py:88
  37.5 15.4 %collective-permute-start.6 = (bf16[1,4,160,512]{3,2,1,0:T(8,128)(2,1)S(1)}, bf16[1,4,160,512]{3,2,1,0:T(8,128)(2,1)S(1)}, u32[]{:S(2)}, u32[]{:S(2)}) collective-permute-start(bf16[1,4,160,512]{3,2,1,0:T(8,128)(2,1)S(1)} %get-tuple-element.492), channel_id=1, source_target_pairs={{0,16},{1,17},{2,18},{3,19},{4,20},{5,21},{6,22},{7,23},{8,24},{9,... | collective-permute-start | bytes 1966088 | tf_op jit(solution)/shard_map/ppermute | solution.py:66
  39.0 15.1 %collective-permute-start.5 = (bf16[1,4,160,512]{3,2,1,0:T(8,128)(2,1)S(1)}, bf16[1,4,160,512]{3,2,1,0:T(8,128)(2,1)}, u32[]{:S(2)}, u32[]{:S(2)}) collective-permute-start(bf16[1,4,160,512]{3,2,1,0:T(8,128)(2,1)S(1)} %get-tuple-element.493), channel_id=1, source_target_pairs={{0,8},{1,9},{2,10},{3,11},{4,12},{5,13},{6,14},{7,15},{8,0},{9,1},... | collective-permute-start | bytes 1966088 | tf_op jit(solution)/shard_map/ppermute | solution.py:66
  41.4 14.2 %collective-permute-start.7 = (bf16[192,1024]{1,0:T(8,128)(2,1)S(1)}, bf16[192,1024]{1,0:T(8,128)(2,1)S(1)}, u32[]{:S(2)}, u32[]{:S(2)}) collective-permute-start(bf16[192,1024]{1,0:T(8,128)(2,1)S(1)} %pad_maximum_fusion.13), channel_id=1, source_target_pairs={{0,1},{1,2},{2,3},{3,0},{4,5},{5,6},{6,7},{7,4},{8,9},{9,10},{10,1... | collective-permute-start | bytes 1179656 | tf_op jit(solution)/shard_map/ppermute | solution.py:84
  55.7 28.4 %collective-permute-start.9 = (bf16[2,4,160,512]{3,2,1,0:T(8,128)(2,1)S(1)}, bf16[2,4,160,512]{3,2,1,0:T(8,128)(2,1)S(1)}, u32[]{:S(2)}, u32[]{:S(2)}) collective-permute-start(bf16[2,4,160,512]{3,2,1,0:T(8,128)(2,1)S(1)} %get-tuple-element.210), channel_id=1, source_target_pairs={{0,8},{1,9},{2,10},{3,11},{4,12},{5,13},{6,14},{7,15},{8,0},{9,1},... | collective-permute-start | bytes 3932168 | tf_op jit(solution)/shard_map/ppermute | solution.py:66
  57.2 27.9 %collective-permute-start.8 = (bf16[2,4,160,512]{3,2,1,0:T(8,128)(2,1)S(1)}, bf16[2,4,160,512]{3,2,1,0:T(8,128)(2,1)S(1)}, u32[]{:S(2)}, u32[]{:S(2)}) collective-permute-start(bf16[2,4,160,512]{3,2,1,0:T(8,128)(2,1)S(1)} %get-tuple-element.209), channel_id=1, source_target_pairs={{0,16},{1,17},{2,18},{3,19},{4,20},{5,21},{6,22},{7,23},{8,24},{9,... | collective-permute-start | bytes 3932168 | tf_op jit(solution)/shard_map/ppermute | solution.py:66
  57.7 27.8 %collective-permute-start.11 = (bf16[192,1024]{1,0:T(8,128)(2,1)S(1)}, bf16[192,1024]{1,0:T(8,128)(2,1)S(1)}, u32[]{:S(2)}, u32[]{:S(2)}) collective-permute-start(bf16[192,1024]{1,0:T(8,128)(2,1)S(1)} %pad_maximum_fusion.13), channel_id=1, source_target_pairs={{0,3},{1,0},{2,1},{3,2},{4,7},{5,4},{6,5},{7,6},{8,11},{9,8},{10,9... | collective-permute-start | bytes 1179656 | tf_op jit(solution)/shard_map/ppermute | solution.py:84
  63.5 22.0 %collective-permute-start.10 = (bf16[192,1024]{1,0:T(8,128)(2,1)S(1)}, bf16[192,1024]{1,0:T(8,128)(2,1)S(1)}, u32[]{:S(2)}, u32[]{:S(2)}) collective-permute-start(bf16[192,1024]{1,0:T(8,128)(2,1)S(1)} %pad_maximum_fusion.13), channel_id=1, source_target_pairs={{0,2},{1,3},{2,0},{3,1},{4,6},{5,7},{6,4},{7,5},{8,10},{9,11},{10,... | collective-permute-start | bytes 1179656 | tf_op jit(solution)/shard_map/ppermute | solution.py:84
  86.2 14.7 %collective-permute-start.12 = (bf16[4,4,160,1024]{3,2,1,0:T(8,128)(2,1)S(1)}, bf16[4,4,160,1024]{3,2,1,0:T(8,128)(2,1)S(1)}, u32[]{:S(2)}, u32[]{:S(2)}) collective-permute-start(bf16[4,4,160,1024]{3,2,1,0:T(8,128)(2,1)S(1)} %constant_dynamic-update-slice_fusion.refs_3_.refs_9_.refs_12_), channel_id=1, source_target_pairs={{0,4},{1,5},{2,6},{3,7},{4,0},{5,1},{6,2},{7,3},{8,12},{9,13},{10,... | collective-permute-start | bytes 15728648 | tf_op jit(solution)/shard_map/ppermute | solution.py:66
  103.2 19.1 %collective-permute-start.15 = (bf16[2,4,96,512]{3,2,1,0:T(8,128)(2,1)}, bf16[2,4,96,512]{3,2,1,0:T(8,128)(2,1)}, u32[]{:S(2)}, u32[]{:S(2)}) collective-permute-start(bf16[2,4,96,512]{3,2,1,0:T(8,128)(2,1)} %maximum_bitcast_fusion.3), channel_id=1, source_target_pairs={{0,16},{1,17},{2,18},{3,19},{4,20},{5,21},{6,22},{7,23},{8,24},{9,... | collective-permute-start | bytes 2359304 | tf_op jit(solution)/shard_map/ppermute | solution.py:66
  104.3 19.7 %collective-permute-start.16 = (bf16[2,4,96,512]{3,2,1,0:T(8,128)(2,1)S(1)}, bf16[2,4,96,512]{3,2,1,0:T(8,128)(2,1)}, u32[]{:S(2)}, u32[]{:S(2)}) collective-permute-start(bf16[2,4,96,512]{3,2,1,0:T(8,128)(2,1)S(1)} %maximum_bitcast_fusion.4), channel_id=1, source_target_pairs={{0,8},{1,9},{2,10},{3,11},{4,12},{5,13},{6,14},{7,15},{8,0},{9,1},... | collective-permute-start | bytes 2359304 | tf_op jit(solution)/shard_map/ppermute | solution.py:66
  126.0 18.9 %collective-permute-start.19 = (bf16[4,4,96,1024]{3,2,1,0:T(8,128)(2,1)S(1)}, bf16[4,4,96,1024]{3,2,1,0:T(8,128)(2,1)S(1)}, u32[]{:S(2)}, u32[]{:S(2)}) collective-permute-start(bf16[4,4,96,1024]{3,2,1,0:T(8,128)(2,1)S(1)} %pad_maximum_fusion.refs_6_.refs_5_), channel_id=1, source_target_pairs={{0,4},{1,5},{2,6},{3,7},{4,0},{5,1},{6,2},{7,3},{8,12},{9,13},{10,... | collective-permute-start | bytes 9437192 | tf_op jit(solution)/shard_map/ppermute | solution.py:66
  127.2 17.4 %collective-permute-start.18 = (bf16[256,1024]{1,0:T(8,128)(2,1)S(1)}, bf16[256,1024]{1,0:T(8,128)(2,1)S(1)}, u32[]{:S(2)}, u32[]{:S(2)}) collective-permute-start(bf16[256,1024]{1,0:T(8,128)(2,1)S(1)} %get-tuple-element.230.refs_0_), channel_id=1, source_target_pairs={{3,2},{2,1},{1,0},{7,6},{6,5},{5,4},{11,10},{10,9},{9,8},{15,14},{... | collective-permute-start | bytes 1572872 | tf_op jit(solution)/shard_map/ppermute | solution.py:88
  128.5 16.4 %collective-permute-start.17 = (bf16[256,1024]{1,0:T(8,128)(2,1)S(1)}, bf16[256,1024]{1,0:T(8,128)(2,1)S(1)}, u32[]{:S(2)}, u32[]{:S(2)}) collective-permute-start(bf16[256,1024]{1,0:T(8,128)(2,1)S(1)} %get-tuple-element.230.refs_0_), channel_id=1, source_target_pairs={{0,1},{1,2},{2,3},{4,5},{5,6},{6,7},{8,9},{9,10},{10,11},{12,13},{... | collective-permute-start | bytes 1572872 | tf_op jit(solution)/shard_map/ppermute | solution.py:88
  144.9 18.3 %collective-permute-start.26 = (bf16[2,4,96,512]{3,2,1,0:T(8,128)(2,1)S(1)}, bf16[2,4,96,512]{3,2,1,0:T(8,128)(2,1)S(1)}, u32[]{:S(2)}, u32[]{:S(2)}) collective-permute-start(bf16[2,4,96,512]{3,2,1,0:T(8,128)(2,1)S(1)} %maximum_bitcast_fusion.6), channel_id=1, source_target_pairs={{0,8},{1,9},{2,10},{3,11},{4,12},{5,13},{6,14},{7,15},{8,0},{9,1},... | collective-permute-start | bytes 2359304 | tf_op jit(solution)/shard_map/ppermute | solution.py:66
  146.4 18.0 %collective-permute-start.25 = (bf16[2,4,96,512]{3,2,1,0:T(8,128)(2,1)S(1)}, bf16[2,4,96,512]{3,2,1,0:T(8,128)(2,1)S(1)}, u32[]{:S(2)}, u32[]{:S(2)}) collective-permute-start(bf16[2,4,96,512]{3,2,1,0:T(8,128)(2,1)S(1)} %maximum_bitcast_fusion.5), channel_id=1, source_target_pairs={{0,16},{1,17},{2,18},{3,19},{4,20},{5,21},{6,22},{7,23},{8,24},{9,... | collective-permute-start | bytes 2359304 | tf_op jit(solution)/shard_map/ppermute | solution.py:66
  147.0 31.5 %collective-permute-start.22 = (bf16[256,1024]{1,0:T(8,128)(2,1)S(1)}, bf16[256,1024]{1,0:T(8,128)(2,1)S(1)}, u32[]{:S(2)}, u32[]{:S(2)}) collective-permute-start(bf16[256,1024]{1,0:T(8,128)(2,1)S(1)} %collective-permute-done.17.refs_1_), channel_id=1, source_target_pairs={{1,2},{2,3},{5,6},{6,7},{9,10},{10,11},{13,14},{14,15},{17,18},{18... | collective-permute-start | bytes 1572872 | tf_op jit(solution)/shard_map/ppermute | solution.py:88
  147.7 30.8 %collective-permute-start.23 = (bf16[256,1024]{1,0:T(8,128)(2,1)S(1)}, bf16[256,1024]{1,0:T(8,128)(2,1)S(1)}, u32[]{:S(2)}, u32[]{:S(2)}) collective-permute-start(bf16[256,1024]{1,0:T(8,128)(2,1)S(1)} %collective-permute-done.18.refs_2_), channel_id=1, source_target_pairs={{2,1},{1,0},{6,5},{5,4},{10,9},{9,8},{14,13},{13,12},{18,17},{17,1... | collective-permute-start | bytes 1572872 | tf_op jit(solution)/shard_map/ppermute | solution.py:88
  149.0 29.5 %collective-permute-start.24 = (bf16[256,1024]{1,0:T(8,128)(2,1)S(1)}, bf16[256,1024]{1,0:T(8,128)(2,1)S(1)}, u32[]{:S(2)}, u32[]{:S(2)}) collective-permute-start(bf16[256,1024]{1,0:T(8,128)(2,1)S(1)} %broadcast_select_fusion.1), channel_id=1, source_target_pairs={{1,3},{2,0},{5,7},{6,4},{9,11},{10,8},{13,15},{14,12},{17,19},{18,... | collective-permute-start | bytes 1572872 | tf_op jit(solution)/shard_map/ppermute | solution.py:88
  178.5 13.2 %collective-permute-start.27 = (bf16[4,4,96,1024]{3,2,1,0:T(8,128)(2,1)S(1)}, bf16[4,4,96,1024]{3,2,1,0:T(8,128)(2,1)}, u32[]{:S(2)}, u32[]{:S(2)}) collective-permute-start(bf16[4,4,96,1024]{3,2,1,0:T(8,128)(2,1)S(1)} %pad_maximum_fusion.1.refs_4_), channel_id=1, source_target_pairs={{0,4},{1,5},{2,6},{3,7},{4,0},{5,1},{6,2},{7,3},{8,12},{9,13},{10,... | collective-permute-start | bytes 9437192 | tf_op jit(solution)/shard_map/ppermute | solution.py:66
  205.3 26.8 %collective-permute-start.31 = (bf16[4,3,128,1024]{3,2,1,0:T(8,128)(2,1)}, bf16[4,3,128,1024]{3,2,1,0:T(8,128)(2,1)}, u32[]{:S(2)}, u32[]{:S(2)}) collective-permute-start(bf16[4,3,128,1024]{3,2,1,0:T(8,128)(2,1)} %get-tuple-element.261), channel_id=1, source_target_pairs={{0,4},{1,5},{2,6},{3,7},{4,0},{5,1},{6,2},{7,3},{8,12},{9,13},{10,... | collective-permute-start | bytes 9437192 | tf_op jit(solution)/shard_map/ppermute | solution.py:66
  227.7 14.0 %collective-permute-start.29 = (bf16[256,1024]{1,0:T(8,128)(2,1)S(1)}, bf16[256,1024]{1,0:T(8,128)(2,1)S(1)}, u32[]{:S(2)}, u32[]{:S(2)}) collective-permute-start(bf16[256,1024]{1,0:T(8,128)(2,1)S(1)} %get-tuple-element.468), channel_id=1, source_target_pairs={{3,2},{2,1},{7,6},{6,5},{11,10},{10,9},{15,14},{14,13},{19,18},{18... | collective-permute-start | bytes 1572872 | tf_op jit(solution)/shard_map/ppermute | solution.py:88
  228.5 13.6 %collective-permute-start.28 = (bf16[256,1024]{1,0:T(8,128)(2,1)S(1)}, bf16[256,1024]{1,0:T(8,128)(2,1)S(1)}, u32[]{:S(2)}, u32[]{:S(2)}) collective-permute-start(bf16[256,1024]{1,0:T(8,128)(2,1)S(1)} %get-tuple-element.468), channel_id=1, source_target_pairs={{0,1},{1,2},{4,5},{5,6},{8,9},{9,10},{12,13},{13,14},{16,17},{17,1... | collective-permute-start | bytes 1572872 | tf_op jit(solution)/shard_map/ppermute | solution.py:88
  234.5 20.0 %collective-permute-start.32 = (bf16[2,3,128,512]{3,2,1,0:T(8,128)(2,1)S(1)}, bf16[2,3,128,512]{3,2,1,0:T(8,128)(2,1)S(1)}, u32[]{:S(2)}, u32[]{:S(2)}) collective-permute-start(bf16[2,3,128,512]{3,2,1,0:T(8,128)(2,1)S(1)} %fusion.9), channel_id=1, source_target_pairs={{0,8},{1,9},{2,10},{3,11},{4,12},{5,13},{6,14},{7,15},{8,0},{9,1},... | collective-permute-start | bytes 2359304 | tf_op jit(solution)/shard_map/ppermute | solution.py:66
  235.8 19.7 %collective-permute-start.33 = (bf16[2,3,128,512]{3,2,1,0:T(8,128)(2,1)S(1)}, bf16[2,3,128,512]{3,2,1,0:T(8,128)(2,1)S(1)}, u32[]{:S(2)}, u32[]{:S(2)}) collective-permute-start(bf16[2,3,128,512]{3,2,1,0:T(8,128)(2,1)S(1)} %fusion.10), channel_id=1, source_target_pairs={{0,16},{1,17},{2,18},{3,19},{4,20},{5,21},{6,22},{7,23},{8,24},{9,... | collective-permute-start | bytes 2359304 | tf_op jit(solution)/shard_map/ppermute | solution.py:66
  236.6 16.6 %collective-permute-start.30 = (bf16[256,1024]{1,0:T(8,128)(2,1)S(1)}, bf16[256,1024]{1,0:T(8,128)(2,1)S(1)}, u32[]{:S(2)}, u32[]{:S(2)}) collective-permute-start(bf16[256,1024]{1,0:T(8,128)(2,1)S(1)} %broadcast_select_fusion), channel_id=1, source_target_pairs={{0,2},{3,1},{4,6},{7,5},{8,10},{11,9},{12,14},{15,13},{16,18},{19,... | collective-permute-start | bytes 1572872 | tf_op jit(solution)/shard_map/ppermute | solution.py:88
  256.4 17.0 %collective-permute-start.35 = (bf16[256,1024]{1,0:T(8,128)(2,1)S(1)}, bf16[256,1024]{1,0:T(8,128)(2,1)S(1)}, u32[]{:S(2)}, u32[]{:S(2)}) collective-permute-start(bf16[256,1024]{1,0:T(8,128)(2,1)S(1)} %get-tuple-element.510), channel_id=1, source_target_pairs={{3,2},{2,1},{1,0},{7,6},{6,5},{5,4},{11,10},{10,9},{9,8},{15,14},{... | collective-permute-start | bytes 1572872 | tf_op jit(solution)/shard_map/ppermute | solution.py:88
  257.7 15.7 %collective-permute-start.34 = (bf16[256,1024]{1,0:T(8,128)(2,1)S(1)}, bf16[256,1024]{1,0:T(8,128)(2,1)S(1)}, u32[]{:S(2)}, u32[]{:S(2)}) collective-permute-start(bf16[256,1024]{1,0:T(8,128)(2,1)S(1)} %get-tuple-element.511), channel_id=1, source_target_pairs={{0,1},{1,2},{2,3},{4,5},{5,6},{6,7},{8,9},{9,10},{10,11},{12,13},{... | collective-permute-start | bytes 1572872 | tf_op jit(solution)/shard_map/ppermute | solution.py:88
  282.4 23.7 %collective-permute-start.41 = (bf16[3,32,1024]{2,1,0:T(8,128)(2,1)S(1)}, bf16[3,32,1024]{2,1,0:T(8,128)(2,1)S(1)}, u32[]{:S(2)}, u32[]{:S(2)}) collective-permute-start(bf16[3,32,1024]{2,1,0:T(8,128)(2,1)S(1)} %pad_maximum_fusion.17), channel_id=1, source_target_pairs={{0,1},{1,0},{2,3},{3,2},{4,5},{5,4},{6,7},{7,6},{8,9},{9,8},{10,11... | collective-permute-start | bytes 589832 | tf_op jit(solution)/shard_map/ppermute | solution.py:66
  284.1 22.0 %collective-permute-start.40 = (bf16[2,3,128,512]{3,2,1,0:T(8,128)(2,1)S(1)}, bf16[2,3,128,512]{3,2,1,0:T(8,128)(2,1)}, u32[]{:S(2)}, u32[]{:S(2)}) collective-permute-start(bf16[2,3,128,512]{3,2,1,0:T(8,128)(2,1)S(1)} %fusion.12), channel_id=1, source_target_pairs={{0,16},{1,17},{2,18},{3,19},{4,20},{5,21},{6,22},{7,23},{8,24},{9,... | collective-permute-start | bytes 2359304 | tf_op jit(solution)/shard_map/ppermute | solution.py:66
  285.1 21.1 %collective-permute-start.39 = (bf16[2,3,128,512]{3,2,1,0:T(8,128)(2,1)S(1)}, bf16[2,3,128,512]{3,2,1,0:T(8,128)(2,1)S(1)}, u32[]{:S(2)}, u32[]{:S(2)}) collective-permute-start(bf16[2,3,128,512]{3,2,1,0:T(8,128)(2,1)S(1)} %fusion.11), channel_id=1, source_target_pairs={{0,8},{1,9},{2,10},{3,11},{4,12},{5,13},{6,14},{7,15},{8,0},{9,1},... | collective-permute-start | bytes 2359304 | tf_op jit(solution)/shard_map/ppermute | solution.py:66
  286.1 20.0 %collective-permute-start.42 = (bf16[3,32,1024]{2,1,0:T(8,128)(2,1)S(1)}, bf16[3,32,1024]{2,1,0:T(8,128)(2,1)S(1)}, u32[]{:S(2)}, u32[]{:S(2)}) collective-permute-start(bf16[3,32,1024]{2,1,0:T(8,128)(2,1)S(1)} %pad_maximum_fusion.18), channel_id=1, source_target_pairs={{0,2},{1,3},{2,0},{3,1},{4,6},{5,7},{6,4},{7,5},{8,10},{9,11},{10,... | collective-permute-start | bytes 589832 | tf_op jit(solution)/shard_map/ppermute | solution.py:66
  287.4 18.8 %collective-permute-start.43 = (bf16[3,32,1024]{2,1,0:T(8,128)(2,1)S(1)}, bf16[3,32,1024]{2,1,0:T(8,128)(2,1)S(1)}, u32[]{:S(2)}, u32[]{:S(2)}) collective-permute-start(bf16[3,32,1024]{2,1,0:T(8,128)(2,1)S(1)} %pad_maximum_fusion.19), channel_id=1, source_target_pairs={{0,3},{1,2},{2,1},{3,0},{4,7},{5,6},{6,5},{7,4},{8,11},{9,10},{10,... | collective-permute-start | bytes 589832 | tf_op jit(solution)/shard_map/ppermute | solution.py:66
  307.1 12.5 %collective-permute-start.45 = (bf16[4,3,128,1024]{3,2,1,0:T(8,128)(2,1)}, bf16[4,3,128,1024]{3,2,1,0:T(8,128)(2,1)S(1)}, u32[]{:S(2)}, u32[]{:S(2)}) collective-permute-start(bf16[4,3,128,1024]{3,2,1,0:T(8,128)(2,1)} %get-tuple-element.323), channel_id=1, source_target_pairs={{0,4},{1,5},{2,6},{3,7},{4,0},{5,1},{6,2},{7,3},{8,12},{9,13},{10,... | collective-permute-start | bytes 9437192 | tf_op jit(solution)/shard_map/ppermute | solution.py:66
  323.9 29.7 %collective-permute-start.52 = (bf16[2,5,128,512]{3,2,1,0:T(8,128)(2,1)S(1)}, bf16[2,5,128,512]{3,2,1,0:T(8,128)(2,1)S(1)}, u32[]{:S(2)}, u32[]{:S(2)}) collective-permute-start(bf16[2,5,128,512]{3,2,1,0:T(8,128)(2,1)S(1)} %fusion.3), channel_id=1, source_target_pairs={{0,8},{1,9},{2,10},{3,11},{4,12},{5,13},{6,14},{7,15},{8,0},{9,1},... | collective-permute-start | bytes 3932168 | tf_op jit(solution)/shard_map/ppermute | solution.py:66
  325.9 29.1 %collective-permute-start.53 = (bf16[2,5,128,512]{3,2,1,0:T(8,128)(2,1)S(1)}, bf16[2,5,128,512]{3,2,1,0:T(8,128)(2,1)S(1)}, u32[]{:S(2)}, u32[]{:S(2)}) collective-permute-start(bf16[2,5,128,512]{3,2,1,0:T(8,128)(2,1)S(1)} %fusion.4), channel_id=1, source_target_pairs={{0,16},{1,17},{2,18},{3,19},{4,20},{5,21},{6,22},{7,23},{8,24},{9,... | collective-permute-start | bytes 3932168 | tf_op jit(solution)/shard_map/ppermute | solution.py:66
  330.5 14.6 %collective-permute-start.51 = (bf16[264,512]{1,0:T(8,128)(2,1)S(1)}, bf16[264,512]{1,0:T(8,128)(2,1)S(1)}, u32[]{:S(2)}, u32[]{:S(2)}) collective-permute-start(bf16[264,512]{1,0:T(8,128)(2,1)S(1)} %get-tuple-element.501), channel_id=1, source_target_pairs={{0,1},{1,2},{2,3},{3,0},{4,5},{5,6},{6,7},{7,4},{8,9},{9,10},{10,1... | collective-permute-start | bytes 811016 | tf_op jit(solution)/shard_map/ppermute | solution.py:84
  330.8 22.7 %collective-permute-start.50 = (bf16[264,512]{1,0:T(8,128)(2,1)S(1)}, bf16[264,512]{1,0:T(8,128)(2,1)S(1)}, u32[]{:S(2)}, u32[]{:S(2)}) collective-permute-start(bf16[264,512]{1,0:T(8,128)(2,1)S(1)} %get-tuple-element.502), channel_id=1, source_target_pairs={{0,2},{1,3},{2,0},{3,1},{4,6},{5,7},{6,4},{7,5},{8,10},{9,11},{10,... | collective-permute-start | bytes 811016 | tf_op jit(solution)/shard_map/ppermute | solution.py:84
  358.1 15.7 %collective-permute-start.55 = (bf16[3,32,1024]{2,1,0:T(8,128)(2,1)S(1)}, bf16[3,32,1024]{2,1,0:T(8,128)(2,1)S(1)}, u32[]{:S(2)}, u32[]{:S(2)}) collective-permute-start(bf16[3,32,1024]{2,1,0:T(8,128)(2,1)S(1)} %pad_maximum_fusion.21), channel_id=1, source_target_pairs={{0,2},{1,3},{2,0},{3,1},{4,6},{5,7},{6,4},{7,5},{8,10},{9,11},{10,... | collective-permute-start | bytes 589832 | tf_op jit(solution)/shard_map/ppermute | solution.py:66
  359.0 15.5 %collective-permute-start.58 = (bf16[1,5,128,512]{3,2,1,0:T(8,128)(2,1)S(1)}, bf16[1,5,128,512]{3,2,1,0:T(8,128)(2,1)S(1)}, u32[]{:S(2)}, u32[]{:S(2)}) collective-permute-start(bf16[1,5,128,512]{3,2,1,0:T(8,128)(2,1)S(1)} %add_convert_fusion.7), channel_id=1, source_target_pairs={{0,8},{1,9},{2,10},{3,11},{4,12},{5,13},{6,14},{7,15},{8,0},{9,1},... | collective-permute-start | bytes 1966088 | tf_op jit(solution)/shard_map/ppermute | solution.py:66
  360.1 15.2 %collective-permute-start.57 = (bf16[1,5,128,512]{3,2,1,0:T(8,128)(2,1)S(1)}, bf16[1,5,128,512]{3,2,1,0:T(8,128)(2,1)S(1)}, u32[]{:S(2)}, u32[]{:S(2)}) collective-permute-start(bf16[1,5,128,512]{3,2,1,0:T(8,128)(2,1)S(1)} %add_convert_fusion.8), channel_id=1, source_target_pairs={{0,16},{1,17},{2,18},{3,19},{4,20},{5,21},{6,22},{7,23},{8,24},{9,... | collective-permute-start | bytes 1966088 | tf_op jit(solution)/shard_map/ppermute | solution.py:66
  361.5 12.3 %collective-permute-start.56 = (bf16[3,32,1024]{2,1,0:T(8,128)(2,1)S(1)}, bf16[3,32,1024]{2,1,0:T(8,128)(2,1)S(1)}, u32[]{:S(2)}, u32[]{:S(2)}) collective-permute-start(bf16[3,32,1024]{2,1,0:T(8,128)(2,1)S(1)} %pad_maximum_fusion.22), channel_id=1, source_target_pairs={{0,3},{1,2},{2,1},{3,0},{4,7},{5,6},{6,5},{7,4},{8,11},{9,10},{10,... | collective-permute-start | bytes 589832 | tf_op jit(solution)/shard_map/ppermute | solution.py:66
  376.4 26.1 %collective-permute-start.65 = (bf16[5,32,1024]{2,1,0:T(8,128)(2,1)S(1)}, bf16[5,32,1024]{2,1,0:T(8,128)(2,1)S(1)}, u32[]{:S(2)}, u32[]{:S(2)}) collective-permute-start(bf16[5,32,1024]{2,1,0:T(8,128)(2,1)S(1)} %pad_maximum_fusion.16), channel_id=1, source_target_pairs={{0,3},{1,2},{2,1},{3,0},{4,7},{5,6},{6,5},{7,4},{8,11},{9,10},{10,... | collective-permute-start | bytes 983048 | tf_op jit(solution)/shard_map/ppermute | solution.py:66
  377.0 31.2 %collective-permute-start.64 = (bf16[5,32,1024]{2,1,0:T(8,128)(2,1)S(1)}, bf16[5,32,1024]{2,1,0:T(8,128)(2,1)S(1)}, u32[]{:S(2)}, u32[]{:S(2)}) collective-permute-start(bf16[5,32,1024]{2,1,0:T(8,128)(2,1)S(1)} %pad_maximum_fusion.15), channel_id=1, source_target_pairs={{0,2},{1,3},{2,0},{3,1},{4,6},{5,7},{6,4},{7,5},{8,10},{9,11},{10,... | collective-permute-start | bytes 983048 | tf_op jit(solution)/shard_map/ppermute | solution.py:66
  379.2 29.0 %collective-permute-start.63 = (bf16[5,32,1024]{2,1,0:T(8,128)(2,1)S(1)}, bf16[5,32,1024]{2,1,0:T(8,128)(2,1)S(1)}, u32[]{:S(2)}, u32[]{:S(2)}) collective-permute-start(bf16[5,32,1024]{2,1,0:T(8,128)(2,1)S(1)} %pad_maximum_fusion.14), channel_id=1, source_target_pairs={{0,1},{1,0},{2,3},{3,2},{4,5},{5,4},{6,7},{7,6},{8,9},{9,8},{10,11... | collective-permute-start | bytes 983048 | tf_op jit(solution)/shard_map/ppermute | solution.py:66
  (79 other events, 616.2 us)

commit v6 on v5

--- a/solution.py
+++ b/solution.py
@@ -15,7 +15,7 @@
 MASKED = -1e30
 AXES = ("dp", "fsdp")
 LANES = 128
-HEADS_AT_ONCE = 2
+HEADS_AT_ONCE = 8
 BF = jnp.bfloat16
 F32 = jnp.float32
 
@@ -395,12 +395,14 @@
     own, others, rest = refs[0], refs[1 : 1 + n_other], refs[1 + n_other :]
     sources, rest = rest[:n_source], rest[n_source:]
     mixed_o, every, q_o, k_o, v_o = rest[:5]
-    scratch = rest[5:8]
+    scratch, sems = rest[5:8], rest[8]
+    for index in range(3):
+        pack.fetch(sources, index, scratch[index], sems.at[index])
     rows = own.shape[0]
     fill_every(every, own, others, pack.fsdp)
-    q_o[...] = mm(own[...], pack.build(sources, 0, scratch[0])).astype(BF)
-    k_o[...] = mm(every[...], pack.build(sources, 1, scratch[1])).astype(BF).reshape(k_o.shape)
-    v_o[...] = mm(every[...], pack.build(sources, 2, scratch[2])).astype(BF).reshape(k_o.shape)
+    q_o[...] = mm(own[...], pack.ready(scratch[0], sems.at[0])).astype(BF)
+    k_o[...] = mm(every[...], pack.ready(scratch[1], sems.at[1])).astype(BF).reshape(k_o.shape)
+    v_o[...] = mm(every[...], pack.ready(scratch[2], sems.at[2])).astype(BF).reshape(k_o.shape)
 
     def some_heads(step, carry):
         places, loaded = [], []
@@ -473,16 +475,18 @@
     sources, rest = refs[4 : 4 + n_source], refs[4 + n_source :]
     outs = 4 + len(pack.grads(3))
     d_mixed_o, sums_o, result_o, grad_o, *grads_o = rest[:outs]
-    scratch, (act_s, normed_s) = rest[outs : outs + 3], rest[outs + 3 :]
+    scratch, (act_s, normed_s, sems) = rest[outs : outs + 3], rest[outs + 3 :]
+    for index in range(3):
+        pack.fetch(sources, index, scratch[index], sems.at[index])
     small = small_rows(small_ref)
-    w_out = pack.build(sources, 0, scratch[0])
+    w_out = pack.ready(scratch[0], sems.at[0])
     resid = first_out[...] + mm(mixed[...], w_out)
     hat, inverse = norm_parts(resid)
     normed_s[...] = (hat * small(7) + small(9)).astype(BF)
-    w_first = pack.build(sources, 1, scratch[1])
+    w_first = pack.ready(scratch[1], sems.at[1])
     pre = mm(normed_s[...], w_first) + small(10)
     act_s[...] = gelu(pre).astype(BF)
-    w_second = pack.build(sources, 2, scratch[2])
+    w_second = pack.ready(scratch[2], sems.at[2])
     result_o[...] = (resid + mm(act_s[...], w_second) + small(11)).astype(BF)
     grad_low = cotangent[...]
     grad_out = grad_low.astype(F32)
@@ -596,18 +600,18 @@
     gains_biases, pix_kv, query, out, mlp, packed = refs[:4], *refs[4:]
     half = packed.shape[1] // 2
 
-    def turned(values, columns):
-        rows = values.shape[0]
+    def turned(values, columns, rowwise=False):
+        rows = values.shape[1 if rowwise else 0]
         eye = lax.broadcasted_iota(jnp.int32, (rows, columns), 0) == lax.broadcasted_iota(jnp.int32, (rows, columns), 1)
-        return tm(values, eye.astype(F32).astype(BF)).astype(BF)
+        return (mm if rowwise else tm)(values, eye.astype(F32).astype(BF)).astype(BF)
 
     packed[0:own], packed[own : 2 * own] = mlp[0], mlp[1]
     packed[2 * own : 3 * own], packed[3 * own : 4 * own] = query[...], out[...]
     small = jnp.concatenate([ref[...].astype(F32) for ref in gains_biases], axis=0).astype(BF)
     last = packed.at[pl.ds(4 * own, own)]
-    last[:, 0:padded] = turned(pix_kv[0], padded)
+    last[:, 0:padded] = turned(pix_kv[0], padded, True)
     last[:, padded:half] = turned(small, half - padded)
-    last[:, half : half + padded] = turned(pix_kv[1], padded)
+    last[:, half : half + padded] = turned(pix_kv[1], padded, True)
     last[:, half + padded :] = jnp.zeros((own, half - padded), BF)
 
 
@@ -652,7 +656,7 @@
     wide, dma = jax.ShapeDtypeStruct, pltpu.SemaphoreType.DMA
     enc_pack = pl.pallas_call(
         partial(pack_kernel, own, padded), out_shape=wide((5 * own, width), BF), name="pack"
-    )(enc_gains, enc_biases, lat_gains, lat_biases, pix_kv, enc_query, enc_out, enc_mlp)
+    )(enc_gains, enc_biases, lat_gains, lat_biases, jnp.transpose(pix_kv, (0, 2, 1)), enc_query, enc_out, enc_mlp)
     in_two = fsdp_size == 4
     enc_parts = exchange_one(enc_pack) if in_two else gather_slots(enc_pack, fsdp_size)
     gain_f = pix_gain.astype(F32)
@@ -730,9 +734,10 @@
         qkv_sources,
         [wide((rows, width), BF)]
         + [wide((fsdp_size * rows, width), BF), wide((rows, width), BF), every, every],
-        [pack.scratch()] * 3,
+        [pack.scratch()] * 3 + [dma((3,))],
         40,
         40,
+        held=False,
     )
     other_sources = sources_of(other_whole, other_got, 3, sizes, me)
     d_mixed, lat_sums, result, grad_mid, *grads_m = kernel_call(
@@ -742,9 +747,10 @@
         other_sources,
         [wide((rows, width), BF), wide((8, width), F32)]
         + [wide((rows, width), BF), wide((rows, width), F32)] + pack.grads(3),
-        [pack.scratch()] * 3 + [pltpu.VMEM((rows, width), BF)] * 2,
+        [pack.scratch()] * 3 + [pltpu.VMEM((rows, width), BF)] * 2 + [dma((3,))],
         44,
         36,
+        held=False,
     )
 
     grads_m = core_terms(grads_m, sizes, me)
@@ -833,7 +839,7 @@
     for place in steps:
         grads_e = far_pair(grads_e, place, sizes, me)
     l_qkv_got, l_other_got, grads_e, d_pix_sums = seal(l_qkv_got, l_other_got, grads_e, d_pix_sums)
-    d_pix_sums = total_over(d_pix_sums, [core] + far + low_bits[::-1][1:], sizes)
+    d_pix_sums = total_over(d_pix_sums, low_bits[::-1][1:] + [core] + far, sizes)
     enc_got = fsdp_swap(grads_e, sizes, my_fsdp)
     l_other_grads = fsdp_sum(l_other_own, l_other_got)
     l_qkv_grads = fsdp_sum(l_qkv_own, l_qkv_got)

time: 418 us -> 411 us (0.983)
    unnamed x128 -> x127, local copies, waits for them, and re-layouts: 20.6 us -> 19 us
  transfers between devices with their start and end apart: 66 -> 66, of which waited for: 36 -> 37; matrix products, arithmetic and copies ran while one was open for 10% -> 10% of each run, Pallas kernels for 14% -> 14%
where the time goes in v6:
time: 411 us; the launch traced here: 406 us
  waiting for transfers between devices  175 us (43%)
  starting transfers between devices  84.5 us (21%)
  Pallas kernels  73.2 us (18%)
  local copies, waits for them, and re-layouts  42.9 us (10%)
  other arithmetic  28.2 us (7%)
    ppermute x45, waiting for transfers between devices, xor_permute(): return lax.ppermute(values, AXES, [(i, i ^ step) for i in range(total)])  114 us
    pallas_call x6, Pallas kernels, kernel_call(): pl.pallas_call(kernel, in_specs=specs, out_specs=[pl.BlockSpec(memory_spa...  71.1 us
    ppermute x45, starting transfers between devices, xor_permute(): return lax.ppermute(values, AXES, [(i, i ^ step) for i in range(total)])  42.6 us
    ppermute x15, waiting for transfers between devices, hop(): return lax.ppermute(values, 'fsdp', pairs)  40.1 us
    ppermute x15, starting transfers between devices, hop(): return lax.ppermute(values, 'fsdp', pairs)  30.8 us
    ppermute x6, waiting for transfers between devices, slot_shift(): lax.ppermute(values, 'fsdp', [(i, (i + j) % size) for i in range(size)])  20.7 us
    unnamed x127, local copies, waits for them, and re-layouts  19 us
    ppermute x6, starting transfers between devices, slot_shift(): lax.ppermute(values, 'fsdp', [(i, (i + j) % size) for i in range(size)])  11 us
  transfers between devices with their start and end apart: 66, of which 37 were waited for; matrix products, arithmetic and copies ran while one was open for 10% of the time, Pallas kernels for 14%

profile of v6, /device:TPU:0, one launch (start us, length us, event | category | flops | bytes accessed | tf_op | source)
XLA Modules:
  0.0 406.5 jit_solution(14934281025155915184)
XLA Ops:
  0.7 2.1 pack.1
  4.0 5.6 %collective-permute-start = (bf16[160,1024]{1,0:T(8,128)(2,1)}, bf16[160,1024]{1,0:T(8,128)(2,1)S(1)}, u32[]{:S(2)}, u32[]{:S(2)}) collective-permute-start(bf16[160,1024]{1,0:T(8,128)(2,1)} %pack.1), channel_id=1, source_target_pairs={{0,1},{1,2},{2,3},{4,5},{5,6},{6,7},{8,9},{9,10},{10,11},{12,13},{... | collective-permute-start | bytes 983048 | tf_op jit(solution)/shard_map/ppermute | solution.py:88
  13.2 2.4 collective-permute-done.1
  22.9 5.5 %collective-permute-done.2 = bf16[160,1024]{1,0:T(8,128)(2,1)} collective-permute-done((bf16[160,1024]{1,0:T(8,128)(2,1)S(1)}, bf16[160,1024]{1,0:T(8,128)(2,1)}, u32[]{:S(2)}, u32[]{:S(2)}) %collective-permute-start.2) | collective-permute-done | bytes 327712 | tf_op jit(solution)/shard_map/ppermute | solution.py:88
  29.5 5.8 %collective-permute-done.3 = bf16[160,1024]{1,0:T(8,128)(2,1)S(1)} collective-permute-done((bf16[160,1024]{1,0:T(8,128)(2,1)S(1)}, bf16[160,1024]{1,0:T(8,128)(2,1)S(1)}, u32[]{:S(2)}, u32[]{:S(2)}) %collective-permute-start.3) | collective-permute-done | bytes 327712 | tf_op jit(solution)/shard_map/ppermute | solution.py:88
  39.8 1.6 collective-permute-start.7
  41.4 9.8 %collective-permute-done.6 = bf16[1,4,160,512]{3,2,1,0:T(8,128)(2,1)S(1)} collective-permute-done((bf16[1,4,160,512]{3,2,1,0:T(8,128)(2,1)S(1)}, bf16[1,4,160,512]{3,2,1,0:T(8,128)(2,1)S(1)}, u32[]{:S(2)}, u32[]{:S(2)}) %collective-permute-start.6) | collective-permute-done | bytes 655392 | tf_op jit(solution)/shard_map/ppermute | solution.py:66
  56.1 5.8 %collective-permute-start.11 = (bf16[192,1024]{1,0:T(8,128)(2,1)S(1)}, bf16[192,1024]{1,0:T(8,128)(2,1)S(1)}, u32[]{:S(2)}, u32[]{:S(2)}) collective-permute-start(bf16[192,1024]{1,0:T(8,128)(2,1)S(1)} %pad_maximum_fusion.13), channel_id=1, source_target_pairs={{0,3},{1,0},{2,1},{3,2},{4,7},{5,4},{6,5},{7,6},{8,11},{9,8},{10,9... | collective-permute-start | bytes 1179656 | tf_op jit(solution)/shard_map/ppermute | solution.py:84
  61.9 20.5 %collective-permute-done.9 = bf16[2,4,160,512]{3,2,1,0:T(8,128)(2,1)S(1)} collective-permute-done((bf16[2,4,160,512]{3,2,1,0:T(8,128)(2,1)S(1)}, bf16[2,4,160,512]{3,2,1,0:T(8,128)(2,1)S(1)}, u32[]{:S(2)}, u32[]{:S(2)}) %collective-permute-start.9) | collective-permute-done | bytes 1310752 | tf_op jit(solution)/shard_map/ppermute | solution.py:66
  86.7 10.0 %collective-permute-done.14 = bf16[1,4,96,512]{3,2,1,0:T(8,128)(2,1)S(1)} collective-permute-done((bf16[1,4,96,512]{3,2,1,0:T(8,128)(2,1)S(1)}, bf16[1,4,96,512]{3,2,1,0:T(8,128)(2,1)S(1)}, u32[]{:S(2)}, u32[]{:S(2)}) %collective-permute-start.14) | collective-permute-done | bytes 393248 | tf_op jit(solution)/shard_map/ppermute | solution.py:66
  99.2 2.3 copy-done.29
  105.2 12.2 %encoder.1 = (f32[16,1024]{1,0:T(8,128)S(1)}, bf16[256,1024]{1,0:T(8,128)(2,1)S(1)}, bf16[256,1024]{1,0:T(8,128)(2,1)S(1)}, bf16[256,384]{1,0:T(8,128)(2,1)S(1)}...) custom-call(s32[1,2]{1,0:T(1,128)S(1)} %copy-done.27, ...), custom_call_target="tpu_custom_call" | custom-call | flops 1073741824 | bytes 37748736 | tf_op jit(solution)/shard_map/encoder/pallas_call | solution.py:322
  118.9 1.8 collective-permute-done.15
  126.8 5.3 %collective-permute-start.17 = (bf16[256,1024]{1,0:T(8,128)(2,1)S(1)}, bf16[256,1024]{1,0:T(8,128)(2,1)S(1)}, u32[]{:S(2)}, u32[]{:S(2)}) collective-permute-start(bf16[256,1024]{1,0:T(8,128)(2,1)S(1)} %get-tuple-element.230.refs_0_), channel_id=1, source_target_pairs={{0,1},{1,2},{2,3},{4,5},{5,6},{6,7},{8,9},{9,10},{10,11},{12,13},{... | collective-permute-start | bytes 1572872 | tf_op jit(solution)/shard_map/ppermute | solution.py:88
  132.9 3.0 collective-permute-done.20
  136.0 6.7 %collective-permute-done.21 = bf16[1,4,96,512]{3,2,1,0:T(8,128)(2,1)S(1)} collective-permute-done((bf16[1,4,96,512]{3,2,1,0:T(8,128)(2,1)S(1)}, bf16[1,4,96,512]{3,2,1,0:T(8,128)(2,1)S(1)}, u32[]{:S(2)}, u32[]{:S(2)}) %collective-permute-start.21) | collective-permute-done | bytes 393248 | tf_op jit(solution)/shard_map/ppermute | solution.py:66
  148.7 12.8 %collective-permute-done.26 = bf16[2,4,96,512]{3,2,1,0:T(8,128)(2,1)S(1)} collective-permute-done((bf16[2,4,96,512]{3,2,1,0:T(8,128)(2,1)S(1)}, bf16[2,4,96,512]{3,2,1,0:T(8,128)(2,1)S(1)}, u32[]{:S(2)}, u32[]{:S(2)}) %collective-permute-start.26) | collective-permute-done | bytes 786464 | tf_op jit(solution)/shard_map/ppermute | solution.py:66
  163.4 13.5 %collective-permute-done.24.refs_5_ = bf16[256,1024]{1,0:T(8,128)(2,1)S(1)} collective-permute-done((bf16[256,1024]{1,0:T(8,128)(2,1)S(1)}, bf16[256,1024]{1,0:T(8,128)(2,1)S(1)}, u32[]{:S(2)}, u32[]{:S(2)}) %collective-permute-start.24) | collective-permute-done | bytes 524320 | tf_op jit(solution)/shard_map/ppermute | solution.py:88
  176.9 9.6 %attention.1 = (bf16[256,1024]{1,0:T(8,128)(2,1)S(1)}, bf16[1024,1024]{1,0:T(8,128)(2,1)S(1)}, bf16[256,1024]{1,0:T(8,128)(2,1)S(1)}, bf16[4,256,1024]{2,1,0:T(8,128)(2,1)S(1)}, bf16[4,256,1024]{2,1,0:T(8,128)(2,1)S(1)}) custom-call(bf16[256,1024]{1,0:T(8,128)(2,1)S(1)} %get-tuple-element.230.refs_0_, bf16[256,1024]{1,0:T(8,128)(2,1)S(1)} %collective-permute-done.17.refs_1_, ...), custom_call_target="tpu_custom_call" | custom-call | flops 1073741824 | bytes 41943040 | tf_op jit(solution)/shard_map/attention/pallas_call | solution.py:322
  189.2 9.3 %latent.1 = (bf16[256,1024]{1,0:T(8,128)(2,1)S(1)}, f32[8,1024]{1,0:T(8,128)S(1)}, bf16[256,1024]{1,0:T(8,128)(2,1)}, f32[256,1024]{1,0:T(8,128)S(1)}, bf16[4,3,...) custom-call(bf16[256,1024]{1,0:T(8,128)(2,1)S(1)} %get-tuple-element.241.refs_0_, ...), custom_call_target="tpu_custom_call" | custom-call | flops 1073741824 | bytes 37748736 | tf_op jit(solution)/shard_map/latent/pallas_call | solution.py:322
  198.7 1.7 copy-done.3
  201.8 20.2 %attention_back.1 = (bf16[3,256,1024]{2,1,0:T(8,128)(2,1)S(1)}, f32[256,1024]{1,0:T(8,128)S(1)}, bf16[4,3,128,1024]{3,2,1,0:T(8,128)(2,1)}, bf16[4,3,128,1024]{3,2,1,0:T(8,128)(2,1)}) custom-call(bf16[256,1024]{1,0:T(8,128)(2,1)S(1)} %get-tuple-element.246.refs_0_, bf16[4,256,1024]{2,1,0:T(8,128)(2,1)S(1)} %get-tuple-element.247.refs_1_, ...), custom_call_target="tpu_custom_call" | custom-call | flops 1073741824 | bytes 75497472 | tf_op jit(solution)/shard_map/attention_back/pallas_call | solution.py:322
  225.6 1.7 copy-done.4
  227.6 2.2 fusion.53
  232.1 2.8 collective-permute-start.30
  235.1 2.1 fusion.51
  237.5 11.1 %collective-permute-done.30 = bf16[256,1024]{1,0:T(8,128)(2,1)S(1)} collective-permute-done((bf16[256,1024]{1,0:T(8,128)(2,1)S(1)}, bf16[256,1024]{1,0:T(8,128)(2,1)S(1)}, u32[]{:S(2)}, u32[]{:S(2)}) %collective-permute-start.30) | collective-permute-done | bytes 524320 | tf_op jit(solution)/shard_map/ppermute | solution.py:88
  253.1 4.6 %collective-permute-start.34 = (bf16[256,1024]{1,0:T(8,128)(2,1)S(1)}, bf16[256,1024]{1,0:T(8,128)(2,1)S(1)}, u32[]{:S(2)}, u32[]{:S(2)}) collective-permute-start(bf16[256,1024]{1,0:T(8,128)(2,1)S(1)} %get-tuple-element.511), channel_id=1, source_target_pairs={{0,1},{1,2},{2,3},{4,5},{5,6},{6,7},{8,9},{9,10},{10,11},{12,13},{... | collective-permute-start | bytes 1572872 | tf_op jit(solution)/shard_map/ppermute | solution.py:88
  259.8 8.0 %collective-permute-done.37 = bf16[1,3,128,512]{3,2,1,0:T(8,128)(2,1)S(1)} collective-permute-done((bf16[1,3,128,512]{3,2,1,0:T(8,128)(2,1)S(1)}, bf16[1,3,128,512]{3,2,1,0:T(8,128)(2,1)S(1)}, u32[]{:S(2)}, u32[]{:S(2)}) %collective-permute-start.37) | collective-permute-done | bytes 393248 | tf_op jit(solution)/shard_map/ppermute | solution.py:66
  269.3 6.9 %encoder_back.1 = (f32[256,1024]{1,0:T(8,128)S(1)}, f32[8,1024]{1,0:T(8,128)S(1)}, bf16[4,2,128,1024]{3,2,1,0:T(8,128)(2,1)}, bf16[4,2,128,1024]{3,2,1,0:T(8,128)(2,1)S(1)}) custom-call(f32[256,1024]{1,0:T(8,128)S(1)} %copy-done.17, f32[256,1024]{1,0:T(8,128)S(1)} %copy-done.15, f32[256,1024]{1,0:T(8,128)S(1)} %copy-done.2, f32[256,1024]{1,0:T(8,128)S(1)} %copy-done.11, ...), custom_call_target="tpu_custom_call" | custom-call | flops 1073741824 | bytes 37748736 | tf_op jit(solution)/shard_map/encoder_back/pallas_call | solution.py:322
  282.8 1.6 collective-permute-start.43
  287.3 12.9 %cross_back.1 = (f32[4,264,512]{2,1,0:T(8,128)}, f32[264,128]{1,0:T(8,128)S(1)}, f32[256,1024]{1,0:T(8,128)}, bf16[4,3,128,1024]{3,2,1,0:T(8,128)(2,1)}, bf16[4,3,128,1024]{3,2,1,0:T(8,128)(2,1)}) custom-call(f32[256,1024]{1,0:T(8,128)S(1)} %get-tuple-element.290.refs_0_, bf16[256,1024]{1,0:T(8,128)(2,1)S(1)} %bitcast.476, bf16[256,1024]{1,0:T(8,128)(2,1)S(1)} %copy-done.22, ...), custom_call_target="tpu_custom_call" | custom-call | flops 1073741824 | bytes 52428800 | tf_op jit(solution)/shard_map/cross_back/pallas_call | solution.py:322
  313.2 1.7 fusion.55
  316.5 1.9 collective-permute-done.46
  324.0 1.7 collective-permute-start.49
  326.1 1.6 collective-permute-start.50
  328.1 7.3 %collective-permute-done.49 = bf16[264,512]{1,0:T(8,128)(2,1)S(1)} collective-permute-done((bf16[264,512]{1,0:T(8,128)(2,1)S(1)}, bf16[264,512]{1,0:T(8,128)(2,1)S(1)}, u32[]{:S(2)}, u32[]{:S(2)}) %collective-permute-start.49) | collective-permute-done | bytes 270368 | tf_op jit(solution)/shard_map/ppermute | solution.py:84
  335.4 4.8 %collective-permute-done.51 = bf16[264,512]{1,0:T(8,128)(2,1)S(1)} collective-permute-done((bf16[264,512]{1,0:T(8,128)(2,1)S(1)}, bf16[264,512]{1,0:T(8,128)(2,1)S(1)}, u32[]{:S(2)}, u32[]{:S(2)}) %collective-permute-start.51) | collective-permute-done | bytes 270368 | tf_op jit(solution)/shard_map/ppermute | solution.py:84
  340.2 8.6 %collective-permute-done.50 = bf16[264,512]{1,0:T(8,128)(2,1)S(1)} collective-permute-done((bf16[264,512]{1,0:T(8,128)(2,1)S(1)}, bf16[264,512]{1,0:T(8,128)(2,1)S(1)}, u32[]{:S(2)}, u32[]{:S(2)}) %collective-permute-start.50) | collective-permute-done | bytes 270368 | tf_op jit(solution)/shard_map/ppermute | solution.py:84
  351.9 1.6 collective-permute-start.54
  356.8 2.1 collective-permute-start.56
  360.0 9.0 %collective-permute-done.55 = bf16[3,32,1024]{2,1,0:T(8,128)(2,1)S(1)} collective-permute-done((bf16[3,32,1024]{2,1,0:T(8,128)(2,1)S(1)}, bf16[3,32,1024]{2,1,0:T(8,128)(2,1)S(1)}, u32[]{:S(2)}, u32[]{:S(2)}) %collective-permute-start.55) | collective-permute-done | bytes 196640 | tf_op jit(solution)/shard_map/ppermute | solution.py:66
  372.7 2.5 collective-permute-start.65
  375.4 2.0 collective-permute-start.63
  377.4 4.1 collective-permute-done.59
  383.8 4.8 %collective-permute-done.61 = f32[2,261]{0,1:T(8,128)S(1)} collective-permute-done((f32[2,261]{0,1:T(8,128)S(1)}, f32[2,261]{0,1:T(8,128)S(1)}, u32[]{:S(2)}, u32[]{:S(2)}) %collective-permute-start.61) | collective-permute-done | bytes 2120 | tf_op jit(solution)/shard_map/ppermute | solution.py:66
  390.1 3.6 collective-permute-done.62
  394.6 6.7 %collective-permute-done.64 = bf16[5,32,1024]{2,1,0:T(8,128)(2,1)S(1)} collective-permute-done((bf16[5,32,1024]{2,1,0:T(8,128)(2,1)S(1)}, bf16[5,32,1024]{2,1,0:T(8,128)(2,1)S(1)}, u32[]{:S(2)}, u32[]{:S(2)}) %collective-permute-start.64) | collective-permute-done | bytes 327712 | tf_op jit(solution)/shard_map/ppermute | solution.py:66
  (370 shorter events, 118.7 us)
Async XLA Ops:
  2.8 12.8 %collective-permute-start.1 = (bf16[160,1024]{1,0:T(8,128)(2,1)}, bf16[160,1024]{1,0:T(8,128)(2,1)S(1)}, u32[]{:S(2)}, u32[]{:S(2)}) collective-permute-start(bf16[160,1024]{1,0:T(8,128)(2,1)} %pack.1), channel_id=1, source_target_pairs={{3,2},{2,1},{1,0},{7,6},{6,5},{5,4},{11,10},{10,9},{9,8},{15,14},{... | collective-permute-start | bytes 983048 | tf_op jit(solution)/shard_map/ppermute | solution.py:88
  4.0 12.8 %collective-permute-start = (bf16[160,1024]{1,0:T(8,128)(2,1)}, bf16[160,1024]{1,0:T(8,128)(2,1)S(1)}, u32[]{:S(2)}, u32[]{:S(2)}) collective-permute-start(bf16[160,1024]{1,0:T(8,128)(2,1)} %pack.1), channel_id=1, source_target_pairs={{0,1},{1,2},{2,3},{4,5},{5,6},{6,7},{8,9},{9,10},{10,11},{12,13},{... | collective-permute-start | bytes 983048 | tf_op jit(solution)/shard_map/ppermute | solution.py:88
  16.9 11.6 %collective-permute-start.2 = (bf16[160,1024]{1,0:T(8,128)(2,1)S(1)}, bf16[160,1024]{1,0:T(8,128)(2,1)}, u32[]{:S(2)}, u32[]{:S(2)}) collective-permute-start(bf16[160,1024]{1,0:T(8,128)(2,1)S(1)} %broadcast_select_fusion.12), channel_id=1, source_target_pairs={{1,3},{2,0},{5,7},{6,4},{9,11},{10,8},{13,15},{14,12},{17,19},{18,... | collective-permute-start | bytes 983048 | tf_op jit(solution)/shard_map/ppermute | solution.py:88
  19.1 16.2 %collective-permute-start.3 = (bf16[160,1024]{1,0:T(8,128)(2,1)S(1)}, bf16[160,1024]{1,0:T(8,128)(2,1)S(1)}, u32[]{:S(2)}, u32[]{:S(2)}) collective-permute-start(bf16[160,1024]{1,0:T(8,128)(2,1)S(1)} %collective-permute-done.1), channel_id=1, source_target_pairs={{2,1},{1,0},{6,5},{5,4},{10,9},{9,8},{14,13},{13,12},{18,17},{17,1... | collective-permute-start | bytes 983048 | tf_op jit(solution)/shard_map/ppermute | solution.py:88
  35.8 15.4 %collective-permute-start.6 = (bf16[1,4,160,512]{3,2,1,0:T(8,128)(2,1)S(1)}, bf16[1,4,160,512]{3,2,1,0:T(8,128)(2,1)S(1)}, u32[]{:S(2)}, u32[]{:S(2)}) collective-permute-start(bf16[1,4,160,512]{3,2,1,0:T(8,128)(2,1)S(1)} %get-tuple-element.492), channel_id=1, source_target_pairs={{0,16},{1,17},{2,18},{3,19},{4,20},{5,21},{6,22},{7,23},{8,24},{9,... | collective-permute-start | bytes 1966088 | tf_op jit(solution)/shard_map/ppermute | solution.py:66
  37.4 15.1 %collective-permute-start.5 = (bf16[1,4,160,512]{3,2,1,0:T(8,128)(2,1)S(1)}, bf16[1,4,160,512]{3,2,1,0:T(8,128)(2,1)}, u32[]{:S(2)}, u32[]{:S(2)}) collective-permute-start(bf16[1,4,160,512]{3,2,1,0:T(8,128)(2,1)S(1)} %get-tuple-element.493), channel_id=1, source_target_pairs={{0,8},{1,9},{2,10},{3,11},{4,12},{5,13},{6,14},{7,15},{8,0},{9,1},... | collective-permute-start | bytes 1966088 | tf_op jit(solution)/shard_map/ppermute | solution.py:66
  39.8 14.2 %collective-permute-start.7 = (bf16[192,1024]{1,0:T(8,128)(2,1)S(1)}, bf16[192,1024]{1,0:T(8,128)(2,1)S(1)}, u32[]{:S(2)}, u32[]{:S(2)}) collective-permute-start(bf16[192,1024]{1,0:T(8,128)(2,1)S(1)} %pad_maximum_fusion.13), channel_id=1, source_target_pairs={{0,1},{1,2},{2,3},{3,0},{4,5},{5,6},{6,7},{7,4},{8,9},{9,10},{10,1... | collective-permute-start | bytes 1179656 | tf_op jit(solution)/shard_map/ppermute | solution.py:84
  54.0 28.4 %collective-permute-start.9 = (bf16[2,4,160,512]{3,2,1,0:T(8,128)(2,1)S(1)}, bf16[2,4,160,512]{3,2,1,0:T(8,128)(2,1)S(1)}, u32[]{:S(2)}, u32[]{:S(2)}) collective-permute-start(bf16[2,4,160,512]{3,2,1,0:T(8,128)(2,1)S(1)} %get-tuple-element.210), channel_id=1, source_target_pairs={{0,8},{1,9},{2,10},{3,11},{4,12},{5,13},{6,14},{7,15},{8,0},{9,1},... | collective-permute-start | bytes 3932168 | tf_op jit(solution)/shard_map/ppermute | solution.py:66
  55.6 27.9 %collective-permute-start.8 = (bf16[2,4,160,512]{3,2,1,0:T(8,128)(2,1)S(1)}, bf16[2,4,160,512]{3,2,1,0:T(8,128)(2,1)S(1)}, u32[]{:S(2)}, u32[]{:S(2)}) collective-permute-start(bf16[2,4,160,512]{3,2,1,0:T(8,128)(2,1)S(1)} %get-tuple-element.209), channel_id=1, source_target_pairs={{0,16},{1,17},{2,18},{3,19},{4,20},{5,21},{6,22},{7,23},{8,24},{9,... | collective-permute-start | bytes 3932168 | tf_op jit(solution)/shard_map/ppermute | solution.py:66
  56.1 27.8 %collective-permute-start.11 = (bf16[192,1024]{1,0:T(8,128)(2,1)S(1)}, bf16[192,1024]{1,0:T(8,128)(2,1)S(1)}, u32[]{:S(2)}, u32[]{:S(2)}) collective-permute-start(bf16[192,1024]{1,0:T(8,128)(2,1)S(1)} %pad_maximum_fusion.13), channel_id=1, source_target_pairs={{0,3},{1,0},{2,1},{3,2},{4,7},{5,4},{6,5},{7,6},{8,11},{9,8},{10,9... | collective-permute-start | bytes 1179656 | tf_op jit(solution)/shard_map/ppermute | solution.py:84
  61.9 22.0 %collective-permute-start.10 = (bf16[192,1024]{1,0:T(8,128)(2,1)S(1)}, bf16[192,1024]{1,0:T(8,128)(2,1)S(1)}, u32[]{:S(2)}, u32[]{:S(2)}) collective-permute-start(bf16[192,1024]{1,0:T(8,128)(2,1)S(1)} %pad_maximum_fusion.13), channel_id=1, source_target_pairs={{0,2},{1,3},{2,0},{3,1},{4,6},{5,7},{6,4},{7,5},{8,10},{9,11},{10,... | collective-permute-start | bytes 1179656 | tf_op jit(solution)/shard_map/ppermute | solution.py:84
  84.6 14.6 %collective-permute-start.12 = (bf16[4,4,160,1024]{3,2,1,0:T(8,128)(2,1)S(1)}, bf16[4,4,160,1024]{3,2,1,0:T(8,128)(2,1)S(1)}, u32[]{:S(2)}, u32[]{:S(2)}) collective-permute-start(bf16[4,4,160,1024]{3,2,1,0:T(8,128)(2,1)S(1)} %constant_dynamic-update-slice_fusion.refs_3_.refs_9_.refs_12_), channel_id=1, source_target_pairs={{0,4},{1,5},{2,6},{3,7},{4,0},{5,1},{6,2},{7,3},{8,12},{9,13},{10,... | collective-permute-start | bytes 15728648 | tf_op jit(solution)/shard_map/ppermute | solution.py:66
  101.5 19.1 %collective-permute-start.15 = (bf16[2,4,96,512]{3,2,1,0:T(8,128)(2,1)}, bf16[2,4,96,512]{3,2,1,0:T(8,128)(2,1)}, u32[]{:S(2)}, u32[]{:S(2)}) collective-permute-start(bf16[2,4,96,512]{3,2,1,0:T(8,128)(2,1)} %maximum_bitcast_fusion.3), channel_id=1, source_target_pairs={{0,16},{1,17},{2,18},{3,19},{4,20},{5,21},{6,22},{7,23},{8,24},{9,... | collective-permute-start | bytes 2359304 | tf_op jit(solution)/shard_map/ppermute | solution.py:66
  102.7 19.7 %collective-permute-start.16 = (bf16[2,4,96,512]{3,2,1,0:T(8,128)(2,1)S(1)}, bf16[2,4,96,512]{3,2,1,0:T(8,128)(2,1)}, u32[]{:S(2)}, u32[]{:S(2)}) collective-permute-start(bf16[2,4,96,512]{3,2,1,0:T(8,128)(2,1)S(1)} %maximum_bitcast_fusion.4), channel_id=1, source_target_pairs={{0,8},{1,9},{2,10},{3,11},{4,12},{5,13},{6,14},{7,15},{8,0},{9,1},... | collective-permute-start | bytes 2359304 | tf_op jit(solution)/shard_map/ppermute | solution.py:66
  124.3 18.9 %collective-permute-start.19 = (bf16[4,4,96,1024]{3,2,1,0:T(8,128)(2,1)S(1)}, bf16[4,4,96,1024]{3,2,1,0:T(8,128)(2,1)S(1)}, u32[]{:S(2)}, u32[]{:S(2)}) collective-permute-start(bf16[4,4,96,1024]{3,2,1,0:T(8,128)(2,1)S(1)} %pad_maximum_fusion.refs_6_.refs_5_), channel_id=1, source_target_pairs={{0,4},{1,5},{2,6},{3,7},{4,0},{5,1},{6,2},{7,3},{8,12},{9,13},{10,... | collective-permute-start | bytes 9437192 | tf_op jit(solution)/shard_map/ppermute | solution.py:66
  125.5 17.4 %collective-permute-start.18 = (bf16[256,1024]{1,0:T(8,128)(2,1)S(1)}, bf16[256,1024]{1,0:T(8,128)(2,1)S(1)}, u32[]{:S(2)}, u32[]{:S(2)}) collective-permute-start(bf16[256,1024]{1,0:T(8,128)(2,1)S(1)} %get-tuple-element.230.refs_0_), channel_id=1, source_target_pairs={{3,2},{2,1},{1,0},{7,6},{6,5},{5,4},{11,10},{10,9},{9,8},{15,14},{... | collective-permute-start | bytes 1572872 | tf_op jit(solution)/shard_map/ppermute | solution.py:88
  126.8 16.4 %collective-permute-start.17 = (bf16[256,1024]{1,0:T(8,128)(2,1)S(1)}, bf16[256,1024]{1,0:T(8,128)(2,1)S(1)}, u32[]{:S(2)}, u32[]{:S(2)}) collective-permute-start(bf16[256,1024]{1,0:T(8,128)(2,1)S(1)} %get-tuple-element.230.refs_0_), channel_id=1, source_target_pairs={{0,1},{1,2},{2,3},{4,5},{5,6},{6,7},{8,9},{9,10},{10,11},{12,13},{... | collective-permute-start | bytes 1572872 | tf_op jit(solution)/shard_map/ppermute | solution.py:88
  143.2 18.3 %collective-permute-start.26 = (bf16[2,4,96,512]{3,2,1,0:T(8,128)(2,1)S(1)}, bf16[2,4,96,512]{3,2,1,0:T(8,128)(2,1)S(1)}, u32[]{:S(2)}, u32[]{:S(2)}) collective-permute-start(bf16[2,4,96,512]{3,2,1,0:T(8,128)(2,1)S(1)} %maximum_bitcast_fusion.6), channel_id=1, source_target_pairs={{0,8},{1,9},{2,10},{3,11},{4,12},{5,13},{6,14},{7,15},{8,0},{9,1},... | collective-permute-start | bytes 2359304 | tf_op jit(solution)/shard_map/ppermute | solution.py:66
  144.7 18.0 %collective-permute-start.25 = (bf16[2,4,96,512]{3,2,1,0:T(8,128)(2,1)S(1)}, bf16[2,4,96,512]{3,2,1,0:T(8,128)(2,1)S(1)}, u32[]{:S(2)}, u32[]{:S(2)}) collective-permute-start(bf16[2,4,96,512]{3,2,1,0:T(8,128)(2,1)S(1)} %maximum_bitcast_fusion.5), channel_id=1, source_target_pairs={{0,16},{1,17},{2,18},{3,19},{4,20},{5,21},{6,22},{7,23},{8,24},{9,... | collective-permute-start | bytes 2359304 | tf_op jit(solution)/shard_map/ppermute | solution.py:66
  145.3 31.6 %collective-permute-start.22 = (bf16[256,1024]{1,0:T(8,128)(2,1)S(1)}, bf16[256,1024]{1,0:T(8,128)(2,1)S(1)}, u32[]{:S(2)}, u32[]{:S(2)}) collective-permute-start(bf16[256,1024]{1,0:T(8,128)(2,1)S(1)} %collective-permute-done.17.refs_1_), channel_id=1, source_target_pairs={{1,2},{2,3},{5,6},{6,7},{9,10},{10,11},{13,14},{14,15},{17,18},{18... | collective-permute-start | bytes 1572872 | tf_op jit(solution)/shard_map/ppermute | solution.py:88
  146.0 30.9 %collective-permute-start.23 = (bf16[256,1024]{1,0:T(8,128)(2,1)S(1)}, bf16[256,1024]{1,0:T(8,128)(2,1)S(1)}, u32[]{:S(2)}, u32[]{:S(2)}) collective-permute-start(bf16[256,1024]{1,0:T(8,128)(2,1)S(1)} %collective-permute-done.18.refs_2_), channel_id=1, source_target_pairs={{2,1},{1,0},{6,5},{5,4},{10,9},{9,8},{14,13},{13,12},{18,17},{17,1... | collective-permute-start | bytes 1572872 | tf_op jit(solution)/shard_map/ppermute | solution.py:88
  147.4 29.5 %collective-permute-start.24 = (bf16[256,1024]{1,0:T(8,128)(2,1)S(1)}, bf16[256,1024]{1,0:T(8,128)(2,1)S(1)}, u32[]{:S(2)}, u32[]{:S(2)}) collective-permute-start(bf16[256,1024]{1,0:T(8,128)(2,1)S(1)} %broadcast_select_fusion.1), channel_id=1, source_target_pairs={{1,3},{2,0},{5,7},{6,4},{9,11},{10,8},{13,15},{14,12},{17,19},{18,... | collective-permute-start | bytes 1572872 | tf_op jit(solution)/shard_map/ppermute | solution.py:88
  176.9 12.3 %collective-permute-start.27 = (bf16[4,4,96,1024]{3,2,1,0:T(8,128)(2,1)S(1)}, bf16[4,4,96,1024]{3,2,1,0:T(8,128)(2,1)}, u32[]{:S(2)}, u32[]{:S(2)}) collective-permute-start(bf16[4,4,96,1024]{3,2,1,0:T(8,128)(2,1)S(1)} %pad_maximum_fusion.1.refs_4_), channel_id=1, source_target_pairs={{0,4},{1,5},{2,6},{3,7},{4,0},{5,1},{6,2},{7,3},{8,12},{9,13},{10,... | collective-permute-start | bytes 9437192 | tf_op jit(solution)/shard_map/ppermute | solution.py:66
  201.3 26.2 %collective-permute-start.31 = (bf16[4,3,128,1024]{3,2,1,0:T(8,128)(2,1)}, bf16[4,3,128,1024]{3,2,1,0:T(8,128)(2,1)}, u32[]{:S(2)}, u32[]{:S(2)}) collective-permute-start(bf16[4,3,128,1024]{3,2,1,0:T(8,128)(2,1)} %get-tuple-element.261), channel_id=1, source_target_pairs={{0,4},{1,5},{2,6},{3,7},{4,0},{5,1},{6,2},{7,3},{8,12},{9,13},{10,... | collective-permute-start | bytes 9437192 | tf_op jit(solution)/shard_map/ppermute | solution.py:66
  223.1 14.1 %collective-permute-start.29 = (bf16[256,1024]{1,0:T(8,128)(2,1)S(1)}, bf16[256,1024]{1,0:T(8,128)(2,1)S(1)}, u32[]{:S(2)}, u32[]{:S(2)}) collective-permute-start(bf16[256,1024]{1,0:T(8,128)(2,1)S(1)} %get-tuple-element.468), channel_id=1, source_target_pairs={{3,2},{2,1},{7,6},{6,5},{11,10},{10,9},{15,14},{14,13},{19,18},{18... | collective-permute-start | bytes 1572872 | tf_op jit(solution)/shard_map/ppermute | solution.py:88
  223.9 13.6 %collective-permute-start.28 = (bf16[256,1024]{1,0:T(8,128)(2,1)S(1)}, bf16[256,1024]{1,0:T(8,128)(2,1)S(1)}, u32[]{:S(2)}, u32[]{:S(2)}) collective-permute-start(bf16[256,1024]{1,0:T(8,128)(2,1)S(1)} %get-tuple-element.468), channel_id=1, source_target_pairs={{0,1},{1,2},{4,5},{5,6},{8,9},{9,10},{12,13},{13,14},{16,17},{17,1... | collective-permute-start | bytes 1572872 | tf_op jit(solution)/shard_map/ppermute | solution.py:88
  230.0 20.0 %collective-permute-start.32 = (bf16[2,3,128,512]{3,2,1,0:T(8,128)(2,1)S(1)}, bf16[2,3,128,512]{3,2,1,0:T(8,128)(2,1)S(1)}, u32[]{:S(2)}, u32[]{:S(2)}) collective-permute-start(bf16[2,3,128,512]{3,2,1,0:T(8,128)(2,1)S(1)} %fusion.9), channel_id=1, source_target_pairs={{0,8},{1,9},{2,10},{3,11},{4,12},{5,13},{6,14},{7,15},{8,0},{9,1},... | collective-permute-start | bytes 2359304 | tf_op jit(solution)/shard_map/ppermute | solution.py:66
  231.2 19.7 %collective-permute-start.33 = (bf16[2,3,128,512]{3,2,1,0:T(8,128)(2,1)S(1)}, bf16[2,3,128,512]{3,2,1,0:T(8,128)(2,1)S(1)}, u32[]{:S(2)}, u32[]{:S(2)}) collective-permute-start(bf16[2,3,128,512]{3,2,1,0:T(8,128)(2,1)S(1)} %fusion.10), channel_id=1, source_target_pairs={{0,16},{1,17},{2,18},{3,19},{4,20},{5,21},{6,22},{7,23},{8,24},{9,... | collective-permute-start | bytes 2359304 | tf_op jit(solution)/shard_map/ppermute | solution.py:66
  232.1 16.5 %collective-permute-start.30 = (bf16[256,1024]{1,0:T(8,128)(2,1)S(1)}, bf16[256,1024]{1,0:T(8,128)(2,1)S(1)}, u32[]{:S(2)}, u32[]{:S(2)}) collective-permute-start(bf16[256,1024]{1,0:T(8,128)(2,1)S(1)} %broadcast_select_fusion), channel_id=1, source_target_pairs={{0,2},{3,1},{4,6},{7,5},{8,10},{11,9},{12,14},{15,13},{16,18},{19,... | collective-permute-start | bytes 1572872 | tf_op jit(solution)/shard_map/ppermute | solution.py:88
  251.8 16.8 %collective-permute-start.35 = (bf16[256,1024]{1,0:T(8,128)(2,1)S(1)}, bf16[256,1024]{1,0:T(8,128)(2,1)S(1)}, u32[]{:S(2)}, u32[]{:S(2)}) collective-permute-start(bf16[256,1024]{1,0:T(8,128)(2,1)S(1)} %get-tuple-element.510), channel_id=1, source_target_pairs={{3,2},{2,1},{1,0},{7,6},{6,5},{5,4},{11,10},{10,9},{9,8},{15,14},{... | collective-permute-start | bytes 1572872 | tf_op jit(solution)/shard_map/ppermute | solution.py:88
  253.1 15.5 %collective-permute-start.34 = (bf16[256,1024]{1,0:T(8,128)(2,1)S(1)}, bf16[256,1024]{1,0:T(8,128)(2,1)S(1)}, u32[]{:S(2)}, u32[]{:S(2)}) collective-permute-start(bf16[256,1024]{1,0:T(8,128)(2,1)S(1)} %get-tuple-element.511), channel_id=1, source_target_pairs={{0,1},{1,2},{2,3},{4,5},{5,6},{6,7},{8,9},{9,10},{10,11},{12,13},{... | collective-permute-start | bytes 1572872 | tf_op jit(solution)/shard_map/ppermute | solution.py:88
  277.6 23.6 %collective-permute-start.41 = (bf16[3,32,1024]{2,1,0:T(8,128)(2,1)S(1)}, bf16[3,32,1024]{2,1,0:T(8,128)(2,1)S(1)}, u32[]{:S(2)}, u32[]{:S(2)}) collective-permute-start(bf16[3,32,1024]{2,1,0:T(8,128)(2,1)S(1)} %pad_maximum_fusion.17), channel_id=1, source_target_pairs={{0,1},{1,0},{2,3},{3,2},{4,5},{5,4},{6,7},{7,6},{8,9},{9,8},{10,11... | collective-permute-start | bytes 589832 | tf_op jit(solution)/shard_map/ppermute | solution.py:66
  279.3 21.9 %collective-permute-start.40 = (bf16[2,3,128,512]{3,2,1,0:T(8,128)(2,1)S(1)}, bf16[2,3,128,512]{3,2,1,0:T(8,128)(2,1)}, u32[]{:S(2)}, u32[]{:S(2)}) collective-permute-start(bf16[2,3,128,512]{3,2,1,0:T(8,128)(2,1)S(1)} %fusion.12), channel_id=1, source_target_pairs={{0,16},{1,17},{2,18},{3,19},{4,20},{5,21},{6,22},{7,23},{8,24},{9,... | collective-permute-start | bytes 2359304 | tf_op jit(solution)/shard_map/ppermute | solution.py:66
  280.2 21.0 %collective-permute-start.39 = (bf16[2,3,128,512]{3,2,1,0:T(8,128)(2,1)S(1)}, bf16[2,3,128,512]{3,2,1,0:T(8,128)(2,1)S(1)}, u32[]{:S(2)}, u32[]{:S(2)}) collective-permute-start(bf16[2,3,128,512]{3,2,1,0:T(8,128)(2,1)S(1)} %fusion.11), channel_id=1, source_target_pairs={{0,8},{1,9},{2,10},{3,11},{4,12},{5,13},{6,14},{7,15},{8,0},{9,1},... | collective-permute-start | bytes 2359304 | tf_op jit(solution)/shard_map/ppermute | solution.py:66
  281.2 20.0 %collective-permute-start.42 = (bf16[3,32,1024]{2,1,0:T(8,128)(2,1)S(1)}, bf16[3,32,1024]{2,1,0:T(8,128)(2,1)S(1)}, u32[]{:S(2)}, u32[]{:S(2)}) collective-permute-start(bf16[3,32,1024]{2,1,0:T(8,128)(2,1)S(1)} %pad_maximum_fusion.18), channel_id=1, source_target_pairs={{0,2},{1,3},{2,0},{3,1},{4,6},{5,7},{6,4},{7,5},{8,10},{9,11},{10,... | collective-permute-start | bytes 589832 | tf_op jit(solution)/shard_map/ppermute | solution.py:66
  282.8 18.4 %collective-permute-start.43 = (bf16[3,32,1024]{2,1,0:T(8,128)(2,1)S(1)}, bf16[3,32,1024]{2,1,0:T(8,128)(2,1)S(1)}, u32[]{:S(2)}, u32[]{:S(2)}) collective-permute-start(bf16[3,32,1024]{2,1,0:T(8,128)(2,1)S(1)} %pad_maximum_fusion.19), channel_id=1, source_target_pairs={{0,3},{1,2},{2,1},{3,0},{4,7},{5,6},{6,5},{7,4},{8,11},{9,10},{10,... | collective-permute-start | bytes 589832 | tf_op jit(solution)/shard_map/ppermute | solution.py:66
  302.3 12.6 %collective-permute-start.45 = (bf16[4,3,128,1024]{3,2,1,0:T(8,128)(2,1)}, bf16[4,3,128,1024]{3,2,1,0:T(8,128)(2,1)S(1)}, u32[]{:S(2)}, u32[]{:S(2)}) collective-permute-start(bf16[4,3,128,1024]{3,2,1,0:T(8,128)(2,1)} %get-tuple-element.323), channel_id=1, source_target_pairs={{0,4},{1,5},{2,6},{3,7},{4,0},{5,1},{6,2},{7,3},{8,12},{9,13},{10,... | collective-permute-start | bytes 9437192 | tf_op jit(solution)/shard_map/ppermute | solution.py:66
  319.2 29.8 %collective-permute-start.52 = (bf16[2,5,128,512]{3,2,1,0:T(8,128)(2,1)S(1)}, bf16[2,5,128,512]{3,2,1,0:T(8,128)(2,1)S(1)}, u32[]{:S(2)}, u32[]{:S(2)}) collective-permute-start(bf16[2,5,128,512]{3,2,1,0:T(8,128)(2,1)S(1)} %fusion.3), channel_id=1, source_target_pairs={{0,8},{1,9},{2,10},{3,11},{4,12},{5,13},{6,14},{7,15},{8,0},{9,1},... | collective-permute-start | bytes 3932168 | tf_op jit(solution)/shard_map/ppermute | solution.py:66
  321.2 29.1 %collective-permute-start.53 = (bf16[2,5,128,512]{3,2,1,0:T(8,128)(2,1)S(1)}, bf16[2,5,128,512]{3,2,1,0:T(8,128)(2,1)S(1)}, u32[]{:S(2)}, u32[]{:S(2)}) collective-permute-start(bf16[2,5,128,512]{3,2,1,0:T(8,128)(2,1)S(1)} %fusion.4), channel_id=1, source_target_pairs={{0,16},{1,17},{2,18},{3,19},{4,20},{5,21},{6,22},{7,23},{8,24},{9,... | collective-permute-start | bytes 3932168 | tf_op jit(solution)/shard_map/ppermute | solution.py:66
  325.7 14.5 %collective-permute-start.51 = (bf16[264,512]{1,0:T(8,128)(2,1)S(1)}, bf16[264,512]{1,0:T(8,128)(2,1)S(1)}, u32[]{:S(2)}, u32[]{:S(2)}) collective-permute-start(bf16[264,512]{1,0:T(8,128)(2,1)S(1)} %get-tuple-element.501), channel_id=1, source_target_pairs={{0,1},{1,2},{2,3},{3,0},{4,5},{5,6},{6,7},{7,4},{8,9},{9,10},{10,1... | collective-permute-start | bytes 811016 | tf_op jit(solution)/shard_map/ppermute | solution.py:84
  326.1 22.7 %collective-permute-start.50 = (bf16[264,512]{1,0:T(8,128)(2,1)S(1)}, bf16[264,512]{1,0:T(8,128)(2,1)S(1)}, u32[]{:S(2)}, u32[]{:S(2)}) collective-permute-start(bf16[264,512]{1,0:T(8,128)(2,1)S(1)} %get-tuple-element.502), channel_id=1, source_target_pairs={{0,2},{1,3},{2,0},{3,1},{4,6},{5,7},{6,4},{7,5},{8,10},{9,11},{10,... | collective-permute-start | bytes 811016 | tf_op jit(solution)/shard_map/ppermute | solution.py:84
  353.5 15.5 %collective-permute-start.55 = (bf16[3,32,1024]{2,1,0:T(8,128)(2,1)S(1)}, bf16[3,32,1024]{2,1,0:T(8,128)(2,1)S(1)}, u32[]{:S(2)}, u32[]{:S(2)}) collective-permute-start(bf16[3,32,1024]{2,1,0:T(8,128)(2,1)S(1)} %pad_maximum_fusion.21), channel_id=1, source_target_pairs={{0,2},{1,3},{2,0},{3,1},{4,6},{5,7},{6,4},{7,5},{8,10},{9,11},{10,... | collective-permute-start | bytes 589832 | tf_op jit(solution)/shard_map/ppermute | solution.py:66
  354.3 15.5 %collective-permute-start.58 = (bf16[1,5,128,512]{3,2,1,0:T(8,128)(2,1)S(1)}, bf16[1,5,128,512]{3,2,1,0:T(8,128)(2,1)S(1)}, u32[]{:S(2)}, u32[]{:S(2)}) collective-permute-start(bf16[1,5,128,512]{3,2,1,0:T(8,128)(2,1)S(1)} %add_convert_fusion.7), channel_id=1, source_target_pairs={{0,8},{1,9},{2,10},{3,11},{4,12},{5,13},{6,14},{7,15},{8,0},{9,1},... | collective-permute-start | bytes 1966088 | tf_op jit(solution)/shard_map/ppermute | solution.py:66
  355.4 15.2 %collective-permute-start.57 = (bf16[1,5,128,512]{3,2,1,0:T(8,128)(2,1)S(1)}, bf16[1,5,128,512]{3,2,1,0:T(8,128)(2,1)S(1)}, u32[]{:S(2)}, u32[]{:S(2)}) collective-permute-start(bf16[1,5,128,512]{3,2,1,0:T(8,128)(2,1)S(1)} %add_convert_fusion.8), channel_id=1, source_target_pairs={{0,16},{1,17},{2,18},{3,19},{4,20},{5,21},{6,22},{7,23},{8,24},{9,... | collective-permute-start | bytes 1966088 | tf_op jit(solution)/shard_map/ppermute | solution.py:66
  356.8 12.3 %collective-permute-start.56 = (bf16[3,32,1024]{2,1,0:T(8,128)(2,1)S(1)}, bf16[3,32,1024]{2,1,0:T(8,128)(2,1)S(1)}, u32[]{:S(2)}, u32[]{:S(2)}) collective-permute-start(bf16[3,32,1024]{2,1,0:T(8,128)(2,1)S(1)} %pad_maximum_fusion.22), channel_id=1, source_target_pairs={{0,3},{1,2},{2,1},{3,0},{4,7},{5,6},{6,5},{7,4},{8,11},{9,10},{10,... | collective-permute-start | bytes 589832 | tf_op jit(solution)/shard_map/ppermute | solution.py:66
  372.7 21.8 %collective-permute-start.65 = (bf16[5,32,1024]{2,1,0:T(8,128)(2,1)S(1)}, bf16[5,32,1024]{2,1,0:T(8,128)(2,1)S(1)}, u32[]{:S(2)}, u32[]{:S(2)}) collective-permute-start(bf16[5,32,1024]{2,1,0:T(8,128)(2,1)S(1)} %pad_maximum_fusion.16), channel_id=1, source_target_pairs={{0,3},{1,2},{2,1},{3,0},{4,7},{5,6},{6,5},{7,4},{8,11},{9,10},{10,... | collective-permute-start | bytes 983048 | tf_op jit(solution)/shard_map/ppermute | solution.py:66
  375.3 26.0 %collective-permute-start.64 = (bf16[5,32,1024]{2,1,0:T(8,128)(2,1)S(1)}, bf16[5,32,1024]{2,1,0:T(8,128)(2,1)S(1)}, u32[]{:S(2)}, u32[]{:S(2)}) collective-permute-start(bf16[5,32,1024]{2,1,0:T(8,128)(2,1)S(1)} %pad_maximum_fusion.15), channel_id=1, source_target_pairs={{0,2},{1,3},{2,0},{3,1},{4,6},{5,7},{6,4},{7,5},{8,10},{9,11},{10,... | collective-permute-start | bytes 983048 | tf_op jit(solution)/shard_map/ppermute | solution.py:66
  375.4 25.9 %collective-permute-start.63 = (bf16[5,32,1024]{2,1,0:T(8,128)(2,1)S(1)}, bf16[5,32,1024]{2,1,0:T(8,128)(2,1)S(1)}, u32[]{:S(2)}, u32[]{:S(2)}) collective-permute-start(bf16[5,32,1024]{2,1,0:T(8,128)(2,1)S(1)} %pad_maximum_fusion.14), channel_id=1, source_target_pairs={{0,1},{1,0},{2,3},{3,2},{4,5},{5,4},{6,7},{7,6},{8,9},{9,8},{10,11... | collective-permute-start | bytes 983048 | tf_op jit(solution)/shard_map/ppermute | solution.py:66
  (79 other events, 620.9 us)

commit v7 on v6

--- a/solution.py
+++ b/solution.py
@@ -571,7 +571,7 @@
         piece = d_pix[:, target * share : last]
         if last < (target + 1) * share:
             piece = jnp.concatenate([piece, jnp.zeros((kept, (target + 1) * share - last), F32)], axis=1)
-        d_pix_o[slot] = piece
+        d_pix_o[slot] = piece.astype(BF)
     d_query_pix = mm(d_scores, pix[...]).astype(BF)
     d_enc_q = mm_t(d_query_pix, kv[:, :padded]).astype(BF)
     hat, inverse = norm_parts(latents[...].astype(F32))
@@ -807,7 +807,7 @@
         [grad_enc, latents.reshape(rows, width), enc_mixed, mixed_pix, probs, pix_low, query_pix, enc_q, small_all]
         + [lat_sums, enc_sums, pix_hat_t],
         enc_sources,
-        [wide((fsdp_size, kept, share), F32), wide((kept, LANES), F32)]
+        [wide((fsdp_size, kept, share), BF), wide((kept, LANES), F32)]
         + [wide((rows, width), F32)] + pack.grads(3),
         [pack.scratch()] * 3
         + [pltpu.VMEM((rows, width), BF)] * 2
@@ -829,9 +829,9 @@
     pieces, grads_e, grads_f, grads_q, d_pix_sums = seal(pieces, grads_e, grads_f, grads_q, d_pix_sums)
 
     grads_e = [[jnp.concatenate(both, axis=1) for both in zip(e, f)] for e, f in zip(grads_e, grads_f)]
-    d_pix_own = pieces[0]
+    d_pix_own = pieces[0].astype(F32)
     for j in range(1, fsdp_size):
-        d_pix_own = d_pix_own + slot_shift(pieces[j].astype(BF), fsdp_size, fsdp_size - j).astype(F32)
+        d_pix_own = d_pix_own + slot_shift(pieces[j], fsdp_size, fsdp_size - j).astype(F32)
     grads_e = far_pair(grads_e, 0, sizes, me)
     d_pix_own, grads_e, grads_q, d_pix_sums = seal(d_pix_own, grads_e, grads_q, d_pix_sums)
 

time: 411 us -> 408 us (level)
  waiting for transfers between devices: 175 us -> 167 us
  starting transfers between devices: 84.5 us -> 90.6 us
    ppermute x45, waiting for transfers between devices: 114 us -> 106 us  [xor_permute(): return lax.ppermute(values, AXES, [(i, i ^ step) for i in range(total)])]
    ppermute x45, starting transfers between devices: 42.6 us -> 48.8 us  [xor_permute(): return lax.ppermute(values, AXES, [(i, i ^ step) for i in range(total)])]
    unnamed x127 -> x121, local copies, waits for them, and re-layouts: 19 us -> 20.6 us
  transfers between devices with their start and end apart: 66 -> 66, of which waited for: 37 -> 39; matrix products, arithmetic and copies ran while one was open for 10% -> 10% of each run, Pallas kernels for 14% -> 14%
where the time goes in v7:
time: 408 us; the launch traced here: 404 us
  waiting for transfers between devices  167 us (41%)
  starting transfers between devices  90.6 us (22%)
  Pallas kernels  72.9 us (18%)
  local copies, waits for them, and re-layouts  45.8 us (11%)
  other arithmetic  25.2 us (6%)
    ppermute x45, waiting for transfers between devices, xor_permute(): return lax.ppermute(values, AXES, [(i, i ^ step) for i in range(total)])  106 us
    pallas_call x6, Pallas kernels, kernel_call(): pl.pallas_call(kernel, in_specs=specs, out_specs=[pl.BlockSpec(memory_spa...  70.8 us
    ppermute x45, starting transfers between devices, xor_permute(): return lax.ppermute(values, AXES, [(i, i ^ step) for i in range(total)])  48.8 us
    ppermute x15, waiting for transfers between devices, hop(): return lax.ppermute(values, 'fsdp', pairs)  39.9 us
    ppermute x15, starting transfers between devices, hop(): return lax.ppermute(values, 'fsdp', pairs)  30.8 us
    ppermute x6, waiting for transfers between devices, slot_shift(): lax.ppermute(values, 'fsdp', [(i, (i + j) % size) for i in range(size)])  20.6 us
    unnamed x121, local copies, waits for them, and re-layouts  20.6 us
    ppermute x6, starting transfers between devices, slot_shift(): lax.ppermute(values, 'fsdp', [(i, (i + j) % size) for i in range(size)])  11 us
  transfers between devices with their start and end apart: 66, of which 39 were waited for; matrix products, arithmetic and copies ran while one was open for 10% of the time, Pallas kernels for 14%

profile of v7, /device:TPU:0, one launch (start us, length us, event | category | flops | bytes accessed | tf_op | source)
XLA Modules:
  0.0 404.0 jit_solution(5198055826573461172)
XLA Ops:
  0.7 2.1 pack.1
  4.0 5.6 %collective-permute-start = (bf16[160,1024]{1,0:T(8,128)(2,1)}, bf16[160,1024]{1,0:T(8,128)(2,1)S(1)}, u32[]{:S(2)}, u32[]{:S(2)}) collective-permute-start(bf16[160,1024]{1,0:T(8,128)(2,1)} %pack.1), channel_id=1, source_target_pairs={{0,1},{1,2},{2,3},{4,5},{5,6},{6,7},{8,9},{9,10},{10,11},{12,13},{... | collective-permute-start | bytes 983048 | tf_op jit(solution)/shard_map/ppermute | solution.py:88
  13.2 2.4 collective-permute-done.1
  23.0 5.5 %collective-permute-done.2 = bf16[160,1024]{1,0:T(8,128)(2,1)} collective-permute-done((bf16[160,1024]{1,0:T(8,128)(2,1)S(1)}, bf16[160,1024]{1,0:T(8,128)(2,1)}, u32[]{:S(2)}, u32[]{:S(2)}) %collective-permute-start.2) | collective-permute-done | bytes 327712 | tf_op jit(solution)/shard_map/ppermute | solution.py:88
  29.5 5.8 %collective-permute-done.3 = bf16[160,1024]{1,0:T(8,128)(2,1)S(1)} collective-permute-done((bf16[160,1024]{1,0:T(8,128)(2,1)S(1)}, bf16[160,1024]{1,0:T(8,128)(2,1)S(1)}, u32[]{:S(2)}, u32[]{:S(2)}) %collective-permute-start.3) | collective-permute-done | bytes 327712 | tf_op jit(solution)/shard_map/ppermute | solution.py:88
  39.8 1.6 collective-permute-start.7
  41.4 9.8 %collective-permute-done.6 = bf16[1,4,160,512]{3,2,1,0:T(8,128)(2,1)S(1)} collective-permute-done((bf16[1,4,160,512]{3,2,1,0:T(8,128)(2,1)S(1)}, bf16[1,4,160,512]{3,2,1,0:T(8,128)(2,1)S(1)}, u32[]{:S(2)}, u32[]{:S(2)}) %collective-permute-start.6) | collective-permute-done | bytes 655392 | tf_op jit(solution)/shard_map/ppermute | solution.py:66
  56.1 5.8 %collective-permute-start.11 = (bf16[192,1024]{1,0:T(8,128)(2,1)S(1)}, bf16[192,1024]{1,0:T(8,128)(2,1)S(1)}, u32[]{:S(2)}, u32[]{:S(2)}) collective-permute-start(bf16[192,1024]{1,0:T(8,128)(2,1)S(1)} %pad_maximum_fusion.13), channel_id=1, source_target_pairs={{0,3},{1,0},{2,1},{3,2},{4,7},{5,4},{6,5},{7,6},{8,11},{9,8},{10,9... | collective-permute-start | bytes 1179656 | tf_op jit(solution)/shard_map/ppermute | solution.py:84
  61.9 20.5 %collective-permute-done.9 = bf16[2,4,160,512]{3,2,1,0:T(8,128)(2,1)S(1)} collective-permute-done((bf16[2,4,160,512]{3,2,1,0:T(8,128)(2,1)S(1)}, bf16[2,4,160,512]{3,2,1,0:T(8,128)(2,1)S(1)}, u32[]{:S(2)}, u32[]{:S(2)}) %collective-permute-start.9) | collective-permute-done | bytes 1310752 | tf_op jit(solution)/shard_map/ppermute | solution.py:66
  86.7 10.0 %collective-permute-done.14 = bf16[1,4,96,512]{3,2,1,0:T(8,128)(2,1)S(1)} collective-permute-done((bf16[1,4,96,512]{3,2,1,0:T(8,128)(2,1)S(1)}, bf16[1,4,96,512]{3,2,1,0:T(8,128)(2,1)S(1)}, u32[]{:S(2)}, u32[]{:S(2)}) %collective-permute-start.14) | collective-permute-done | bytes 393248 | tf_op jit(solution)/shard_map/ppermute | solution.py:66
  98.5 2.3 copy-done.29
  104.5 12.2 %encoder.1 = (f32[16,1024]{1,0:T(8,128)S(1)}, bf16[256,1024]{1,0:T(8,128)(2,1)S(1)}, bf16[256,1024]{1,0:T(8,128)(2,1)S(1)}, bf16[256,384]{1,0:T(8,128)(2,1)S(1)}...) custom-call(s32[1,2]{1,0:T(1,128)S(1)} %copy-done.27, ...), custom_call_target="tpu_custom_call" | custom-call | flops 1073741824 | bytes 37748736 | tf_op jit(solution)/shard_map/encoder/pallas_call | solution.py:322
  118.1 1.6 collective-permute-done.15
  125.8 5.3 %collective-permute-start.17 = (bf16[256,1024]{1,0:T(8,128)(2,1)S(1)}, bf16[256,1024]{1,0:T(8,128)(2,1)S(1)}, u32[]{:S(2)}, u32[]{:S(2)}) collective-permute-start(bf16[256,1024]{1,0:T(8,128)(2,1)S(1)} %get-tuple-element.230.refs_0_), channel_id=1, source_target_pairs={{0,1},{1,2},{2,3},{4,5},{5,6},{6,7},{8,9},{9,10},{10,11},{12,13},{... | collective-permute-start | bytes 1572872 | tf_op jit(solution)/shard_map/ppermute | solution.py:88
  132.1 2.8 collective-permute-done.20
  135.0 6.7 %collective-permute-done.21 = bf16[1,4,96,512]{3,2,1,0:T(8,128)(2,1)S(1)} collective-permute-done((bf16[1,4,96,512]{3,2,1,0:T(8,128)(2,1)S(1)}, bf16[1,4,96,512]{3,2,1,0:T(8,128)(2,1)S(1)}, u32[]{:S(2)}, u32[]{:S(2)}) %collective-permute-start.21) | collective-permute-done | bytes 393248 | tf_op jit(solution)/shard_map/ppermute | solution.py:66
  147.6 12.8 %collective-permute-done.26 = bf16[2,4,96,512]{3,2,1,0:T(8,128)(2,1)S(1)} collective-permute-done((bf16[2,4,96,512]{3,2,1,0:T(8,128)(2,1)S(1)}, bf16[2,4,96,512]{3,2,1,0:T(8,128)(2,1)S(1)}, u32[]{:S(2)}, u32[]{:S(2)}) %collective-permute-start.26) | collective-permute-done | bytes 786464 | tf_op jit(solution)/shard_map/ppermute | solution.py:66
  162.4 13.5 %collective-permute-done.24.refs_5_ = bf16[256,1024]{1,0:T(8,128)(2,1)S(1)} collective-permute-done((bf16[256,1024]{1,0:T(8,128)(2,1)S(1)}, bf16[256,1024]{1,0:T(8,128)(2,1)S(1)}, u32[]{:S(2)}, u32[]{:S(2)}) %collective-permute-start.24) | collective-permute-done | bytes 524320 | tf_op jit(solution)/shard_map/ppermute | solution.py:88
  175.9 9.6 %attention.1 = (bf16[256,1024]{1,0:T(8,128)(2,1)S(1)}, bf16[1024,1024]{1,0:T(8,128)(2,1)S(1)}, bf16[256,1024]{1,0:T(8,128)(2,1)S(1)}, bf16[4,256,1024]{2,1,0:T(8,128)(2,1)S(1)}, bf16[4,256,1024]{2,1,0:T(8,128)(2,1)S(1)}) custom-call(bf16[256,1024]{1,0:T(8,128)(2,1)S(1)} %get-tuple-element.230.refs_0_, bf16[256,1024]{1,0:T(8,128)(2,1)S(1)} %collective-permute-done.17.refs_1_, ...), custom_call_target="tpu_custom_call" | custom-call | flops 1073741824 | bytes 41943040 | tf_op jit(solution)/shard_map/attention/pallas_call | solution.py:322
  188.1 9.3 %latent.1 = (bf16[256,1024]{1,0:T(8,128)(2,1)S(1)}, f32[8,1024]{1,0:T(8,128)S(1)}, bf16[256,1024]{1,0:T(8,128)(2,1)}, f32[256,1024]{1,0:T(8,128)S(1)}, bf16[4,3,...) custom-call(bf16[256,1024]{1,0:T(8,128)(2,1)S(1)} %get-tuple-element.241.refs_0_, ...), custom_call_target="tpu_custom_call" | custom-call | flops 1073741824 | bytes 37748736 | tf_op jit(solution)/shard_map/latent/pallas_call | solution.py:322
  197.7 1.7 copy-done.3
  200.8 20.2 %attention_back.1 = (bf16[3,256,1024]{2,1,0:T(8,128)(2,1)S(1)}, f32[256,1024]{1,0:T(8,128)S(1)}, bf16[4,3,128,1024]{3,2,1,0:T(8,128)(2,1)}, bf16[4,3,128,1024]{3,2,1,0:T(8,128)(2,1)}) custom-call(bf16[256,1024]{1,0:T(8,128)(2,1)S(1)} %get-tuple-element.246.refs_0_, bf16[4,256,1024]{2,1,0:T(8,128)(2,1)S(1)} %get-tuple-element.247.refs_1_, ...), custom_call_target="tpu_custom_call" | custom-call | flops 1073741824 | bytes 75497472 | tf_op jit(solution)/shard_map/attention_back/pallas_call | solution.py:322
  226.7 2.2 fusion.53
  231.2 2.8 collective-permute-start.30
  234.2 2.2 fusion.51
  236.5 11.0 %collective-permute-done.30 = bf16[256,1024]{1,0:T(8,128)(2,1)S(1)} collective-permute-done((bf16[256,1024]{1,0:T(8,128)(2,1)S(1)}, bf16[256,1024]{1,0:T(8,128)(2,1)S(1)}, u32[]{:S(2)}, u32[]{:S(2)}) %collective-permute-start.30) | collective-permute-done | bytes 524320 | tf_op jit(solution)/shard_map/ppermute | solution.py:88
  252.2 4.6 %collective-permute-start.34 = (bf16[256,1024]{1,0:T(8,128)(2,1)S(1)}, bf16[256,1024]{1,0:T(8,128)(2,1)S(1)}, u32[]{:S(2)}, u32[]{:S(2)}) collective-permute-start(bf16[256,1024]{1,0:T(8,128)(2,1)S(1)} %get-tuple-element.511), channel_id=1, source_target_pairs={{0,1},{1,2},{2,3},{4,5},{5,6},{6,7},{8,9},{9,10},{10,11},{12,13},{... | collective-permute-start | bytes 1572872 | tf_op jit(solution)/shard_map/ppermute | solution.py:88
  258.9 8.0 %collective-permute-done.37 = bf16[1,3,128,512]{3,2,1,0:T(8,128)(2,1)S(1)} collective-permute-done((bf16[1,3,128,512]{3,2,1,0:T(8,128)(2,1)S(1)}, bf16[1,3,128,512]{3,2,1,0:T(8,128)(2,1)S(1)}, u32[]{:S(2)}, u32[]{:S(2)}) %collective-permute-start.37) | collective-permute-done | bytes 393248 | tf_op jit(solution)/shard_map/ppermute | solution.py:66
  268.4 6.8 %encoder_back.1 = (f32[256,1024]{1,0:T(8,128)S(1)}, f32[8,1024]{1,0:T(8,128)S(1)}, bf16[4,2,128,1024]{3,2,1,0:T(8,128)(2,1)}, bf16[4,2,128,1024]{3,2,1,0:T(8,128)(2,1)S(1)}) custom-call(f32[256,1024]{1,0:T(8,128)S(1)} %copy-done.17, f32[256,1024]{1,0:T(8,128)S(1)} %copy-done.15, f32[256,1024]{1,0:T(8,128)S(1)} %copy-done.2, f32[256,1024]{1,0:T(8,128)S(1)} %copy-done.11, ...), custom_call_target="tpu_custom_call" | custom-call | flops 1073741824 | bytes 37748736 | tf_op jit(solution)/shard_map/encoder_back/pallas_call | solution.py:322
  281.6 1.7 collective-permute-start.43
  286.3 12.8 %cross_back.1 = (bf16[4,264,512]{2,1,0:T(8,128)(2,1)S(1)}, f32[264,128]{1,0:T(8,128)S(1)}, f32[256,1024]{1,0:T(8,128)}, bf16[4,3,128,1024]{3,2,1,0:T(8,128)(2,1)}, bf16[4,3,128,1024]{3,2,1,0:T(8,128)(2,1)}) custom-call(f32[256,1024]{1,0:T(8,128)S(1)} %get-tuple-element.290.refs_0_, bf16[256,1024]{1,0:T(8,128)(2,1)S(1)} %bitcast.473, ...), custom_call_target="tpu_custom_call" | custom-call | flops 1073741824 | bytes 52428800 | tf_op jit(solution)/shard_map/cross_back/pallas_call | solution.py:322
  311.2 1.7 fusion.55
  312.9 2.2 fusion.49
  321.7 1.6 collective-permute-start.49
  323.7 1.6 collective-permute-start.50
  325.7 8.2 %collective-permute-done.49 = bf16[264,512]{1,0:T(8,128)(2,1)S(1)} collective-permute-done((bf16[264,512]{1,0:T(8,128)(2,1)S(1)}, bf16[264,512]{1,0:T(8,128)(2,1)S(1)}, u32[]{:S(2)}, u32[]{:S(2)}) %collective-permute-start.49) | collective-permute-done | bytes 270368 | tf_op jit(solution)/shard_map/ppermute | solution.py:84
  333.9 4.0 %collective-permute-done.51 = bf16[264,512]{1,0:T(8,128)(2,1)S(1)} collective-permute-done((bf16[264,512]{1,0:T(8,128)(2,1)S(1)}, bf16[264,512]{1,0:T(8,128)(2,1)S(1)}, u32[]{:S(2)}, u32[]{:S(2)}) %collective-permute-start.51) | collective-permute-done | bytes 270368 | tf_op jit(solution)/shard_map/ppermute | solution.py:84
  338.0 8.4 %collective-permute-done.50 = bf16[264,512]{1,0:T(8,128)(2,1)S(1)} collective-permute-done((bf16[264,512]{1,0:T(8,128)(2,1)S(1)}, bf16[264,512]{1,0:T(8,128)(2,1)S(1)}, u32[]{:S(2)}, u32[]{:S(2)}) %collective-permute-start.50) | collective-permute-done | bytes 270368 | tf_op jit(solution)/shard_map/ppermute | solution.py:84
  346.8 1.7 collective-permute-done.53
  351.2 1.7 collective-permute-start.55
  355.3 1.8 collective-permute-start.56
  358.2 8.5 %collective-permute-done.55 = bf16[3,32,1024]{2,1,0:T(8,128)(2,1)S(1)} collective-permute-done((bf16[3,32,1024]{2,1,0:T(8,128)(2,1)S(1)}, bf16[3,32,1024]{2,1,0:T(8,128)(2,1)S(1)}, u32[]{:S(2)}, u32[]{:S(2)}) %collective-permute-start.55) | collective-permute-done | bytes 196640 | tf_op jit(solution)/shard_map/ppermute | solution.py:66
  370.4 2.4 collective-permute-start.65
  373.0 2.1 collective-permute-start.63
  377.5 4.4 %collective-permute-start.61 = (f32[2,261]{0,1:T(8,128)S(1)}, f32[2,261]{0,1:T(8,128)S(1)}, u32[]{:S(2)}, u32[]{:S(2)}) collective-permute-start(f32[2,261]{0,1:T(8,128)S(1)} %add.791), channel_id=1, source_target_pairs={{0,8},{1,9},{2,10},{3,11},{4,12},{5,13},{6,14},{7,15},{8,0},{9,1},... | collective-permute-start | bytes 6272 | tf_op jit(solution)/shard_map/ppermute | solution.py:66
  382.8 3.1 collective-permute-done.61
  388.5 2.5 collective-permute-done.62
  391.9 6.9 %collective-permute-done.64 = bf16[5,32,1024]{2,1,0:T(8,128)(2,1)S(1)} collective-permute-done((bf16[5,32,1024]{2,1,0:T(8,128)(2,1)S(1)}, bf16[5,32,1024]{2,1,0:T(8,128)(2,1)S(1)}, u32[]{:S(2)}, u32[]{:S(2)}) %collective-permute-start.64) | collective-permute-done | bytes 327712 | tf_op jit(solution)/shard_map/ppermute | solution.py:66
  (363 shorter events, 119.5 us)
Async XLA Ops:
  2.8 12.8 %collective-permute-start.1 = (bf16[160,1024]{1,0:T(8,128)(2,1)}, bf16[160,1024]{1,0:T(8,128)(2,1)S(1)}, u32[]{:S(2)}, u32[]{:S(2)}) collective-permute-start(bf16[160,1024]{1,0:T(8,128)(2,1)} %pack.1), channel_id=1, source_target_pairs={{3,2},{2,1},{1,0},{7,6},{6,5},{5,4},{11,10},{10,9},{9,8},{15,14},{... | collective-permute-start | bytes 983048 | tf_op jit(solution)/shard_map/ppermute | solution.py:88
  4.0 12.8 %collective-permute-start = (bf16[160,1024]{1,0:T(8,128)(2,1)}, bf16[160,1024]{1,0:T(8,128)(2,1)S(1)}, u32[]{:S(2)}, u32[]{:S(2)}) collective-permute-start(bf16[160,1024]{1,0:T(8,128)(2,1)} %pack.1), channel_id=1, source_target_pairs={{0,1},{1,2},{2,3},{4,5},{5,6},{6,7},{8,9},{9,10},{10,11},{12,13},{... | collective-permute-start | bytes 983048 | tf_op jit(solution)/shard_map/ppermute | solution.py:88
  16.9 11.6 %collective-permute-start.2 = (bf16[160,1024]{1,0:T(8,128)(2,1)S(1)}, bf16[160,1024]{1,0:T(8,128)(2,1)}, u32[]{:S(2)}, u32[]{:S(2)}) collective-permute-start(bf16[160,1024]{1,0:T(8,128)(2,1)S(1)} %broadcast_select_fusion.12), channel_id=1, source_target_pairs={{1,3},{2,0},{5,7},{6,4},{9,11},{10,8},{13,15},{14,12},{17,19},{18,... | collective-permute-start | bytes 983048 | tf_op jit(solution)/shard_map/ppermute | solution.py:88
  19.1 16.2 %collective-permute-start.3 = (bf16[160,1024]{1,0:T(8,128)(2,1)S(1)}, bf16[160,1024]{1,0:T(8,128)(2,1)S(1)}, u32[]{:S(2)}, u32[]{:S(2)}) collective-permute-start(bf16[160,1024]{1,0:T(8,128)(2,1)S(1)} %collective-permute-done.1), channel_id=1, source_target_pairs={{2,1},{1,0},{6,5},{5,4},{10,9},{9,8},{14,13},{13,12},{18,17},{17,1... | collective-permute-start | bytes 983048 | tf_op jit(solution)/shard_map/ppermute | solution.py:88
  35.8 15.4 %collective-permute-start.6 = (bf16[1,4,160,512]{3,2,1,0:T(8,128)(2,1)S(1)}, bf16[1,4,160,512]{3,2,1,0:T(8,128)(2,1)S(1)}, u32[]{:S(2)}, u32[]{:S(2)}) collective-permute-start(bf16[1,4,160,512]{3,2,1,0:T(8,128)(2,1)S(1)} %get-tuple-element.492), channel_id=1, source_target_pairs={{0,16},{1,17},{2,18},{3,19},{4,20},{5,21},{6,22},{7,23},{8,24},{9,... | collective-permute-start | bytes 1966088 | tf_op jit(solution)/shard_map/ppermute | solution.py:66
  37.4 15.1 %collective-permute-start.5 = (bf16[1,4,160,512]{3,2,1,0:T(8,128)(2,1)S(1)}, bf16[1,4,160,512]{3,2,1,0:T(8,128)(2,1)}, u32[]{:S(2)}, u32[]{:S(2)}) collective-permute-start(bf16[1,4,160,512]{3,2,1,0:T(8,128)(2,1)S(1)} %get-tuple-element.493), channel_id=1, source_target_pairs={{0,8},{1,9},{2,10},{3,11},{4,12},{5,13},{6,14},{7,15},{8,0},{9,1},... | collective-permute-start | bytes 1966088 | tf_op jit(solution)/shard_map/ppermute | solution.py:66
  39.8 14.2 %collective-permute-start.7 = (bf16[192,1024]{1,0:T(8,128)(2,1)S(1)}, bf16[192,1024]{1,0:T(8,128)(2,1)S(1)}, u32[]{:S(2)}, u32[]{:S(2)}) collective-permute-start(bf16[192,1024]{1,0:T(8,128)(2,1)S(1)} %pad_maximum_fusion.13), channel_id=1, source_target_pairs={{0,1},{1,2},{2,3},{3,0},{4,5},{5,6},{6,7},{7,4},{8,9},{9,10},{10,1... | collective-permute-start | bytes 1179656 | tf_op jit(solution)/shard_map/ppermute | solution.py:84
  54.0 28.4 %collective-permute-start.9 = (bf16[2,4,160,512]{3,2,1,0:T(8,128)(2,1)S(1)}, bf16[2,4,160,512]{3,2,1,0:T(8,128)(2,1)S(1)}, u32[]{:S(2)}, u32[]{:S(2)}) collective-permute-start(bf16[2,4,160,512]{3,2,1,0:T(8,128)(2,1)S(1)} %get-tuple-element.210), channel_id=1, source_target_pairs={{0,8},{1,9},{2,10},{3,11},{4,12},{5,13},{6,14},{7,15},{8,0},{9,1},... | collective-permute-start | bytes 3932168 | tf_op jit(solution)/shard_map/ppermute | solution.py:66
  55.6 27.9 %collective-permute-start.8 = (bf16[2,4,160,512]{3,2,1,0:T(8,128)(2,1)S(1)}, bf16[2,4,160,512]{3,2,1,0:T(8,128)(2,1)S(1)}, u32[]{:S(2)}, u32[]{:S(2)}) collective-permute-start(bf16[2,4,160,512]{3,2,1,0:T(8,128)(2,1)S(1)} %get-tuple-element.209), channel_id=1, source_target_pairs={{0,16},{1,17},{2,18},{3,19},{4,20},{5,21},{6,22},{7,23},{8,24},{9,... | collective-permute-start | bytes 3932168 | tf_op jit(solution)/shard_map/ppermute | solution.py:66
  56.1 27.8 %collective-permute-start.11 = (bf16[192,1024]{1,0:T(8,128)(2,1)S(1)}, bf16[192,1024]{1,0:T(8,128)(2,1)S(1)}, u32[]{:S(2)}, u32[]{:S(2)}) collective-permute-start(bf16[192,1024]{1,0:T(8,128)(2,1)S(1)} %pad_maximum_fusion.13), channel_id=1, source_target_pairs={{0,3},{1,0},{2,1},{3,2},{4,7},{5,4},{6,5},{7,6},{8,11},{9,8},{10,9... | collective-permute-start | bytes 1179656 | tf_op jit(solution)/shard_map/ppermute | solution.py:84
  61.9 22.0 %collective-permute-start.10 = (bf16[192,1024]{1,0:T(8,128)(2,1)S(1)}, bf16[192,1024]{1,0:T(8,128)(2,1)S(1)}, u32[]{:S(2)}, u32[]{:S(2)}) collective-permute-start(bf16[192,1024]{1,0:T(8,128)(2,1)S(1)} %pad_maximum_fusion.13), channel_id=1, source_target_pairs={{0,2},{1,3},{2,0},{3,1},{4,6},{5,7},{6,4},{7,5},{8,10},{9,11},{10,... | collective-permute-start | bytes 1179656 | tf_op jit(solution)/shard_map/ppermute | solution.py:84
  84.6 13.9 %collective-permute-start.12 = (bf16[4,4,160,1024]{3,2,1,0:T(8,128)(2,1)S(1)}, bf16[4,4,160,1024]{3,2,1,0:T(8,128)(2,1)S(1)}, u32[]{:S(2)}, u32[]{:S(2)}) collective-permute-start(bf16[4,4,160,1024]{3,2,1,0:T(8,128)(2,1)S(1)} %constant_dynamic-update-slice_fusion.refs_3_.refs_9_.refs_12_), channel_id=1, source_target_pairs={{0,4},{1,5},{2,6},{3,7},{4,0},{5,1},{6,2},{7,3},{8,12},{9,13},{10,... | collective-permute-start | bytes 15728648 | tf_op jit(solution)/shard_map/ppermute | solution.py:66
  100.8 18.9 %collective-permute-start.15 = (bf16[2,4,96,512]{3,2,1,0:T(8,128)(2,1)S(1)}, bf16[2,4,96,512]{3,2,1,0:T(8,128)(2,1)}, u32[]{:S(2)}, u32[]{:S(2)}) collective-permute-start(bf16[2,4,96,512]{3,2,1,0:T(8,128)(2,1)S(1)} %maximum_bitcast_fusion.3), channel_id=1, source_target_pairs={{0,16},{1,17},{2,18},{3,19},{4,20},{5,21},{6,22},{7,23},{8,24},{9,... | collective-permute-start | bytes 2359304 | tf_op jit(solution)/shard_map/ppermute | solution.py:66
  102.0 19.3 %collective-permute-start.16 = (bf16[2,4,96,512]{3,2,1,0:T(8,128)(2,1)S(1)}, bf16[2,4,96,512]{3,2,1,0:T(8,128)(2,1)}, u32[]{:S(2)}, u32[]{:S(2)}) collective-permute-start(bf16[2,4,96,512]{3,2,1,0:T(8,128)(2,1)S(1)} %maximum_bitcast_fusion.4), channel_id=1, source_target_pairs={{0,8},{1,9},{2,10},{3,11},{4,12},{5,13},{6,14},{7,15},{8,0},{9,1},... | collective-permute-start | bytes 2359304 | tf_op jit(solution)/shard_map/ppermute | solution.py:66
  123.2 18.9 %collective-permute-start.19 = (bf16[4,4,96,1024]{3,2,1,0:T(8,128)(2,1)S(1)}, bf16[4,4,96,1024]{3,2,1,0:T(8,128)(2,1)S(1)}, u32[]{:S(2)}, u32[]{:S(2)}) collective-permute-start(bf16[4,4,96,1024]{3,2,1,0:T(8,128)(2,1)S(1)} %pad_maximum_fusion.refs_6_.refs_5_), channel_id=1, source_target_pairs={{0,4},{1,5},{2,6},{3,7},{4,0},{5,1},{6,2},{7,3},{8,12},{9,13},{10,... | collective-permute-start | bytes 9437192 | tf_op jit(solution)/shard_map/ppermute | solution.py:66
  124.5 17.3 %collective-permute-start.18 = (bf16[256,1024]{1,0:T(8,128)(2,1)S(1)}, bf16[256,1024]{1,0:T(8,128)(2,1)S(1)}, u32[]{:S(2)}, u32[]{:S(2)}) collective-permute-start(bf16[256,1024]{1,0:T(8,128)(2,1)S(1)} %get-tuple-element.230.refs_0_), channel_id=1, source_target_pairs={{3,2},{2,1},{1,0},{7,6},{6,5},{5,4},{11,10},{10,9},{9,8},{15,14},{... | collective-permute-start | bytes 1572872 | tf_op jit(solution)/shard_map/ppermute | solution.py:88
  125.8 16.4 %collective-permute-start.17 = (bf16[256,1024]{1,0:T(8,128)(2,1)S(1)}, bf16[256,1024]{1,0:T(8,128)(2,1)S(1)}, u32[]{:S(2)}, u32[]{:S(2)}) collective-permute-start(bf16[256,1024]{1,0:T(8,128)(2,1)S(1)} %get-tuple-element.230.refs_0_), channel_id=1, source_target_pairs={{0,1},{1,2},{2,3},{4,5},{5,6},{6,7},{8,9},{9,10},{10,11},{12,13},{... | collective-permute-start | bytes 1572872 | tf_op jit(solution)/shard_map/ppermute | solution.py:88
  142.1 18.3 %collective-permute-start.26 = (bf16[2,4,96,512]{3,2,1,0:T(8,128)(2,1)S(1)}, bf16[2,4,96,512]{3,2,1,0:T(8,128)(2,1)S(1)}, u32[]{:S(2)}, u32[]{:S(2)}) collective-permute-start(bf16[2,4,96,512]{3,2,1,0:T(8,128)(2,1)S(1)} %maximum_bitcast_fusion.6), channel_id=1, source_target_pairs={{0,8},{1,9},{2,10},{3,11},{4,12},{5,13},{6,14},{7,15},{8,0},{9,1},... | collective-permute-start | bytes 2359304 | tf_op jit(solution)/shard_map/ppermute | solution.py:66
  143.6 18.0 %collective-permute-start.25 = (bf16[2,4,96,512]{3,2,1,0:T(8,128)(2,1)S(1)}, bf16[2,4,96,512]{3,2,1,0:T(8,128)(2,1)S(1)}, u32[]{:S(2)}, u32[]{:S(2)}) collective-permute-start(bf16[2,4,96,512]{3,2,1,0:T(8,128)(2,1)S(1)} %maximum_bitcast_fusion.5), channel_id=1, source_target_pairs={{0,16},{1,17},{2,18},{3,19},{4,20},{5,21},{6,22},{7,23},{8,24},{9,... | collective-permute-start | bytes 2359304 | tf_op jit(solution)/shard_map/ppermute | solution.py:66
  144.2 31.6 %collective-permute-start.22 = (bf16[256,1024]{1,0:T(8,128)(2,1)S(1)}, bf16[256,1024]{1,0:T(8,128)(2,1)S(1)}, u32[]{:S(2)}, u32[]{:S(2)}) collective-permute-start(bf16[256,1024]{1,0:T(8,128)(2,1)S(1)} %collective-permute-done.17.refs_1_), channel_id=1, source_target_pairs={{1,2},{2,3},{5,6},{6,7},{9,10},{10,11},{13,14},{14,15},{17,18},{18... | collective-permute-start | bytes 1572872 | tf_op jit(solution)/shard_map/ppermute | solution.py:88
  144.9 30.9 %collective-permute-start.23 = (bf16[256,1024]{1,0:T(8,128)(2,1)S(1)}, bf16[256,1024]{1,0:T(8,128)(2,1)S(1)}, u32[]{:S(2)}, u32[]{:S(2)}) collective-permute-start(bf16[256,1024]{1,0:T(8,128)(2,1)S(1)} %collective-permute-done.18.refs_2_), channel_id=1, source_target_pairs={{2,1},{1,0},{6,5},{5,4},{10,9},{9,8},{14,13},{13,12},{18,17},{17,1... | collective-permute-start | bytes 1572872 | tf_op jit(solution)/shard_map/ppermute | solution.py:88
  146.3 29.5 %collective-permute-start.24 = (bf16[256,1024]{1,0:T(8,128)(2,1)S(1)}, bf16[256,1024]{1,0:T(8,128)(2,1)S(1)}, u32[]{:S(2)}, u32[]{:S(2)}) collective-permute-start(bf16[256,1024]{1,0:T(8,128)(2,1)S(1)} %broadcast_select_fusion.1), channel_id=1, source_target_pairs={{1,3},{2,0},{5,7},{6,4},{9,11},{10,8},{13,15},{14,12},{17,19},{18,... | collective-permute-start | bytes 1572872 | tf_op jit(solution)/shard_map/ppermute | solution.py:88
  175.8 12.3 %collective-permute-start.27 = (bf16[4,4,96,1024]{3,2,1,0:T(8,128)(2,1)S(1)}, bf16[4,4,96,1024]{3,2,1,0:T(8,128)(2,1)}, u32[]{:S(2)}, u32[]{:S(2)}) collective-permute-start(bf16[4,4,96,1024]{3,2,1,0:T(8,128)(2,1)S(1)} %pad_maximum_fusion.1.refs_4_), channel_id=1, source_target_pairs={{0,4},{1,5},{2,6},{3,7},{4,0},{5,1},{6,2},{7,3},{8,12},{9,13},{10,... | collective-permute-start | bytes 9437192 | tf_op jit(solution)/shard_map/ppermute | solution.py:66
  200.3 26.3 %collective-permute-start.31 = (bf16[4,3,128,1024]{3,2,1,0:T(8,128)(2,1)}, bf16[4,3,128,1024]{3,2,1,0:T(8,128)(2,1)}, u32[]{:S(2)}, u32[]{:S(2)}) collective-permute-start(bf16[4,3,128,1024]{3,2,1,0:T(8,128)(2,1)} %get-tuple-element.261), channel_id=1, source_target_pairs={{0,4},{1,5},{2,6},{3,7},{4,0},{5,1},{6,2},{7,3},{8,12},{9,13},{10,... | collective-permute-start | bytes 9437192 | tf_op jit(solution)/shard_map/ppermute | solution.py:66
  222.1 14.3 %collective-permute-start.29 = (bf16[256,1024]{1,0:T(8,128)(2,1)S(1)}, bf16[256,1024]{1,0:T(8,128)(2,1)S(1)}, u32[]{:S(2)}, u32[]{:S(2)}) collective-permute-start(bf16[256,1024]{1,0:T(8,128)(2,1)S(1)} %get-tuple-element.468), channel_id=1, source_target_pairs={{3,2},{2,1},{7,6},{6,5},{11,10},{10,9},{15,14},{14,13},{19,18},{18... | collective-permute-start | bytes 1572872 | tf_op jit(solution)/shard_map/ppermute | solution.py:88
  222.9 13.6 %collective-permute-start.28 = (bf16[256,1024]{1,0:T(8,128)(2,1)S(1)}, bf16[256,1024]{1,0:T(8,128)(2,1)S(1)}, u32[]{:S(2)}, u32[]{:S(2)}) collective-permute-start(bf16[256,1024]{1,0:T(8,128)(2,1)S(1)} %get-tuple-element.468), channel_id=1, source_target_pairs={{0,1},{1,2},{4,5},{5,6},{8,9},{9,10},{12,13},{13,14},{16,17},{17,1... | collective-permute-start | bytes 1572872 | tf_op jit(solution)/shard_map/ppermute | solution.py:88
  229.1 20.0 %collective-permute-start.32 = (bf16[2,3,128,512]{3,2,1,0:T(8,128)(2,1)S(1)}, bf16[2,3,128,512]{3,2,1,0:T(8,128)(2,1)S(1)}, u32[]{:S(2)}, u32[]{:S(2)}) collective-permute-start(bf16[2,3,128,512]{3,2,1,0:T(8,128)(2,1)S(1)} %fusion.9), channel_id=1, source_target_pairs={{0,8},{1,9},{2,10},{3,11},{4,12},{5,13},{6,14},{7,15},{8,0},{9,1},... | collective-permute-start | bytes 2359304 | tf_op jit(solution)/shard_map/ppermute | solution.py:66
  230.4 19.7 %collective-permute-start.33 = (bf16[2,3,128,512]{3,2,1,0:T(8,128)(2,1)S(1)}, bf16[2,3,128,512]{3,2,1,0:T(8,128)(2,1)S(1)}, u32[]{:S(2)}, u32[]{:S(2)}) collective-permute-start(bf16[2,3,128,512]{3,2,1,0:T(8,128)(2,1)S(1)} %fusion.10), channel_id=1, source_target_pairs={{0,16},{1,17},{2,18},{3,19},{4,20},{5,21},{6,22},{7,23},{8,24},{9,... | collective-permute-start | bytes 2359304 | tf_op jit(solution)/shard_map/ppermute | solution.py:66
  231.2 16.4 %collective-permute-start.30 = (bf16[256,1024]{1,0:T(8,128)(2,1)S(1)}, bf16[256,1024]{1,0:T(8,128)(2,1)S(1)}, u32[]{:S(2)}, u32[]{:S(2)}) collective-permute-start(bf16[256,1024]{1,0:T(8,128)(2,1)S(1)} %broadcast_select_fusion), channel_id=1, source_target_pairs={{0,2},{3,1},{4,6},{7,5},{8,10},{11,9},{12,14},{15,13},{16,18},{19,... | collective-permute-start | bytes 1572872 | tf_op jit(solution)/shard_map/ppermute | solution.py:88
  250.9 16.8 %collective-permute-start.35 = (bf16[256,1024]{1,0:T(8,128)(2,1)S(1)}, bf16[256,1024]{1,0:T(8,128)(2,1)S(1)}, u32[]{:S(2)}, u32[]{:S(2)}) collective-permute-start(bf16[256,1024]{1,0:T(8,128)(2,1)S(1)} %get-tuple-element.510), channel_id=1, source_target_pairs={{3,2},{2,1},{1,0},{7,6},{6,5},{5,4},{11,10},{10,9},{9,8},{15,14},{... | collective-permute-start | bytes 1572872 | tf_op jit(solution)/shard_map/ppermute | solution.py:88
  252.2 15.5 %collective-permute-start.34 = (bf16[256,1024]{1,0:T(8,128)(2,1)S(1)}, bf16[256,1024]{1,0:T(8,128)(2,1)S(1)}, u32[]{:S(2)}, u32[]{:S(2)}) collective-permute-start(bf16[256,1024]{1,0:T(8,128)(2,1)S(1)} %get-tuple-element.511), channel_id=1, source_target_pairs={{0,1},{1,2},{2,3},{4,5},{5,6},{6,7},{8,9},{9,10},{10,11},{12,13},{... | collective-permute-start | bytes 1572872 | tf_op jit(solution)/shard_map/ppermute | solution.py:88
  276.5 23.5 %collective-permute-start.41 = (bf16[3,32,1024]{2,1,0:T(8,128)(2,1)S(1)}, bf16[3,32,1024]{2,1,0:T(8,128)(2,1)S(1)}, u32[]{:S(2)}, u32[]{:S(2)}) collective-permute-start(bf16[3,32,1024]{2,1,0:T(8,128)(2,1)S(1)} %pad_maximum_fusion.17), channel_id=1, source_target_pairs={{0,1},{1,0},{2,3},{3,2},{4,5},{5,4},{6,7},{7,6},{8,9},{9,8},{10,11... | collective-permute-start | bytes 589832 | tf_op jit(solution)/shard_map/ppermute | solution.py:66
  278.3 21.9 %collective-permute-start.40 = (bf16[2,3,128,512]{3,2,1,0:T(8,128)(2,1)S(1)}, bf16[2,3,128,512]{3,2,1,0:T(8,128)(2,1)}, u32[]{:S(2)}, u32[]{:S(2)}) collective-permute-start(bf16[2,3,128,512]{3,2,1,0:T(8,128)(2,1)S(1)} %fusion.12), channel_id=1, source_target_pairs={{0,16},{1,17},{2,18},{3,19},{4,20},{5,21},{6,22},{7,23},{8,24},{9,... | collective-permute-start | bytes 2359304 | tf_op jit(solution)/shard_map/ppermute | solution.py:66
  279.2 21.0 %collective-permute-start.39 = (bf16[2,3,128,512]{3,2,1,0:T(8,128)(2,1)S(1)}, bf16[2,3,128,512]{3,2,1,0:T(8,128)(2,1)S(1)}, u32[]{:S(2)}, u32[]{:S(2)}) collective-permute-start(bf16[2,3,128,512]{3,2,1,0:T(8,128)(2,1)S(1)} %fusion.11), channel_id=1, source_target_pairs={{0,8},{1,9},{2,10},{3,11},{4,12},{5,13},{6,14},{7,15},{8,0},{9,1},... | collective-permute-start | bytes 2359304 | tf_op jit(solution)/shard_map/ppermute | solution.py:66
  280.2 19.9 %collective-permute-start.42 = (bf16[3,32,1024]{2,1,0:T(8,128)(2,1)S(1)}, bf16[3,32,1024]{2,1,0:T(8,128)(2,1)S(1)}, u32[]{:S(2)}, u32[]{:S(2)}) collective-permute-start(bf16[3,32,1024]{2,1,0:T(8,128)(2,1)S(1)} %pad_maximum_fusion.18), channel_id=1, source_target_pairs={{0,2},{1,3},{2,0},{3,1},{4,6},{5,7},{6,4},{7,5},{8,10},{9,11},{10,... | collective-permute-start | bytes 589832 | tf_op jit(solution)/shard_map/ppermute | solution.py:66
  281.6 18.5 %collective-permute-start.43 = (bf16[3,32,1024]{2,1,0:T(8,128)(2,1)S(1)}, bf16[3,32,1024]{2,1,0:T(8,128)(2,1)S(1)}, u32[]{:S(2)}, u32[]{:S(2)}) collective-permute-start(bf16[3,32,1024]{2,1,0:T(8,128)(2,1)S(1)} %pad_maximum_fusion.19), channel_id=1, source_target_pairs={{0,3},{1,2},{2,1},{3,0},{4,7},{5,6},{6,5},{7,4},{8,11},{9,10},{10,... | collective-permute-start | bytes 589832 | tf_op jit(solution)/shard_map/ppermute | solution.py:66
  301.2 11.7 %collective-permute-start.45 = (bf16[4,3,128,1024]{3,2,1,0:T(8,128)(2,1)}, bf16[4,3,128,1024]{3,2,1,0:T(8,128)(2,1)}, u32[]{:S(2)}, u32[]{:S(2)}) collective-permute-start(bf16[4,3,128,1024]{3,2,1,0:T(8,128)(2,1)} %get-tuple-element.323), channel_id=1, source_target_pairs={{0,4},{1,5},{2,6},{3,7},{4,0},{5,1},{6,2},{7,3},{8,12},{9,13},{10,... | collective-permute-start | bytes 9437192 | tf_op jit(solution)/shard_map/ppermute | solution.py:66
  317.1 29.7 %collective-permute-start.52 = (bf16[2,5,128,512]{3,2,1,0:T(8,128)(2,1)S(1)}, bf16[2,5,128,512]{3,2,1,0:T(8,128)(2,1)S(1)}, u32[]{:S(2)}, u32[]{:S(2)}) collective-permute-start(bf16[2,5,128,512]{3,2,1,0:T(8,128)(2,1)S(1)} %fusion.3), channel_id=1, source_target_pairs={{0,8},{1,9},{2,10},{3,11},{4,12},{5,13},{6,14},{7,15},{8,0},{9,1},... | collective-permute-start | bytes 3932168 | tf_op jit(solution)/shard_map/ppermute | solution.py:66
  319.1 29.4 %collective-permute-start.53 = (bf16[2,5,128,512]{3,2,1,0:T(8,128)(2,1)S(1)}, bf16[2,5,128,512]{3,2,1,0:T(8,128)(2,1)S(1)}, u32[]{:S(2)}, u32[]{:S(2)}) collective-permute-start(bf16[2,5,128,512]{3,2,1,0:T(8,128)(2,1)S(1)} %fusion.4), channel_id=1, source_target_pairs={{0,16},{1,17},{2,18},{3,19},{4,20},{5,21},{6,22},{7,23},{8,24},{9,... | collective-permute-start | bytes 3932168 | tf_op jit(solution)/shard_map/ppermute | solution.py:66
  321.7 12.2 %collective-permute-start.49 = (bf16[264,512]{1,0:T(8,128)(2,1)S(1)}, bf16[264,512]{1,0:T(8,128)(2,1)S(1)}, u32[]{:S(2)}, u32[]{:S(2)}) collective-permute-start(bf16[264,512]{1,0:T(8,128)(2,1)S(1)} %get-tuple-element.500), channel_id=1, source_target_pairs={{0,3},{1,0},{2,1},{3,2},{4,7},{5,4},{6,5},{7,6},{8,11},{9,8},{10,9... | collective-permute-start | bytes 811016 | tf_op jit(solution)/shard_map/ppermute | solution.py:84
  323.3 14.7 %collective-permute-start.51 = (bf16[264,512]{1,0:T(8,128)(2,1)S(1)}, bf16[264,512]{1,0:T(8,128)(2,1)S(1)}, u32[]{:S(2)}, u32[]{:S(2)}) collective-permute-start(bf16[264,512]{1,0:T(8,128)(2,1)S(1)} %get-tuple-element.501), channel_id=1, source_target_pairs={{0,1},{1,2},{2,3},{3,0},{4,5},{5,6},{6,7},{7,4},{8,9},{9,10},{10,1... | collective-permute-start | bytes 811016 | tf_op jit(solution)/shard_map/ppermute | solution.py:84
  323.7 22.6 %collective-permute-start.50 = (bf16[264,512]{1,0:T(8,128)(2,1)S(1)}, bf16[264,512]{1,0:T(8,128)(2,1)S(1)}, u32[]{:S(2)}, u32[]{:S(2)}) collective-permute-start(bf16[264,512]{1,0:T(8,128)(2,1)S(1)} %get-tuple-element.502), channel_id=1, source_target_pairs={{0,2},{1,3},{2,0},{3,1},{4,6},{5,7},{6,4},{7,5},{8,10},{9,11},{10,... | collective-permute-start | bytes 811016 | tf_op jit(solution)/shard_map/ppermute | solution.py:84
  351.2 15.5 %collective-permute-start.55 = (bf16[3,32,1024]{2,1,0:T(8,128)(2,1)S(1)}, bf16[3,32,1024]{2,1,0:T(8,128)(2,1)S(1)}, u32[]{:S(2)}, u32[]{:S(2)}) collective-permute-start(bf16[3,32,1024]{2,1,0:T(8,128)(2,1)S(1)} %pad_maximum_fusion.21), channel_id=1, source_target_pairs={{0,2},{1,3},{2,0},{3,1},{4,6},{5,7},{6,4},{7,5},{8,10},{9,11},{10,... | collective-permute-start | bytes 589832 | tf_op jit(solution)/shard_map/ppermute | solution.py:66
  352.9 14.4 %collective-permute-start.58 = (bf16[1,5,128,512]{3,2,1,0:T(8,128)(2,1)S(1)}, bf16[1,5,128,512]{3,2,1,0:T(8,128)(2,1)S(1)}, u32[]{:S(2)}, u32[]{:S(2)}) collective-permute-start(bf16[1,5,128,512]{3,2,1,0:T(8,128)(2,1)S(1)} %add_convert_fusion.7), channel_id=1, source_target_pairs={{0,8},{1,9},{2,10},{3,11},{4,12},{5,13},{6,14},{7,15},{8,0},{9,1},... | collective-permute-start | bytes 1966088 | tf_op jit(solution)/shard_map/ppermute | solution.py:66
  353.9 14.0 %collective-permute-start.57 = (bf16[1,5,128,512]{3,2,1,0:T(8,128)(2,1)S(1)}, bf16[1,5,128,512]{3,2,1,0:T(8,128)(2,1)S(1)}, u32[]{:S(2)}, u32[]{:S(2)}) collective-permute-start(bf16[1,5,128,512]{3,2,1,0:T(8,128)(2,1)S(1)} %add_convert_fusion.8), channel_id=1, source_target_pairs={{0,16},{1,17},{2,18},{3,19},{4,20},{5,21},{6,22},{7,23},{8,24},{9,... | collective-permute-start | bytes 1966088 | tf_op jit(solution)/shard_map/ppermute | solution.py:66
  370.4 21.5 %collective-permute-start.65 = (bf16[5,32,1024]{2,1,0:T(8,128)(2,1)S(1)}, bf16[5,32,1024]{2,1,0:T(8,128)(2,1)S(1)}, u32[]{:S(2)}, u32[]{:S(2)}) collective-permute-start(bf16[5,32,1024]{2,1,0:T(8,128)(2,1)S(1)} %pad_maximum_fusion.16), channel_id=1, source_target_pairs={{0,3},{1,2},{2,1},{3,0},{4,7},{5,6},{6,5},{7,4},{8,11},{9,10},{10,... | collective-permute-start | bytes 983048 | tf_op jit(solution)/shard_map/ppermute | solution.py:66
  372.9 25.9 %collective-permute-start.64 = (bf16[5,32,1024]{2,1,0:T(8,128)(2,1)S(1)}, bf16[5,32,1024]{2,1,0:T(8,128)(2,1)S(1)}, u32[]{:S(2)}, u32[]{:S(2)}) collective-permute-start(bf16[5,32,1024]{2,1,0:T(8,128)(2,1)S(1)} %pad_maximum_fusion.15), channel_id=1, source_target_pairs={{0,2},{1,3},{2,0},{3,1},{4,6},{5,7},{6,4},{7,5},{8,10},{9,11},{10,... | collective-permute-start | bytes 983048 | tf_op jit(solution)/shard_map/ppermute | solution.py:66
  373.0 25.8 %collective-permute-start.63 = (bf16[5,32,1024]{2,1,0:T(8,128)(2,1)S(1)}, bf16[5,32,1024]{2,1,0:T(8,128)(2,1)S(1)}, u32[]{:S(2)}, u32[]{:S(2)}) collective-permute-start(bf16[5,32,1024]{2,1,0:T(8,128)(2,1)S(1)} %pad_maximum_fusion.14), channel_id=1, source_target_pairs={{0,1},{1,0},{2,3},{3,2},{4,5},{5,4},{6,7},{7,6},{8,9},{9,8},{10,11... | collective-permute-start | bytes 983048 | tf_op jit(solution)/shard_map/ppermute | solution.py:66
  (76 other events, 579.6 us)
